TPU v7x, 256 devices: a whole 4x4x8 slice. The times are simulated.
256 devices in a mesh: term: 16 (over x, y), sector: 16 (over z, core).
Axes of the slice: x: 4, y: 4, z: 8, core: 2. Of those that a mesh axis runs over, the one named last changes fastest.
Arguments:
- wavefunction: float32 [16, 512, 512], P('sector'), may hold values from -120 to 120
- precond: float32 [16, 512, 512], P('sector', 'term'), may hold values from 0.05 to 4
- left_ops: float32 [16, 64, 512, 512], P('sector', 'term'), may hold values from -0.5 to 4.5
- right_ops: float32 [16, 64, 512, 512], P('sector', 'term'), may hold values from -1 to 2
- out_sector: int32 [16, 64], P('sector', 'term'), may hold values from 0 to 15, as said below
- live_counts: int32 [16, 16], P('sector', 'term'), may hold values from 1 to 4, as said below
Outputs:
- first_image: float32 [16, 512, 512], P('sector', 'term')
- correction: float32 [16, 512, 512], P('sector', 'term')
- second_image: float32 [16, 512, 512], P('sector', 'term')
Inputs may be any that keep to these rules, and one draw needn't show every extreme that they name: Each term moves the charge by at most one sector: out_sector[s, j] differs from s by at most 1. `live_counts`: in every sector some device has all 4 slots live.
All inputs are finite; a program needn't handle non-finite values.
Results may differ from a plain program's by a relative error of at most 0.0003.
Values sent between devices are 32-bit elements; how exact they have to be, the bound alone decides.
No kernel may reach another device: no remote copies, remote signals or barrier semaphores. Data moves between devices by JAX's collectives and lax.ppermute only.
A program may use at most 64 MiB of HBM per device.

v0:
```python
import functools

import jax
import jax.numpy as jnp
from jax import lax
from jax.sharding import Mesh
from jax.sharding import PartitionSpec as P

TERM = ("term_0", "term_1")
SECTOR = ("sector_0", "sector_1")
TERM_SECTOR = ("term_0", "term_1", "sector_0", "sector_1")


def from_partner(value, axis, apart):
    mask = 2**apart
    pairs = [(source, source ^ mask) for source in range(lax.axis_size(axis))]
    return lax.ppermute(value, axis, pairs)


def from_behind(block, axis, distance):
    devices = range(lax.axis_size(axis))
    route = [(i - distance, i) for i in devices if i - distance in devices]
    return lax.ppermute(block, axis, route)


def split_up(x, dim, peers):
    shape = x.shape
    blocks = x.reshape(*shape[:dim], peers, shape[dim] // peers, *shape[dim + 1 :])
    return jnp.moveaxis(blocks, dim, 0)


def summed_on_arrival(x, axis, dim):
    blocks = split_up(x, dim, lax.axis_size(axis))
    arrived = lax.all_to_all(blocks, axis, split_axis=0, concat_axis=0, tiled=True)
    return arrived.sum(axis=0)


def over_axes(x, axes):
    return functools.reduce(lax.psum, axes, x)


def in_order(blocks, dim):
    blocks = jnp.moveaxis(blocks, 0, dim)
    shape = blocks.shape
    return blocks.reshape(*shape[:dim], shape[dim] * shape[dim + 1], *shape[dim + 2 :])


def sent_to_all(x, axis):
    peers = lax.axis_size(axis)
    return lax.all_to_all(jnp.broadcast_to(x[None], (peers, *x.shape)), axis, 0, 0, tiled=True)


def gathered_copies(x, axis, dim):
    return in_order(sent_to_all(x, axis), dim)


def matmul(first_op, second_op):
    return jnp.dot(
        first_op, second_op, precision=lax.Precision.HIGHEST, preferred_element_type=jnp.float32
    )


def term_rows(vector, left_stack, right_stack, offsets, kept, migrated, row_count):
    width = vector.shape[1]
    totals = jnp.zeros((row_count, 3, width), jnp.float32)

    def add_slot(slot_id, running):
        left_rows = left_stack[slot_id]
        product = matmul(matmul(left_rows, vector), right_stack[slot_id])
        return running.at[:, offsets[slot_id]].add(product)

    totals = lax.fori_loop(jnp.zeros((), jnp.int32), kept, add_slot, totals)
    accepted, moved_left, moved_right, moved_offset = migrated

    def add_moved(running):
        product = matmul(matmul(moved_left, vector), moved_right)
        return running.at[:, moved_offset].add(product)

    totals = lax.cond(accepted, add_moved, lambda running: running, totals)
    return totals.reshape(row_count, 3 * width)


def per_device(wavefunction, precond, left_ops, right_ops, out_sector, live_counts):
    term_count = lax.axis_size(TERM)
    width = wavefunction.shape[1]
    slab_rows = width // term_count
    first_own = lax.axis_index(TERM) * slab_rows
    sector_id = lax.axis_index(SECTOR)
    center = wavefunction[0]
    left_stack = left_ops[0]
    right_stack = right_ops[0]
    offsets = out_sector[0] - sector_id + 1
    count_here = live_counts[0, 0]
    last_slot = jnp.maximum(count_here - 1, 0)
    send_left = lax.dynamic_index_in_dim(left_stack, last_slot, 0, keepdims=False)
    send_right = lax.dynamic_index_in_dim(right_stack, last_slot, 0, keepdims=False)
    send_meta = jnp.stack([count_here, offsets[last_slot]]).astype(jnp.float32)
    top_bit = term_count.bit_length() - 2
    got_left, got_right, got_meta = from_partner((send_left, send_right, send_meta), TERM, top_bit)
    partner_count = got_meta[0].astype(jnp.int32)
    giving = count_here - partner_count >= 2
    accepted = partner_count - count_here >= 2
    kept = count_here - giving.astype(jnp.int32)
    migrated = (accepted, got_left, got_right, got_meta[1].astype(jnp.int32))

    def apply_hamiltonian(vector):
        whole = term_rows(vector, left_stack, right_stack, offsets, kept, migrated, width).reshape(
            width, 3, width
        )
        upward = from_behind(whole[:, 2], SECTOR, 1)
        downward = from_behind(whole[:, 0], SECTOR, -1)
        return summed_on_arrival(whole[:, 1] + upward + downward, TERM, 0)

    first_image = apply_hamiltonian(center)
    own_rows = lax.dynamic_slice_in_dim(center, first_own, slab_rows, 0)
    scaling = precond[0]
    cross, norm_sq, scaled_cross, scaled_norm = (
        over_axes(jnp.sum(own_rows * first_image), TERM_SECTOR),
        over_axes(jnp.sum(own_rows * own_rows), TERM_SECTOR),
        over_axes(jnp.sum(own_rows * scaling * first_image), TERM_SECTOR),
        over_axes(jnp.sum(own_rows * scaling * own_rows), TERM_SECTOR),
    )
    rayleigh = cross / norm_sq
    raw = scaling * (first_image - rayleigh * own_rows)
    correlation_sum = scaled_cross - rayleigh * scaled_norm
    correction = raw - correlation_sum / norm_sq * own_rows
    full_correction = gathered_copies(correction, TERM, 0)
    second_image = apply_hamiltonian(full_correction)
    return (first_image[None], correction[None], second_image[None])


def solution(mesh):
    torus = Mesh(mesh.devices.reshape(4, 4, 8, 2), ("term_0", "term_1", "sector_0", "sector_1"))
    placed = (
        P(SECTOR, None, None),
        P(SECTOR, TERM, None),
        P(SECTOR, TERM, None, None),
        P(SECTOR, TERM, None, None),
        P(SECTOR, TERM),
        P(SECTOR, TERM),
    )
    return jax.shard_map(
        per_device,
        mesh=torus,
        in_specs=placed,
        out_specs=(P(SECTOR, TERM, None), P(SECTOR, TERM, None), P(SECTOR, TERM, None)),
        check_vma=False,
    )
```

profile of v0, /device:TPU:64, one launch (start us, length us, event | category | flops | bytes accessed | tf_op | source)
XLA Modules:
  0.0 263.6 jit_solution(5863111210950391909)
XLA Ops:
  0.6 0.0 copy-start.4
  1.3 0.7 subtract_add_fusion
  2.0 0.6 constant_dynamic-slice_fusion
  2.5 0.7 add_convert_fusion
  3.3 3.0 %collective-permute-start = (f32[2]{0:T(128)S(1)}, f32[2]{0:T(128)S(1)}, u32[]{:S(2)}, u32[]{:S(2)}) collective-permute-start(f32[2]{0:T(128)S(1)} %add_convert_fusion), channel_id=1, source_target_pairs={{0,128},{16,144},{32,160},{48,176},{64,192},{80,208},{96,224},{112... | collective-permute-start | bytes 32 | tf_op jit(solution)/shard_map/ppermute | solution.py:17
  6.3 2.3 dynamic-slice_bitcast_fusion.1
  8.6 0.0 copy-start.3
  8.6 0.5 collective-permute-start.1
  9.1 2.3 dynamic-slice_bitcast_fusion
  11.4 3.0 %collective-permute-start.2 = (f32[512,512]{1,0:T(8,128)}, f32[512,512]{1,0:T(8,128)}, u32[]{:S(2)}, u32[]{:S(2)}) collective-permute-start(f32[512,512]{1,0:T(8,128)} %dynamic-slice_bitcast_fusion), channel_id=1, source_target_pairs={{0,128},{16,144},{32,160},{48,176},{64,192},{80,208},{96,224},{112... | collective-permute-start | bytes 3145736 | tf_op jit(solution)/shard_map/ppermute | solution.py:17
  14.5 0.0 copy-done.4
  14.5 0.0 collective-permute-done
  14.5 0.6 fusion.25
  15.7 0.4 broadcast.89.clone
  16.1 0.0 copy-done.3
  16.1 10.4 %while.30 = (s32[]{:T(128)}, f32[512,3,512]{2,0,1:T(8,128)S(1)}, s32[]{:T(128)}, s32[4]{0:T(128)S(1)}, f32[4,512,512]{2,1,0:T(8,128)}, /*index=5*/f32[512,512]{1...) while((s32[]{:T(128)}, f32[512,3,512]{2,0,1:T(8,128)S(1)}, ...), condition=%wide.region_2.3_spmd, body=%wide.region_0.2_spmd.sunk | while | flops 3221749760 | bytes 7341290 | solution.py:72
  16.1 0.6 dynamic_slice.73
  18.7 0.7 and_reduce_fusion.6
  19.4 3.4 %fusion.57 = f32[512,512]{1,0:T(8,128)S(1)} fusion(f32[512,512]{1,0:T(8,128)} %get-tuple-element.340, f32[4,512,512]{2,1,0:T(8,128)} %get-tuple-element.339, s32[]{:T(128)S(6)} %select_n.42), kind=kOutput, calls=%fused_computation.4.clone.1 | convolution fusion | flops 1610612736 | bytes 3145732 | tf_op jit(solution)/shard_map/while/body/dot_general | solution.py:58
  22.8 3.7 %fusion.58 = f32[512,3,512]{2,0,1:T(8,128)S(1)} fusion(f32[512,3,512]{2,0,1:T(8,128)S(1)} %get-tuple-element.323, s32[]{:T(128)} %select_n.43, f32[512,512]{1,0:T(8,128)S(1)} %fusion.57, f32[4,512,512]{2,1,0:T(8,128)} %get-tuple-element.341, s32[]{:T(128)S(6)} %select_n.42, pred[]{:T(512)} %and_reduce_fusion.6), kind=kOutput, calls=%fused_computation.2.clone.1 | convolution fusion | flops 1611137024 | bytes 4195332 | tf_op jit(solution)/shard_map/while/body/dot_general | solution.py:58
  27.2 9.3 %collective-permute-done.1 = f32[512,512]{1,0:T(8,128)} collective-permute-done((f32[512,512]{1,0:T(8,128)}, f32[512,512]{1,0:T(8,128)}, u32[]{:S(2)}, u32[]{:S(2)}) %collective-permute-start.1) | collective-permute-done | bytes 1048608 | tf_op jit(solution)/shard_map/ppermute | solution.py:17
  36.5 21.0 %collective-permute-done.2 = f32[512,512]{1,0:T(8,128)} collective-permute-done((f32[512,512]{1,0:T(8,128)}, f32[512,512]{1,0:T(8,128)}, u32[]{:S(2)}, u32[]{:S(2)}) %collective-permute-start.2) | collective-permute-done | bytes 1048608 | tf_op jit(solution)/shard_map/ppermute | solution.py:17
  57.5 0.2 slice_bitcast_fusion.4
  57.7 1.9 collective-permute-start.3
  59.6 0.0 copy-start.1
  59.6 3.8 %collective-permute-start.4 = (f32[512,512]{1,0:T(8,128)S(1)}, f32[512,512]{1,0:T(8,128)S(1)}, u32[]{:S(2)}, u32[]{:S(2)}) collective-permute-start(f32[512,512]{1,0:T(8,128)S(1)} %get-tuple-element.218), channel_id=1, source_target_pairs={{1,0},{2,1},{3,2},{4,3},{5,4},{6,5},{7,6},{8,7},{9,8},{10,9},{11,1... | collective-permute-start | bytes 3145736 | tf_op jit(solution)/shard_map/ppermute | solution.py:23
  63.4 10.4 %collective-permute-done.3 = f32[512,512]{1,0:T(8,128)S(1)} collective-permute-done((f32[512,512]{1,0:T(8,128)S(1)}, f32[512,512]{1,0:T(8,128)S(1)}, u32[]{:S(2)}, u32[]{:S(2)}) %collective-permute-start.3) | collective-permute-done | bytes 1048608 | tf_op jit(solution)/shard_map/ppermute | solution.py:23
  73.8 1.9 collective-permute-done.4
  75.7 1.4 fusion.21
  77.1 13.2 %all-to-all-start = ((f32[16,32,512]{2,1,0:T(8,128)}), f32[16,32,512]{2,1,0:T(8,128)S(1)}, u32[]{:S(2)}, u32[]{:S(2)}) async-start(f32[16,32,512]{2,1,0:T(8,128)} %bitcast.155), calls=%async_computation | async-start | bytes 2097152 | tf_op jit(solution)/shard_map/all_to_all | solution.py:34
  90.2 16.6 %all-to-all-done = f32[16,32,512]{2,1,0:T(8,128)S(1)} async-done(((f32[16,32,512]{2,1,0:T(8,128)}), f32[16,32,512]{2,1,0:T(8,128)S(1)}, u32[]{:S(2)}, u32[]{:S(2)}) %all-to-all-start) | async-done | bytes 1048608 | tf_op jit(solution)/shard_map/all_to_all | solution.py:34
  106.8 0.1 reduce_sum.54
  106.9 0.0 copy-done.1
  106.9 0.0 copy-start
  106.9 1.6 fusion.24
  108.5 9.8 %all-reduce.2 = (f32[]{:T(128)}, f32[]{:T(128)}, f32[]{:T(128)}, f32[]{:T(128)}) all-reduce(f32[]{:T(128)} %get-tuple-element.168, f32[]{:T(128)} %get-tuple-element.169, f32[]{:T(128)} %get-tuple-element.170, f32[]{:T(128)} %get-tuple-element.167), channel_id=1, replica_groups=mesh['term_0'=4,'term_1'=4,'sector_0'=8,'sector_1'=2] {'term_0'}, use_global_device_ids=true, to_apply=%region_18.19 | all-reduce | flops 4 | bytes 32 | tf_op jit(solution)/shard_map/psum | solution.py:39
  118.3 9.9 %all-reduce.1 = (f32[]{:T(128)}, f32[]{:T(128)}, f32[]{:T(128)}, f32[]{:T(128)}) all-reduce(f32[]{:T(128)} %get-tuple-element.207, f32[]{:T(128)} %get-tuple-element.208, f32[]{:T(128)} %get-tuple-element.209, f32[]{:T(128)} %get-tuple-element.210), channel_id=1, replica_groups=mesh['term_0'=4,'term_1'=4,'sector_0'=8,'sector_1'=2] {'term_1'}, use_global_device_ids=true, to_apply=%region_19.20 | all-reduce | flops 4 | bytes 32 | tf_op jit(solution)/shard_map/psum | solution.py:39
  128.2 18.4 %all-reduce = (f32[]{:T(128)}, f32[]{:T(128)}, f32[]{:T(128)}, f32[]{:T(128)}) all-reduce(f32[]{:T(128)} %get-tuple-element.203, f32[]{:T(128)} %get-tuple-element.204, f32[]{:T(128)} %get-tuple-element.205, f32[]{:T(128)} %get-tuple-element.206), channel_id=1, replica_groups=mesh['term_0'=4,'term_1'=4,'sector_0'=8,'sector_1'=2] {'sector_0'}, use_global_device_ids=true, to_apply=%region_20.21 | all-reduce | flops 4 | bytes 32 | tf_op jit(solution)/shard_map/psum | solution.py:39
  146.5 3.1 %all-reduce.3 = (f32[]{:T(128)}, f32[]{:T(128)}, f32[]{:T(128)}, f32[]{:T(128)}) all-reduce(f32[]{:T(128)} %get-tuple-element.199, f32[]{:T(128)} %get-tuple-element.200, f32[]{:T(128)} %get-tuple-element.201, f32[]{:T(128)} %get-tuple-element.202), channel_id=1, replica_groups=mesh['term_0'=4,'term_1'=4,'sector_0'=8,'sector_1'=2] {'sector_1'}, use_global_device_ids=true, to_apply=%region_21.22 | all-reduce | flops 4 | bytes 32 | tf_op jit(solution)/shard_map/psum | solution.py:39
  152.9 0.9 multiply_subtract_fusion
  153.7 0.0 copy-start.2
  153.8 1.1 broadcast_in_dim.14
  154.9 3.8 %all-to-all-start.1 = ((f32[16,32,512]{2,1,0:T(8,128)}), f32[16,32,512]{2,1,0:T(8,128)S(1)}, u32[]{:S(2)}, u32[]{:S(2)}) async-start(f32[16,32,512]{2,1,0:T(8,128)} %broadcast_in_dim.14), calls=%async_computation.1 | async-start | bytes 2097152 | tf_op jit(solution)/shard_map/all_to_all | solution.py:50
  158.7 18.2 %all-to-all-done.1 = f32[16,32,512]{2,1,0:T(8,128)S(1)} async-done(((f32[16,32,512]{2,1,0:T(8,128)}), f32[16,32,512]{2,1,0:T(8,128)S(1)}, u32[]{:S(2)}, u32[]{:S(2)}) %all-to-all-start.1) | async-done | bytes 1048608 | tf_op jit(solution)/shard_map/all_to_all | solution.py:50
  176.9 2.1 broadcast.89
  179.0 0.0 copy-done
  179.0 0.0 copy-done.2
  179.0 11.3 %while.31 = (s32[]{:T(128)}, f32[512,3,512]{2,0,1:T(8,128)}, s32[]{:T(128)}, s32[4]{0:T(128)S(1)}, f32[4,512,512]{2,1,0:T(8,128)}, /*index=5*/f32[512,512]{1,0:T...) while((s32[]{:T(128)}, f32[512,3,512]{2,0,1:T(8,128)}, ...), condition=%wide.region_29.30_spmd, body=%wide.region_27.29_spmd.sunk | while | flops 3221749760 | bytes 7341290 | solution.py:72
  179.0 0.6 dynamic_slice.76
  181.4 0.7 and_reduce_fusion.7
  182.1 3.1 %fusion.63 = f32[512,512]{1,0:T(8,128)S(1)} fusion(f32[512,512]{1,0:T(8,128)S(1)} %get-tuple-element.379, f32[4,512,512]{2,1,0:T(8,128)} %get-tuple-element.378, s32[]{:T(128)S(6)} %select_n.44), kind=kOutput, calls=%fused_computation.19.clone.1 | convolution fusion | flops 1610612736 | bytes 3145732 | tf_op jit(solution)/shard_map/while/body/dot_general | solution.py:58
  185.2 5.0 %fusion.64 = f32[512,3,512]{2,0,1:T(8,128)} fusion(f32[512,3,512]{2,0,1:T(8,128)} %get-tuple-element.362, s32[]{:T(128)} %select_n.45, f32[512,512]{1,0:T(8,128)S(1)} %fusion.63, f32[4,512,512]{2,1,0:T(8,128)} %get-tuple-element.380, s32[]{:T(128)S(6)} %select_n.44, pred[]{:T(512)} %and_reduce_fusion.7), kind=kOutput, calls=%fused_computation.17.clone.1 | convolution fusion | flops 1611137024 | bytes 4195332 | tf_op jit(solution)/shard_map/while/body/dot_general | solution.py:58
  190.2 1.7 slice_bitcast_fusion.1
  192.0 1.9 collective-permute-start.5
  193.9 3.6 %collective-permute-start.6 = (f32[512,512]{1,0:T(8,128)S(1)}, f32[512,512]{1,0:T(8,128)S(1)}, u32[]{:S(2)}, u32[]{:S(2)}) collective-permute-start(f32[512,512]{1,0:T(8,128)S(1)} %get-tuple-element.216), channel_id=1, source_target_pairs={{1,0},{2,1},{3,2},{4,3},{5,4},{6,5},{7,6},{8,7},{9,8},{10,9},{11,1... | collective-permute-start | bytes 3145736 | tf_op jit(solution)/shard_map/ppermute | solution.py:23
  197.5 10.5 %collective-permute-done.5 = f32[512,512]{1,0:T(8,128)S(1)} collective-permute-done((f32[512,512]{1,0:T(8,128)S(1)}, f32[512,512]{1,0:T(8,128)S(1)}, u32[]{:S(2)}, u32[]{:S(2)}) %collective-permute-start.5) | collective-permute-done | bytes 1048608 | tf_op jit(solution)/shard_map/ppermute | solution.py:23
  208.1 1.8 collective-permute-done.6
  209.8 1.6 fusion.19
  211.4 51.5 %all_to_all.15 = f32[16,32,512]{2,1,0:T(8,128)S(1)} all-to-all(f32[16,32,512]{2,1,0:T(8,128)S(1)} %bitcast.156), channel_id=1, replica_groups=mesh['term_0'=4,'term_1'=4,'sector_0'=8,'sector_1'=2] {'term_0','term_1'}, dimensions={0} | all-to-all | bytes 2097152 | tf_op jit(solution)/shard_map/all_to_all | solution.py:34
  262.9 0.7 reduce_sum.59
  (3 shorter events, 0.0 us)
Async XLA Ops:
  0.6 13.8 %copy-start.4 = (s32[1,4]{1,0:T(1,128)S(1)}, s32[1,4]{1,0:T(1,128)}, u32[]{:S(2)}) copy-start(s32[1,4]{1,0:T(1,128)} %param.26) | copy-start | bytes 52
  3.3 11.2 %collective-permute-start = (f32[2]{0:T(128)S(1)}, f32[2]{0:T(128)S(1)}, u32[]{:S(2)}, u32[]{:S(2)}) collective-permute-start(f32[2]{0:T(128)S(1)} %add_convert_fusion), channel_id=1, source_target_pairs={{0,128},{16,144},{32,160},{48,176},{64,192},{80,208},{96,224},{112... | collective-permute-start | bytes 32 | tf_op jit(solution)/shard_map/ppermute | solution.py:17
  8.6 7.5 %copy-start.3 = (s32[3]{0:T(128)S(1)}, s32[3]{0:T(128)}, u32[]{:S(2)}) copy-start(s32[3]{0:T(128)} %constant.131.clone.1) | copy-start | bytes 40
  8.6 27.9 %collective-permute-start.1 = (f32[512,512]{1,0:T(8,128)}, f32[512,512]{1,0:T(8,128)}, u32[]{:S(2)}, u32[]{:S(2)}) collective-permute-start(f32[512,512]{1,0:T(8,128)} %dynamic-slice_bitcast_fusion.1), channel_id=1, source_target_pairs={{0,128},{16,144},{32,160},{48,176},{64,192},{80,208},{96,224},{112... | collective-permute-start | bytes 3145736 | tf_op jit(solution)/shard_map/ppermute | solution.py:17
  11.4 46.1 %collective-permute-start.2 = (f32[512,512]{1,0:T(8,128)}, f32[512,512]{1,0:T(8,128)}, u32[]{:S(2)}, u32[]{:S(2)}) collective-permute-start(f32[512,512]{1,0:T(8,128)} %dynamic-slice_bitcast_fusion), channel_id=1, source_target_pairs={{0,128},{16,144},{32,160},{48,176},{64,192},{80,208},{96,224},{112... | collective-permute-start | bytes 3145736 | tf_op jit(solution)/shard_map/ppermute | solution.py:17
  57.7 16.1 %collective-permute-start.3 = (f32[512,512]{1,0:T(8,128)S(1)}, f32[512,512]{1,0:T(8,128)S(1)}, u32[]{:S(2)}, u32[]{:S(2)}) collective-permute-start(f32[512,512]{1,0:T(8,128)S(1)} %get-tuple-element.217), channel_id=1, source_target_pairs={{0,1},{1,2},{2,3},{3,4},{4,5},{5,6},{6,7},{7,8},{8,9},{9,10},{10,1... | collective-permute-start | bytes 3145736 | tf_op jit(solution)/shard_map/ppermute | solution.py:23
  59.6 47.3 %copy-start.1 = (f32[1,32,512]{2,1,0:T(8,128)S(1)}, f32[1,32,512]{2,1,0:T(8,128)}, u32[]{:S(2)}) copy-start(f32[1,32,512]{2,1,0:T(8,128)} %param.23) | copy-start | bytes 196612
  59.6 16.1 %collective-permute-start.4 = (f32[512,512]{1,0:T(8,128)S(1)}, f32[512,512]{1,0:T(8,128)S(1)}, u32[]{:S(2)}, u32[]{:S(2)}) collective-permute-start(f32[512,512]{1,0:T(8,128)S(1)} %get-tuple-element.218), channel_id=1, source_target_pairs={{1,0},{2,1},{3,2},{4,3},{5,4},{6,5},{7,6},{8,7},{9,8},{10,9},{11,1... | collective-permute-start | bytes 3145736 | tf_op jit(solution)/shard_map/ppermute | solution.py:23
  77.1 29.7 %all-to-all-start = ((f32[16,32,512]{2,1,0:T(8,128)}), f32[16,32,512]{2,1,0:T(8,128)S(1)}, u32[]{:S(2)}, u32[]{:S(2)}) async-start(f32[16,32,512]{2,1,0:T(8,128)} %bitcast.155), calls=%async_computation | async-start | bytes 2097152 | tf_op jit(solution)/shard_map/all_to_all | solution.py:34
  106.9 72.1 %copy-start = (f32[32,512]{1,0:T(8,128)}, f32[32,512]{1,0:T(8,128)S(1)}, u32[]{:S(2)}) copy-start(f32[32,512]{1,0:T(8,128)S(1)} %reduce_sum.54) | copy-start | bytes 196612
  153.7 25.2 %copy-start.2 = (f32[1,32,512]{2,1,0:T(8,128)}, f32[1,32,512]{2,1,0:T(8,128)S(1)}, u32[]{:S(2)}) copy-start(f32[1,32,512]{2,1,0:T(8,128)S(1)} %multiply_subtract_fusion) | copy-start | bytes 196612
  154.9 22.0 %all-to-all-start.1 = ((f32[16,32,512]{2,1,0:T(8,128)}), f32[16,32,512]{2,1,0:T(8,128)S(1)}, u32[]{:S(2)}, u32[]{:S(2)}) async-start(f32[16,32,512]{2,1,0:T(8,128)} %broadcast_in_dim.14), calls=%async_computation.1 | async-start | bytes 2097152 | tf_op jit(solution)/shard_map/all_to_all | solution.py:50
  192.0 16.1 %collective-permute-start.5 = (f32[512,512]{1,0:T(8,128)S(1)}, f32[512,512]{1,0:T(8,128)S(1)}, u32[]{:S(2)}, u32[]{:S(2)}) collective-permute-start(f32[512,512]{1,0:T(8,128)S(1)} %get-tuple-element.215), channel_id=1, source_target_pairs={{0,1},{1,2},{2,3},{3,4},{4,5},{5,6},{6,7},{7,8},{8,9},{9,10},{10,1... | collective-permute-start | bytes 3145736 | tf_op jit(solution)/shard_map/ppermute | solution.py:23
  193.9 15.9 %collective-permute-start.6 = (f32[512,512]{1,0:T(8,128)S(1)}, f32[512,512]{1,0:T(8,128)S(1)}, u32[]{:S(2)}, u32[]{:S(2)}) collective-permute-start(f32[512,512]{1,0:T(8,128)S(1)} %get-tuple-element.216), channel_id=1, source_target_pairs={{1,0},{2,1},{3,2},{4,3},{5,4},{6,5},{7,6},{8,7},{9,8},{10,9},{11,1... | collective-permute-start | bytes 3145736 | tf_op jit(solution)/shard_map/ppermute | solution.py:23
where the time goes:
time: 268 us; the launch traced here: 264 us
  blocking collectives  92.7 us (35%)
  waiting for transfers between devices  89.6 us (33%)
  starting transfers between devices  34.8 us (13%)
  matrix products  15.2 us (6%)
  local copies, waits for them, and re-layouts  12.4 us (5%)
  other arithmetic  9 us (3%)
  between operations  5.97 us (2%)
  loops' own time  3.82 us (1%)
    all_to_all x1, blocking collectives, summed_on_arrival(): lax.all_to_all(blocks, axis, split_axis=0, concat_axis=0, tiled=True)  51.5 us
    psum x4, blocking collectives, over_axes(): return functools.reduce(lax.psum, axes, x)  41.2 us
    ppermute x3, waiting for transfers between devices, from_partner(): return lax.ppermute(value, axis, pairs)  30.3 us
    ppermute x4, waiting for transfers between devices, from_behind(): return lax.ppermute(block, axis, route)  24.6 us
    all_to_all x1, waiting for transfers between devices, sent_to_all(): lax.all_to_all(jnp.broadcast_to(x[None], (peers, *x.shape)), axis, 0, 0,...  18.2 us
    all_to_all x1, waiting for transfers between devices, summed_on_arrival(): lax.all_to_all(blocks, axis, split_axis=0, concat_axis=0, tiled=True)  16.6 us
    dot_general x4, matrix products, matmul(): jnp.dot(first_op, second_op, precision=lax.Precision.HIGHEST, preferred_e...  15.2 us
    all_to_all x1, starting transfers between devices, summed_on_arrival(): lax.all_to_all(blocks, axis, split_axis=0, concat_axis=0, tiled=True)  13.2 us
  transfers between devices with their start and end apart: 9, of which 8 were waited for; matrix products, arithmetic and copies ran while one was open for 5% of the time, Pallas kernels for 0%

commit v1 on v0

v1 whole, which is shorter than its diff:
```python
import functools

import jax
import jax.numpy as jnp
from jax import lax
from jax.experimental import pallas as pl
from jax.experimental.pallas import tpu as pltpu
from jax.sharding import Mesh
from jax.sharding import PartitionSpec as P

TERM = ("term_0", "term_1")
SECTOR = ("sector_0", "sector_1")
TERM_SECTOR = ("term_0", "term_1", "sector_0", "sector_1")
CHUNKS = 2


def shifted(block, distance):
    count = lax.axis_size(SECTOR)
    route = [(i, i + distance) for i in range(count) if 0 <= i + distance < count]
    return lax.ppermute(block, SECTOR, route)


def halves(x):
    high = x.astype(jnp.bfloat16)
    low = (x - high.astype(jnp.float32)).astype(jnp.bfloat16)
    return high, low


def product(a_high, a_low, b_high, b_low):
    dot = functools.partial(jnp.dot, preferred_element_type=jnp.float32)
    return dot(a_high, b_high) + (dot(a_high, b_low) + dot(a_low, b_high))


def accumulate(slot, meta, left, right, field_high, field_low, outs):
    peers, rows, width = left.shape[1:]

    @pl.when(slot == 0)
    def _():
        for out in outs:
            out[...] = jnp.zeros_like(out)

    @pl.when(slot < meta[0])
    def _():
        left_high, left_low = halves(left[0].reshape(peers * rows, width))
        inner = product(left_high, left_low, field_high[...], field_low[...])
        inner_high, inner_low = halves(inner)
        right_high, right_low = halves(right[0])
        result = product(inner_high, inner_low, right_high, right_low)
        result = result.reshape(peers, rows, width)
        for side in range(3):

            @pl.when(meta[1 + slot] == side)
            def _(out=outs[side]):
                out[...] += result


def first_kernel(meta, left, right, field, low_out, mid_out, high_out, field_high, field_low):
    slot = pl.program_id(0)

    @pl.when(slot == 0)
    def _():
        field_high[...], field_low[...] = halves(field[...])

    accumulate(slot, meta, left, right, field_high, field_low, (low_out, mid_out, high_out))


def second_kernel(meta, coefs, left, right, field, scaling, *rest):
    images = rest[:CHUNKS]
    low_out, mid_out, high_out, field_high, field_low = rest[CHUNKS:]
    slot = pl.program_id(0)

    @pl.when(slot == 0)
    def _():
        for c in range(CHUNKS):
            peers, rows, width = images[c].shape
            base = pl.ds(c * rows, rows)
            vector = field[:, base]
            raw = scaling[:, base] * (images[c][...] - coefs[0] * vector)
            correction = raw - coefs[1] * vector
            field_high[:, base], field_low[:, base] = halves(correction)

    peers, slab, width = field.shape
    accumulate(
        slot,
        meta,
        left,
        right,
        field_high.reshape(peers * slab, width),
        field_low.reshape(peers * slab, width),
        (low_out, mid_out, high_out),
    )


def image_chunk(chunk, meta, left_stack, right_stack, field, extra=None):
    slots, width, _ = right_stack.shape
    peers = left_stack.shape[1]
    slab = left_stack.shape[2]
    rows = slab // CHUNKS

    def live(slot, meta, *_):
        return jnp.minimum(slot, meta[0] - 1)

    left_spec = pl.BlockSpec(
        (1, peers, rows, width), lambda i, m, *r: (live(i, m), 0, chunk, 0)
    )
    right_spec = pl.BlockSpec((1, width, width), lambda i, m, *r: (live(i, m), 0, 0))

    def whole(shape):
        return pl.BlockSpec(shape, lambda i, m, *r: (0,) * len(shape))

    out_shape = (peers, rows, width)
    if extra is None:
        body, scalars, fields = first_kernel, (meta,), (field,)
        scratch_shape = (width, width)
    else:
        coefs, scaling, images = extra
        body, scalars, fields = second_kernel, (meta, coefs), (field, scaling, *images)
        scratch_shape = (peers, slab, width)
    return pl.pallas_call(
        body,
        out_shape=[jax.ShapeDtypeStruct(out_shape, jnp.float32)] * 3,
        grid_spec=pltpu.PrefetchScalarGridSpec(
            num_scalar_prefetch=len(scalars),
            grid=(slots,),
            in_specs=[left_spec, right_spec, *[whole(x.shape) for x in fields]],
            out_specs=[whole(out_shape)] * 3,
            scratch_shapes=[pltpu.VMEM(scratch_shape, jnp.bfloat16)] * 2,
        ),
        compiler_params=pltpu.CompilerParams(
            dimension_semantics=("arbitrary",), vmem_limit_bytes=32 << 20
        ),
        cost_estimate=pl.CostEstimate(
            flops=slots * 9 * width * width * width // CHUNKS,
            bytes_accessed=slots * 6 * width * width,
            transcendentals=0,
        ),
    )(*scalars, left_stack, right_stack, *fields)


def summed(blocks):
    low, mid, high = blocks
    total = mid + shifted(high, 1) + shifted(low, -1)
    return lax.all_to_all(total, TERM, 0, 0, tiled=True).sum(axis=0)


def copied(x):
    peers = lax.axis_size(TERM)
    return lax.all_to_all(jnp.broadcast_to(x[None], (peers, *x.shape)), TERM, 0, 0, tiled=True)


def per_device(wavefunction, precond, left_ops, right_ops, out_sector, live_counts):
    peers = lax.axis_size(TERM)
    width = wavefunction.shape[1]
    slots = left_ops.shape[1]
    slab = width // peers
    field = wavefunction[0]
    blocked = field.reshape(peers, slab, width)
    left_stack = left_ops[0].reshape(slots, peers, slab, width)
    right_stack = right_ops[0]
    scaling = precond[0]
    meta = jnp.concatenate([live_counts[0], out_sector[0] - lax.axis_index(SECTOR) + 1])

    full_scaling = copied(scaling)
    image_blocks = [image_chunk(c, meta, left_stack, right_stack, field) for c in range(CHUNKS)]
    images = [summed(b) for b in image_blocks]
    first_image = jnp.concatenate(images, axis=0)
    full_images = [copied(x) for x in images]
    own = lax.dynamic_index_in_dim(blocked, lax.axis_index(TERM), 0, keepdims=False)
    scaled = own * scaling
    sums = (
        jnp.sum(own * first_image),
        jnp.sum(own * own),
        jnp.sum(scaled * first_image),
        jnp.sum(scaled * own),
    )
    cross, norm_sq, scaled_cross, scaled_norm = lax.psum(sums, TERM_SECTOR)
    rayleigh = cross / norm_sq
    share = (scaled_cross - rayleigh * scaled_norm) / norm_sq
    correction = scaling * (first_image - rayleigh * own) - share * own
    coefs = jnp.stack([rayleigh, share])
    second_blocks = [
        image_chunk(
            c, meta, left_stack, right_stack, blocked, (coefs, full_scaling, full_images)
        )
        for c in range(CHUNKS)
    ]
    second_image = jnp.concatenate([summed(b) for b in second_blocks], axis=0)
    return (first_image[None], correction[None], second_image[None])


def solution(mesh):
    torus = Mesh(mesh.devices.reshape(4, 4, 8, 2), ("term_0", "term_1", "sector_0", "sector_1"))
    placed = (
        P(SECTOR, None, None),
        P(SECTOR, TERM, None),
        P(SECTOR, TERM, None, None),
        P(SECTOR, TERM, None, None),
        P(SECTOR, TERM),
        P(SECTOR, TERM),
    )
    return jax.shard_map(
        per_device,
        mesh=torus,
        in_specs=placed,
        out_specs=(P(SECTOR, TERM, None), P(SECTOR, TERM, None), P(SECTOR, TERM, None)),
        check_vma=False,
    )
```

time: 268 us -> 240 us (0.90)
  the two profiles are of different devices: /device:TPU:64 before, /device:TPU:1 now
where the time goes in v1:
time: 240 us; the launch traced here: 238 us
  blocking collectives  82.7 us (34%)
  starting transfers between devices  68.1 us (28%)
  waiting for transfers between devices  46.7 us (19%)
  local copies, waits for them, and re-layouts  14.4 us (6%)
  Pallas kernels  10.8 us (4%)
  other arithmetic  10.7 us (4%)
  between operations  4.69 us (2%)
    psum x1, blocking collectives, per_device(): cross, norm_sq, scaled_cross, scaled_norm = lax.psum(sums, TERM_SECTOR)  82.7 us
    all_to_all x4, waiting for transfers between devices, summed(): return lax.all_to_all(total, TERM, 0, 0, tiled=True).sum(axis=0)  37.2 us
    ppermute x8, starting transfers between devices, shifted(): return lax.ppermute(block, SECTOR, route)  32.3 us
    all_to_all x4, starting transfers between devices, summed(): return lax.all_to_all(total, TERM, 0, 0, tiled=True).sum(axis=0)  21.1 us
    all_to_all x3, starting transfers between devices, copied(): lax.all_to_all(jnp.broadcast_to(x[None], (peers, *x.shape)), TERM, 0, 0,...  14.7 us
    pallas_call x4, Pallas kernels, image_chunk(): pl.pallas_call(body, out_shape=[jax.ShapeDtypeStruct(out_shape, jnp.float...  10.8 us
    unnamed x16, local copies, waits for them, and re-layouts  10.8 us
    all_to_all x3, waiting for transfers between devices, copied(): lax.all_to_all(jnp.broadcast_to(x[None], (peers, *x.shape)), TERM, 0, 0,...  9.16 us
  transfers between devices with their start and end apart: 15, of which 6 were waited for; matrix products, arithmetic and copies ran while one was open for 4% of the time, Pallas kernels for 4%

profile of v1, /device:TPU:1, one launch (start us, length us, event | category | flops | bytes accessed | tf_op | source)
XLA Modules:
  0.0 238.1 jit_solution(1934044969880559801)
XLA Ops:
  0.6 1.9 broadcast_in_dim.11
  2.6 7.6 %all-to-all-start.2 = ((f32[16,32,512]{2,1,0:T(8,128)}), f32[16,32,512]{2,1,0:T(8,128)S(1)}, u32[]{:S(2)}, u32[]{:S(2)}) async-start(f32[16,32,512]{2,1,0:T(8,128)} %broadcast_in_dim.11), calls=%async_computation.2 | async-start | bytes 2097152 | tf_op jit(solution)/shard_map/all_to_all | solution.py:148
  10.8 0.7 add_bitcast_fusion
  11.5 0.1 pad_add_fusion.meta
  11.5 0.0 copy-start
  11.5 2.2 copy-done
  13.7 0.0 copy-start.2
  13.7 2.2 copy-done.2
  15.9 0.0 copy-start.4
  15.9 1.2 copy-done.4
  17.1 2.1 shard_map.85
  19.3 6.4 %collective-permute-start.1 = (f32[16,16,512]{2,1,0:T(8,128)S(1)}, f32[16,16,512]{2,1,0:T(8,128)S(1)}, u32[]{:S(2)}, u32[]{:S(2)}) collective-permute-start(f32[16,16,512]{2,1,0:T(8,128)S(1)} %get-tuple-element.17), channel_id=1, source_target_pairs={{1,0},{2,1},{3,2},{4,3},{5,4},{6,5},{7,6},{8,7},{9,8},{10,9},{11,1... | collective-permute-start | bytes 1572872 | tf_op jit(solution)/shard_map/ppermute | solution.py:20
  25.7 1.9 collective-permute-start
  27.7 2.9 %shard_map.86 = (f32[16,16,512]{2,1,0:T(8,128)}, f32[16,16,512]{2,1,0:T(8,128)S(1)}, f32[16,16,512]{2,1,0:T(8,128)S(1)}) custom-call(s32[5]{0:T(128)S(1)} %pad_add_fusion.meta, f32[4,16,32,512]{3,2,1,0:T(8,128)S(1)} %bitcast.35, f32[4,512,512]{2,1,0:T(8,128)S(1)} %bitcast.39, f32[512,512]{1,0:T(8,128)S(1)} %bitcast.43), custom_call_target="tpu_custom_call" | custom-call | flops 2415919104 | bytes 6291456 | tf_op jit(solution)/shard_map/pallas_call | solution.py:119
  30.6 6.0 %collective-permute-start.3 = (f32[16,16,512]{2,1,0:T(8,128)}, f32[16,16,512]{2,1,0:T(8,128)}, u32[]{:S(2)}, u32[]{:S(2)}) collective-permute-start(f32[16,16,512]{2,1,0:T(8,128)} %get-tuple-element.20), channel_id=1, source_target_pairs={{1,0},{2,1},{3,2},{4,3},{5,4},{6,5},{7,6},{8,7},{9,8},{10,9},{11,1... | collective-permute-start | bytes 1572872 | tf_op jit(solution)/shard_map/ppermute | solution.py:20
  36.6 1.9 collective-permute-start.2
  38.6 0.0 collective-permute-done.1
  38.6 0.0 collective-permute-done
  38.6 1.0 add_add_fusion.3
  39.6 0.0 copy-start.5
  39.6 0.0 copy-start.7
  39.6 0.0 all-to-all-done.2.scaling
  39.6 8.8 %all-to-all-start = ((f32[16,16,512]{2,1,0:T(8,128)}), f32[16,16,512]{2,1,0:T(8,128)}, u32[]{:S(2)}, u32[]{:S(2)}) async-start(f32[16,16,512]{2,1,0:T(8,128)} %add_add_fusion.3), calls=%async_computation | async-start | bytes 1048576 | tf_op jit(solution)/shard_map/all_to_all | solution.py:143
  48.4 0.0 collective-permute-done.3
  48.4 0.0 collective-permute-done.2
  48.4 2.2 add_add_fusion.2
  50.6 9.5 %all-to-all-done = f32[16,16,512]{2,1,0:T(8,128)} async-done(((f32[16,16,512]{2,1,0:T(8,128)}), f32[16,16,512]{2,1,0:T(8,128)}, u32[]{:S(2)}, u32[]{:S(2)}) %all-to-all-start) | async-done | bytes 524320 | tf_op jit(solution)/shard_map/all_to_all | solution.py:143
  60.1 3.6 %all-to-all-start.1 = ((f32[16,16,512]{2,1,0:T(8,128)}), f32[16,16,512]{2,1,0:T(8,128)S(1)}, u32[]{:S(2)}, u32[]{:S(2)}) async-start(f32[16,16,512]{2,1,0:T(8,128)} %add_add_fusion.2), calls=%async_computation.1 | async-start | bytes 1048576 | tf_op jit(solution)/shard_map/all_to_all | solution.py:143
  63.6 1.1 reduce_sum.72
  64.7 9.2 %all-to-all-done.1 = f32[16,16,512]{2,1,0:T(8,128)S(1)} async-done(((f32[16,16,512]{2,1,0:T(8,128)}), f32[16,16,512]{2,1,0:T(8,128)S(1)}, u32[]{:S(2)}, u32[]{:S(2)}) %all-to-all-start.1) | async-done | bytes 524320 | tf_op jit(solution)/shard_map/all_to_all | solution.py:143
  74.0 0.9 broadcast_in_dim.12
  74.8 3.6 %all-to-all-start.3 = ((f32[16,16,512]{2,1,0:T(8,128)}), f32[16,16,512]{2,1,0:T(8,128)S(1)}, u32[]{:S(2)}, u32[]{:S(2)}) async-start(f32[16,16,512]{2,1,0:T(8,128)} %broadcast_in_dim.12), calls=%async_computation.3 | async-start | bytes 1048576 | tf_op jit(solution)/shard_map/all_to_all | solution.py:148
  78.5 9.2 %all-to-all-done.3.rest_0_ = f32[16,16,512]{2,1,0:T(8,128)S(1)} async-done(((f32[16,16,512]{2,1,0:T(8,128)}), f32[16,16,512]{2,1,0:T(8,128)S(1)}, u32[]{:S(2)}, u32[]{:S(2)}) %all-to-all-start.3) | async-done | bytes 524320 | tf_op jit(solution)/shard_map/all_to_all | solution.py:148
  87.6 0.9 broadcast_in_dim.13
  88.5 3.6 %all-to-all-start.4 = ((f32[16,16,512]{2,1,0:T(8,128)}), f32[16,16,512]{2,1,0:T(8,128)S(1)}, u32[]{:S(2)}, u32[]{:S(2)}) async-start(f32[16,16,512]{2,1,0:T(8,128)} %broadcast_in_dim.13), calls=%async_computation.4 | async-start | bytes 1048576 | tf_op jit(solution)/shard_map/all_to_all | solution.py:148
  92.1 0.0 copy-done.5
  92.1 0.0 copy-done.7
  92.1 1.3 fusion.4
  93.4 82.7 %all-reduce = (f32[]{:T(128)}, f32[]{:T(128)}, f32[]{:T(128)}, f32[]{:T(128)}) all-reduce(f32[]{:T(128)} %get-tuple-element.28, f32[]{:T(128)} %get-tuple-element.29, f32[]{:T(128)} %get-tuple-element.30, f32[]{:T(128)} %get-tuple-element.27), channel_id=1, replica_groups=mesh['term_0'=4,'term_1'=4,'sector_0'=8,'sector_1'=2] {'term_0','term_1'..., use_global_device_ids=true, to_apply=%region_7.8 | all-reduce | flops 4 | bytes 32 | tf_op jit(solution)/shard_map/psum | solution.py:176
  179.2 0.1 pad_maximum_fusion.1.coefs
  179.3 0.0 all-to-all-done.4.rest_1_
  179.3 0.0 copy-start.1
  179.3 2.2 copy-done.1
  181.5 0.0 copy-start.3
  181.5 2.2 copy-done.3
  183.7 2.4 shard_map.88
  186.0 6.2 %collective-permute-start.7 = (f32[16,16,512]{2,1,0:T(8,128)S(1)}, f32[16,16,512]{2,1,0:T(8,128)S(1)}, u32[]{:S(2)}, u32[]{:S(2)}) collective-permute-start(f32[16,16,512]{2,1,0:T(8,128)S(1)} %get-tuple-element.26), channel_id=1, source_target_pairs={{1,0},{2,1},{3,2},{4,3},{5,4},{6,5},{7,6},{8,7},{9,8},{10,9},{11,1... | collective-permute-start | bytes 1572872 | tf_op jit(solution)/shard_map/ppermute | solution.py:20
  192.2 1.9 collective-permute-start.6
  194.1 3.4 %shard_map.87 = (f32[16,16,512]{2,1,0:T(8,128)}, f32[16,16,512]{2,1,0:T(8,128)S(1)}, f32[16,16,512]{2,1,0:T(8,128)}) custom-call(s32[5]{0:T(128)S(1)} %pad_add_fusion.meta, f32[2]{0:T(128)S(1)} %pad_maximum_fusion.1.coefs, f32[4,16,32,512]{3,2,1,0:T(8,128)S(1)} %bitcast.37, f32[4,512,512]{2,1,0:T(8,128)S(1)} %bitcast.41, f32[16,32,512]{2,1,0:T(8,128)S(1)} %bitcast.46, ...), custom_call_target="tpu_custom_call" | custom-call | flops 2415919104 | bytes 6291456 | tf_op jit(solution)/shard_map/pallas_call | solution.py:119
  197.5 0.8 copy-done.6
  198.3 6.0 %collective-permute-start.5 = (f32[16,16,512]{2,1,0:T(8,128)}, f32[16,16,512]{2,1,0:T(8,128)S(1)}, u32[]{:S(2)}, u32[]{:S(2)}) collective-permute-start(f32[16,16,512]{2,1,0:T(8,128)} %get-tuple-element.23), channel_id=1, source_target_pairs={{1,0},{2,1},{3,2},{4,3},{5,4},{6,5},{7,6},{8,7},{9,8},{10,9},{11,1... | collective-permute-start | bytes 1572872 | tf_op jit(solution)/shard_map/ppermute | solution.py:20
  204.3 1.9 collective-permute-start.4
  206.2 0.0 collective-permute-done.7
  206.2 0.0 collective-permute-done.6
  206.2 1.0 add_add_fusion
  207.2 5.1 %all-to-all-start.6 = ((f32[16,16,512]{2,1,0:T(8,128)}), f32[16,16,512]{2,1,0:T(8,128)S(1)}, u32[]{:S(2)}, u32[]{:S(2)}) async-start(f32[16,16,512]{2,1,0:T(8,128)} %add_add_fusion), calls=%async_computation.6 | async-start | bytes 1048576 | tf_op jit(solution)/shard_map/all_to_all | solution.py:143
  212.3 0.0 collective-permute-done.5
  212.3 0.3 collective-permute-done.4
  212.6 2.0 add_add_fusion.1
  214.6 9.0 %all-to-all-done.6 = f32[16,16,512]{2,1,0:T(8,128)S(1)} async-done(((f32[16,16,512]{2,1,0:T(8,128)}), f32[16,16,512]{2,1,0:T(8,128)S(1)}, u32[]{:S(2)}, u32[]{:S(2)}) %all-to-all-start.6) | async-done | bytes 524320 | tf_op jit(solution)/shard_map/all_to_all | solution.py:143
  223.6 3.6 %all-to-all-start.5 = ((f32[16,16,512]{2,1,0:T(8,128)}), f32[16,16,512]{2,1,0:T(8,128)S(1)}, u32[]{:S(2)}, u32[]{:S(2)}) async-start(f32[16,16,512]{2,1,0:T(8,128)} %add_add_fusion.1), calls=%async_computation.5 | async-start | bytes 1048576 | tf_op jit(solution)/shard_map/all_to_all | solution.py:143
  227.2 0.7 fusion.1
  227.9 9.5 %all-to-all-done.5 = f32[16,16,512]{2,1,0:T(8,128)S(1)} async-done(((f32[16,16,512]{2,1,0:T(8,128)}), f32[16,16,512]{2,1,0:T(8,128)S(1)}, u32[]{:S(2)}, u32[]{:S(2)}) %all-to-all-start.5) | async-done | bytes 524320 | tf_op jit(solution)/shard_map/all_to_all | solution.py:143
  237.5 0.6 maximum_bitcast_fusion
  (4 shorter events, 0.1 us)
Async XLA Ops:
  2.6 37.0 %all-to-all-start.2 = ((f32[16,32,512]{2,1,0:T(8,128)}), f32[16,32,512]{2,1,0:T(8,128)S(1)}, u32[]{:S(2)}, u32[]{:S(2)}) async-start(f32[16,32,512]{2,1,0:T(8,128)} %broadcast_in_dim.11), calls=%async_computation.2 | async-start | bytes 2097152 | tf_op jit(solution)/shard_map/all_to_all | solution.py:148
  11.5 2.2 copy-start
  13.7 2.2 copy-start.2
  15.9 1.2 copy-start.4
  19.3 19.3 %collective-permute-start.1 = (f32[16,16,512]{2,1,0:T(8,128)S(1)}, f32[16,16,512]{2,1,0:T(8,128)S(1)}, u32[]{:S(2)}, u32[]{:S(2)}) collective-permute-start(f32[16,16,512]{2,1,0:T(8,128)S(1)} %get-tuple-element.17), channel_id=1, source_target_pairs={{1,0},{2,1},{3,2},{4,3},{5,4},{6,5},{7,6},{8,7},{9,8},{10,9},{11,1... | collective-permute-start | bytes 1572872 | tf_op jit(solution)/shard_map/ppermute | solution.py:20
  25.7 12.8 %collective-permute-start = (f32[16,16,512]{2,1,0:T(8,128)S(1)}, f32[16,16,512]{2,1,0:T(8,128)S(1)}, u32[]{:S(2)}, u32[]{:S(2)}) collective-permute-start(f32[16,16,512]{2,1,0:T(8,128)S(1)} %get-tuple-element.16), channel_id=1, source_target_pairs={{0,1},{1,2},{2,3},{3,4},{4,5},{5,6},{6,7},{7,8},{8,9},{9,10},{10,1... | collective-permute-start | bytes 1572872 | tf_op jit(solution)/shard_map/ppermute | solution.py:20
  30.6 17.8 %collective-permute-start.3 = (f32[16,16,512]{2,1,0:T(8,128)}, f32[16,16,512]{2,1,0:T(8,128)}, u32[]{:S(2)}, u32[]{:S(2)}) collective-permute-start(f32[16,16,512]{2,1,0:T(8,128)} %get-tuple-element.20), channel_id=1, source_target_pairs={{1,0},{2,1},{3,2},{4,3},{5,4},{6,5},{7,6},{8,7},{9,8},{10,9},{11,1... | collective-permute-start | bytes 1572872 | tf_op jit(solution)/shard_map/ppermute | solution.py:20
  36.6 11.8 %collective-permute-start.2 = (f32[16,16,512]{2,1,0:T(8,128)S(1)}, f32[16,16,512]{2,1,0:T(8,128)}, u32[]{:S(2)}, u32[]{:S(2)}) collective-permute-start(f32[16,16,512]{2,1,0:T(8,128)S(1)} %get-tuple-element.19), channel_id=1, source_target_pairs={{0,1},{1,2},{2,3},{3,4},{4,5},{5,6},{6,7},{7,8},{8,9},{9,10},{10,1... | collective-permute-start | bytes 1572872 | tf_op jit(solution)/shard_map/ppermute | solution.py:20
  39.6 52.5 %copy-start.5 = (f32[1,512,512]{2,1,0:T(8,128)S(1)}, f32[1,512,512]{2,1,0:T(8,128)}, u32[]{:S(2)}) copy-start(f32[1,512,512]{2,1,0:T(8,128)} %param.6) | copy-start | bytes 3145732
  39.6 52.5 %copy-start.7 = (f32[1,32,512]{2,1,0:T(8,128)S(1)}, f32[1,32,512]{2,1,0:T(8,128)}, u32[]{:S(2)}) copy-start(f32[1,32,512]{2,1,0:T(8,128)} %param.7) | copy-start | bytes 196612
  39.6 20.5 %all-to-all-start = ((f32[16,16,512]{2,1,0:T(8,128)}), f32[16,16,512]{2,1,0:T(8,128)}, u32[]{:S(2)}, u32[]{:S(2)}) async-start(f32[16,16,512]{2,1,0:T(8,128)} %add_add_fusion.3), calls=%async_computation | async-start | bytes 1048576 | tf_op jit(solution)/shard_map/all_to_all | solution.py:143
  60.1 13.9 %all-to-all-start.1 = ((f32[16,16,512]{2,1,0:T(8,128)}), f32[16,16,512]{2,1,0:T(8,128)S(1)}, u32[]{:S(2)}, u32[]{:S(2)}) async-start(f32[16,16,512]{2,1,0:T(8,128)} %add_add_fusion.2), calls=%async_computation.1 | async-start | bytes 1048576 | tf_op jit(solution)/shard_map/all_to_all | solution.py:143
  74.8 12.8 %all-to-all-start.3 = ((f32[16,16,512]{2,1,0:T(8,128)}), f32[16,16,512]{2,1,0:T(8,128)S(1)}, u32[]{:S(2)}, u32[]{:S(2)}) async-start(f32[16,16,512]{2,1,0:T(8,128)} %broadcast_in_dim.12), calls=%async_computation.3 | async-start | bytes 1048576 | tf_op jit(solution)/shard_map/all_to_all | solution.py:148
  88.5 90.8 %all-to-all-start.4 = ((f32[16,16,512]{2,1,0:T(8,128)}), f32[16,16,512]{2,1,0:T(8,128)S(1)}, u32[]{:S(2)}, u32[]{:S(2)}) async-start(f32[16,16,512]{2,1,0:T(8,128)} %broadcast_in_dim.13), calls=%async_computation.4 | async-start | bytes 1048576 | tf_op jit(solution)/shard_map/all_to_all | solution.py:148
  179.3 2.2 copy-start.1
  181.5 2.2 copy-start.3
  186.0 20.2 %collective-permute-start.7 = (f32[16,16,512]{2,1,0:T(8,128)S(1)}, f32[16,16,512]{2,1,0:T(8,128)S(1)}, u32[]{:S(2)}, u32[]{:S(2)}) collective-permute-start(f32[16,16,512]{2,1,0:T(8,128)S(1)} %get-tuple-element.26), channel_id=1, source_target_pairs={{1,0},{2,1},{3,2},{4,3},{5,4},{6,5},{7,6},{8,7},{9,8},{10,9},{11,1... | collective-permute-start | bytes 1572872 | tf_op jit(solution)/shard_map/ppermute | solution.py:20
  192.2 14.0 %collective-permute-start.6 = (f32[16,16,512]{2,1,0:T(8,128)S(1)}, f32[16,16,512]{2,1,0:T(8,128)S(1)}, u32[]{:S(2)}, u32[]{:S(2)}) collective-permute-start(f32[16,16,512]{2,1,0:T(8,128)S(1)} %get-tuple-element.25), channel_id=1, source_target_pairs={{0,1},{1,2},{2,3},{3,4},{4,5},{5,6},{6,7},{7,8},{8,9},{9,10},{10,1... | collective-permute-start | bytes 1572872 | tf_op jit(solution)/shard_map/ppermute | solution.py:20
  197.5 0.8 copy-start.6
  198.3 14.1 %collective-permute-start.5 = (f32[16,16,512]{2,1,0:T(8,128)}, f32[16,16,512]{2,1,0:T(8,128)S(1)}, u32[]{:S(2)}, u32[]{:S(2)}) collective-permute-start(f32[16,16,512]{2,1,0:T(8,128)} %get-tuple-element.23), channel_id=1, source_target_pairs={{1,0},{2,1},{3,2},{4,3},{5,4},{6,5},{7,6},{8,7},{9,8},{10,9},{11,1... | collective-permute-start | bytes 1572872 | tf_op jit(solution)/shard_map/ppermute | solution.py:20
  204.3 8.3 %collective-permute-start.4 = (f32[16,16,512]{2,1,0:T(8,128)}, f32[16,16,512]{2,1,0:T(8,128)S(1)}, u32[]{:S(2)}, u32[]{:S(2)}) collective-permute-start(f32[16,16,512]{2,1,0:T(8,128)} %get-tuple-element.22), channel_id=1, source_target_pairs={{0,1},{1,2},{2,3},{3,4},{4,5},{5,6},{6,7},{7,8},{8,9},{9,10},{10,1... | collective-permute-start | bytes 1572872 | tf_op jit(solution)/shard_map/ppermute | solution.py:20
  207.2 16.4 %all-to-all-start.6 = ((f32[16,16,512]{2,1,0:T(8,128)}), f32[16,16,512]{2,1,0:T(8,128)S(1)}, u32[]{:S(2)}, u32[]{:S(2)}) async-start(f32[16,16,512]{2,1,0:T(8,128)} %add_add_fusion), calls=%async_computation.6 | async-start | bytes 1048576 | tf_op jit(solution)/shard_map/all_to_all | solution.py:143
  223.6 13.8 %all-to-all-start.5 = ((f32[16,16,512]{2,1,0:T(8,128)}), f32[16,16,512]{2,1,0:T(8,128)S(1)}, u32[]{:S(2)}, u32[]{:S(2)}) async-start(f32[16,16,512]{2,1,0:T(8,128)} %add_add_fusion.1), calls=%async_computation.5 | async-start | bytes 1048576 | tf_op jit(solution)/shard_map/all_to_all | solution.py:143

commit v2 on v1

v2 whole, which is shorter than its diff:
```python
import functools

import jax
import jax.numpy as jnp
from jax import lax
from jax.experimental import pallas as pl
from jax.experimental.pallas import tpu as pltpu
from jax.sharding import Mesh
from jax.sharding import PartitionSpec as P

TERM = ("term_0", "term_1")
SECTOR = ("sector_0", "sector_1")
LANES = 128
EXTRA = 8
MIB = 1 << 20
F32 = jnp.float32


def shifted(block, distance):
    count = lax.axis_size(SECTOR)
    route = [(i, i + distance) for i in range(count) if 0 <= i + distance < count]
    return lax.ppermute(block, SECTOR, route)


def swapped(x):
    return lax.all_to_all(x, TERM, 0, 0, tiled=True)


def over_sectors(x):
    for axis in SECTOR[::-1]:
        count = lax.axis_size(axis)
        mask = 1
        while mask < count:
            x = x + lax.ppermute(x, axis, [(i, i ^ mask) for i in range(count)])
            mask *= 2
    return x


def halves(x):
    high = x.astype(jnp.bfloat16)
    low = (x - high.astype(F32)).astype(jnp.bfloat16)
    return high, low


def product(a_high, a_low, b_high, b_low):
    dot = functools.partial(jnp.dot, preferred_element_type=F32)
    return dot(a_high, b_high) + (dot(a_high, b_low) + dot(a_low, b_high))


def accumulate(sector, count, target, left, right, field_high, field_low, outs):
    slot = pl.program_id(0)

    @pl.when(slot == 0)
    def _():
        for out in outs:
            out[...] = jnp.zeros_like(out)

    @pl.when(slot < count[0, 0])
    def _():
        left_high, left_low = halves(left[0])
        inner = product(left_high, left_low, field_high[...], field_low[...])
        inner_high, inner_low = halves(inner)
        right_high, right_low = halves(right[0])
        result = product(inner_high, inner_low, right_high, right_low)
        for side, out in enumerate(outs):

            @pl.when(target[0, slot] - sector == side - 1)
            def _(out=out):
                out[...] += result


def first_kernel(count, target, left, right, field, low_out, mid_out, high_out, f_high, f_low):
    @pl.when(pl.program_id(0) == 0)
    def _():
        f_high[...], f_low[...] = halves(field[...])

    outs = (low_out, mid_out, high_out)
    accumulate(lax.axis_index(SECTOR), count, target, left, right, f_high, f_low, outs)


def coefficients(sums):
    cross, norm_sq = sums[0:1, 0:1], sums[1:2, 0:1]
    scaled_cross, scaled_norm = sums[2:3, 0:1], sums[3:4, 0:1]
    rayleigh = cross / norm_sq
    share = (scaled_cross - rayleigh * scaled_norm) / norm_sq
    return rayleigh, share


def second_kernel(
    count, target, left, right, sums, field, scaling, image, low_out, mid_out, high_out, f_high, f_low
):
    @pl.when(pl.program_id(0) == 0)
    def _():
        rayleigh, share = coefficients(sums[...])
        vector = field[...]
        correction = scaling[...] * (image[...] - rayleigh * vector) - share * vector
        f_high[...], f_low[...] = halves(correction)

    outs = (low_out, mid_out, high_out)
    accumulate(lax.axis_index(SECTOR), count, target, left, right, f_high, f_low, outs)


def partial_image(body, counts, targets, left_stack, right_stack, fields):
    slots, width, _ = right_stack.shape

    def operand(i, count, target):
        return (jnp.minimum(i, count[0, 0] - 1), 0, 0)

    def whole(shape):
        return pl.BlockSpec(shape, lambda i, *_: (0,) * len(shape))

    block = (width, width)
    return pl.pallas_call(
        body,
        out_shape=[jax.ShapeDtypeStruct(block, F32)] * 3,
        grid_spec=pltpu.PrefetchScalarGridSpec(
            num_scalar_prefetch=2,
            grid=(slots,),
            in_specs=[
                pl.BlockSpec((1, width, width), operand),
                pl.BlockSpec((1, width, width), operand),
                *[whole(x.shape) for x in fields],
            ],
            out_specs=[whole(block)] * 3,
            scratch_shapes=[pltpu.VMEM(block, jnp.bfloat16)] * 2,
        ),
        compiler_params=pltpu.CompilerParams(
            dimension_semantics=("arbitrary",), vmem_limit_bytes=48 * MIB
        ),
        cost_estimate=pl.CostEstimate(
            flops=slots * 12 * width**3, bytes_accessed=slots * 8 * width**2, transcendentals=0
        ),
    )(counts, targets, left_stack, right_stack, *fields)


def tiles(x, slab, width):
    return [(c * slab, slice(c * LANES, (c + 1) * LANES)) for c in range(width // LANES)]


def combine_kernel(mid, upward, downward, field, scaling, packed, totals):
    peers, slab, width = mid.shape
    where = tiles(mid, slab, width)
    cross = jnp.zeros((slab, width), F32)
    scaled_cross = jnp.zeros((slab, width), F32)
    for peer in range(peers):
        total = mid[peer] + (upward[peer] + downward[peer])
        for row, lanes in where:
            packed[peer, row : row + slab] = total[:, lanes]
        weighted = field[peer] * total
        cross += weighted
        scaled_cross += scaling[peer] * weighted
    me = lax.axis_index(TERM)
    own = field[me]
    square = own * own
    parts = [cross, square, scaled_cross, scaling[me] * square]
    line = lax.broadcasted_iota(jnp.int32, (EXTRA, LANES), 0)
    tile = jnp.zeros((EXTRA, LANES), F32)
    for i, part in enumerate(parts):
        tile = jnp.where(line == i, jnp.sum(part, keepdims=True), tile)
    totals[...] = tile
    for peer in range(peers):
        packed[peer, len(where) * slab :] = totals[...]


def gathered_kernel(arrived, image, copies, sums):
    peers, slab, width = copies.shape
    total = arrived[0]
    for peer in range(1, peers):
        total += arrived[peer]
    where = tiles(image, slab, width)
    for row, lanes in where:
        image[:, lanes] = total[row : row + slab]
    for peer in range(peers):
        copies[peer] = image[...]
    sums[...] = total[len(where) * slab :]


def small_call(body, out_shapes, args, scratch=()):
    return pl.pallas_call(
        body,
        out_shape=[jax.ShapeDtypeStruct(s, F32) for s in out_shapes],
        scratch_shapes=scratch,
        compiler_params=pltpu.CompilerParams(vmem_limit_bytes=32 * MIB),
    )(*args)


def per_device(wavefunction, precond, left_ops, right_ops, out_sector, live_counts):
    peers = lax.axis_size(TERM)
    width = wavefunction.shape[1]
    slab = width // peers
    split = (peers, slab, width)
    packed_rows = slab * (width // LANES) + EXTRA
    field = wavefunction[0]
    scaling = precond[0]
    image_of = functools.partial(
        partial_image,
        counts=live_counts,
        targets=out_sector,
        left_stack=left_ops[0],
        right_stack=right_ops[0],
    )

    low, mid, high = image_of(first_kernel, fields=(field,))
    upward, downward = shifted(high, 1), shifted(low, -1)
    scaling_late, _ = lax.optimization_barrier((scaling, mid))
    full_scaling = swapped(jnp.broadcast_to(scaling_late[None], split))
    (packed,) = small_call(
        combine_kernel,
        [(peers, packed_rows, LANES)],
        [*[x.reshape(split) for x in (mid, upward, downward, field)], full_scaling],
        [pltpu.VMEM((EXTRA, LANES), F32)],
    )
    first_image, copies, sums = small_call(
        gathered_kernel, [(slab, width), split, (EXTRA, LANES)], [swapped(packed)]
    )
    full_image = swapped(copies)
    sums = over_sectors(sums)

    own = lax.dynamic_index_in_dim(
        field.reshape(split), lax.axis_index(TERM), 0, keepdims=False
    )
    rayleigh, share = coefficients(sums)
    correction = scaling * (first_image - rayleigh * own) - share * own

    fields = (sums, field, full_scaling.reshape(field.shape), full_image.reshape(field.shape))
    low, mid, high = image_of(second_kernel, fields=fields)
    total = mid + shifted(high, 1) + shifted(low, -1)
    second_image = swapped(total.reshape(split)).sum(axis=0)
    return (first_image[None], correction[None], second_image[None])


def solution(mesh):
    torus = Mesh(mesh.devices.reshape(4, 4, 8, 2), ("term_0", "term_1", "sector_0", "sector_1"))
    placed = (
        P(SECTOR, None, None),
        P(SECTOR, TERM, None),
        P(SECTOR, TERM, None, None),
        P(SECTOR, TERM, None, None),
        P(SECTOR, TERM),
        P(SECTOR, TERM),
    )
    return jax.shard_map(
        per_device,
        mesh=torus,
        in_specs=placed,
        out_specs=(P(SECTOR, TERM, None), P(SECTOR, TERM, None), P(SECTOR, TERM, None)),
        check_vma=False,
    )
```

time: 240 us -> 147 us (0.61)
  the two profiles are of different devices: /device:TPU:1 before, /device:TPU:65 now
where the time goes in v2:
time: 147 us; the launch traced here: 146 us
  blocking collectives  42.7 us (29%)
  waiting for transfers between devices  37.8 us (26%)
  starting transfers between devices  31.9 us (22%)
  Pallas kernels  23.2 us (16%)
  between operations  4.62 us (3%)
  local copies, waits for them, and re-layouts  3.6 us (2%)
  other arithmetic  2.72 us (2%)
    all_to_all x2, blocking collectives, swapped(): return lax.all_to_all(x, TERM, 0, 0, tiled=True)  42.7 us
    pallas_call x2, Pallas kernels, partial_image(): pl.pallas_call(body, out_shape=[jax.ShapeDtypeStruct(block, F32)] * 3, gr...  21.5 us
    ppermute x4, starting transfers between devices, shifted(): return lax.ppermute(block, SECTOR, route)  14.5 us
    ppermute x4, waiting for transfers between devices, shifted(): return lax.ppermute(block, SECTOR, route)  14.2 us
    all_to_all x2, waiting for transfers between devices, swapped(): return lax.all_to_all(x, TERM, 0, 0, tiled=True)  12.2 us
    ppermute x4, waiting for transfers between devices, over_sectors(): x = x + lax.ppermute(x, axis, [(i, i ^ mask) for i in range(count)])  11.3 us
    all_to_all x2, starting transfers between devices, swapped(): return lax.all_to_all(x, TERM, 0, 0, tiled=True)  10.4 us
    ppermute x4, starting transfers between devices, over_sectors(): x = x + lax.ppermute(x, axis, [(i, i ^ mask) for i in range(count)])  6.94 us
  transfers between devices with their start and end apart: 10, of which 7 were waited for; matrix products, arithmetic and copies ran while one was open for 1% of the time, Pallas kernels for 0%

profile of v2, /device:TPU:65, one launch (start us, length us, event | category | flops | bytes accessed | tf_op | source)
XLA Modules:
  0.0 146.5 jit_solution(10692483762066116396)
XLA Ops:
  1.3 0.0 copy-start
  1.3 1.2 copy-done
  2.5 0.0 copy-start.2
  2.5 0.7 copy-done.2
  3.2 0.0 copy-start.5
  3.2 10.3 %shard_map.85 = (f32[512,512]{1,0:T(8,128)S(1)}, f32[512,512]{1,0:T(8,128)S(1)}, f32[512,512]{1,0:T(8,128)S(1)}) custom-call(s32[1,1]{1,0:T(1,128)S(6)} %copy.9.count, s32[1,4]{1,0:T(1,128)S(1)} %copy-done.2, f32[4,512,512]{2,1,0:T(8,128)} %bitcast.40, f32[4,512,512]{2,1,0:T(8,128)} %bitcast.42, f32[512,512]{1,0:T(8,128)S(1)} %bitcast.29), custom_call_target="tpu_custom_call" | custom-call | flops 6442450944 | bytes 8388608 | tf_op jit(solution)/shard_map/pallas_call | solution.py:113
  13.5 4.1 %collective-permute-start = (f32[512,512]{1,0:T(8,128)S(1)}, f32[512,512]{1,0:T(8,128)S(1)}, u32[]{:S(2)}, u32[]{:S(2)}) collective-permute-start(f32[512,512]{1,0:T(8,128)S(1)} %get-tuple-element.14), channel_id=1, source_target_pairs={{0,1},{1,2},{2,3},{3,4},{4,5},{5,6},{6,7},{7,8},{8,9},{9,10},{10,1... | collective-permute-start | bytes 3145736 | tf_op jit(solution)/shard_map/ppermute | solution.py:22
  17.6 1.9 %collective-permute-start.1 = (f32[512,512]{1,0:T(8,128)S(1)}, f32[512,512]{1,0:T(8,128)S(1)}, u32[]{:S(2)}, u32[]{:S(2)}) collective-permute-start(f32[512,512]{1,0:T(8,128)S(1)} %get-tuple-element.15), channel_id=1, source_target_pairs={{1,0},{2,1},{3,2},{4,3},{5,4},{6,5},{7,6},{8,7},{9,8},{10,9},{11,1... | collective-permute-start | bytes 3145736 | tf_op jit(solution)/shard_map/ppermute | solution.py:22
  19.5 0.0 copy-done.5
  19.5 0.1 broadcast_in_dim.15
  19.6 22.3 %all_to_all.20.scaling = f32[16,32,512]{2,1,0:T(8,128)S(1)} all-to-all(f32[16,32,512]{2,1,0:T(8,128)S(1)} %broadcast_in_dim.15), channel_id=1, replica_groups=mesh['term_0'=4,'term_1'=4,'sector_0'=8,'sector_1'=2] {'term_0','term_1'}, dimensions={0} | all-to-all | bytes 2097152 | tf_op jit(solution)/shard_map/all_to_all | solution.py:26
  41.9 0.0 collective-permute-done
  41.9 0.0 collective-permute-done.1
  41.9 0.5 shard_map.86
  42.4 0.0 copy-start.1
  42.4 0.0 copy-start.3
  42.4 20.4 %all_to_all.21.arrived = f32[16,136,128]{2,1,0:T(8,128)S(1)} all-to-all(f32[16,136,128]{2,1,0:T(8,128)S(1)} %shard_map.86), channel_id=1, replica_groups=mesh['term_0'=4,'term_1'=4,'sector_0'=8,'sector_1'=2] {'term_0','term_1'}, dimensions={0} | all-to-all | bytes 2228224 | tf_op jit(solution)/shard_map/all_to_all | solution.py:26
  62.8 1.2 shard_map.87
  64.0 3.7 %all-to-all-start.2 = ((f32[16,32,512]{2,1,0:T(8,128)}), f32[16,32,512]{2,1,0:T(8,128)S(1)}, u32[]{:S(2)}, u32[]{:S(2)}) async-start(f32[16,32,512]{2,1,0:T(8,128)} %get-tuple-element.19), calls=%async_computation.2 | async-start | bytes 2097152 | tf_op jit(solution)/shard_map/all_to_all | solution.py:26
  67.7 2.7 %collective-permute-start.2 = (f32[8,128]{1,0:T(8,128)S(1)}, f32[8,128]{1,0:T(8,128)S(1)}, u32[]{:S(2)}, u32[]{:S(2)}) collective-permute-start(f32[8,128]{1,0:T(8,128)S(1)} %get-tuple-element.18), channel_id=1, source_target_pairs={{0,1},{1,0},{2,3},{3,2},{4,5},{5,4},{6,7},{7,6},{8,9},{9,8},{10,11... | collective-permute-start | bytes 12296 | tf_op jit(solution)/shard_map/ppermute | solution.py:34
  70.4 0.8 collective-permute-done.2
  71.2 3.4 %collective-permute-start.3 = (f32[8,128]{1,0:T(8,128)S(1)}, f32[8,128]{1,0:T(8,128)S(1)}, u32[]{:S(2)}, u32[]{:S(2)}) collective-permute-start(f32[8,128]{1,0:T(8,128)S(1)} %add.25), channel_id=1, source_target_pairs={{0,2},{2,0},{4,6},{6,4},{8,10},{10,8},{12,14},{14,12},{1,3},{3,1},... | collective-permute-start | bytes 12296 | tf_op jit(solution)/shard_map/ppermute | solution.py:34
  74.6 1.3 collective-permute-done.3
  75.9 0.0 collective-permute-start.4
  75.9 3.6 %collective-permute-done.4 = f32[8,128]{1,0:T(8,128)S(1)} collective-permute-done((f32[8,128]{1,0:T(8,128)S(1)}, f32[8,128]{1,0:T(8,128)S(1)}, u32[]{:S(2)}, u32[]{:S(2)}) %collective-permute-start.4) | collective-permute-done | bytes 4128 | tf_op jit(solution)/shard_map/ppermute | solution.py:34
  79.6 0.8 collective-permute-start.5
  80.4 5.6 %collective-permute-done.5 = f32[8,128]{1,0:T(8,128)S(1)} collective-permute-done((f32[8,128]{1,0:T(8,128)S(1)}, f32[8,128]{1,0:T(8,128)S(1)}, u32[]{:S(2)}, u32[]{:S(2)}) %collective-permute-start.5) | collective-permute-done | bytes 4128 | tf_op jit(solution)/shard_map/ppermute | solution.py:34
  86.0 0.0 all-to-all-done.2
  86.0 0.0 copy-start.4
  86.0 1.0 copy-done.4
  87.0 0.0 copy-done.1
  87.0 0.0 copy-done.3
  87.0 11.3 %shard_map.88 = (f32[512,512]{1,0:T(8,128)S(1)}, f32[512,512]{1,0:T(8,128)S(1)}, f32[512,512]{1,0:T(8,128)S(1)}) custom-call(s32[1,1]{1,0:T(1,128)S(6)} %copy.9.count, s32[1,4]{1,0:T(1,128)S(1)} %copy-done.3, f32[4,512,512]{2,1,0:T(8,128)} %bitcast.41, f32[4,512,512]{2,1,0:T(8,128)} %bitcast.43, f32[8,128]{1,0:T(8,128)S(1)} %add.28.sums, ...), custom_call_target="tpu_custom_call" | custom-call | flops 6442450944 | bytes 8388608 | tf_op jit(solution)/shard_map/pallas_call | solution.py:113
  98.2 0.0 copy-start.6
  98.2 6.6 %collective-permute-start.6 = (f32[512,512]{1,0:T(8,128)S(1)}, f32[512,512]{1,0:T(8,128)S(1)}, u32[]{:S(2)}, u32[]{:S(2)}) collective-permute-start(f32[512,512]{1,0:T(8,128)S(1)} %get-tuple-element.21), channel_id=1, source_target_pairs={{0,1},{1,2},{2,3},{3,4},{4,5},{5,6},{6,7},{7,8},{8,9},{9,10},{10,1... | collective-permute-start | bytes 3145736 | tf_op jit(solution)/shard_map/ppermute | solution.py:22
  104.8 1.9 %collective-permute-start.7 = (f32[512,512]{1,0:T(8,128)S(1)}, f32[512,512]{1,0:T(8,128)S(1)}, u32[]{:S(2)}, u32[]{:S(2)}) collective-permute-start(f32[512,512]{1,0:T(8,128)S(1)} %get-tuple-element.22), channel_id=1, source_target_pairs={{1,0},{2,1},{3,2},{4,3},{5,4},{6,5},{7,6},{8,7},{9,8},{10,9},{11,1... | collective-permute-start | bytes 3145736 | tf_op jit(solution)/shard_map/ppermute | solution.py:22
  106.8 9.8 %collective-permute-done.6 = f32[512,512]{1,0:T(8,128)S(1)} collective-permute-done((f32[512,512]{1,0:T(8,128)S(1)}, f32[512,512]{1,0:T(8,128)S(1)}, u32[]{:S(2)}, u32[]{:S(2)}) %collective-permute-start.6) | collective-permute-done | bytes 1048608 | tf_op jit(solution)/shard_map/ppermute | solution.py:22
  116.6 4.4 %collective-permute-done.7 = f32[512,512]{1,0:T(8,128)S(1)} collective-permute-done((f32[512,512]{1,0:T(8,128)S(1)}, f32[512,512]{1,0:T(8,128)S(1)}, u32[]{:S(2)}, u32[]{:S(2)}) %collective-permute-start.7) | collective-permute-done | bytes 1048608 | tf_op jit(solution)/shard_map/ppermute | solution.py:22
  120.9 1.4 add_add_fusion
  122.3 6.8 %all-to-all-start.3 = ((f32[16,32,512]{2,1,0:T(8,128)}), f32[16,32,512]{2,1,0:T(8,128)S(1)}, u32[]{:S(2)}, u32[]{:S(2)}) async-start(f32[16,32,512]{2,1,0:T(8,128)} %bitcast.16), calls=%async_computation.3 | async-start | bytes 2097152 | tf_op jit(solution)/shard_map/all_to_all | solution.py:26
  129.1 0.6 fusion.2
  132.9 0.0 copy-done.6
  132.9 0.7 fusion
  133.6 12.2 %all-to-all-done.3 = f32[16,32,512]{2,1,0:T(8,128)S(1)} async-done(((f32[16,32,512]{2,1,0:T(8,128)}), f32[16,32,512]{2,1,0:T(8,128)S(1)}, u32[]{:S(2)}, u32[]{:S(2)}) %all-to-all-start.3) | async-done | bytes 1048608 | tf_op jit(solution)/shard_map/all_to_all | solution.py:26
  145.8 0.7 reduce_sum.9
  (4 shorter events, 0.0 us)
Async XLA Ops:
  1.3 1.2 copy-start
  2.5 0.7 copy-start.2
  3.2 16.3 %copy-start.5 = (f32[1,32,512]{2,1,0:T(8,128)S(1)}, f32[1,32,512]{2,1,0:T(8,128)}, u32[]{:S(2)}) copy-start(f32[1,32,512]{2,1,0:T(8,128)} %param.7) | copy-start | bytes 196612
  13.5 28.5 %collective-permute-start = (f32[512,512]{1,0:T(8,128)S(1)}, f32[512,512]{1,0:T(8,128)S(1)}, u32[]{:S(2)}, u32[]{:S(2)}) collective-permute-start(f32[512,512]{1,0:T(8,128)S(1)} %get-tuple-element.14), channel_id=1, source_target_pairs={{0,1},{1,2},{2,3},{3,4},{4,5},{5,6},{6,7},{7,8},{8,9},{9,10},{10,1... | collective-permute-start | bytes 3145736 | tf_op jit(solution)/shard_map/ppermute | solution.py:22
  17.6 24.4 %collective-permute-start.1 = (f32[512,512]{1,0:T(8,128)S(1)}, f32[512,512]{1,0:T(8,128)S(1)}, u32[]{:S(2)}, u32[]{:S(2)}) collective-permute-start(f32[512,512]{1,0:T(8,128)S(1)} %get-tuple-element.15), channel_id=1, source_target_pairs={{1,0},{2,1},{3,2},{4,3},{5,4},{6,5},{7,6},{8,7},{9,8},{10,9},{11,1... | collective-permute-start | bytes 3145736 | tf_op jit(solution)/shard_map/ppermute | solution.py:22
  42.4 44.5 %copy-start.1 = (f32[1,512,512]{2,1,0:T(8,128)S(1)}, f32[1,512,512]{2,1,0:T(8,128)}, u32[]{:S(2)}) copy-start(f32[1,512,512]{2,1,0:T(8,128)} %param.6) | copy-start | bytes 3145732
  42.4 44.5 %copy-start.3 = (s32[1,4]{1,0:T(1,128)S(1)}, s32[1,4]{1,0:T(1,128)}, u32[]{:S(2)}) copy-start(s32[1,4]{1,0:T(1,128)} %target.3) | copy-start | bytes 52
  64.0 22.0 %all-to-all-start.2 = ((f32[16,32,512]{2,1,0:T(8,128)}), f32[16,32,512]{2,1,0:T(8,128)S(1)}, u32[]{:S(2)}, u32[]{:S(2)}) async-start(f32[16,32,512]{2,1,0:T(8,128)} %get-tuple-element.19), calls=%async_computation.2 | async-start | bytes 2097152 | tf_op jit(solution)/shard_map/all_to_all | solution.py:26
  67.7 3.6 %collective-permute-start.2 = (f32[8,128]{1,0:T(8,128)S(1)}, f32[8,128]{1,0:T(8,128)S(1)}, u32[]{:S(2)}, u32[]{:S(2)}) collective-permute-start(f32[8,128]{1,0:T(8,128)S(1)} %get-tuple-element.18), channel_id=1, source_target_pairs={{0,1},{1,0},{2,3},{3,2},{4,5},{5,4},{6,7},{7,6},{8,9},{9,8},{10,11... | collective-permute-start | bytes 12296 | tf_op jit(solution)/shard_map/ppermute | solution.py:34
  71.2 4.7 %collective-permute-start.3 = (f32[8,128]{1,0:T(8,128)S(1)}, f32[8,128]{1,0:T(8,128)S(1)}, u32[]{:S(2)}, u32[]{:S(2)}) collective-permute-start(f32[8,128]{1,0:T(8,128)S(1)} %add.25), channel_id=1, source_target_pairs={{0,2},{2,0},{4,6},{6,4},{8,10},{10,8},{12,14},{14,12},{1,3},{3,1},... | collective-permute-start | bytes 12296 | tf_op jit(solution)/shard_map/ppermute | solution.py:34
  75.9 3.7 %collective-permute-start.4 = (f32[8,128]{1,0:T(8,128)S(1)}, f32[8,128]{1,0:T(8,128)S(1)}, u32[]{:S(2)}, u32[]{:S(2)}) collective-permute-start(f32[8,128]{1,0:T(8,128)S(1)} %add.26), channel_id=1, source_target_pairs={{0,4},{2,6},{4,0},{6,2},{8,12},{10,14},{12,8},{14,10},{1,5},{3,7},... | collective-permute-start | bytes 12296 | tf_op jit(solution)/shard_map/ppermute | solution.py:34
  79.6 6.4 %collective-permute-start.5 = (f32[8,128]{1,0:T(8,128)S(1)}, f32[8,128]{1,0:T(8,128)S(1)}, u32[]{:S(2)}, u32[]{:S(2)}) collective-permute-start(f32[8,128]{1,0:T(8,128)S(1)} %add.27), channel_id=1, source_target_pairs={{0,8},{2,10},{4,12},{6,14},{8,0},{10,2},{12,4},{14,6},{1,9},{3,11}... | collective-permute-start | bytes 12296 | tf_op jit(solution)/shard_map/ppermute | solution.py:34
  86.0 1.0 copy-start.4
  98.2 34.7 %copy-start.6 = (f32[32,512]{1,0:T(8,128)S(1)}, f32[32,512]{1,0:T(8,128)}, u32[]{:S(2)}) copy-start(f32[32,512]{1,0:T(8,128)} %get-tuple-element.17) | copy-start | bytes 196612
  98.2 18.3 %collective-permute-start.6 = (f32[512,512]{1,0:T(8,128)S(1)}, f32[512,512]{1,0:T(8,128)S(1)}, u32[]{:S(2)}, u32[]{:S(2)}) collective-permute-start(f32[512,512]{1,0:T(8,128)S(1)} %get-tuple-element.21), channel_id=1, source_target_pairs={{0,1},{1,2},{2,3},{3,4},{4,5},{5,6},{6,7},{7,8},{8,9},{9,10},{10,1... | collective-permute-start | bytes 3145736 | tf_op jit(solution)/shard_map/ppermute | solution.py:22
  104.8 16.1 %collective-permute-start.7 = (f32[512,512]{1,0:T(8,128)S(1)}, f32[512,512]{1,0:T(8,128)S(1)}, u32[]{:S(2)}, u32[]{:S(2)}) collective-permute-start(f32[512,512]{1,0:T(8,128)S(1)} %get-tuple-element.22), channel_id=1, source_target_pairs={{1,0},{2,1},{3,2},{4,3},{5,4},{6,5},{7,6},{8,7},{9,8},{10,9},{11,1... | collective-permute-start | bytes 3145736 | tf_op jit(solution)/shard_map/ppermute | solution.py:22
  122.3 23.5 %all-to-all-start.3 = ((f32[16,32,512]{2,1,0:T(8,128)}), f32[16,32,512]{2,1,0:T(8,128)S(1)}, u32[]{:S(2)}, u32[]{:S(2)}) async-start(f32[16,32,512]{2,1,0:T(8,128)} %bitcast.16), calls=%async_computation.3 | async-start | bytes 2097152 | tf_op jit(solution)/shard_map/all_to_all | solution.py:26

commit v3 on v2

--- a/solution.py
+++ b/solution.py
@@ -13,13 +13,16 @@
 LANES = 128
 EXTRA = 8
 MIB = 1 << 20
+KERNEL_VMEM = 20 * MIB
 F32 = jnp.float32
 
 
-def shifted(block, distance):
+def moved(crossing, local):
     count = lax.axis_size(SECTOR)
-    route = [(i, i + distance) for i in range(count) if 0 <= i + distance < count]
-    return lax.ppermute(block, SECTOR, route)
+    upward = [(i, i + 1) for i in range(1, count - 1, 2)]
+    downward = [(j, i) for i, j in upward]
+    swap = [(i, i ^ 1) for i in range(count)]
+    return lax.ppermute(crossing, SECTOR, upward + downward), lax.ppermute(local, SECTOR, swap)
 
 
 def swapped(x):
@@ -62,19 +65,23 @@
         inner_high, inner_low = halves(inner)
         right_high, right_low = halves(right[0])
         result = product(inner_high, inner_low, right_high, right_low)
-        for side, out in enumerate(outs):
-
-            @pl.when(target[0, slot] - sector == side - 1)
+        goal = target[0, slot]
+        kept = goal == sector
+        swapped_here = goal == (sector ^ 1)
+        roles = (jnp.logical_not(kept | swapped_here), kept, swapped_here)
+        for role, out in zip(roles, outs):
+
+            @pl.when(role)
             def _(out=out):
                 out[...] += result
 
 
-def first_kernel(count, target, left, right, field, low_out, mid_out, high_out, f_high, f_low):
+def first_kernel(count, target, left, right, field, crossing, kept, local, f_high, f_low):
     @pl.when(pl.program_id(0) == 0)
     def _():
         f_high[...], f_low[...] = halves(field[...])
 
-    outs = (low_out, mid_out, high_out)
+    outs = (crossing, kept, local)
     accumulate(lax.axis_index(SECTOR), count, target, left, right, f_high, f_low, outs)
 
 
@@ -87,7 +94,7 @@
 
 
 def second_kernel(
-    count, target, left, right, sums, field, scaling, image, low_out, mid_out, high_out, f_high, f_low
+    count, target, left, right, sums, field, scaling, image, crossing, kept, local, f_high, f_low
 ):
     @pl.when(pl.program_id(0) == 0)
     def _():
@@ -96,36 +103,43 @@
         correction = scaling[...] * (image[...] - rayleigh * vector) - share * vector
         f_high[...], f_low[...] = halves(correction)
 
-    outs = (low_out, mid_out, high_out)
+    outs = (crossing, kept, local)
     accumulate(lax.axis_index(SECTOR), count, target, left, right, f_high, f_low, outs)
 
 
-def partial_image(body, counts, targets, left_stack, right_stack, fields):
+def partial_image(body, counts, targets, left_stack, right_stack, fields, streamed=False):
     slots, width, _ = right_stack.shape
 
-    def operand(i, count, target):
+    def operand(i, count):
         return (jnp.minimum(i, count[0, 0] - 1), 0, 0)
 
-    def whole(shape):
-        return pl.BlockSpec(shape, lambda i, *_: (0,) * len(shape))
-
+    in_vmem = pl.BlockSpec(memory_space=pltpu.VMEM)
+    targets, left_stack, right_stack = (
+        pltpu.with_memory_space_constraint(x, pltpu.HBM)
+        for x in (targets, left_stack, right_stack)
+    )
     block = (width, width)
+    field_spec = in_vmem
+    if streamed:
+        fields = [pltpu.with_memory_space_constraint(x, pltpu.HBM) for x in fields]
+        field_spec = pl.BlockSpec(block, lambda i, *_: (0, 0), pipeline_mode=pl.Buffered(1))
     return pl.pallas_call(
         body,
         out_shape=[jax.ShapeDtypeStruct(block, F32)] * 3,
         grid_spec=pltpu.PrefetchScalarGridSpec(
-            num_scalar_prefetch=2,
+            num_scalar_prefetch=1,
             grid=(slots,),
             in_specs=[
+                pl.BlockSpec(targets.shape, lambda i, *_: (0, 0), memory_space=pltpu.SMEM),
                 pl.BlockSpec((1, width, width), operand),
                 pl.BlockSpec((1, width, width), operand),
-                *[whole(x.shape) for x in fields],
+                *[field_spec] * len(fields),
             ],
-            out_specs=[whole(block)] * 3,
+            out_specs=[in_vmem] * 3,
             scratch_shapes=[pltpu.VMEM(block, jnp.bfloat16)] * 2,
         ),
         compiler_params=pltpu.CompilerParams(
-            dimension_semantics=("arbitrary",), vmem_limit_bytes=48 * MIB
+            dimension_semantics=("arbitrary",), vmem_limit_bytes=KERNEL_VMEM
         ),
         cost_estimate=pl.CostEstimate(
             flops=slots * 12 * width**3, bytes_accessed=slots * 8 * width**2, transcendentals=0
@@ -137,13 +151,13 @@
     return [(c * slab, slice(c * LANES, (c + 1) * LANES)) for c in range(width // LANES)]
 
 
-def combine_kernel(mid, upward, downward, field, scaling, packed, totals):
+def combine_kernel(mid, crossed, local, field, scaling, packed, totals):
     peers, slab, width = mid.shape
     where = tiles(mid, slab, width)
     cross = jnp.zeros((slab, width), F32)
     scaled_cross = jnp.zeros((slab, width), F32)
     for peer in range(peers):
-        total = mid[peer] + (upward[peer] + downward[peer])
+        total = mid[peer] + (crossed[peer] + local[peer])
         for row, lanes in where:
             packed[peer, row : row + slab] = total[:, lanes]
         weighted = field[peer] * total
@@ -162,7 +176,7 @@
         packed[peer, len(where) * slab :] = totals[...]
 
 
-def gathered_kernel(arrived, image, copies, sums):
+def gathered_kernel(arrived, image, copies, sums, sent):
     peers, slab, width = copies.shape
     total = arrived[0]
     for peer in range(1, peers):
@@ -170,15 +184,24 @@
     where = tiles(image, slab, width)
     for row, lanes in where:
         image[:, lanes] = total[row : row + slab]
-    for peer in range(peers):
-        copies[peer] = image[...]
+    fills = [pltpu.make_async_copy(image, copies.at[i], sent.at[i]) for i in range(peers)]
+    for fill in fills:
+        fill.start()
     sums[...] = total[len(where) * slab :]
-
-
-def small_call(body, out_shapes, args, scratch=()):
+    for fill in fills:
+        fill.wait()
+
+
+def small_call(body, out_shapes, args, scratch=(), spaces=None):
+    spaces = spaces or [pltpu.VMEM] * len(out_shapes)
     return pl.pallas_call(
         body,
-        out_shape=[jax.ShapeDtypeStruct(s, F32) for s in out_shapes],
+        in_specs=[pl.BlockSpec(memory_space=pltpu.VMEM)] * len(args),
+        out_specs=[pl.BlockSpec(memory_space=space) for space in spaces],
+        out_shape=[
+            pltpu.HBM(s, F32) if space == pltpu.HBM else jax.ShapeDtypeStruct(s, F32)
+            for s, space in zip(out_shapes, spaces)
+        ],
         scratch_shapes=scratch,
         compiler_params=pltpu.CompilerParams(vmem_limit_bytes=32 * MIB),
     )(*args)
@@ -200,18 +223,19 @@
         right_stack=right_ops[0],
     )
 
-    low, mid, high = image_of(first_kernel, fields=(field,))
-    upward, downward = shifted(high, 1), shifted(low, -1)
+    crossing, mid, local = image_of(first_kernel, fields=(field,), streamed=True)
+    crossed, local = moved(crossing, local)
     scaling_late, _ = lax.optimization_barrier((scaling, mid))
     full_scaling = swapped(jnp.broadcast_to(scaling_late[None], split))
     (packed,) = small_call(
         combine_kernel,
         [(peers, packed_rows, LANES)],
-        [*[x.reshape(split) for x in (mid, upward, downward, field)], full_scaling],
+        [*[x.reshape(split) for x in (mid, crossed, local, field)], full_scaling],
         [pltpu.VMEM((EXTRA, LANES), F32)],
     )
     first_image, copies, sums = small_call(
-        gathered_kernel, [(slab, width), split, (EXTRA, LANES)], [swapped(packed)]
+        gathered_kernel, [(slab, width), split, (EXTRA, LANES)], [swapped(packed)],
+        [pltpu.SemaphoreType.DMA((peers,))], [pltpu.VMEM, pltpu.HBM, pltpu.VMEM],
     )
     full_image = swapped(copies)
     sums = over_sectors(sums)
@@ -223,8 +247,9 @@
     correction = scaling * (first_image - rayleigh * own) - share * own
 
     fields = (sums, field, full_scaling.reshape(field.shape), full_image.reshape(field.shape))
-    low, mid, high = image_of(second_kernel, fields=fields)
-    total = mid + shifted(high, 1) + shifted(low, -1)
+    crossing, mid, local = image_of(second_kernel, fields=fields)
+    crossed, local = moved(crossing, local)
+    total = mid + crossed + local
     second_image = swapped(total.reshape(split)).sum(axis=0)
     return (first_image[None], correction[None], second_image[None])
 

time: 147 us -> 138 us (0.939)
  the two profiles are of different devices: /device:TPU:65 before, /device:TPU:64 now
where the time goes in v3:
time: 138 us
  blocking collectives  45.9 us (33%)
  waiting for transfers between devices  38.6 us (28%)
  Pallas kernels  22.9 us (17%)
  starting transfers between devices  21.9 us (16%)
  between operations  4.74 us (3%)
  other arithmetic  2.71 us (2%)
    all_to_all x2, blocking collectives, swapped(): return lax.all_to_all(x, TERM, 0, 0, tiled=True)  45.9 us
    pallas_call x2, Pallas kernels, partial_image(): pl.pallas_call(body, out_shape=[jax.ShapeDtypeStruct(block, F32)] * 3, gr...  20.7 us
    ppermute x2, waiting for transfers between devices, moved(): lax.ppermute(crossing, SECTOR, upward + downward)  14.1 us
    all_to_all x2, waiting for transfers between devices, swapped(): return lax.all_to_all(x, TERM, 0, 0, tiled=True)  13.2 us
    ppermute x4, waiting for transfers between devices, over_sectors(): x = x + lax.ppermute(x, axis, [(i, i ^ mask) for i in range(count)])  11.4 us
    all_to_all x2, starting transfers between devices, swapped(): return lax.all_to_all(x, TERM, 0, 0, tiled=True)  10.7 us
    ppermute x4, starting transfers between devices, over_sectors(): x = x + lax.ppermute(x, axis, [(i, i ^ mask) for i in range(count)])  7.06 us
    ppermute x2, starting transfers between devices, moved(): lax.ppermute(crossing, SECTOR, upward + downward)  3.97 us
  transfers between devices with their start and end apart: 10, of which 6 were waited for; matrix products, arithmetic and copies ran while one was open for 1% of the time, Pallas kernels for 0%

profile of v3, /device:TPU:64, one launch (start us, length us, event | category | flops | bytes accessed | tf_op | source)
XLA Modules:
  0.0 137.6 jit_solution(8535432034798779842)
XLA Ops:
  1.3 0.0 copy-start.1
  1.3 0.0 copy-start
  1.3 10.4 %shard_map.85 = (f32[512,512]{1,0:T(8,128)S(1)}, f32[512,512]{1,0:T(8,128)S(1)}, f32[512,512]{1,0:T(8,128)S(1)}) custom-call(s32[1,1]{1,0:T(1,128)S(6)} %copy.9.count, s32[1,4]{1,0:T(1,128)} %target.3, f32[4,512,512]{2,1,0:T(8,128)} %bitcast.40, f32[4,512,512]{2,1,0:T(8,128)} %bitcast.42, f32[512,512]{1,0:T(8,128)} %bitcast.29), custom_call_target="tpu_custom_call" | custom-call | flops 6442450944 | bytes 8388608 | tf_op jit(solution)/shard_map/pallas_call | solution.py:126
  11.7 1.9 %collective-permute-start = (f32[512,512]{1,0:T(8,128)S(1)}, f32[512,512]{1,0:T(8,128)S(1)}, u32[]{:S(2)}, u32[]{:S(2)}) collective-permute-start(f32[512,512]{1,0:T(8,128)S(1)} %get-tuple-element.14), channel_id=1, source_target_pairs={{1,2},{3,4},{5,6},{7,8},{9,10},{11,12},{13,14},{2,1},{4,3},{6,5},{... | collective-permute-start | bytes 3145736 | tf_op jit(solution)/shard_map/ppermute | solution.py:25
  13.6 0.1 collective-permute-start.1
  13.7 0.0 copy-done.1
  13.7 0.1 broadcast_in_dim.15
  13.8 25.4 %all_to_all.20.scaling = f32[16,32,512]{2,1,0:T(8,128)S(1)} all-to-all(f32[16,32,512]{2,1,0:T(8,128)S(1)} %broadcast_in_dim.15), channel_id=1, replica_groups=mesh['term_0'=4,'term_1'=4,'sector_0'=8,'sector_1'=2] {'term_0','term_1'}, dimensions={0} | all-to-all | bytes 2097152 | tf_op jit(solution)/shard_map/all_to_all | solution.py:29
  39.3 0.0 collective-permute-done
  39.3 0.0 collective-permute-done.1
  39.3 0.0 copy-done
  39.3 0.4 shard_map.86
  39.7 20.5 %all_to_all.21.arrived = f32[16,136,128]{2,1,0:T(8,128)S(1)} all-to-all(f32[16,136,128]{2,1,0:T(8,128)S(1)} %shard_map.86), channel_id=1, replica_groups=mesh['term_0'=4,'term_1'=4,'sector_0'=8,'sector_1'=2] {'term_0','term_1'}, dimensions={0} | all-to-all | bytes 2228224 | tf_op jit(solution)/shard_map/all_to_all | solution.py:29
  60.2 1.8 %shard_map.87 = (f32[32,512]{1,0:T(8,128)}, f32[16,32,512]{2,1,0:T(8,128)}, f32[8,128]{1,0:T(8,128)S(1)}) custom-call(f32[16,136,128]{2,1,0:T(8,128)S(1)} %all_to_all.21.arrived), custom_call_target="tpu_custom_call" | custom-call | tf_op jit(solution)/shard_map/pallas_call | solution.py:197
  62.0 3.7 %all-to-all-start.2 = ((f32[16,32,512]{2,1,0:T(8,128)}), f32[16,32,512]{2,1,0:T(8,128)S(1)}, u32[]{:S(2)}, u32[]{:S(2)}) async-start(f32[16,32,512]{2,1,0:T(8,128)} %get-tuple-element.19), calls=%async_computation.2 | async-start | bytes 2097152 | tf_op jit(solution)/shard_map/all_to_all | solution.py:29
  65.7 0.1 collective-permute-start.2
  65.8 1.2 collective-permute-done.2
  67.0 3.6 %collective-permute-start.3 = (f32[8,128]{1,0:T(8,128)S(1)}, f32[8,128]{1,0:T(8,128)S(1)}, u32[]{:S(2)}, u32[]{:S(2)}) collective-permute-start(f32[8,128]{1,0:T(8,128)S(1)} %add.25), channel_id=1, source_target_pairs={{0,2},{2,0},{4,6},{6,4},{8,10},{10,8},{12,14},{14,12},{1,3},{3,1},... | collective-permute-start | bytes 12296 | tf_op jit(solution)/shard_map/ppermute | solution.py:37
  70.5 1.6 %collective-permute-done.3 = f32[8,128]{1,0:T(8,128)S(1)} collective-permute-done((f32[8,128]{1,0:T(8,128)S(1)}, f32[8,128]{1,0:T(8,128)S(1)}, u32[]{:S(2)}, u32[]{:S(2)}) %collective-permute-start.3) | collective-permute-done | bytes 4128 | tf_op jit(solution)/shard_map/ppermute | solution.py:37
  72.1 0.0 collective-permute-start.4
  72.1 4.5 %collective-permute-done.4 = f32[8,128]{1,0:T(8,128)S(1)} collective-permute-done((f32[8,128]{1,0:T(8,128)S(1)}, f32[8,128]{1,0:T(8,128)S(1)}, u32[]{:S(2)}, u32[]{:S(2)}) %collective-permute-start.4) | collective-permute-done | bytes 4128 | tf_op jit(solution)/shard_map/ppermute | solution.py:37
  76.6 3.4 %collective-permute-start.5 = (f32[8,128]{1,0:T(8,128)S(1)}, f32[8,128]{1,0:T(8,128)S(1)}, u32[]{:S(2)}, u32[]{:S(2)}) collective-permute-start(f32[8,128]{1,0:T(8,128)S(1)} %add.27), channel_id=1, source_target_pairs={{0,8},{2,10},{4,12},{6,14},{8,0},{10,2},{12,4},{14,6},{1,9},{3,11}... | collective-permute-start | bytes 12296 | tf_op jit(solution)/shard_map/ppermute | solution.py:37
  80.0 4.1 %collective-permute-done.5 = f32[8,128]{1,0:T(8,128)S(1)} collective-permute-done((f32[8,128]{1,0:T(8,128)S(1)}, f32[8,128]{1,0:T(8,128)S(1)}, u32[]{:S(2)}, u32[]{:S(2)}) %collective-permute-start.5) | collective-permute-done | bytes 4128 | tf_op jit(solution)/shard_map/ppermute | solution.py:37
  84.2 0.0 all-to-all-done.2
  84.2 10.3 %shard_map.88 = (f32[512,512]{1,0:T(8,128)S(1)}, f32[512,512]{1,0:T(8,128)S(1)}, f32[512,512]{1,0:T(8,128)S(1)}) custom-call(s32[1,1]{1,0:T(1,128)S(6)} %copy.9.count, s32[1,4]{1,0:T(1,128)} %target.3, f32[4,512,512]{2,1,0:T(8,128)} %bitcast.41, f32[4,512,512]{2,1,0:T(8,128)} %bitcast.43, f32[8,128]{1,0:T(8,128)S(1)} %add.28.sums, f32[512,512]{1,0:T(8,128)S(1)} %bitcast.31, ...), custom_call_target="tpu_custom_call" | custom-call | flops 6442450944 | bytes 8388608 | tf_op jit(solution)/shard_map/pallas_call | solution.py:126
  94.5 0.0 copy-start.2
  94.5 2.1 %collective-permute-start.6 = (f32[512,512]{1,0:T(8,128)S(1)}, f32[512,512]{1,0:T(8,128)S(1)}, u32[]{:S(2)}, u32[]{:S(2)}) collective-permute-start(f32[512,512]{1,0:T(8,128)S(1)} %get-tuple-element.21), channel_id=1, source_target_pairs={{1,2},{3,4},{5,6},{7,8},{9,10},{11,12},{13,14},{2,1},{4,3},{6,5},{... | collective-permute-start | bytes 3145736 | tf_op jit(solution)/shard_map/ppermute | solution.py:25
  96.6 0.1 collective-permute-start.7
  96.7 14.1 %collective-permute-done.6 = f32[512,512]{1,0:T(8,128)S(1)} collective-permute-done((f32[512,512]{1,0:T(8,128)S(1)}, f32[512,512]{1,0:T(8,128)S(1)}, u32[]{:S(2)}, u32[]{:S(2)}) %collective-permute-start.6) | collective-permute-done | bytes 1048608 | tf_op jit(solution)/shard_map/ppermute | solution.py:25
  110.8 0.0 collective-permute-done.7
  110.8 1.3 add_add_fusion
  112.1 7.1 %all-to-all-start.3 = ((f32[16,32,512]{2,1,0:T(8,128)}), f32[16,32,512]{2,1,0:T(8,128)S(1)}, u32[]{:S(2)}, u32[]{:S(2)}) async-start(f32[16,32,512]{2,1,0:T(8,128)} %bitcast.16), calls=%async_computation.3 | async-start | bytes 2097152 | tf_op jit(solution)/shard_map/all_to_all | solution.py:29
  119.2 0.6 fusion.2
  123.1 0.0 copy-done.2
  123.1 0.7 fusion
  123.7 13.2 %all-to-all-done.3 = f32[16,32,512]{2,1,0:T(8,128)S(1)} async-done(((f32[16,32,512]{2,1,0:T(8,128)}), f32[16,32,512]{2,1,0:T(8,128)S(1)}, u32[]{:S(2)}, u32[]{:S(2)}) %all-to-all-start.3) | async-done | bytes 1048608 | tf_op jit(solution)/shard_map/all_to_all | solution.py:29
  136.9 0.7 reduce_sum.9
  (4 shorter events, 0.0 us)
Async XLA Ops:
  1.3 12.4 %copy-start.1 = (f32[1,32,512]{2,1,0:T(8,128)S(1)}, f32[1,32,512]{2,1,0:T(8,128)}, u32[]{:S(2)}) copy-start(f32[1,32,512]{2,1,0:T(8,128)} %param.7) | copy-start | bytes 196612
  1.3 38.0 %copy-start = (f32[1,512,512]{2,1,0:T(8,128)S(1)}, f32[1,512,512]{2,1,0:T(8,128)}, u32[]{:S(2)}) copy-start(f32[1,512,512]{2,1,0:T(8,128)} %param.6) | copy-start | bytes 3145732
  11.7 27.6 %collective-permute-start = (f32[512,512]{1,0:T(8,128)S(1)}, f32[512,512]{1,0:T(8,128)S(1)}, u32[]{:S(2)}, u32[]{:S(2)}) collective-permute-start(f32[512,512]{1,0:T(8,128)S(1)} %get-tuple-element.14), channel_id=1, source_target_pairs={{1,2},{3,4},{5,6},{7,8},{9,10},{11,12},{13,14},{2,1},{4,3},{6,5},{... | collective-permute-start | bytes 3145736 | tf_op jit(solution)/shard_map/ppermute | solution.py:25
  13.6 25.7 %collective-permute-start.1 = (f32[512,512]{1,0:T(8,128)S(1)}, f32[512,512]{1,0:T(8,128)S(1)}, u32[]{:S(2)}, u32[]{:S(2)}) collective-permute-start(f32[512,512]{1,0:T(8,128)S(1)} %get-tuple-element.15), channel_id=1, source_target_pairs={{0,1},{1,0},{2,3},{3,2},{4,5},{5,4},{6,7},{7,6},{8,9},{9,8},{10,11... | collective-permute-start | bytes 3145736 | tf_op jit(solution)/shard_map/ppermute | solution.py:25
  62.0 22.1 %all-to-all-start.2 = ((f32[16,32,512]{2,1,0:T(8,128)}), f32[16,32,512]{2,1,0:T(8,128)S(1)}, u32[]{:S(2)}, u32[]{:S(2)}) async-start(f32[16,32,512]{2,1,0:T(8,128)} %get-tuple-element.19), calls=%async_computation.2 | async-start | bytes 2097152 | tf_op jit(solution)/shard_map/all_to_all | solution.py:29
  65.7 1.3 collective-permute-start.2
  67.0 5.2 %collective-permute-start.3 = (f32[8,128]{1,0:T(8,128)S(1)}, f32[8,128]{1,0:T(8,128)S(1)}, u32[]{:S(2)}, u32[]{:S(2)}) collective-permute-start(f32[8,128]{1,0:T(8,128)S(1)} %add.25), channel_id=1, source_target_pairs={{0,2},{2,0},{4,6},{6,4},{8,10},{10,8},{12,14},{14,12},{1,3},{3,1},... | collective-permute-start | bytes 12296 | tf_op jit(solution)/shard_map/ppermute | solution.py:37
  72.1 4.5 %collective-permute-start.4 = (f32[8,128]{1,0:T(8,128)S(1)}, f32[8,128]{1,0:T(8,128)S(1)}, u32[]{:S(2)}, u32[]{:S(2)}) collective-permute-start(f32[8,128]{1,0:T(8,128)S(1)} %add.26), channel_id=1, source_target_pairs={{0,4},{2,6},{4,0},{6,2},{8,12},{10,14},{12,8},{14,10},{1,5},{3,7},... | collective-permute-start | bytes 12296 | tf_op jit(solution)/shard_map/ppermute | solution.py:37
  76.6 7.5 %collective-permute-start.5 = (f32[8,128]{1,0:T(8,128)S(1)}, f32[8,128]{1,0:T(8,128)S(1)}, u32[]{:S(2)}, u32[]{:S(2)}) collective-permute-start(f32[8,128]{1,0:T(8,128)S(1)} %add.27), channel_id=1, source_target_pairs={{0,8},{2,10},{4,12},{6,14},{8,0},{10,2},{12,4},{14,6},{1,9},{3,11}... | collective-permute-start | bytes 12296 | tf_op jit(solution)/shard_map/ppermute | solution.py:37
  94.5 28.6 %copy-start.2 = (f32[32,512]{1,0:T(8,128)S(1)}, f32[32,512]{1,0:T(8,128)}, u32[]{:S(2)}) copy-start(f32[32,512]{1,0:T(8,128)} %get-tuple-element.17) | copy-start | bytes 196612
  94.5 16.2 %collective-permute-start.6 = (f32[512,512]{1,0:T(8,128)S(1)}, f32[512,512]{1,0:T(8,128)S(1)}, u32[]{:S(2)}, u32[]{:S(2)}) collective-permute-start(f32[512,512]{1,0:T(8,128)S(1)} %get-tuple-element.21), channel_id=1, source_target_pairs={{1,2},{3,4},{5,6},{7,8},{9,10},{11,12},{13,14},{2,1},{4,3},{6,5},{... | collective-permute-start | bytes 3145736 | tf_op jit(solution)/shard_map/ppermute | solution.py:25
  96.6 14.2 %collective-permute-start.7 = (f32[512,512]{1,0:T(8,128)S(1)}, f32[512,512]{1,0:T(8,128)S(1)}, u32[]{:S(2)}, u32[]{:S(2)}) collective-permute-start(f32[512,512]{1,0:T(8,128)S(1)} %get-tuple-element.22), channel_id=1, source_target_pairs={{0,1},{1,0},{2,3},{3,2},{4,5},{5,4},{6,7},{7,6},{8,9},{9,8},{10,11... | collective-permute-start | bytes 3145736 | tf_op jit(solution)/shard_map/ppermute | solution.py:25
  112.1 24.8 %all-to-all-start.3 = ((f32[16,32,512]{2,1,0:T(8,128)}), f32[16,32,512]{2,1,0:T(8,128)S(1)}, u32[]{:S(2)}, u32[]{:S(2)}) async-start(f32[16,32,512]{2,1,0:T(8,128)} %bitcast.16), calls=%async_computation.3 | async-start | bytes 2097152 | tf_op jit(solution)/shard_map/all_to_all | solution.py:29

commit v4 on v3

--- a/solution.py
+++ b/solution.py
@@ -25,17 +25,33 @@
     return lax.ppermute(crossing, SECTOR, upward + downward), lax.ppermute(local, SECTOR, swap)
 
 
+def from_ring(x, axis):
+    size = lax.axis_size(axis)
+    steps = [[(i, (i + k) % size) for i in range(size)] for k in range(1, size)]
+    return [x, *[lax.ppermute(x, axis, pairs) for pairs in steps]]
+
+
 def swapped(x):
     return lax.all_to_all(x, TERM, 0, 0, tiled=True)
 
 
-def over_sectors(x):
+def sector_steps():
     for axis in SECTOR[::-1]:
         count = lax.axis_size(axis)
         mask = 1
         while mask < count:
-            x = x + lax.ppermute(x, axis, [(i, i ^ mask) for i in range(count)])
+            yield functools.partial(exchanged, axis=axis, mask=mask)
             mask *= 2
+
+
+def exchanged(x, axis, mask):
+    pairs = [(i, i ^ mask) for i in range(lax.axis_size(axis))]
+    return x + lax.ppermute(x, axis, pairs)
+
+
+def over_sectors(x, steps=slice(None)):
+    for step in list(sector_steps())[steps]:
+        x = step(x)
     return x
 
 
@@ -85,29 +101,42 @@
     accumulate(lax.axis_index(SECTOR), count, target, left, right, f_high, f_low, outs)
 
 
-def coefficients(sums):
-    cross, norm_sq = sums[0:1, 0:1], sums[1:2, 0:1]
-    scaled_cross, scaled_norm = sums[2:3, 0:1], sums[3:4, 0:1]
-    rayleigh = cross / norm_sq
-    share = (scaled_cross - rayleigh * scaled_norm) / norm_sq
-    return rayleigh, share
-
-
 def second_kernel(
-    count, target, left, right, sums, field, scaling, image, crossing, kept, local, f_high, f_low
+    count,
+    target,
+    left,
+    right,
+    sums,
+    field,
+    image,
+    *rest,
 ):
+    ring, (crossing, kept, local, overlap, f_high, f_low) = rest[:-6], rest[-6:]
+    peers, slab, width = field.shape
+
     @pl.when(pl.program_id(0) == 0)
     def _():
-        rayleigh, share = coefficients(sums[...])
-        vector = field[...]
-        correction = scaling[...] * (image[...] - rayleigh * vector) - share * vector
-        f_high[...], f_low[...] = halves(correction)
+        rayleigh = sums[0:1, 0:1] / sums[1:2, 0:1]
+        along_0, along_1 = (lax.axis_index(axis) for axis in TERM)
+        size = ring[0].shape[0]
+        weighted = jnp.zeros((slab, width), F32)
+        for j, scaling in enumerate(ring):
+            for k in range(size):
+                peer = lax.rem(along_0 + len(ring) - j, len(ring)) * size
+                peer += lax.rem(along_1 + size - k, size)
+                vector = field[peer]
+                raw = scaling[k] * (image[peer] - rayleigh * vector)
+                f_high[peer], f_low[peer] = halves(raw)
+                weighted += vector * raw
+        overlap[...] = jnp.broadcast_to(jnp.sum(weighted, keepdims=True), overlap.shape)
 
     outs = (crossing, kept, local)
+    flat = (peers * slab, width)
+    f_high, f_low = f_high.reshape(flat), f_low.reshape(flat)
     accumulate(lax.axis_index(SECTOR), count, target, left, right, f_high, f_low, outs)
 
 
-def partial_image(body, counts, targets, left_stack, right_stack, fields, streamed=False):
+def partial_image(body, counts, targets, left_stack, right_stack, fields, extra=(), scratch=None, streamed=False):
     slots, width, _ = right_stack.shape
 
     def operand(i, count):
@@ -125,7 +154,7 @@
         field_spec = pl.BlockSpec(block, lambda i, *_: (0, 0), pipeline_mode=pl.Buffered(1))
     return pl.pallas_call(
         body,
-        out_shape=[jax.ShapeDtypeStruct(block, F32)] * 3,
+        out_shape=[jax.ShapeDtypeStruct(x, F32) for x in (*[block] * 3, *extra)],
         grid_spec=pltpu.PrefetchScalarGridSpec(
             num_scalar_prefetch=1,
             grid=(slots,),
@@ -135,8 +164,8 @@
                 pl.BlockSpec((1, width, width), operand),
                 *[field_spec] * len(fields),
             ],
-            out_specs=[in_vmem] * 3,
-            scratch_shapes=[pltpu.VMEM(block, jnp.bfloat16)] * 2,
+            out_specs=[in_vmem] * (3 + len(extra)),
+            scratch_shapes=[pltpu.VMEM(scratch or block, jnp.bfloat16)] * 2,
         ),
         compiler_params=pltpu.CompilerParams(
             dimension_semantics=("arbitrary",), vmem_limit_bytes=KERNEL_VMEM
@@ -151,32 +180,25 @@
     return [(c * slab, slice(c * LANES, (c + 1) * LANES)) for c in range(width // LANES)]
 
 
-def combine_kernel(mid, crossed, local, field, scaling, packed, totals):
+def combine_kernel(mid, crossed, local, field, packed, sums):
     peers, slab, width = mid.shape
     where = tiles(mid, slab, width)
     cross = jnp.zeros((slab, width), F32)
-    scaled_cross = jnp.zeros((slab, width), F32)
     for peer in range(peers):
         total = mid[peer] + (crossed[peer] + local[peer])
         for row, lanes in where:
             packed[peer, row : row + slab] = total[:, lanes]
-        weighted = field[peer] * total
-        cross += weighted
-        scaled_cross += scaling[peer] * weighted
-    me = lax.axis_index(TERM)
-    own = field[me]
-    square = own * own
-    parts = [cross, square, scaled_cross, scaling[me] * square]
+        cross += field[peer] * total
+    own = field[lax.axis_index(TERM)]
     line = lax.broadcasted_iota(jnp.int32, (EXTRA, LANES), 0)
-    tile = jnp.zeros((EXTRA, LANES), F32)
-    for i, part in enumerate(parts):
-        tile = jnp.where(line == i, jnp.sum(part, keepdims=True), tile)
-    totals[...] = tile
+    sums[...] = jnp.where(
+        line == 0, jnp.sum(cross, keepdims=True), jnp.sum(own * own, keepdims=True)
+    )
     for peer in range(peers):
-        packed[peer, len(where) * slab :] = totals[...]
-
-
-def gathered_kernel(arrived, image, copies, sums, sent):
+        packed[peer, len(where) * slab :] = sums[...]
+
+
+def gathered_kernel(arrived, image, copies, sums):
     peers, slab, width = copies.shape
     total = arrived[0]
     for peer in range(1, peers):
@@ -184,12 +206,9 @@
     where = tiles(image, slab, width)
     for row, lanes in where:
         image[:, lanes] = total[row : row + slab]
-    fills = [pltpu.make_async_copy(image, copies.at[i], sent.at[i]) for i in range(peers)]
-    for fill in fills:
-        fill.start()
+    for peer in range(peers):
+        copies[peer] = image[...]
     sums[...] = total[len(where) * slab :]
-    for fill in fills:
-        fill.wait()
 
 
 def small_call(body, out_shapes, args, scratch=(), spaces=None):
@@ -197,7 +216,10 @@
     return pl.pallas_call(
         body,
         in_specs=[pl.BlockSpec(memory_space=pltpu.VMEM)] * len(args),
-        out_specs=[pl.BlockSpec(memory_space=space) for space in spaces],
+        out_specs=[
+            pl.BlockSpec() if space == pltpu.HBM else pl.BlockSpec(memory_space=space)
+            for space in spaces
+        ],
         out_shape=[
             pltpu.HBM(s, F32) if space == pltpu.HBM else jax.ShapeDtypeStruct(s, F32)
             for s, space in zip(out_shapes, spaces)
@@ -226,31 +248,44 @@
     crossing, mid, local = image_of(first_kernel, fields=(field,), streamed=True)
     crossed, local = moved(crossing, local)
     scaling_late, _ = lax.optimization_barrier((scaling, mid))
-    full_scaling = swapped(jnp.broadcast_to(scaling_late[None], split))
+    stacked = jnp.stack(from_ring(scaling_late, TERM[1]))
+    crossed, stacked = lax.optimization_barrier((crossed, stacked))
+    ring = from_ring(stacked, TERM[0])
     (packed,) = small_call(
         combine_kernel,
         [(peers, packed_rows, LANES)],
-        [*[x.reshape(split) for x in (mid, crossed, local, field)], full_scaling],
+        [x.reshape(split) for x in (mid, crossed, local, field)],
         [pltpu.VMEM((EXTRA, LANES), F32)],
     )
+    arrived, *ring = lax.optimization_barrier((swapped(packed), *ring))
     first_image, copies, sums = small_call(
-        gathered_kernel, [(slab, width), split, (EXTRA, LANES)], [swapped(packed)],
-        [pltpu.SemaphoreType.DMA((peers,))], [pltpu.VMEM, pltpu.HBM, pltpu.VMEM],
+        gathered_kernel,
+        [(slab, width), split, (EXTRA, LANES)],
+        [arrived],
+        spaces=[pltpu.VMEM, pltpu.HBM, pltpu.VMEM],
     )
     full_image = swapped(copies)
     sums = over_sectors(sums)
 
+    fields = (sums, field.reshape(split), full_image, *ring)
+    crossing, mid, local, overlap = image_of(
+        second_kernel, fields=fields, extra=[(EXTRA, LANES)], scratch=split
+    )
+    crossed, local = moved(crossing, local)
+    overlap = over_sectors(overlap, slice(0, 2))
+    crossed, overlap = lax.optimization_barrier((crossed, overlap))
+    total = mid + crossed + local
+    overlap = over_sectors(overlap, slice(2, None))
+    arrived = swapped(total.reshape(split))
+
+    norm_sq = sums[1:2, 0:1]
+    rayleigh = sums[0:1, 0:1] / norm_sq
+    share = overlap[0:1, 0:1] / norm_sq
     own = lax.dynamic_index_in_dim(
         field.reshape(split), lax.axis_index(TERM), 0, keepdims=False
     )
-    rayleigh, share = coefficients(sums)
     correction = scaling * (first_image - rayleigh * own) - share * own
-
-    fields = (sums, field, full_scaling.reshape(field.shape), full_image.reshape(field.shape))
-    crossing, mid, local = image_of(second_kernel, fields=fields)
-    crossed, local = moved(crossing, local)
-    total = mid + crossed + local
-    second_image = swapped(total.reshape(split)).sum(axis=0)
+    second_image = arrived.sum(axis=0) - share * first_image
     return (first_image[None], correction[None], second_image[None])
 
 

time: 138 us -> 142 us (1.029)
  blocking collectives: 45.9 us -> 0 us
  starting transfers between devices: 21.9 us -> 60.6 us
  waiting for transfers between devices: 38.6 us -> 61.8 us
  Pallas kernels: 22.9 us -> 11.3 us
    all_to_all x2 -> x0, blocking collectives: 45.9 us -> none  [swapped(): return lax.all_to_all(x, TERM, 0, 0, tiled=True)]
    ppermute x4 -> x14, waiting for transfers between devices: 11.4 us -> 56 us  [the longest x8 28.7 us: exchanged(): return x + lax.ppermute(x, axis, pairs)]
    ppermute x4 -> x14, starting transfers between devices: 7.06 us -> 21.3 us  [the longest x8 13.3 us: exchanged(): return x + lax.ppermute(x, axis, pairs)]
    ppermute x2, waiting for transfers between devices: 14.1 us -> 2.19 us  [moved(): lax.ppermute(crossing, SECTOR, upward + downward)]
    pallas_call x2, Pallas kernels: 20.7 us -> 8.83 us  [partial_image(): pl.pallas_call(body, out_shape=[jax.ShapeDtypeStruct(x, F32) for x in (*[...]
    all_to_all x2 -> x3, waiting for transfers between devices: 13.2 us -> 3.62 us  [swapped(): return lax.all_to_all(x, TERM, 0, 0, tiled=True)]
    ppermute x2, starting transfers between devices: 3.97 us -> 13.2 us  [moved(): lax.ppermute(crossing, SECTOR, upward + downward)]
    ppermute x2, starting transfers between devices: 0.19 us -> 8.09 us  [moved(): lax.ppermute(local, SECTOR, swap)]
  transfers between devices with their start and end apart: 10 -> 21, of which waited for: 6 -> 15; matrix products, arithmetic and copies ran while one was open for 1% -> 1% of each run, Pallas kernels for 0% -> 0%
where the time goes in v4:
time: 142 us; the launch traced here: 141 us
  waiting for transfers between devices  61.8 us (44%)
  starting transfers between devices  60.6 us (43%)
  Pallas kernels  11.3 us (8%)
  between operations  4.09 us (3%)
  other arithmetic  2.17 us (2%)
    ppermute x8, waiting for transfers between devices, exchanged(): return x + lax.ppermute(x, axis, pairs)  28.7 us
    ppermute x6, waiting for transfers between devices, from_ring(): return [x, *[lax.ppermute(x, axis, pairs) for pairs in steps]]  27.3 us
    all_to_all x3, starting transfers between devices, swapped(): return lax.all_to_all(x, TERM, 0, 0, tiled=True)  18 us
    ppermute x8, starting transfers between devices, exchanged(): return x + lax.ppermute(x, axis, pairs)  13.3 us
    ppermute x2, starting transfers between devices, moved(): lax.ppermute(crossing, SECTOR, upward + downward)  13.2 us
    pallas_call x2, Pallas kernels, partial_image(): pl.pallas_call(body, out_shape=[jax.ShapeDtypeStruct(x, F32) for x in (*[...  8.83 us
    ppermute x6, starting transfers between devices, from_ring(): return [x, *[lax.ppermute(x, axis, pairs) for pairs in steps]]  8.09 us
    ppermute x2, starting transfers between devices, moved(): lax.ppermute(local, SECTOR, swap)  8.09 us
  transfers between devices with their start and end apart: 21, of which 15 were waited for; matrix products, arithmetic and copies ran while one was open for 1% of the time, Pallas kernels for 0%

profile of v4, /device:TPU:64, one launch (start us, length us, event | category | flops | bytes accessed | tf_op | source)
XLA Modules:
  0.0 141.1 jit_solution(12396574316047222124)
XLA Ops:
  1.3 0.0 copy-start.1
  1.3 0.0 copy-start
  1.3 4.4 %shard_map.85 = (f32[512,512]{1,0:T(8,128)S(1)}, f32[512,512]{1,0:T(8,128)S(1)}, f32[512,512]{1,0:T(8,128)S(1)}) custom-call(s32[1,1]{1,0:T(1,128)S(6)} %copy.9.count, s32[1,4]{1,0:T(1,128)} %target.3, f32[4,512,512]{2,1,0:T(8,128)} %bitcast.45, f32[4,512,512]{2,1,0:T(8,128)} %bitcast.47, f32[512,512]{1,0:T(8,128)} %bitcast.31), custom_call_target="tpu_custom_call" | custom-call | flops 6442450944 | bytes 8388608 | tf_op jit(solution)/shard_map/pallas_call | solution.py:155
  5.7 7.4 %collective-permute-start = (f32[512,512]{1,0:T(8,128)S(1)}, f32[512,512]{1,0:T(8,128)S(1)}, u32[]{:S(2)}, u32[]{:S(2)}) collective-permute-start(f32[512,512]{1,0:T(8,128)S(1)} %get-tuple-element.24), channel_id=1, source_target_pairs={{1,2},{3,4},{5,6},{7,8},{9,10},{11,12},{13,14},{2,1},{4,3},{6,5},{... | collective-permute-start | bytes 3145736 | tf_op jit(solution)/shard_map/ppermute | solution.py:25
  13.1 2.6 %collective-permute-start.4 = (f32[512,512]{1,0:T(8,128)S(1)}, f32[512,512]{1,0:T(8,128)S(1)}, u32[]{:S(2)}, u32[]{:S(2)}) collective-permute-start(f32[512,512]{1,0:T(8,128)S(1)} %get-tuple-element.27), channel_id=1, source_target_pairs={{0,1},{1,0},{2,3},{3,2},{4,5},{5,4},{6,7},{7,6},{8,9},{9,8},{10,11... | collective-permute-start | bytes 3145736 | tf_op jit(solution)/shard_map/ppermute | solution.py:25
  15.7 0.0 copy-done.1
  15.7 0.6 collective-permute-start.3
  16.3 0.8 collective-permute-start.2
  17.2 0.6 collective-permute-start.1
  17.7 2.8 %collective-permute-done.3 = f32[32,512]{1,0:T(8,128)S(1)} collective-permute-done((f32[32,512]{1,0:T(8,128)S(1)}, f32[32,512]{1,0:T(8,128)S(1)}, u32[]{:S(2)}, u32[]{:S(2)}) %collective-permute-start.3) | collective-permute-done | bytes 65568 | tf_op jit(solution)/shard_map/ppermute | solution.py:31
  20.5 1.8 %collective-permute-done.2 = f32[32,512]{1,0:T(8,128)S(1)} collective-permute-done((f32[32,512]{1,0:T(8,128)S(1)}, f32[32,512]{1,0:T(8,128)S(1)}, u32[]{:S(2)}, u32[]{:S(2)}) %collective-permute-start.2) | collective-permute-done | bytes 65568 | tf_op jit(solution)/shard_map/ppermute | solution.py:31
  22.3 1.1 collective-permute-done.1
  23.4 2.2 %collective-permute-done = f32[512,512]{1,0:T(8,128)S(1)} collective-permute-done((f32[512,512]{1,0:T(8,128)S(1)}, f32[512,512]{1,0:T(8,128)S(1)}, u32[]{:S(2)}, u32[]{:S(2)}) %collective-permute-start) | collective-permute-done | bytes 1048608 | tf_op jit(solution)/shard_map/ppermute | solution.py:25
  25.6 0.0 collective-permute-done.4
  25.6 0.0 copy-done
  25.6 1.3 shard_map.86
  27.0 7.3 %all-to-all-start = ((f32[16,136,128]{2,1,0:T(8,128)}), f32[16,136,128]{2,1,0:T(8,128)S(1)}, u32[]{:S(2)}, u32[]{:S(2)}) async-start(f32[16,136,128]{2,1,0:T(8,128)} %shard_map.86), calls=%async_computation | async-start | bytes 2228224 | tf_op jit(solution)/shard_map/all_to_all | solution.py:35
  34.3 1.9 %collective-permute-start.5 = (f32[4,32,512]{2,1,0:T(8,128)S(1)}, f32[4,32,512]{2,1,0:T(8,128)S(1)}, u32[]{:S(2)}, u32[]{:S(2)}) collective-permute-start(f32[4,32,512]{2,1,0:T(8,128)S(1)} %pad_maximum_fusion.rest_0_), channel_id=1, source_target_pairs={{0,64},{64,128},{128,192},{192,0},{1,65},{65,129},{129,193},{193,1... | collective-permute-start | bytes 786440 | tf_op jit(solution)/shard_map/ppermute | solution.py:31
  36.2 2.7 %collective-permute-start.6 = (f32[4,32,512]{2,1,0:T(8,128)S(1)}, f32[4,32,512]{2,1,0:T(8,128)S(1)}, u32[]{:S(2)}, u32[]{:S(2)}) collective-permute-start(f32[4,32,512]{2,1,0:T(8,128)S(1)} %pad_maximum_fusion.rest_0_), channel_id=1, source_target_pairs={{0,128},{64,192},{128,0},{192,64},{1,129},{65,193},{129,1},{193,65... | collective-permute-start | bytes 786440 | tf_op jit(solution)/shard_map/ppermute | solution.py:31
  38.9 1.5 %collective-permute-start.7 = (f32[4,32,512]{2,1,0:T(8,128)S(1)}, f32[4,32,512]{2,1,0:T(8,128)S(1)}, u32[]{:S(2)}, u32[]{:S(2)}) collective-permute-start(f32[4,32,512]{2,1,0:T(8,128)S(1)} %pad_maximum_fusion.rest_0_), channel_id=1, source_target_pairs={{0,192},{64,0},{128,64},{192,128},{1,193},{65,1},{129,65},{193,129... | collective-permute-start | bytes 786440 | tf_op jit(solution)/shard_map/ppermute | solution.py:31
  40.4 15.6 %collective-permute-done.5.rest_1_ = f32[4,32,512]{2,1,0:T(8,128)S(1)} collective-permute-done((f32[4,32,512]{2,1,0:T(8,128)S(1)}, f32[4,32,512]{2,1,0:T(8,128)S(1)}, u32[]{:S(2)}, u32[]{:S(2)}) %collective-permute-start.5) | collective-permute-done | bytes 262176 | tf_op jit(solution)/shard_map/ppermute | solution.py:31
  56.0 6.0 %collective-permute-done.6.rest_2_ = f32[4,32,512]{2,1,0:T(8,128)S(1)} collective-permute-done((f32[4,32,512]{2,1,0:T(8,128)S(1)}, f32[4,32,512]{2,1,0:T(8,128)S(1)}, u32[]{:S(2)}, u32[]{:S(2)}) %collective-permute-start.6) | collective-permute-done | bytes 262176 | tf_op jit(solution)/shard_map/ppermute | solution.py:31
  62.0 0.0 collective-permute-done.7.rest_3_
  62.0 0.0 all-to-all-done.arrived
  62.0 1.2 shard_map.87
  63.2 5.0 %all-to-all-start.1 = ((f32[16,32,512]{2,1,0:T(8,128)}), f32[16,32,512]{2,1,0:T(8,128)S(1)}, u32[]{:S(2)}, u32[]{:S(2)}) async-start(f32[16,32,512]{2,1,0:T(8,128)} %get-tuple-element.32), calls=%async_computation.1 | async-start | bytes 2097152 | tf_op jit(solution)/shard_map/all_to_all | solution.py:35
  68.2 0.4 collective-permute-start.8
  68.5 0.9 collective-permute-done.8
  69.4 4.4 %collective-permute-start.9 = (f32[8,128]{1,0:T(8,128)S(1)}, f32[8,128]{1,0:T(8,128)S(1)}, u32[]{:S(2)}, u32[]{:S(2)}) collective-permute-start(f32[8,128]{1,0:T(8,128)S(1)} %add.37), channel_id=1, source_target_pairs={{0,2},{2,0},{4,6},{6,4},{8,10},{10,8},{12,14},{14,12},{1,3},{3,1},... | collective-permute-start | bytes 12296 | tf_op jit(solution)/shard_map/ppermute | solution.py:49
  73.9 1.6 %collective-permute-done.9 = f32[8,128]{1,0:T(8,128)S(1)} collective-permute-done((f32[8,128]{1,0:T(8,128)S(1)}, f32[8,128]{1,0:T(8,128)S(1)}, u32[]{:S(2)}, u32[]{:S(2)}) %collective-permute-start.9) | collective-permute-done | bytes 4128 | tf_op jit(solution)/shard_map/ppermute | solution.py:49
  75.4 0.0 collective-permute-start.10
  75.5 4.5 %collective-permute-done.10 = f32[8,128]{1,0:T(8,128)S(1)} collective-permute-done((f32[8,128]{1,0:T(8,128)S(1)}, f32[8,128]{1,0:T(8,128)S(1)}, u32[]{:S(2)}, u32[]{:S(2)}) %collective-permute-start.10) | collective-permute-done | bytes 4128 | tf_op jit(solution)/shard_map/ppermute | solution.py:49
  80.0 4.2 %collective-permute-start.11 = (f32[8,128]{1,0:T(8,128)S(1)}, f32[8,128]{1,0:T(8,128)S(1)}, u32[]{:S(2)}, u32[]{:S(2)}) collective-permute-start(f32[8,128]{1,0:T(8,128)S(1)} %add.39), channel_id=1, source_target_pairs={{0,8},{2,10},{4,12},{6,14},{8,0},{10,2},{12,4},{14,6},{1,9},{3,11}... | collective-permute-start | bytes 12296 | tf_op jit(solution)/shard_map/ppermute | solution.py:49
  84.2 3.3 %collective-permute-done.11 = f32[8,128]{1,0:T(8,128)S(1)} collective-permute-done((f32[8,128]{1,0:T(8,128)S(1)}, f32[8,128]{1,0:T(8,128)S(1)}, u32[]{:S(2)}, u32[]{:S(2)}) %collective-permute-start.11) | collective-permute-done | bytes 4128 | tf_op jit(solution)/shard_map/ppermute | solution.py:49
  87.5 0.0 all-to-all-done.1.image
  87.5 4.4 %shard_map.88 = (f32[512,512]{1,0:T(8,128)S(1)}, f32[512,512]{1,0:T(8,128)S(1)}, f32[512,512]{1,0:T(8,128)S(1)}, f32[8,128]{1,0:T(8,128)S(1)}) custom-call(s32[1,1]{1,0:T(1,128)S(6)} %copy.9.count, s32[1,4]{1,0:T(1,128)} %target.3, f32[4,512,512]{2,1,0:T(8,128)} %bitcast.46, f32[4,512,512]{2,1,0:T(8,128)} %bitcast.48, f32[8,128]{1,0:T(8,128)S(1)} %add.40.sums, ...), custom_call_target="tpu_custom_call" | custom-call | flops 6442450944 | bytes 8388608 | tf_op jit(solution)/shard_map/pallas_call | solution.py:155
  91.9 0.0 copy-start.2
  91.9 5.8 %collective-permute-start.12 = (f32[512,512]{1,0:T(8,128)S(1)}, f32[512,512]{1,0:T(8,128)S(1)}, u32[]{:S(2)}, u32[]{:S(2)}) collective-permute-start(f32[512,512]{1,0:T(8,128)S(1)} %get-tuple-element.37), channel_id=1, source_target_pairs={{1,2},{3,4},{5,6},{7,8},{9,10},{11,12},{13,14},{2,1},{4,3},{6,5},{... | collective-permute-start | bytes 3145736 | tf_op jit(solution)/shard_map/ppermute | solution.py:25
  97.7 5.5 %collective-permute-start.17 = (f32[512,512]{1,0:T(8,128)S(1)}, f32[512,512]{1,0:T(8,128)S(1)}, u32[]{:S(2)}, u32[]{:S(2)}) collective-permute-start(f32[512,512]{1,0:T(8,128)S(1)} %get-tuple-element.42), channel_id=1, source_target_pairs={{0,1},{1,0},{2,3},{3,2},{4,5},{5,4},{6,7},{7,6},{8,9},{9,8},{10,11... | collective-permute-start | bytes 3145736 | tf_op jit(solution)/shard_map/ppermute | solution.py:25
  103.2 0.1 collective-permute-start.13
  103.3 2.2 %collective-permute-done.13 = f32[8,128]{1,0:T(8,128)S(1)} collective-permute-done((f32[8,128]{1,0:T(8,128)S(1)}, f32[8,128]{1,0:T(8,128)S(1)}, u32[]{:S(2)}, u32[]{:S(2)}) %collective-permute-start.13) | collective-permute-done | bytes 4128 | tf_op jit(solution)/shard_map/ppermute | solution.py:49
  105.5 0.3 collective-permute-start.14
  105.8 9.9 %collective-permute-done.14 = f32[8,128]{1,0:T(8,128)S(1)} collective-permute-done((f32[8,128]{1,0:T(8,128)S(1)}, f32[8,128]{1,0:T(8,128)S(1)}, u32[]{:S(2)}, u32[]{:S(2)}) %collective-permute-start.14) | collective-permute-done | bytes 4128 | tf_op jit(solution)/shard_map/ppermute | solution.py:49
  115.7 0.0 collective-permute-done.12
  115.7 0.0 collective-permute-done.17
  115.7 1.4 add_add_fusion
  117.1 5.7 %all-to-all-start.2 = ((f32[16,32,512]{2,1,0:T(8,128)}), f32[16,32,512]{2,1,0:T(8,128)S(1)}, u32[]{:S(2)}, u32[]{:S(2)}) async-start(f32[16,32,512]{2,1,0:T(8,128)} %bitcast.18), calls=%async_computation.2 | async-start | bytes 2097152 | tf_op jit(solution)/shard_map/all_to_all | solution.py:35
  122.7 0.1 collective-permute-start.15
  122.8 4.5 %collective-permute-done.15 = f32[8,128]{1,0:T(8,128)S(1)} collective-permute-done((f32[8,128]{1,0:T(8,128)S(1)}, f32[8,128]{1,0:T(8,128)S(1)}, u32[]{:S(2)}, u32[]{:S(2)}) %collective-permute-start.15) | collective-permute-done | bytes 4128 | tf_op jit(solution)/shard_map/ppermute | solution.py:49
  127.3 3.8 %collective-permute-start.16 = (f32[8,128]{1,0:T(8,128)S(1)}, f32[8,128]{1,0:T(8,128)S(1)}, u32[]{:S(2)}, u32[]{:S(2)}) collective-permute-start(f32[8,128]{1,0:T(8,128)S(1)} %add.45), channel_id=1, source_target_pairs={{0,8},{2,10},{4,12},{6,14},{8,0},{10,2},{12,4},{14,6},{1,9},{3,11}... | collective-permute-start | bytes 12296 | tf_op jit(solution)/shard_map/ppermute | solution.py:49
  131.1 0.5 fusion.2
  133.0 1.8 %collective-permute-done.16 = f32[8,128]{1,0:T(8,128)S(1)} collective-permute-done((f32[8,128]{1,0:T(8,128)S(1)}, f32[8,128]{1,0:T(8,128)S(1)}, u32[]{:S(2)}, u32[]{:S(2)}) %collective-permute-start.16) | collective-permute-done | bytes 4128 | tf_op jit(solution)/shard_map/ppermute | solution.py:49
  134.9 0.5 slice.11
  136.7 3.6 %all-to-all-done.2 = f32[16,32,512]{2,1,0:T(8,128)S(1)} async-done(((f32[16,32,512]{2,1,0:T(8,128)}), f32[16,32,512]{2,1,0:T(8,128)S(1)}, u32[]{:S(2)}, u32[]{:S(2)}) %all-to-all-start.2) | async-done | bytes 1048608 | tf_op jit(solution)/shard_map/all_to_all | solution.py:35
  140.3 0.1 reduce_sum.9
  140.4 0.0 copy-done.2
  140.4 0.7 subtract_bitcast_fusion
  (9 shorter events, 0.0 us)
Async XLA Ops:
  1.3 14.4 %copy-start.1 = (f32[1,32,512]{2,1,0:T(8,128)S(1)}, f32[1,32,512]{2,1,0:T(8,128)}, u32[]{:S(2)}) copy-start(f32[1,32,512]{2,1,0:T(8,128)} %param.7) | copy-start | bytes 196612
  1.3 24.3 %copy-start = (f32[1,512,512]{2,1,0:T(8,128)S(1)}, f32[1,512,512]{2,1,0:T(8,128)}, u32[]{:S(2)}) copy-start(f32[1,512,512]{2,1,0:T(8,128)} %param.6) | copy-start | bytes 3145732
  5.7 19.9 %collective-permute-start = (f32[512,512]{1,0:T(8,128)S(1)}, f32[512,512]{1,0:T(8,128)S(1)}, u32[]{:S(2)}, u32[]{:S(2)}) collective-permute-start(f32[512,512]{1,0:T(8,128)S(1)} %get-tuple-element.24), channel_id=1, source_target_pairs={{1,2},{3,4},{5,6},{7,8},{9,10},{11,12},{13,14},{2,1},{4,3},{6,5},{... | collective-permute-start | bytes 3145736 | tf_op jit(solution)/shard_map/ppermute | solution.py:25
  13.1 12.5 %collective-permute-start.4 = (f32[512,512]{1,0:T(8,128)S(1)}, f32[512,512]{1,0:T(8,128)S(1)}, u32[]{:S(2)}, u32[]{:S(2)}) collective-permute-start(f32[512,512]{1,0:T(8,128)S(1)} %get-tuple-element.27), channel_id=1, source_target_pairs={{0,1},{1,0},{2,3},{3,2},{4,5},{5,4},{6,7},{7,6},{8,9},{9,8},{10,11... | collective-permute-start | bytes 3145736 | tf_op jit(solution)/shard_map/ppermute | solution.py:25
  15.7 4.8 %collective-permute-start.3 = (f32[32,512]{1,0:T(8,128)S(1)}, f32[32,512]{1,0:T(8,128)S(1)}, u32[]{:S(2)}, u32[]{:S(2)}) collective-permute-start(f32[32,512]{1,0:T(8,128)S(1)} %bitcast.38), channel_id=1, source_target_pairs={{0,48},{16,0},{32,16},{48,32},{1,49},{17,1},{33,17},{49,33},{2,50}... | collective-permute-start | bytes 196616 | tf_op jit(solution)/shard_map/ppermute | solution.py:31
  16.3 6.0 %collective-permute-start.2 = (f32[32,512]{1,0:T(8,128)S(1)}, f32[32,512]{1,0:T(8,128)S(1)}, u32[]{:S(2)}, u32[]{:S(2)}) collective-permute-start(f32[32,512]{1,0:T(8,128)S(1)} %bitcast.39), channel_id=1, source_target_pairs={{0,32},{16,48},{32,0},{48,16},{1,33},{17,49},{33,1},{49,17},{2,34}... | collective-permute-start | bytes 196616 | tf_op jit(solution)/shard_map/ppermute | solution.py:31
  17.2 6.2 %collective-permute-start.1 = (f32[32,512]{1,0:T(8,128)S(1)}, f32[32,512]{1,0:T(8,128)S(1)}, u32[]{:S(2)}, u32[]{:S(2)}) collective-permute-start(f32[32,512]{1,0:T(8,128)S(1)} %bitcast.40), channel_id=1, source_target_pairs={{0,16},{16,32},{32,48},{48,0},{1,17},{17,33},{33,49},{49,1},{2,18}... | collective-permute-start | bytes 196616 | tf_op jit(solution)/shard_map/ppermute | solution.py:31
  27.0 35.1 %all-to-all-start = ((f32[16,136,128]{2,1,0:T(8,128)}), f32[16,136,128]{2,1,0:T(8,128)S(1)}, u32[]{:S(2)}, u32[]{:S(2)}) async-start(f32[16,136,128]{2,1,0:T(8,128)} %shard_map.86), calls=%async_computation | async-start | bytes 2228224 | tf_op jit(solution)/shard_map/all_to_all | solution.py:35
  34.3 21.7 %collective-permute-start.5 = (f32[4,32,512]{2,1,0:T(8,128)S(1)}, f32[4,32,512]{2,1,0:T(8,128)S(1)}, u32[]{:S(2)}, u32[]{:S(2)}) collective-permute-start(f32[4,32,512]{2,1,0:T(8,128)S(1)} %pad_maximum_fusion.rest_0_), channel_id=1, source_target_pairs={{0,64},{64,128},{128,192},{192,0},{1,65},{65,129},{129,193},{193,1... | collective-permute-start | bytes 786440 | tf_op jit(solution)/shard_map/ppermute | solution.py:31
  36.2 25.8 %collective-permute-start.6 = (f32[4,32,512]{2,1,0:T(8,128)S(1)}, f32[4,32,512]{2,1,0:T(8,128)S(1)}, u32[]{:S(2)}, u32[]{:S(2)}) collective-permute-start(f32[4,32,512]{2,1,0:T(8,128)S(1)} %pad_maximum_fusion.rest_0_), channel_id=1, source_target_pairs={{0,128},{64,192},{128,0},{192,64},{1,129},{65,193},{129,1},{193,65... | collective-permute-start | bytes 786440 | tf_op jit(solution)/shard_map/ppermute | solution.py:31
  38.9 23.1 %collective-permute-start.7 = (f32[4,32,512]{2,1,0:T(8,128)S(1)}, f32[4,32,512]{2,1,0:T(8,128)S(1)}, u32[]{:S(2)}, u32[]{:S(2)}) collective-permute-start(f32[4,32,512]{2,1,0:T(8,128)S(1)} %pad_maximum_fusion.rest_0_), channel_id=1, source_target_pairs={{0,192},{64,0},{128,64},{192,128},{1,193},{65,1},{129,65},{193,129... | collective-permute-start | bytes 786440 | tf_op jit(solution)/shard_map/ppermute | solution.py:31
  63.2 24.3 %all-to-all-start.1 = ((f32[16,32,512]{2,1,0:T(8,128)}), f32[16,32,512]{2,1,0:T(8,128)S(1)}, u32[]{:S(2)}, u32[]{:S(2)}) async-start(f32[16,32,512]{2,1,0:T(8,128)} %get-tuple-element.32), calls=%async_computation.1 | async-start | bytes 2097152 | tf_op jit(solution)/shard_map/all_to_all | solution.py:35
  68.2 1.3 collective-permute-start.8
  69.4 6.0 %collective-permute-start.9 = (f32[8,128]{1,0:T(8,128)S(1)}, f32[8,128]{1,0:T(8,128)S(1)}, u32[]{:S(2)}, u32[]{:S(2)}) collective-permute-start(f32[8,128]{1,0:T(8,128)S(1)} %add.37), channel_id=1, source_target_pairs={{0,2},{2,0},{4,6},{6,4},{8,10},{10,8},{12,14},{14,12},{1,3},{3,1},... | collective-permute-start | bytes 12296 | tf_op jit(solution)/shard_map/ppermute | solution.py:49
  75.4 4.5 %collective-permute-start.10 = (f32[8,128]{1,0:T(8,128)S(1)}, f32[8,128]{1,0:T(8,128)S(1)}, u32[]{:S(2)}, u32[]{:S(2)}) collective-permute-start(f32[8,128]{1,0:T(8,128)S(1)} %add.38), channel_id=1, source_target_pairs={{0,4},{2,6},{4,0},{6,2},{8,12},{10,14},{12,8},{14,10},{1,5},{3,7},... | collective-permute-start | bytes 12296 | tf_op jit(solution)/shard_map/ppermute | solution.py:49
  80.0 7.5 %collective-permute-start.11 = (f32[8,128]{1,0:T(8,128)S(1)}, f32[8,128]{1,0:T(8,128)S(1)}, u32[]{:S(2)}, u32[]{:S(2)}) collective-permute-start(f32[8,128]{1,0:T(8,128)S(1)} %add.39), channel_id=1, source_target_pairs={{0,8},{2,10},{4,12},{6,14},{8,0},{10,2},{12,4},{14,6},{1,9},{3,11}... | collective-permute-start | bytes 12296 | tf_op jit(solution)/shard_map/ppermute | solution.py:49
  91.9 48.5 %copy-start.2 = (f32[32,512]{1,0:T(8,128)S(1)}, f32[32,512]{1,0:T(8,128)}, u32[]{:S(2)}) copy-start(f32[32,512]{1,0:T(8,128)} %get-tuple-element.30) | copy-start | bytes 196612
  91.9 23.8 %collective-permute-start.12 = (f32[512,512]{1,0:T(8,128)S(1)}, f32[512,512]{1,0:T(8,128)S(1)}, u32[]{:S(2)}, u32[]{:S(2)}) collective-permute-start(f32[512,512]{1,0:T(8,128)S(1)} %get-tuple-element.37), channel_id=1, source_target_pairs={{1,2},{3,4},{5,6},{7,8},{9,10},{11,12},{13,14},{2,1},{4,3},{6,5},{... | collective-permute-start | bytes 3145736 | tf_op jit(solution)/shard_map/ppermute | solution.py:25
  97.7 18.0 %collective-permute-start.17 = (f32[512,512]{1,0:T(8,128)S(1)}, f32[512,512]{1,0:T(8,128)S(1)}, u32[]{:S(2)}, u32[]{:S(2)}) collective-permute-start(f32[512,512]{1,0:T(8,128)S(1)} %get-tuple-element.42), channel_id=1, source_target_pairs={{0,1},{1,0},{2,3},{3,2},{4,5},{5,4},{6,7},{7,6},{8,9},{9,8},{10,11... | collective-permute-start | bytes 3145736 | tf_op jit(solution)/shard_map/ppermute | solution.py:25
  103.2 2.3 %collective-permute-start.13 = (f32[8,128]{1,0:T(8,128)S(1)}, f32[8,128]{1,0:T(8,128)S(1)}, u32[]{:S(2)}, u32[]{:S(2)}) collective-permute-start(f32[8,128]{1,0:T(8,128)S(1)} %get-tuple-element.38), channel_id=1, source_target_pairs={{0,1},{1,0},{2,3},{3,2},{4,5},{5,4},{6,7},{7,6},{8,9},{9,8},{10,11... | collective-permute-start | bytes 12296 | tf_op jit(solution)/shard_map/ppermute | solution.py:49
  105.5 10.2 %collective-permute-start.14 = (f32[8,128]{1,0:T(8,128)S(1)}, f32[8,128]{1,0:T(8,128)S(1)}, u32[]{:S(2)}, u32[]{:S(2)}) collective-permute-start(f32[8,128]{1,0:T(8,128)S(1)} %add.43), channel_id=1, source_target_pairs={{0,2},{2,0},{4,6},{6,4},{8,10},{10,8},{12,14},{14,12},{1,3},{3,1},... | collective-permute-start | bytes 12296 | tf_op jit(solution)/shard_map/ppermute | solution.py:49
  117.1 23.3 %all-to-all-start.2 = ((f32[16,32,512]{2,1,0:T(8,128)}), f32[16,32,512]{2,1,0:T(8,128)S(1)}, u32[]{:S(2)}, u32[]{:S(2)}) async-start(f32[16,32,512]{2,1,0:T(8,128)} %bitcast.18), calls=%async_computation.2 | async-start | bytes 2097152 | tf_op jit(solution)/shard_map/all_to_all | solution.py:35
  122.7 4.6 %collective-permute-start.15 = (f32[8,128]{1,0:T(8,128)S(1)}, f32[8,128]{1,0:T(8,128)S(1)}, u32[]{:S(2)}, u32[]{:S(2)}) collective-permute-start(f32[8,128]{1,0:T(8,128)S(1)} %add.44), channel_id=1, source_target_pairs={{0,4},{2,6},{4,0},{6,2},{8,12},{10,14},{12,8},{14,10},{1,5},{3,7},... | collective-permute-start | bytes 12296 | tf_op jit(solution)/shard_map/ppermute | solution.py:49
  127.3 7.5 %collective-permute-start.16 = (f32[8,128]{1,0:T(8,128)S(1)}, f32[8,128]{1,0:T(8,128)S(1)}, u32[]{:S(2)}, u32[]{:S(2)}) collective-permute-start(f32[8,128]{1,0:T(8,128)S(1)} %add.45), channel_id=1, source_target_pairs={{0,8},{2,10},{4,12},{6,14},{8,0},{10,2},{12,4},{14,6},{1,9},{3,11}... | collective-permute-start | bytes 12296 | tf_op jit(solution)/shard_map/ppermute | solution.py:49

commit v5 on v4

--- a/solution.py
+++ b/solution.py
@@ -23,12 +23,6 @@
     downward = [(j, i) for i, j in upward]
     swap = [(i, i ^ 1) for i in range(count)]
     return lax.ppermute(crossing, SECTOR, upward + downward), lax.ppermute(local, SECTOR, swap)
-
-
-def from_ring(x, axis):
-    size = lax.axis_size(axis)
-    steps = [[(i, (i + k) % size) for i in range(size)] for k in range(1, size)]
-    return [x, *[lax.ppermute(x, axis, pairs) for pairs in steps]]
 
 
 def swapped(x):
@@ -102,32 +96,19 @@
 
 
 def second_kernel(
-    count,
-    target,
-    left,
-    right,
-    sums,
-    field,
-    image,
-    *rest,
+    count, target, left, right, sums, field, gathered, crossing, kept, local, overlap, f_high, f_low
 ):
-    ring, (crossing, kept, local, overlap, f_high, f_low) = rest[:-6], rest[-6:]
     peers, slab, width = field.shape
 
     @pl.when(pl.program_id(0) == 0)
     def _():
         rayleigh = sums[0:1, 0:1] / sums[1:2, 0:1]
-        along_0, along_1 = (lax.axis_index(axis) for axis in TERM)
-        size = ring[0].shape[0]
         weighted = jnp.zeros((slab, width), F32)
-        for j, scaling in enumerate(ring):
-            for k in range(size):
-                peer = lax.rem(along_0 + len(ring) - j, len(ring)) * size
-                peer += lax.rem(along_1 + size - k, size)
-                vector = field[peer]
-                raw = scaling[k] * (image[peer] - rayleigh * vector)
-                f_high[peer], f_low[peer] = halves(raw)
-                weighted += vector * raw
+        for peer in range(peers):
+            vector = field[peer]
+            raw = gathered[peer, slab:] * (gathered[peer, :slab] - rayleigh * vector)
+            f_high[peer], f_low[peer] = halves(raw)
+            weighted += vector * raw
         overlap[...] = jnp.broadcast_to(jnp.sum(weighted, keepdims=True), overlap.shape)
 
     outs = (crossing, kept, local)
@@ -198,8 +179,9 @@
         packed[peer, len(where) * slab :] = sums[...]
 
 
-def gathered_kernel(arrived, image, copies, sums):
-    peers, slab, width = copies.shape
+def gathered_kernel(arrived, scaling, image, copies, sums):
+    peers = copies.shape[0]
+    slab, width = image.shape
     total = arrived[0]
     for peer in range(1, peers):
         total += arrived[peer]
@@ -207,7 +189,8 @@
     for row, lanes in where:
         image[:, lanes] = total[row : row + slab]
     for peer in range(peers):
-        copies[peer] = image[...]
+        copies[peer, :slab] = image[...]
+        copies[peer, slab:] = scaling[...]
     sums[...] = total[len(where) * slab :]
 
 
@@ -247,27 +230,22 @@
 
     crossing, mid, local = image_of(first_kernel, fields=(field,), streamed=True)
     crossed, local = moved(crossing, local)
-    scaling_late, _ = lax.optimization_barrier((scaling, mid))
-    stacked = jnp.stack(from_ring(scaling_late, TERM[1]))
-    crossed, stacked = lax.optimization_barrier((crossed, stacked))
-    ring = from_ring(stacked, TERM[0])
     (packed,) = small_call(
         combine_kernel,
         [(peers, packed_rows, LANES)],
         [x.reshape(split) for x in (mid, crossed, local, field)],
         [pltpu.VMEM((EXTRA, LANES), F32)],
     )
-    arrived, *ring = lax.optimization_barrier((swapped(packed), *ring))
     first_image, copies, sums = small_call(
         gathered_kernel,
-        [(slab, width), split, (EXTRA, LANES)],
-        [arrived],
+        [(slab, width), (peers, 2 * slab, width), (EXTRA, LANES)],
+        [swapped(packed), scaling],
         spaces=[pltpu.VMEM, pltpu.HBM, pltpu.VMEM],
     )
-    full_image = swapped(copies)
+    gathered = swapped(copies)
     sums = over_sectors(sums)
 
-    fields = (sums, field.reshape(split), full_image, *ring)
+    fields = (sums, field.reshape(split), gathered)
     crossing, mid, local, overlap = image_of(
         second_kernel, fields=fields, extra=[(EXTRA, LANES)], scratch=split
     )

time: 142 us -> 141 us (level)
  starting transfers between devices: 60.6 us -> 26.5 us
  blocking collectives: 0 us -> 25 us
  Pallas kernels: 11.3 us -> 22 us
  waiting for transfers between devices: 61.8 us -> 59.2 us
    ppermute x6 -> x0, waiting for transfers between devices: 27.3 us -> none  [from_ring(): return [x, *[lax.ppermute(x, axis, pairs) for pairs in steps]]]
    all_to_all x0 -> x1, blocking collectives: none -> 25 us  [swapped(): return lax.all_to_all(x, TERM, 0, 0, tiled=True)]
    all_to_all x3 -> x2, waiting for transfers between devices: 3.62 us -> 15.9 us  [swapped(): return lax.all_to_all(x, TERM, 0, 0, tiled=True)]
    pallas_call x2, Pallas kernels: 8.83 us -> 20.2 us  [partial_image(): pl.pallas_call(body, out_shape=[jax.ShapeDtypeStruct(x, F32) for x in (*[...]
    all_to_all x3 -> x2, starting transfers between devices: 18 us -> 7.96 us  [swapped(): return lax.all_to_all(x, TERM, 0, 0, tiled=True)]
    ppermute x2, waiting for transfers between devices: 2.19 us -> 12.1 us  [moved(): lax.ppermute(crossing, SECTOR, upward + downward)]
    ppermute x2, starting transfers between devices: 13.2 us -> 3.84 us  [moved(): lax.ppermute(crossing, SECTOR, upward + downward)]
    ppermute x6 -> x0, starting transfers between devices: 8.09 us -> none  [from_ring(): return [x, *[lax.ppermute(x, axis, pairs) for pairs in steps]]]
  transfers between devices with their start and end apart: 21 -> 14, of which waited for: 15 -> 11; matrix products, arithmetic and copies ran while one was open for 1% -> 1% of each run, Pallas kernels for 0% -> 0%
where the time goes in v5:
time: 141 us; the launch traced here: 140 us
  waiting for transfers between devices  59.2 us (42%)
  starting transfers between devices  26.5 us (19%)
  blocking collectives  25 us (18%)
  Pallas kernels  22 us (16%)
  between operations  4.08 us (3%)
  other arithmetic  2.13 us (2%)
    ppermute x8, waiting for transfers between devices, exchanged(): return x + lax.ppermute(x, axis, pairs)  31.1 us
    all_to_all x1, blocking collectives, swapped(): return lax.all_to_all(x, TERM, 0, 0, tiled=True)  25 us
    pallas_call x2, Pallas kernels, partial_image(): pl.pallas_call(body, out_shape=[jax.ShapeDtypeStruct(x, F32) for x in (*[...  20.2 us
    all_to_all x2, waiting for transfers between devices, swapped(): return lax.all_to_all(x, TERM, 0, 0, tiled=True)  15.9 us
    ppermute x2, waiting for transfers between devices, moved(): lax.ppermute(crossing, SECTOR, upward + downward)  12.1 us
    ppermute x8, starting transfers between devices, exchanged(): return x + lax.ppermute(x, axis, pairs)  8.94 us
    all_to_all x2, starting transfers between devices, swapped(): return lax.all_to_all(x, TERM, 0, 0, tiled=True)  7.96 us
    ppermute x2, starting transfers between devices, moved(): lax.ppermute(local, SECTOR, swap)  5.75 us
  transfers between devices with their start and end apart: 14, of which 11 were waited for; matrix products, arithmetic and copies ran while one was open for 1% of the time, Pallas kernels for 0%

profile of v5, /device:TPU:64, one launch (start us, length us, event | category | flops | bytes accessed | tf_op | source)
XLA Modules:
  0.0 140.0 jit_solution(1156864503513098380)
XLA Ops:
  1.3 0.0 copy-start
  1.3 10.1 %shard_map.85 = (f32[512,512]{1,0:T(8,128)S(1)}, f32[512,512]{1,0:T(8,128)S(1)}, f32[512,512]{1,0:T(8,128)S(1)}) custom-call(s32[1,1]{1,0:T(1,128)S(6)} %copy.9.count, s32[1,4]{1,0:T(1,128)} %target.3, f32[4,512,512]{2,1,0:T(8,128)} %bitcast.36, f32[4,512,512]{2,1,0:T(8,128)} %bitcast.38, f32[512,512]{1,0:T(8,128)} %bitcast.27), custom_call_target="tpu_custom_call" | custom-call | flops 6442450944 | bytes 8388608 | tf_op jit(solution)/shard_map/pallas_call | solution.py:136
  11.4 1.9 %collective-permute-start = (f32[512,512]{1,0:T(8,128)S(1)}, f32[512,512]{1,0:T(8,128)S(1)}, u32[]{:S(2)}, u32[]{:S(2)}) collective-permute-start(f32[512,512]{1,0:T(8,128)S(1)} %get-tuple-element.16), channel_id=1, source_target_pairs={{1,2},{3,4},{5,6},{7,8},{9,10},{11,12},{13,14},{2,1},{4,3},{6,5},{... | collective-permute-start | bytes 3145736 | tf_op jit(solution)/shard_map/ppermute | solution.py:25
  13.3 2.1 %collective-permute-start.1 = (f32[512,512]{1,0:T(8,128)S(1)}, f32[512,512]{1,0:T(8,128)S(1)}, u32[]{:S(2)}, u32[]{:S(2)}) collective-permute-start(f32[512,512]{1,0:T(8,128)S(1)} %get-tuple-element.17), channel_id=1, source_target_pairs={{0,1},{1,0},{2,3},{3,2},{4,5},{5,4},{6,7},{7,6},{8,9},{9,8},{10,11... | collective-permute-start | bytes 3145736 | tf_op jit(solution)/shard_map/ppermute | solution.py:25
  15.4 12.1 %collective-permute-done = f32[512,512]{1,0:T(8,128)S(1)} collective-permute-done((f32[512,512]{1,0:T(8,128)S(1)}, f32[512,512]{1,0:T(8,128)S(1)}, u32[]{:S(2)}, u32[]{:S(2)}) %collective-permute-start) | collective-permute-done | bytes 1048608 | tf_op jit(solution)/shard_map/ppermute | solution.py:25
  27.5 0.0 collective-permute-done.1
  27.5 0.0 copy-done
  27.5 0.3 shard_map.86
  27.9 0.0 copy-start.1
  27.9 25.0 %all_to_all.15.arrived = f32[16,136,128]{2,1,0:T(8,128)S(1)} all-to-all(f32[16,136,128]{2,1,0:T(8,128)S(1)} %shard_map.86), channel_id=1, replica_groups=mesh['term_0'=4,'term_1'=4,'sector_0'=8,'sector_1'=2] {'term_0','term_1'}, dimensions={0} | all-to-all | bytes 2228224 | tf_op jit(solution)/shard_map/all_to_all | solution.py:29
  52.9 0.0 copy-done.1
  52.9 1.6 %shard_map.87 = (f32[32,512]{1,0:T(8,128)}, f32[16,64,512]{2,1,0:T(8,128)}, f32[8,128]{1,0:T(8,128)S(1)}) custom-call(f32[16,136,128]{2,1,0:T(8,128)S(1)} %all_to_all.15.arrived, f32[32,512]{1,0:T(8,128)S(1)} %bitcast.34), custom_call_target="tpu_custom_call" | custom-call | tf_op jit(solution)/shard_map/pallas_call | solution.py:199
  54.4 3.7 %all-to-all-start.1 = ((f32[16,64,512]{2,1,0:T(8,128)}), f32[16,64,512]{2,1,0:T(8,128)S(1)}, u32[]{:S(2)}, u32[]{:S(2)}) async-start(f32[16,64,512]{2,1,0:T(8,128)} %get-tuple-element.20), calls=%async_computation.1 | async-start | bytes 4194304 | tf_op jit(solution)/shard_map/all_to_all | solution.py:29
  58.2 0.1 collective-permute-start.2
  58.3 1.2 collective-permute-done.2
  59.4 2.3 %collective-permute-start.3 = (f32[8,128]{1,0:T(8,128)S(1)}, f32[8,128]{1,0:T(8,128)S(1)}, u32[]{:S(2)}, u32[]{:S(2)}) collective-permute-start(f32[8,128]{1,0:T(8,128)S(1)} %add.37), channel_id=1, source_target_pairs={{0,2},{2,0},{4,6},{6,4},{8,10},{10,8},{12,14},{14,12},{1,3},{3,1},... | collective-permute-start | bytes 12296 | tf_op jit(solution)/shard_map/ppermute | solution.py:43
  61.8 1.6 %collective-permute-done.3 = f32[8,128]{1,0:T(8,128)S(1)} collective-permute-done((f32[8,128]{1,0:T(8,128)S(1)}, f32[8,128]{1,0:T(8,128)S(1)}, u32[]{:S(2)}, u32[]{:S(2)}) %collective-permute-start.3) | collective-permute-done | bytes 4128 | tf_op jit(solution)/shard_map/ppermute | solution.py:43
  63.3 0.0 collective-permute-start.4
  63.3 4.5 %collective-permute-done.4 = f32[8,128]{1,0:T(8,128)S(1)} collective-permute-done((f32[8,128]{1,0:T(8,128)S(1)}, f32[8,128]{1,0:T(8,128)S(1)}, u32[]{:S(2)}, u32[]{:S(2)}) %collective-permute-start.4) | collective-permute-done | bytes 4128 | tf_op jit(solution)/shard_map/ppermute | solution.py:43
  67.9 4.7 %collective-permute-start.5 = (f32[8,128]{1,0:T(8,128)S(1)}, f32[8,128]{1,0:T(8,128)S(1)}, u32[]{:S(2)}, u32[]{:S(2)}) collective-permute-start(f32[8,128]{1,0:T(8,128)S(1)} %add.39), channel_id=1, source_target_pairs={{0,8},{2,10},{4,12},{6,14},{8,0},{10,2},{12,4},{14,6},{1,9},{3,11}... | collective-permute-start | bytes 12296 | tf_op jit(solution)/shard_map/ppermute | solution.py:43
  72.6 2.8 %collective-permute-done.5 = f32[8,128]{1,0:T(8,128)S(1)} collective-permute-done((f32[8,128]{1,0:T(8,128)S(1)}, f32[8,128]{1,0:T(8,128)S(1)}, u32[]{:S(2)}, u32[]{:S(2)}) %collective-permute-start.5) | collective-permute-done | bytes 4128 | tf_op jit(solution)/shard_map/ppermute | solution.py:43
  75.4 12.3 %all-to-all-done.1.gathered = f32[16,64,512]{2,1,0:T(8,128)S(1)} async-done(((f32[16,64,512]{2,1,0:T(8,128)}), f32[16,64,512]{2,1,0:T(8,128)S(1)}, u32[]{:S(2)}, u32[]{:S(2)}) %all-to-all-start.1) | async-done | bytes 2097184 | tf_op jit(solution)/shard_map/all_to_all | solution.py:29
  87.7 10.1 %shard_map.88 = (f32[512,512]{1,0:T(8,128)S(1)}, f32[512,512]{1,0:T(8,128)S(1)}, f32[512,512]{1,0:T(8,128)S(1)}, f32[8,128]{1,0:T(8,128)S(1)}) custom-call(s32[1,1]{1,0:T(1,128)S(6)} %copy.9.count, s32[1,4]{1,0:T(1,128)} %target.3, f32[4,512,512]{2,1,0:T(8,128)} %bitcast.37, f32[4,512,512]{2,1,0:T(8,128)} %bitcast.39, f32[8,128]{1,0:T(8,128)S(1)} %add.40.sums, ...), custom_call_target="tpu_custom_call" | custom-call | flops 6442450944 | bytes 8388608 | tf_op jit(solution)/shard_map/pallas_call | solution.py:136
  97.8 1.9 %collective-permute-start.6 = (f32[512,512]{1,0:T(8,128)S(1)}, f32[512,512]{1,0:T(8,128)S(1)}, u32[]{:S(2)}, u32[]{:S(2)}) collective-permute-start(f32[512,512]{1,0:T(8,128)S(1)} %get-tuple-element.21), channel_id=1, source_target_pairs={{1,2},{3,4},{5,6},{7,8},{9,10},{11,12},{13,14},{2,1},{4,3},{6,5},{... | collective-permute-start | bytes 3145736 | tf_op jit(solution)/shard_map/ppermute | solution.py:25
  99.7 3.6 %collective-permute-start.11 = (f32[512,512]{1,0:T(8,128)S(1)}, f32[512,512]{1,0:T(8,128)S(1)}, u32[]{:S(2)}, u32[]{:S(2)}) collective-permute-start(f32[512,512]{1,0:T(8,128)S(1)} %get-tuple-element.26), channel_id=1, source_target_pairs={{0,1},{1,0},{2,3},{3,2},{4,5},{5,4},{6,7},{7,6},{8,9},{9,8},{10,11... | collective-permute-start | bytes 3145736 | tf_op jit(solution)/shard_map/ppermute | solution.py:25
  103.3 0.1 collective-permute-start.7
  103.4 2.2 %collective-permute-done.7 = f32[8,128]{1,0:T(8,128)S(1)} collective-permute-done((f32[8,128]{1,0:T(8,128)S(1)}, f32[8,128]{1,0:T(8,128)S(1)}, u32[]{:S(2)}, u32[]{:S(2)}) %collective-permute-start.7) | collective-permute-done | bytes 4128 | tf_op jit(solution)/shard_map/ppermute | solution.py:43
  105.6 0.3 collective-permute-start.8
  105.9 10.1 %collective-permute-done.8 = f32[8,128]{1,0:T(8,128)S(1)} collective-permute-done((f32[8,128]{1,0:T(8,128)S(1)}, f32[8,128]{1,0:T(8,128)S(1)}, u32[]{:S(2)}, u32[]{:S(2)}) %collective-permute-start.8) | collective-permute-done | bytes 4128 | tf_op jit(solution)/shard_map/ppermute | solution.py:43
  116.0 0.0 collective-permute-done.6
  116.0 0.0 collective-permute-done.11
  116.0 1.4 add_add_fusion
  117.4 0.0 copy-start.2
  117.4 4.2 %all-to-all-start.2 = ((f32[16,32,512]{2,1,0:T(8,128)}), f32[16,32,512]{2,1,0:T(8,128)S(1)}, u32[]{:S(2)}, u32[]{:S(2)}) async-start(f32[16,32,512]{2,1,0:T(8,128)} %bitcast.14), calls=%async_computation.2 | async-start | bytes 2097152 | tf_op jit(solution)/shard_map/all_to_all | solution.py:29
  121.6 0.1 collective-permute-start.9
  121.7 4.5 %collective-permute-done.9 = f32[8,128]{1,0:T(8,128)S(1)} collective-permute-done((f32[8,128]{1,0:T(8,128)S(1)}, f32[8,128]{1,0:T(8,128)S(1)}, u32[]{:S(2)}, u32[]{:S(2)}) %collective-permute-start.9) | collective-permute-done | bytes 4128 | tf_op jit(solution)/shard_map/ppermute | solution.py:43
  126.2 1.3 collective-permute-start.10
  127.5 0.5 fusion.2
  129.4 4.3 %collective-permute-done.10 = f32[8,128]{1,0:T(8,128)S(1)} collective-permute-done((f32[8,128]{1,0:T(8,128)S(1)}, f32[8,128]{1,0:T(8,128)S(1)}, u32[]{:S(2)}, u32[]{:S(2)}) %collective-permute-start.10) | collective-permute-done | bytes 4128 | tf_op jit(solution)/shard_map/ppermute | solution.py:43
  133.7 0.5 slice.11
  135.6 3.6 %all-to-all-done.2 = f32[16,32,512]{2,1,0:T(8,128)S(1)} async-done(((f32[16,32,512]{2,1,0:T(8,128)}), f32[16,32,512]{2,1,0:T(8,128)S(1)}, u32[]{:S(2)}, u32[]{:S(2)}) %all-to-all-start.2) | async-done | bytes 1048608 | tf_op jit(solution)/shard_map/all_to_all | solution.py:29
  139.2 0.1 reduce_sum.9
  139.3 0.0 copy-done.2
  139.3 0.7 subtract_bitcast_fusion
  (8 shorter events, 0.0 us)
Async XLA Ops:
  1.3 26.2 %copy-start = (f32[1,512,512]{2,1,0:T(8,128)S(1)}, f32[1,512,512]{2,1,0:T(8,128)}, u32[]{:S(2)}) copy-start(f32[1,512,512]{2,1,0:T(8,128)} %param.6) | copy-start | bytes 3145732
  11.4 16.1 %collective-permute-start = (f32[512,512]{1,0:T(8,128)S(1)}, f32[512,512]{1,0:T(8,128)S(1)}, u32[]{:S(2)}, u32[]{:S(2)}) collective-permute-start(f32[512,512]{1,0:T(8,128)S(1)} %get-tuple-element.16), channel_id=1, source_target_pairs={{1,2},{3,4},{5,6},{7,8},{9,10},{11,12},{13,14},{2,1},{4,3},{6,5},{... | collective-permute-start | bytes 3145736 | tf_op jit(solution)/shard_map/ppermute | solution.py:25
  13.3 14.2 %collective-permute-start.1 = (f32[512,512]{1,0:T(8,128)S(1)}, f32[512,512]{1,0:T(8,128)S(1)}, u32[]{:S(2)}, u32[]{:S(2)}) collective-permute-start(f32[512,512]{1,0:T(8,128)S(1)} %get-tuple-element.17), channel_id=1, source_target_pairs={{0,1},{1,0},{2,3},{3,2},{4,5},{5,4},{6,7},{7,6},{8,9},{9,8},{10,11... | collective-permute-start | bytes 3145736 | tf_op jit(solution)/shard_map/ppermute | solution.py:25
  27.9 25.0 %copy-start.1 = (f32[1,32,512]{2,1,0:T(8,128)S(1)}, f32[1,32,512]{2,1,0:T(8,128)}, u32[]{:S(2)}) copy-start(f32[1,32,512]{2,1,0:T(8,128)} %param.7) | copy-start | bytes 196612
  54.4 33.3 %all-to-all-start.1 = ((f32[16,64,512]{2,1,0:T(8,128)}), f32[16,64,512]{2,1,0:T(8,128)S(1)}, u32[]{:S(2)}, u32[]{:S(2)}) async-start(f32[16,64,512]{2,1,0:T(8,128)} %get-tuple-element.20), calls=%async_computation.1 | async-start | bytes 4194304 | tf_op jit(solution)/shard_map/all_to_all | solution.py:29
  58.2 1.3 collective-permute-start.2
  59.4 3.9 %collective-permute-start.3 = (f32[8,128]{1,0:T(8,128)S(1)}, f32[8,128]{1,0:T(8,128)S(1)}, u32[]{:S(2)}, u32[]{:S(2)}) collective-permute-start(f32[8,128]{1,0:T(8,128)S(1)} %add.37), channel_id=1, source_target_pairs={{0,2},{2,0},{4,6},{6,4},{8,10},{10,8},{12,14},{14,12},{1,3},{3,1},... | collective-permute-start | bytes 12296 | tf_op jit(solution)/shard_map/ppermute | solution.py:43
  63.3 4.5 %collective-permute-start.4 = (f32[8,128]{1,0:T(8,128)S(1)}, f32[8,128]{1,0:T(8,128)S(1)}, u32[]{:S(2)}, u32[]{:S(2)}) collective-permute-start(f32[8,128]{1,0:T(8,128)S(1)} %add.38), channel_id=1, source_target_pairs={{0,4},{2,6},{4,0},{6,2},{8,12},{10,14},{12,8},{14,10},{1,5},{3,7},... | collective-permute-start | bytes 12296 | tf_op jit(solution)/shard_map/ppermute | solution.py:43
  67.9 7.5 %collective-permute-start.5 = (f32[8,128]{1,0:T(8,128)S(1)}, f32[8,128]{1,0:T(8,128)S(1)}, u32[]{:S(2)}, u32[]{:S(2)}) collective-permute-start(f32[8,128]{1,0:T(8,128)S(1)} %add.39), channel_id=1, source_target_pairs={{0,8},{2,10},{4,12},{6,14},{8,0},{10,2},{12,4},{14,6},{1,9},{3,11}... | collective-permute-start | bytes 12296 | tf_op jit(solution)/shard_map/ppermute | solution.py:43
  97.8 18.2 %collective-permute-start.6 = (f32[512,512]{1,0:T(8,128)S(1)}, f32[512,512]{1,0:T(8,128)S(1)}, u32[]{:S(2)}, u32[]{:S(2)}) collective-permute-start(f32[512,512]{1,0:T(8,128)S(1)} %get-tuple-element.21), channel_id=1, source_target_pairs={{1,2},{3,4},{5,6},{7,8},{9,10},{11,12},{13,14},{2,1},{4,3},{6,5},{... | collective-permute-start | bytes 3145736 | tf_op jit(solution)/shard_map/ppermute | solution.py:25
  99.7 16.3 %collective-permute-start.11 = (f32[512,512]{1,0:T(8,128)S(1)}, f32[512,512]{1,0:T(8,128)S(1)}, u32[]{:S(2)}, u32[]{:S(2)}) collective-permute-start(f32[512,512]{1,0:T(8,128)S(1)} %get-tuple-element.26), channel_id=1, source_target_pairs={{0,1},{1,0},{2,3},{3,2},{4,5},{5,4},{6,7},{7,6},{8,9},{9,8},{10,11... | collective-permute-start | bytes 3145736 | tf_op jit(solution)/shard_map/ppermute | solution.py:25
  103.3 2.3 %collective-permute-start.7 = (f32[8,128]{1,0:T(8,128)S(1)}, f32[8,128]{1,0:T(8,128)S(1)}, u32[]{:S(2)}, u32[]{:S(2)}) collective-permute-start(f32[8,128]{1,0:T(8,128)S(1)} %get-tuple-element.22), channel_id=1, source_target_pairs={{0,1},{1,0},{2,3},{3,2},{4,5},{5,4},{6,7},{7,6},{8,9},{9,8},{10,11... | collective-permute-start | bytes 12296 | tf_op jit(solution)/shard_map/ppermute | solution.py:43
  105.6 10.4 %collective-permute-start.8 = (f32[8,128]{1,0:T(8,128)S(1)}, f32[8,128]{1,0:T(8,128)S(1)}, u32[]{:S(2)}, u32[]{:S(2)}) collective-permute-start(f32[8,128]{1,0:T(8,128)S(1)} %add.43), channel_id=1, source_target_pairs={{0,2},{2,0},{4,6},{6,4},{8,10},{10,8},{12,14},{14,12},{1,3},{3,1},... | collective-permute-start | bytes 12296 | tf_op jit(solution)/shard_map/ppermute | solution.py:43
  117.4 21.9 %copy-start.2 = (f32[32,512]{1,0:T(8,128)S(1)}, f32[32,512]{1,0:T(8,128)}, u32[]{:S(2)}) copy-start(f32[32,512]{1,0:T(8,128)} %get-tuple-element.18) | copy-start | bytes 196612
  117.4 21.8 %all-to-all-start.2 = ((f32[16,32,512]{2,1,0:T(8,128)}), f32[16,32,512]{2,1,0:T(8,128)S(1)}, u32[]{:S(2)}, u32[]{:S(2)}) async-start(f32[16,32,512]{2,1,0:T(8,128)} %bitcast.14), calls=%async_computation.2 | async-start | bytes 2097152 | tf_op jit(solution)/shard_map/all_to_all | solution.py:29
  121.6 4.6 %collective-permute-start.9 = (f32[8,128]{1,0:T(8,128)S(1)}, f32[8,128]{1,0:T(8,128)S(1)}, u32[]{:S(2)}, u32[]{:S(2)}) collective-permute-start(f32[8,128]{1,0:T(8,128)S(1)} %add.44), channel_id=1, source_target_pairs={{0,4},{2,6},{4,0},{6,2},{8,12},{10,14},{12,8},{14,10},{1,5},{3,7},... | collective-permute-start | bytes 12296 | tf_op jit(solution)/shard_map/ppermute | solution.py:43
  126.2 7.5 %collective-permute-start.10 = (f32[8,128]{1,0:T(8,128)S(1)}, f32[8,128]{1,0:T(8,128)S(1)}, u32[]{:S(2)}, u32[]{:S(2)}) collective-permute-start(f32[8,128]{1,0:T(8,128)S(1)} %add.45), channel_id=1, source_target_pairs={{0,8},{2,10},{4,12},{6,14},{8,0},{10,2},{12,4},{14,6},{1,9},{3,11}... | collective-permute-start | bytes 12296 | tf_op jit(solution)/shard_map/ppermute | solution.py:43

commit v6 on v5

--- a/solution.py
+++ b/solution.py
@@ -12,6 +12,7 @@
 SECTOR = ("sector_0", "sector_1")
 LANES = 128
 EXTRA = 8
+HALVES = 2
 MIB = 1 << 20
 KERNEL_VMEM = 20 * MIB
 F32 = jnp.float32
@@ -23,6 +24,23 @@
     downward = [(j, i) for i, j in upward]
     swap = [(i, i ^ 1) for i in range(count)]
     return lax.ppermute(crossing, SECTOR, upward + downward), lax.ppermute(local, SECTOR, swap)
+
+
+def rotated(x):
+    terms, sectors = lax.axis_size(TERM), lax.axis_size(SECTOR)
+    pairs = [
+        (t * sectors + (s + t) % sectors, t * sectors + s)
+        for t in range(terms)
+        for s in range(sectors)
+    ]
+    return lax.ppermute(x, (*TERM, *SECTOR), pairs)
+
+
+def exchanged_along(pieces, axis):
+    size = len(pieces)
+    routes = [[(i, (i + k) % size) for i in range(size)] for k in range(size)]
+    sent = [lax.ppermute(pieces[k], axis, routes[k]) for k in range(1, size)]
+    return [pieces[0], *sent]
 
 
 def swapped(x):
@@ -43,8 +61,8 @@
     return x + lax.ppermute(x, axis, pairs)
 
 
-def over_sectors(x, steps=slice(None)):
-    for step in list(sector_steps())[steps]:
+def over_sectors(x):
+    for step in sector_steps():
         x = step(x)
     return x
 
@@ -67,6 +85,8 @@
     def _():
         for out in outs:
             out[...] = jnp.zeros_like(out)
+
+    peers, rows, width = outs[0].shape
 
     @pl.when(slot < count[0, 0])
     def _():
@@ -79,25 +99,27 @@
         kept = goal == sector
         swapped_here = goal == (sector ^ 1)
         roles = (jnp.logical_not(kept | swapped_here), kept, swapped_here)
-        for role, out in zip(roles, outs):
+        result = result.reshape(peers, HALVES * rows, width)
+        for i, role in enumerate(roles):
 
             @pl.when(role)
-            def _(out=out):
-                out[...] += result
-
-
-def first_kernel(count, target, left, right, field, crossing, kept, local, f_high, f_low):
+            def _(i=i):
+                for half in range(HALVES):
+                    outs[i * HALVES + half][...] += result[:, half * rows : (half + 1) * rows]
+
+
+def first_kernel(count, target, left, right, field, *rest):
+    *outs, f_high, f_low = rest
+
     @pl.when(pl.program_id(0) == 0)
     def _():
         f_high[...], f_low[...] = halves(field[...])
 
-    outs = (crossing, kept, local)
     accumulate(lax.axis_index(SECTOR), count, target, left, right, f_high, f_low, outs)
 
 
-def second_kernel(
-    count, target, left, right, sums, field, gathered, crossing, kept, local, overlap, f_high, f_low
-):
+def second_kernel(count, target, left, right, sums, field, gathered, *rest):
+    *outs, overlap, f_high, f_low = rest
     peers, slab, width = field.shape
 
     @pl.when(pl.program_id(0) == 0)
@@ -111,13 +133,12 @@
             weighted += vector * raw
         overlap[...] = jnp.broadcast_to(jnp.sum(weighted, keepdims=True), overlap.shape)
 
-    outs = (crossing, kept, local)
     flat = (peers * slab, width)
     f_high, f_low = f_high.reshape(flat), f_low.reshape(flat)
     accumulate(lax.axis_index(SECTOR), count, target, left, right, f_high, f_low, outs)
 
 
-def partial_image(body, counts, targets, left_stack, right_stack, fields, extra=(), scratch=None, streamed=False):
+def partial_image(body, counts, targets, left_stack, right_stack, fields, split, extra=(), scratch=None, streamed=False):
     slots, width, _ = right_stack.shape
 
     def operand(i, count):
@@ -129,13 +150,15 @@
         for x in (targets, left_stack, right_stack)
     )
     block = (width, width)
+    part = (split[0], split[1] // HALVES, width)
+    parts = 3 * HALVES
     field_spec = in_vmem
     if streamed:
         fields = [pltpu.with_memory_space_constraint(x, pltpu.HBM) for x in fields]
         field_spec = pl.BlockSpec(block, lambda i, *_: (0, 0), pipeline_mode=pl.Buffered(1))
     return pl.pallas_call(
         body,
-        out_shape=[jax.ShapeDtypeStruct(x, F32) for x in (*[block] * 3, *extra)],
+        out_shape=[jax.ShapeDtypeStruct(x, F32) for x in (*[part] * parts, *extra)],
         grid_spec=pltpu.PrefetchScalarGridSpec(
             num_scalar_prefetch=1,
             grid=(slots,),
@@ -145,7 +168,7 @@
                 pl.BlockSpec((1, width, width), operand),
                 *[field_spec] * len(fields),
             ],
-            out_specs=[in_vmem] * (3 + len(extra)),
+            out_specs=[in_vmem] * (parts + len(extra)),
             scratch_shapes=[pltpu.VMEM(scratch or block, jnp.bfloat16)] * 2,
         ),
         compiler_params=pltpu.CompilerParams(
@@ -157,41 +180,107 @@
     )(counts, targets, left_stack, right_stack, *fields)
 
 
-def tiles(x, slab, width):
-    return [(c * slab, slice(c * LANES, (c + 1) * LANES)) for c in range(width // LANES)]
-
-
-def combine_kernel(mid, crossed, local, field, packed, sums):
-    peers, slab, width = mid.shape
-    where = tiles(mid, slab, width)
-    cross = jnp.zeros((slab, width), F32)
-    for peer in range(peers):
-        total = mid[peer] + (crossed[peer] + local[peer])
-        for row, lanes in where:
-            packed[peer, row : row + slab] = total[:, lanes]
-        cross += field[peer] * total
-    own = field[lax.axis_index(TERM)]
-    line = lax.broadcasted_iota(jnp.int32, (EXTRA, LANES), 0)
-    sums[...] = jnp.where(
+def place(half, along, across, size):
+    return along * size + across if half == 0 else across * size + along
+
+
+def spread(half, pieces, kept, crossed, local, weight=None):
+    peers, rows, width = kept.shape
+    size = len(pieces)
+    me = lax.axis_index(TERM[half])
+    weighted = jnp.zeros((rows, width), F32)
+    for k, piece in enumerate(pieces):
+        for across in range(size):
+            peer = place(half, lax.rem(me + k, size), across, size)
+            total = kept[peer] + (crossed[peer] + local[peer])
+            piece[across * rows : (across + 1) * rows] = total
+            if weight is not None:
+                weighted += weight[peer, half * rows : (half + 1) * rows] * total
+    return weighted
+
+
+def first_spread(half, kept, crossed, local, field, *rest):
+    *pieces, tail = rest
+    rows = kept.shape[1]
+    cross = spread(half, pieces, kept, crossed, local, field)
+    own = field[lax.axis_index(TERM), half * rows : (half + 1) * rows]
+    line = lax.broadcasted_iota(jnp.int32, tail.shape, 0)
+    tail[...] = jnp.where(
         line == 0, jnp.sum(cross, keepdims=True), jnp.sum(own * own, keepdims=True)
     )
-    for peer in range(peers):
-        packed[peer, len(where) * slab :] = sums[...]
-
-
-def gathered_kernel(arrived, scaling, image, copies, sums):
-    peers = copies.shape[0]
-    slab, width = image.shape
-    total = arrived[0]
-    for peer in range(1, peers):
-        total += arrived[peer]
-    where = tiles(image, slab, width)
-    for row, lanes in where:
-        image[:, lanes] = total[row : row + slab]
+    for piece in pieces:
+        piece[len(pieces) * rows :] = tail[...]
+
+
+def second_spread(half, kept, crossed, local, *rest):
+    if half == 0:
+        spread(half, rest, kept, crossed, local)
+        return
+    tail, *pieces = rest
+    spread(half, pieces, kept, crossed, local)
+    lanes = tail.shape[1]
+    for piece in pieces:
+        for start in range(0, piece.shape[1], lanes):
+            piece[len(pieces) * kept.shape[1] :, start : start + lanes] = tail[...]
+
+
+def relay(axis, rows, *refs):
+    size = len(refs) // 2
+    arrived, pieces = refs[:size], refs[size:]
+    me = lax.axis_index(axis)
+
+    def summed(where):
+        return functools.reduce(lambda x, y: x + y, [ref[where] for ref in arrived])
+
+    for k, piece in enumerate(pieces):
+        start = pl.multiple_of(lax.rem(me + k, size) * rows, rows)
+        piece[:rows] = summed(pl.ds(start, rows))
+        if piece.shape[0] > rows:
+            piece[rows:] = summed(pl.ds(size * rows, piece.shape[0] - rows))
+
+
+def landed(refs, rows):
+    size = len(refs) // HALVES
+    groups = [refs[h * size : (h + 1) * size] for h in range(HALVES)]
+    totals = [functools.reduce(lambda x, y: x + y, [r[...] for r in g]) for g in groups]
+    tails = [t[rows:] for t in totals if t.shape[0] > rows]
+    return [t[:rows] for t in totals], functools.reduce(lambda x, y: x + y, tails)
+
+
+def first_landing(*refs):
+    *arrived, scaling, image, copies, sums = refs
+    peers, slab = copies.shape[0], image.shape[0]
+    rows = slab // HALVES
+    parts, tail = landed(arrived, rows)
+    for half, part in enumerate(parts):
+        image[half * rows : (half + 1) * rows] = part
     for peer in range(peers):
         copies[peer, :slab] = image[...]
         copies[peer, slab:] = scaling[...]
-    sums[...] = total[len(where) * slab :]
+    sums[...] = tail[:, : sums.shape[1]]
+
+
+def second_landing(*refs):
+    *arrived, sums, first_image, scaling, own, correction, image = refs
+    rows = image.shape[0] // HALVES
+    parts, tail = landed(arrived, rows)
+    rayleigh = sums[0:1, 0:1] / sums[1:2, 0:1]
+    share = tail[0:1, 0:1] / sums[1:2, 0:1]
+    vector = own[...]
+    correction[...] = scaling[...] * (first_image[...] - rayleigh * vector) - share * vector
+    for half, part in enumerate(parts):
+        lines = slice(half * rows, (half + 1) * rows)
+        image[lines] = part - share * first_image[lines]
+
+
+def relayed(half, pieces, rows):
+    arrived = exchanged_along(pieces, TERM[half])
+    other = TERM[1 - half]
+    shape = (rows + pieces[0].shape[0] - len(pieces) * rows, pieces[0].shape[1])
+    onward = small_call(
+        functools.partial(relay, other, rows), [shape] * len(pieces), arrived
+    )
+    return exchanged_along(onward, other)
 
 
 def small_call(body, out_shapes, args, scratch=(), spaces=None):
@@ -217,8 +306,10 @@
     width = wavefunction.shape[1]
     slab = width // peers
     split = (peers, slab, width)
-    packed_rows = slab * (width // LANES) + EXTRA
+    rows = slab // HALVES
+    size = lax.axis_size(TERM[0])
     field = wavefunction[0]
+    blocked = field.reshape(split)
     scaling = precond[0]
     image_of = functools.partial(
         partial_image,
@@ -226,44 +317,52 @@
         targets=out_sector,
         left_stack=left_ops[0],
         right_stack=right_ops[0],
-    )
-
-    crossing, mid, local = image_of(first_kernel, fields=(field,), streamed=True)
-    crossed, local = moved(crossing, local)
-    (packed,) = small_call(
-        combine_kernel,
-        [(peers, packed_rows, LANES)],
-        [x.reshape(split) for x in (mid, crossed, local, field)],
-        [pltpu.VMEM((EXTRA, LANES), F32)],
-    )
+        split=split,
+    )
+
+    def moved_parts(parts):
+        crossing, kept, local = (parts[i * HALVES : (i + 1) * HALVES] for i in range(3))
+        return [(k, *moved(c, l)) for c, k, l in zip(crossing, kept, local)]
+
+    parts = moved_parts(image_of(first_kernel, fields=(field,), streamed=True))
+    arrived = []
+    for half in range(HALVES):
+        pieces = small_call(
+            functools.partial(first_spread, half),
+            [(size * rows + EXTRA, width)] * size,
+            [*parts[half], blocked],
+            [pltpu.VMEM((EXTRA, width), F32)],
+        )
+        arrived += relayed(half, pieces, rows)
     first_image, copies, sums = small_call(
-        gathered_kernel,
+        first_landing,
         [(slab, width), (peers, 2 * slab, width), (EXTRA, LANES)],
-        [swapped(packed), scaling],
+        [*arrived, scaling],
         spaces=[pltpu.VMEM, pltpu.HBM, pltpu.VMEM],
     )
     gathered = swapped(copies)
     sums = over_sectors(sums)
 
-    fields = (sums, field.reshape(split), gathered)
-    crossing, mid, local, overlap = image_of(
-        second_kernel, fields=fields, extra=[(EXTRA, LANES)], scratch=split
-    )
-    crossed, local = moved(crossing, local)
-    overlap = over_sectors(overlap, slice(0, 2))
-    crossed, overlap = lax.optimization_barrier((crossed, overlap))
-    total = mid + crossed + local
-    overlap = over_sectors(overlap, slice(2, None))
-    arrived = swapped(total.reshape(split))
-
-    norm_sq = sums[1:2, 0:1]
-    rayleigh = sums[0:1, 0:1] / norm_sq
-    share = overlap[0:1, 0:1] / norm_sq
-    own = lax.dynamic_index_in_dim(
-        field.reshape(split), lax.axis_index(TERM), 0, keepdims=False
-    )
-    correction = scaling * (first_image - rayleigh * own) - share * own
-    second_image = arrived.sum(axis=0) - share * first_image
+    *parts, overlap = image_of(
+        second_kernel, fields=(sums, blocked, gathered), extra=[(EXTRA, LANES)], scratch=split
+    )
+    parts = moved_parts(parts)
+    overlap = rotated(overlap)
+    arrived = []
+    for half in range(HALVES):
+        tail = [overlap] if half else []
+        pieces = small_call(
+            functools.partial(second_spread, half),
+            [(size * rows + EXTRA * half, width)] * size,
+            [*parts[half], *tail],
+        )
+        arrived += relayed(half, pieces, rows)
+    own = lax.dynamic_index_in_dim(blocked, lax.axis_index(TERM), 0, keepdims=False)
+    correction, second_image = small_call(
+        second_landing,
+        [(slab, width)] * 2,
+        [*arrived, sums, first_image, scaling, own],
+    )
     return (first_image[None], correction[None], second_image[None])
 
 

time: 141 us -> 136 us (0.965)
  starting transfers between devices: 26.5 us -> 90.6 us
  waiting for transfers between devices: 59.2 us -> 31.8 us
  blocking collectives: 25 us -> 0 us
  Pallas kernels: 22 us -> 11.9 us
  between operations: 4.08 us -> 1.49 us
  other arithmetic: 2.13 us -> 0.01 us
    ppermute x0 -> x25, starting transfers between devices: none -> 52.3 us  [the longest x24 51.7 us: exchanged_along(): sent = [lax.ppermute(pieces[k], axis, routes[k]) for k in range(1, size)]]
    all_to_all x1 -> x0, blocking collectives: 25 us -> none  [swapped(): return lax.all_to_all(x, TERM, 0, 0, tiled=True)]
    ppermute x8 -> x4, waiting for transfers between devices: 31.1 us -> 11.2 us  [exchanged(): return x + lax.ppermute(x, axis, pairs)]
    pallas_call x2, Pallas kernels: 20.2 us -> 8.82 us  [partial_image(): pl.pallas_call(body, out_shape=[jax.ShapeDtypeStruct(x, F32) for x in (*[...]
    ppermute x2 -> x4, waiting for transfers between devices: 12.1 us -> 2.26 us  [moved(): lax.ppermute(crossing, SECTOR, upward + downward)]
    ppermute x2 -> x4, starting transfers between devices: 3.84 us -> 13.1 us  [moved(): lax.ppermute(crossing, SECTOR, upward + downward)]
    ppermute x0 -> x25, waiting for transfers between devices: none -> 7.46 us  [the longest x24 7.46 us: exchanged_along(): sent = [lax.ppermute(pieces[k], axis, routes[k]) for k in range(1, size)]]
    ppermute x2 -> x4, starting transfers between devices: 5.75 us -> 12.6 us  [moved(): lax.ppermute(local, SECTOR, swap)]
  transfers between devices with their start and end apart: 14 -> 38, of which waited for: 11 -> 14; matrix products, arithmetic and copies ran while one was open for 1% -> 0% of each run, Pallas kernels for 0% -> 1%
where the time goes in v6:
time: 136 us
  starting transfers between devices  90.6 us (67%)
  waiting for transfers between devices  31.8 us (23%)
  Pallas kernels  11.9 us (9%)
  between operations  1.49 us (1%)
    ppermute x24, starting transfers between devices, exchanged_along(): sent = [lax.ppermute(pieces[k], axis, routes[k]) for k in range(1, size)]  51.7 us
    ppermute x4, starting transfers between devices, moved(): lax.ppermute(crossing, SECTOR, upward + downward)  13.1 us
    ppermute x4, starting transfers between devices, moved(): lax.ppermute(local, SECTOR, swap)  12.6 us
    ppermute x4, waiting for transfers between devices, exchanged(): return x + lax.ppermute(x, axis, pairs)  11.2 us
    all_to_all x1, waiting for transfers between devices, swapped(): return lax.all_to_all(x, TERM, 0, 0, tiled=True)  10.9 us
    pallas_call x2, Pallas kernels, partial_image(): pl.pallas_call(body, out_shape=[jax.ShapeDtypeStruct(x, F32) for x in (*[...  8.82 us
    ppermute x24, waiting for transfers between devices, exchanged_along(): sent = [lax.ppermute(pieces[k], axis, routes[k]) for k in range(1, size)]  7.46 us
    all_to_all x1, starting transfers between devices, swapped(): return lax.all_to_all(x, TERM, 0, 0, tiled=True)  6.79 us
  transfers between devices with their start and end apart: 38, of which 14 were waited for; matrix products, arithmetic and copies ran while one was open for 0% of the time, Pallas kernels for 1%

profile of v6, /device:TPU:64, one launch (start us, length us, event | category | flops | bytes accessed | tf_op | source)
XLA Modules:
  0.0 135.8 jit_solution(1465043558166413381)
XLA Ops:
  1.3 4.4 %shard_map.85 = (f32[16,16,512]{2,1,0:T(8,128)S(1)}, f32[16,16,512]{2,1,0:T(8,128)S(1)}, f32[16,16,512]{2,1,0:T(8,128)S(1)}, f32[16,16,512]{2,1,0:T(8,128)S(1)},...) custom-call(s32[1,1]{1,0:T(1,128)S(6)} %copy.9.count, s32[1,4]{1,0:T(1,128)} %target.3, f32[4,512,512]{2,1,0:T(8,128)} %bitcast.18, ...), custom_call_target="tpu_custom_call" | custom-call | flops 6442450944 | bytes 8388608 | tf_op jit(solution)/shard_map/pallas_call | solution.py:159
  5.7 0.0 copy-start.1
  5.7 7.3 %collective-permute-start = (f32[16,16,512]{2,1,0:T(8,128)S(1)}, f32[16,16,512]{2,1,0:T(8,128)S(1)}, u32[]{:S(2)}, u32[]{:S(2)}) collective-permute-start(f32[16,16,512]{2,1,0:T(8,128)S(1)} %get-tuple-element.54), channel_id=1, source_target_pairs={{1,2},{3,4},{5,6},{7,8},{9,10},{11,12},{13,14},{2,1},{4,3},{6,5},{... | collective-permute-start | bytes 1572872 | tf_op jit(solution)/shard_map/ppermute | solution.py:26
  13.0 2.6 %collective-permute-start.1 = (f32[16,16,512]{2,1,0:T(8,128)S(1)}, f32[16,16,512]{2,1,0:T(8,128)S(1)}, u32[]{:S(2)}, u32[]{:S(2)}) collective-permute-start(f32[16,16,512]{2,1,0:T(8,128)S(1)} %get-tuple-element.55), channel_id=1, source_target_pairs={{0,1},{1,0},{2,3},{3,2},{4,5},{5,4},{6,7},{7,6},{8,9},{9,8},{10,11... | collective-permute-start | bytes 1572872 | tf_op jit(solution)/shard_map/ppermute | solution.py:26
  15.6 1.9 %collective-permute-start.8 = (f32[16,16,512]{2,1,0:T(8,128)S(1)}, f32[16,16,512]{2,1,0:T(8,128)S(1)}, u32[]{:S(2)}, u32[]{:S(2)}) collective-permute-start(f32[16,16,512]{2,1,0:T(8,128)S(1)} %get-tuple-element.65), channel_id=1, source_target_pairs={{1,2},{3,4},{5,6},{7,8},{9,10},{11,12},{13,14},{2,1},{4,3},{6,5},{... | collective-permute-start | bytes 1572872 | tf_op jit(solution)/shard_map/ppermute | solution.py:26
  17.5 0.1 collective-permute-start.9
  17.6 2.3 %collective-permute-done.crossed = f32[16,16,512]{2,1,0:T(8,128)S(1)} collective-permute-done((f32[16,16,512]{2,1,0:T(8,128)S(1)}, f32[16,16,512]{2,1,0:T(8,128)S(1)}, u32[]{:S(2)}, u32[]{:S(2)}) %collective-permute-start) | collective-permute-done | bytes 524320 | tf_op jit(solution)/shard_map/ppermute | solution.py:26
  19.8 0.2 shard_map.86
  20.1 3.8 %collective-permute-start.2 = (f32[72,512]{1,0:T(8,128)S(1)}, f32[72,512]{1,0:T(8,128)S(1)}, u32[]{:S(2)}, u32[]{:S(2)}) collective-permute-start(f32[72,512]{1,0:T(8,128)S(1)} %get-tuple-element.57), channel_id=1, source_target_pairs={{0,64},{64,128},{128,192},{192,0},{1,65},{65,129},{129,193},{193,1... | collective-permute-start | bytes 442376 | tf_op jit(solution)/shard_map/ppermute | solution.py:42
  23.8 2.7 %collective-permute-start.3 = (f32[72,512]{1,0:T(8,128)S(1)}, f32[72,512]{1,0:T(8,128)S(1)}, u32[]{:S(2)}, u32[]{:S(2)}) collective-permute-start(f32[72,512]{1,0:T(8,128)S(1)} %get-tuple-element.58), channel_id=1, source_target_pairs={{0,128},{64,192},{128,0},{192,64},{1,129},{65,193},{129,1},{193,65... | collective-permute-start | bytes 442376 | tf_op jit(solution)/shard_map/ppermute | solution.py:42
  26.6 1.4 %collective-permute-start.4 = (f32[72,512]{1,0:T(8,128)S(1)}, f32[72,512]{1,0:T(8,128)S(1)}, u32[]{:S(2)}, u32[]{:S(2)}) collective-permute-start(f32[72,512]{1,0:T(8,128)S(1)} %get-tuple-element.59), channel_id=1, source_target_pairs={{0,192},{64,0},{128,64},{192,128},{1,193},{65,1},{129,65},{193,129... | collective-permute-start | bytes 442376 | tf_op jit(solution)/shard_map/ppermute | solution.py:42
  28.0 0.0 collective-permute-done.8.crossed
  28.0 0.2 shard_map.88
  28.3 1.7 %collective-permute-start.10 = (f32[72,512]{1,0:T(8,128)S(1)}, f32[72,512]{1,0:T(8,128)S(1)}, u32[]{:S(2)}, u32[]{:S(2)}) collective-permute-start(f32[72,512]{1,0:T(8,128)S(1)} %get-tuple-element.68), channel_id=1, source_target_pairs={{0,16},{16,32},{32,48},{48,0},{1,17},{17,33},{33,49},{49,1},{2,18}... | collective-permute-start | bytes 442376 | tf_op jit(solution)/shard_map/ppermute | solution.py:42
  29.9 1.7 %collective-permute-start.11 = (f32[72,512]{1,0:T(8,128)S(1)}, f32[72,512]{1,0:T(8,128)S(1)}, u32[]{:S(2)}, u32[]{:S(2)}) collective-permute-start(f32[72,512]{1,0:T(8,128)S(1)} %get-tuple-element.69), channel_id=1, source_target_pairs={{0,32},{16,48},{32,0},{48,16},{1,33},{17,49},{33,1},{49,17},{2,34}... | collective-permute-start | bytes 442376 | tf_op jit(solution)/shard_map/ppermute | solution.py:42
  31.6 2.5 %collective-permute-start.12 = (f32[72,512]{1,0:T(8,128)S(1)}, f32[72,512]{1,0:T(8,128)S(1)}, u32[]{:S(2)}, u32[]{:S(2)}) collective-permute-start(f32[72,512]{1,0:T(8,128)S(1)} %get-tuple-element.70), channel_id=1, source_target_pairs={{0,48},{16,0},{32,16},{48,32},{1,49},{17,1},{33,17},{49,33},{2,50}... | collective-permute-start | bytes 442376 | tf_op jit(solution)/shard_map/ppermute | solution.py:42
  34.2 1.0 collective-permute-start.5
  35.2 2.1 %collective-permute-start.6 = (f32[24,512]{1,0:T(8,128)S(1)}, f32[24,512]{1,0:T(8,128)S(1)}, u32[]{:S(2)}, u32[]{:S(2)}) collective-permute-start(f32[24,512]{1,0:T(8,128)S(1)} %get-tuple-element.62), channel_id=1, source_target_pairs={{0,32},{16,48},{32,0},{48,16},{1,33},{17,49},{33,1},{49,17},{2,34}... | collective-permute-start | bytes 147464 | tf_op jit(solution)/shard_map/ppermute | solution.py:42
  37.4 1.5 %collective-permute-start.7 = (f32[24,512]{1,0:T(8,128)S(1)}, f32[24,512]{1,0:T(8,128)S(1)}, u32[]{:S(2)}, u32[]{:S(2)}) collective-permute-start(f32[24,512]{1,0:T(8,128)S(1)} %get-tuple-element.63), channel_id=1, source_target_pairs={{0,48},{16,0},{32,16},{48,32},{1,49},{17,1},{33,17},{49,33},{2,50}... | collective-permute-start | bytes 147464 | tf_op jit(solution)/shard_map/ppermute | solution.py:42
  38.8 0.5 collective-permute-done.11.refs_2_
  39.3 0.5 collective-permute-done.12.refs_3_
  39.8 1.4 %collective-permute-start.13 = (f32[24,512]{1,0:T(8,128)S(1)}, f32[24,512]{1,0:T(8,128)S(1)}, u32[]{:S(2)}, u32[]{:S(2)}) collective-permute-start(f32[24,512]{1,0:T(8,128)S(1)} %get-tuple-element.72), channel_id=1, source_target_pairs={{0,64},{64,128},{128,192},{192,0},{1,65},{65,129},{129,193},{193,1... | collective-permute-start | bytes 147464 | tf_op jit(solution)/shard_map/ppermute | solution.py:42
  41.2 3.0 %collective-permute-start.14 = (f32[24,512]{1,0:T(8,128)S(1)}, f32[24,512]{1,0:T(8,128)S(1)}, u32[]{:S(2)}, u32[]{:S(2)}) collective-permute-start(f32[24,512]{1,0:T(8,128)S(1)} %get-tuple-element.73), channel_id=1, source_target_pairs={{0,128},{64,192},{128,0},{192,64},{1,129},{65,193},{129,1},{193,65... | collective-permute-start | bytes 147464 | tf_op jit(solution)/shard_map/ppermute | solution.py:42
  44.2 1.4 %collective-permute-start.15 = (f32[24,512]{1,0:T(8,128)S(1)}, f32[24,512]{1,0:T(8,128)S(1)}, u32[]{:S(2)}, u32[]{:S(2)}) collective-permute-start(f32[24,512]{1,0:T(8,128)S(1)} %get-tuple-element.74), channel_id=1, source_target_pairs={{0,192},{64,0},{128,64},{192,128},{1,193},{65,1},{129,65},{193,129... | collective-permute-start | bytes 147464 | tf_op jit(solution)/shard_map/ppermute | solution.py:42
  45.6 0.0 collective-permute-done.13.refs_5_
  45.6 1.2 collective-permute-done.14.refs_6_
  46.8 1.5 %collective-permute-done.15.refs_7_ = f32[24,512]{1,0:T(8,128)S(1)} collective-permute-done((f32[24,512]{1,0:T(8,128)S(1)}, f32[24,512]{1,0:T(8,128)S(1)}, u32[]{:S(2)}, u32[]{:S(2)}) %collective-permute-start.15) | collective-permute-done | bytes 49184 | tf_op jit(solution)/shard_map/ppermute | solution.py:42
  48.3 1.5 %shard_map.90 = (f32[32,512]{1,0:T(8,128)}, f32[16,64,512]{2,1,0:T(8,128)}, f32[8,128]{1,0:T(8,128)S(1)}) custom-call(f32[24,512]{1,0:T(8,128)S(1)} %get-tuple-element.60.refs_0_, f32[24,512]{1,0:T(8,128)S(1)} %collective-permute-done.5.refs_1_, f32[24,512]{1,0:T(8,128)S(1)} %collective-permute-done.6.refs_2_, f32[24,512]{1,0:T(8,128)S(1)} %collective-permute-done.7.refs_3_, ...), custom_call_target="tpu_custom_call" | custom-call | tf_op jit(solution)/shard_map/pallas_call | solution.py:288
  49.8 6.8 %all-to-all-start = ((f32[16,64,512]{2,1,0:T(8,128)}), f32[16,64,512]{2,1,0:T(8,128)S(1)}, u32[]{:S(2)}, u32[]{:S(2)}) async-start(f32[16,64,512]{2,1,0:T(8,128)} %get-tuple-element.77), calls=%async_computation | async-start | bytes 4194304 | tf_op jit(solution)/shard_map/all_to_all | solution.py:47
  56.6 0.1 collective-permute-start.16
  56.7 1.2 collective-permute-done.16
  57.9 1.3 collective-permute-start.17
  59.2 2.3 %collective-permute-done.17 = f32[8,128]{1,0:T(8,128)S(1)} collective-permute-done((f32[8,128]{1,0:T(8,128)S(1)}, f32[8,128]{1,0:T(8,128)S(1)}, u32[]{:S(2)}, u32[]{:S(2)}) %collective-permute-start.17) | collective-permute-done | bytes 4128 | tf_op jit(solution)/shard_map/ppermute | solution.py:61
  61.5 0.0 collective-permute-start.18
  61.5 4.5 %collective-permute-done.18 = f32[8,128]{1,0:T(8,128)S(1)} collective-permute-done((f32[8,128]{1,0:T(8,128)S(1)}, f32[8,128]{1,0:T(8,128)S(1)}, u32[]{:S(2)}, u32[]{:S(2)}) %collective-permute-start.18) | collective-permute-done | bytes 4128 | tf_op jit(solution)/shard_map/ppermute | solution.py:61
  66.0 4.3 %collective-permute-start.19 = (f32[8,128]{1,0:T(8,128)S(1)}, f32[8,128]{1,0:T(8,128)S(1)}, u32[]{:S(2)}, u32[]{:S(2)}) collective-permute-start(f32[8,128]{1,0:T(8,128)S(1)} %add.21), channel_id=1, source_target_pairs={{0,8},{2,10},{4,12},{6,14},{8,0},{10,2},{12,4},{14,6},{1,9},{3,11}... | collective-permute-start | bytes 12296 | tf_op jit(solution)/shard_map/ppermute | solution.py:61
  70.3 3.2 %collective-permute-done.19 = f32[8,128]{1,0:T(8,128)S(1)} collective-permute-done((f32[8,128]{1,0:T(8,128)S(1)}, f32[8,128]{1,0:T(8,128)S(1)}, u32[]{:S(2)}, u32[]{:S(2)}) %collective-permute-start.19) | collective-permute-done | bytes 4128 | tf_op jit(solution)/shard_map/ppermute | solution.py:61
  73.5 10.9 %all-to-all-done.gathered = f32[16,64,512]{2,1,0:T(8,128)S(1)} async-done(((f32[16,64,512]{2,1,0:T(8,128)}), f32[16,64,512]{2,1,0:T(8,128)S(1)}, u32[]{:S(2)}, u32[]{:S(2)}) %all-to-all-start) | async-done | bytes 2097184 | tf_op jit(solution)/shard_map/all_to_all | solution.py:47
  84.4 4.4 %shard_map.91 = (f32[16,16,512]{2,1,0:T(8,128)S(1)}, f32[16,16,512]{2,1,0:T(8,128)S(1)}, f32[16,16,512]{2,1,0:T(8,128)S(1)}, f32[16,16,512]{2,1,0:T(8,128)S(1)},...) custom-call(s32[1,1]{1,0:T(1,128)S(6)} %copy.9.count, s32[1,4]{1,0:T(1,128)} %target.3, ...), custom_call_target="tpu_custom_call" | custom-call | flops 6442450944 | bytes 8388608 | tf_op jit(solution)/shard_map/pallas_call | solution.py:159
  88.8 0.0 copy-start.2
  88.9 2.1 %collective-permute-start.20 = (f32[16,16,512]{2,1,0:T(8,128)S(1)}, f32[16,16,512]{2,1,0:T(8,128)S(1)}, u32[]{:S(2)}, u32[]{:S(2)}) collective-permute-start(f32[16,16,512]{2,1,0:T(8,128)S(1)} %get-tuple-element.79), channel_id=1, source_target_pairs={{1,2},{3,4},{5,6},{7,8},{9,10},{11,12},{13,14},{2,1},{4,3},{6,5},{... | collective-permute-start | bytes 1572872 | tf_op jit(solution)/shard_map/ppermute | solution.py:26
  90.9 9.8 %collective-permute-start.21 = (f32[16,16,512]{2,1,0:T(8,128)S(1)}, f32[16,16,512]{2,1,0:T(8,128)S(1)}, u32[]{:S(2)}, u32[]{:S(2)}) collective-permute-start(f32[16,16,512]{2,1,0:T(8,128)S(1)} %get-tuple-element.80), channel_id=1, source_target_pairs={{0,1},{1,0},{2,3},{3,2},{4,5},{5,4},{6,7},{7,6},{8,9},{9,8},{10,11... | collective-permute-start | bytes 1572872 | tf_op jit(solution)/shard_map/ppermute | solution.py:26
  100.8 1.9 %collective-permute-start.28 = (f32[16,16,512]{2,1,0:T(8,128)S(1)}, f32[16,16,512]{2,1,0:T(8,128)S(1)}, u32[]{:S(2)}, u32[]{:S(2)}) collective-permute-start(f32[16,16,512]{2,1,0:T(8,128)S(1)} %get-tuple-element.90), channel_id=1, source_target_pairs={{1,2},{3,4},{5,6},{7,8},{9,10},{11,12},{13,14},{2,1},{4,3},{6,5},{... | collective-permute-start | bytes 1572872 | tf_op jit(solution)/shard_map/ppermute | solution.py:26
  102.7 0.1 collective-permute-start.29
  102.8 0.0 collective-permute-done.21.local
  102.8 0.1 shard_map.92
  102.9 1.7 %collective-permute-start.22 = (f32[64,512]{1,0:T(8,128)S(1)}, f32[64,512]{1,0:T(8,128)S(1)}, u32[]{:S(2)}, u32[]{:S(2)}) collective-permute-start(f32[64,512]{1,0:T(8,128)S(1)} %get-tuple-element.82), channel_id=1, source_target_pairs={{0,64},{64,128},{128,192},{192,0},{1,65},{65,129},{129,193},{193,1... | collective-permute-start | bytes 393224 | tf_op jit(solution)/shard_map/ppermute | solution.py:42
  104.6 0.6 collective-permute-start.30
  105.2 7.8 %collective-permute-start.23 = (f32[64,512]{1,0:T(8,128)S(1)}, f32[64,512]{1,0:T(8,128)S(1)}, u32[]{:S(2)}, u32[]{:S(2)}) collective-permute-start(f32[64,512]{1,0:T(8,128)S(1)} %get-tuple-element.83), channel_id=1, source_target_pairs={{0,128},{64,192},{128,0},{192,64},{1,129},{65,193},{129,1},{193,65... | collective-permute-start | bytes 393224 | tf_op jit(solution)/shard_map/ppermute | solution.py:42
  113.0 0.1 shard_map.94
  113.1 2.0 %collective-permute-start.31 = (f32[72,512]{1,0:T(8,128)S(1)}, f32[72,512]{1,0:T(8,128)S(1)}, u32[]{:S(2)}, u32[]{:S(2)}) collective-permute-start(f32[72,512]{1,0:T(8,128)S(1)} %get-tuple-element.94), channel_id=1, source_target_pairs={{0,16},{16,32},{32,48},{48,0},{1,17},{17,33},{33,49},{49,1},{2,18}... | collective-permute-start | bytes 442376 | tf_op jit(solution)/shard_map/ppermute | solution.py:42
  115.2 1.5 %collective-permute-start.32 = (f32[72,512]{1,0:T(8,128)S(1)}, f32[72,512]{1,0:T(8,128)S(1)}, u32[]{:S(2)}, u32[]{:S(2)}) collective-permute-start(f32[72,512]{1,0:T(8,128)S(1)} %get-tuple-element.95), channel_id=1, source_target_pairs={{0,32},{16,48},{32,0},{48,16},{1,33},{17,49},{33,1},{49,17},{2,34}... | collective-permute-start | bytes 442376 | tf_op jit(solution)/shard_map/ppermute | solution.py:42
  116.7 2.5 %collective-permute-start.33 = (f32[72,512]{1,0:T(8,128)S(1)}, f32[72,512]{1,0:T(8,128)S(1)}, u32[]{:S(2)}, u32[]{:S(2)}) collective-permute-start(f32[72,512]{1,0:T(8,128)S(1)} %get-tuple-element.96), channel_id=1, source_target_pairs={{0,48},{16,0},{32,16},{48,32},{1,49},{17,1},{33,17},{49,33},{2,50}... | collective-permute-start | bytes 442376 | tf_op jit(solution)/shard_map/ppermute | solution.py:42
  119.3 1.5 %collective-permute-start.25 = (f32[16,512]{1,0:T(8,128)S(1)}, f32[16,512]{1,0:T(8,128)S(1)}, u32[]{:S(2)}, u32[]{:S(2)}) collective-permute-start(f32[16,512]{1,0:T(8,128)S(1)} %get-tuple-element.86), channel_id=1, source_target_pairs={{0,16},{16,32},{32,48},{48,0},{1,17},{17,33},{33,49},{49,1},{2,18}... | collective-permute-start | bytes 98312 | tf_op jit(solution)/shard_map/ppermute | solution.py:42
  120.8 0.5 collective-permute-start.26
  121.3 2.5 %collective-permute-start.27 = (f32[16,512]{1,0:T(8,128)S(1)}, f32[16,512]{1,0:T(8,128)S(1)}, u32[]{:S(2)}, u32[]{:S(2)}) collective-permute-start(f32[16,512]{1,0:T(8,128)S(1)} %get-tuple-element.88), channel_id=1, source_target_pairs={{0,48},{16,0},{32,16},{48,32},{1,49},{17,1},{33,17},{49,33},{2,50}... | collective-permute-start | bytes 98312 | tf_op jit(solution)/shard_map/ppermute | solution.py:42
  123.8 0.5 collective-permute-done.33.refs_3_
  124.3 3.0 %collective-permute-start.34 = (f32[24,512]{1,0:T(8,128)S(1)}, f32[24,512]{1,0:T(8,128)S(1)}, u32[]{:S(2)}, u32[]{:S(2)}) collective-permute-start(f32[24,512]{1,0:T(8,128)S(1)} %get-tuple-element.98), channel_id=1, source_target_pairs={{0,64},{64,128},{128,192},{192,0},{1,65},{65,129},{129,193},{193,1... | collective-permute-start | bytes 147464 | tf_op jit(solution)/shard_map/ppermute | solution.py:42
  127.3 3.7 %collective-permute-start.35 = (f32[24,512]{1,0:T(8,128)S(1)}, f32[24,512]{1,0:T(8,128)S(1)}, u32[]{:S(2)}, u32[]{:S(2)}) collective-permute-start(f32[24,512]{1,0:T(8,128)S(1)} %get-tuple-element.99), channel_id=1, source_target_pairs={{0,128},{64,192},{128,0},{192,64},{1,129},{65,193},{129,1},{193,65... | collective-permute-start | bytes 147464 | tf_op jit(solution)/shard_map/ppermute | solution.py:42
  131.0 0.7 collective-permute-start.36
  131.8 0.4 collective-permute-done.34.refs_5_
  132.1 1.5 %collective-permute-done.35.refs_6_ = f32[24,512]{1,0:T(8,128)S(1)} collective-permute-done((f32[24,512]{1,0:T(8,128)S(1)}, f32[24,512]{1,0:T(8,128)S(1)}, u32[]{:S(2)}, u32[]{:S(2)}) %collective-permute-start.35) | collective-permute-done | bytes 49184 | tf_op jit(solution)/shard_map/ppermute | solution.py:42
  133.6 1.5 %collective-permute-done.36.refs_7_ = f32[24,512]{1,0:T(8,128)S(1)} collective-permute-done((f32[24,512]{1,0:T(8,128)S(1)}, f32[24,512]{1,0:T(8,128)S(1)}, u32[]{:S(2)}, u32[]{:S(2)}) %collective-permute-start.36) | collective-permute-done | bytes 49184 | tf_op jit(solution)/shard_map/ppermute | solution.py:42
  135.1 0.7 shard_map.96
  (35 shorter events, 0.2 us)
Async XLA Ops:
  1.3 18.6 %copy-start = (f32[1,512,512]{2,1,0:T(8,128)S(1)}, f32[1,512,512]{2,1,0:T(8,128)}, u32[]{:S(2)}) copy-start(f32[1,512,512]{2,1,0:T(8,128)} %param.6) | copy-start | bytes 3145732
  5.7 42.6 %copy-start.1 = (f32[1,32,512]{2,1,0:T(8,128)S(1)}, f32[1,32,512]{2,1,0:T(8,128)}, u32[]{:S(2)}) copy-start(f32[1,32,512]{2,1,0:T(8,128)} %param.7) | copy-start | bytes 196612
  5.7 14.1 %collective-permute-start = (f32[16,16,512]{2,1,0:T(8,128)S(1)}, f32[16,16,512]{2,1,0:T(8,128)S(1)}, u32[]{:S(2)}, u32[]{:S(2)}) collective-permute-start(f32[16,16,512]{2,1,0:T(8,128)S(1)} %get-tuple-element.54), channel_id=1, source_target_pairs={{1,2},{3,4},{5,6},{7,8},{9,10},{11,12},{13,14},{2,1},{4,3},{6,5},{... | collective-permute-start | bytes 1572872 | tf_op jit(solution)/shard_map/ppermute | solution.py:26
  13.0 6.9 %collective-permute-start.1 = (f32[16,16,512]{2,1,0:T(8,128)S(1)}, f32[16,16,512]{2,1,0:T(8,128)S(1)}, u32[]{:S(2)}, u32[]{:S(2)}) collective-permute-start(f32[16,16,512]{2,1,0:T(8,128)S(1)} %get-tuple-element.55), channel_id=1, source_target_pairs={{0,1},{1,0},{2,3},{3,2},{4,5},{5,4},{6,7},{7,6},{8,9},{9,8},{10,11... | collective-permute-start | bytes 1572872 | tf_op jit(solution)/shard_map/ppermute | solution.py:26
  15.6 12.5 %collective-permute-start.8 = (f32[16,16,512]{2,1,0:T(8,128)S(1)}, f32[16,16,512]{2,1,0:T(8,128)S(1)}, u32[]{:S(2)}, u32[]{:S(2)}) collective-permute-start(f32[16,16,512]{2,1,0:T(8,128)S(1)} %get-tuple-element.65), channel_id=1, source_target_pairs={{1,2},{3,4},{5,6},{7,8},{9,10},{11,12},{13,14},{2,1},{4,3},{6,5},{... | collective-permute-start | bytes 1572872 | tf_op jit(solution)/shard_map/ppermute | solution.py:26
  17.5 10.5 %collective-permute-start.9 = (f32[16,16,512]{2,1,0:T(8,128)S(1)}, f32[16,16,512]{2,1,0:T(8,128)S(1)}, u32[]{:S(2)}, u32[]{:S(2)}) collective-permute-start(f32[16,16,512]{2,1,0:T(8,128)S(1)} %get-tuple-element.66), channel_id=1, source_target_pairs={{0,1},{1,0},{2,3},{3,2},{4,5},{5,4},{6,7},{7,6},{8,9},{9,8},{10,11... | collective-permute-start | bytes 1572872 | tf_op jit(solution)/shard_map/ppermute | solution.py:26
  20.1 11.5 %collective-permute-start.2 = (f32[72,512]{1,0:T(8,128)S(1)}, f32[72,512]{1,0:T(8,128)S(1)}, u32[]{:S(2)}, u32[]{:S(2)}) collective-permute-start(f32[72,512]{1,0:T(8,128)S(1)} %get-tuple-element.57), channel_id=1, source_target_pairs={{0,64},{64,128},{128,192},{192,0},{1,65},{65,129},{129,193},{193,1... | collective-permute-start | bytes 442376 | tf_op jit(solution)/shard_map/ppermute | solution.py:42
  23.8 10.3 %collective-permute-start.3 = (f32[72,512]{1,0:T(8,128)S(1)}, f32[72,512]{1,0:T(8,128)S(1)}, u32[]{:S(2)}, u32[]{:S(2)}) collective-permute-start(f32[72,512]{1,0:T(8,128)S(1)} %get-tuple-element.58), channel_id=1, source_target_pairs={{0,128},{64,192},{128,0},{192,64},{1,129},{65,193},{129,1},{193,65... | collective-permute-start | bytes 442376 | tf_op jit(solution)/shard_map/ppermute | solution.py:42
  26.6 7.6 %collective-permute-start.4 = (f32[72,512]{1,0:T(8,128)S(1)}, f32[72,512]{1,0:T(8,128)S(1)}, u32[]{:S(2)}, u32[]{:S(2)}) collective-permute-start(f32[72,512]{1,0:T(8,128)S(1)} %get-tuple-element.59), channel_id=1, source_target_pairs={{0,192},{64,0},{128,64},{192,128},{1,193},{65,1},{129,65},{193,129... | collective-permute-start | bytes 442376 | tf_op jit(solution)/shard_map/ppermute | solution.py:42
  28.3 9.1 %collective-permute-start.10 = (f32[72,512]{1,0:T(8,128)S(1)}, f32[72,512]{1,0:T(8,128)S(1)}, u32[]{:S(2)}, u32[]{:S(2)}) collective-permute-start(f32[72,512]{1,0:T(8,128)S(1)} %get-tuple-element.68), channel_id=1, source_target_pairs={{0,16},{16,32},{32,48},{48,0},{1,17},{17,33},{33,49},{49,1},{2,18}... | collective-permute-start | bytes 442376 | tf_op jit(solution)/shard_map/ppermute | solution.py:42
  29.9 9.4 %collective-permute-start.11 = (f32[72,512]{1,0:T(8,128)S(1)}, f32[72,512]{1,0:T(8,128)S(1)}, u32[]{:S(2)}, u32[]{:S(2)}) collective-permute-start(f32[72,512]{1,0:T(8,128)S(1)} %get-tuple-element.69), channel_id=1, source_target_pairs={{0,32},{16,48},{32,0},{48,16},{1,33},{17,49},{33,1},{49,17},{2,34}... | collective-permute-start | bytes 442376 | tf_op jit(solution)/shard_map/ppermute | solution.py:42
  31.6 8.2 %collective-permute-start.12 = (f32[72,512]{1,0:T(8,128)S(1)}, f32[72,512]{1,0:T(8,128)S(1)}, u32[]{:S(2)}, u32[]{:S(2)}) collective-permute-start(f32[72,512]{1,0:T(8,128)S(1)} %get-tuple-element.70), channel_id=1, source_target_pairs={{0,48},{16,0},{32,16},{48,32},{1,49},{17,1},{33,17},{49,33},{2,50}... | collective-permute-start | bytes 442376 | tf_op jit(solution)/shard_map/ppermute | solution.py:42
  34.2 10.0 %collective-permute-start.5 = (f32[24,512]{1,0:T(8,128)S(1)}, f32[24,512]{1,0:T(8,128)S(1)}, u32[]{:S(2)}, u32[]{:S(2)}) collective-permute-start(f32[24,512]{1,0:T(8,128)S(1)} %get-tuple-element.61), channel_id=1, source_target_pairs={{0,16},{16,32},{32,48},{48,0},{1,17},{17,33},{33,49},{49,1},{2,18}... | collective-permute-start | bytes 147464 | tf_op jit(solution)/shard_map/ppermute | solution.py:42
  35.2 10.4 %collective-permute-start.6 = (f32[24,512]{1,0:T(8,128)S(1)}, f32[24,512]{1,0:T(8,128)S(1)}, u32[]{:S(2)}, u32[]{:S(2)}) collective-permute-start(f32[24,512]{1,0:T(8,128)S(1)} %get-tuple-element.62), channel_id=1, source_target_pairs={{0,32},{16,48},{32,0},{48,16},{1,33},{17,49},{33,1},{49,17},{2,34}... | collective-permute-start | bytes 147464 | tf_op jit(solution)/shard_map/ppermute | solution.py:42
  37.4 8.3 %collective-permute-start.7 = (f32[24,512]{1,0:T(8,128)S(1)}, f32[24,512]{1,0:T(8,128)S(1)}, u32[]{:S(2)}, u32[]{:S(2)}) collective-permute-start(f32[24,512]{1,0:T(8,128)S(1)} %get-tuple-element.63), channel_id=1, source_target_pairs={{0,48},{16,0},{32,16},{48,32},{1,49},{17,1},{33,17},{49,33},{2,50}... | collective-permute-start | bytes 147464 | tf_op jit(solution)/shard_map/ppermute | solution.py:42
  39.8 5.8 %collective-permute-start.13 = (f32[24,512]{1,0:T(8,128)S(1)}, f32[24,512]{1,0:T(8,128)S(1)}, u32[]{:S(2)}, u32[]{:S(2)}) collective-permute-start(f32[24,512]{1,0:T(8,128)S(1)} %get-tuple-element.72), channel_id=1, source_target_pairs={{0,64},{64,128},{128,192},{192,0},{1,65},{65,129},{129,193},{193,1... | collective-permute-start | bytes 147464 | tf_op jit(solution)/shard_map/ppermute | solution.py:42
  41.2 5.6 %collective-permute-start.14 = (f32[24,512]{1,0:T(8,128)S(1)}, f32[24,512]{1,0:T(8,128)S(1)}, u32[]{:S(2)}, u32[]{:S(2)}) collective-permute-start(f32[24,512]{1,0:T(8,128)S(1)} %get-tuple-element.73), channel_id=1, source_target_pairs={{0,128},{64,192},{128,0},{192,64},{1,129},{65,193},{129,1},{193,65... | collective-permute-start | bytes 147464 | tf_op jit(solution)/shard_map/ppermute | solution.py:42
  44.2 4.1 %collective-permute-start.15 = (f32[24,512]{1,0:T(8,128)S(1)}, f32[24,512]{1,0:T(8,128)S(1)}, u32[]{:S(2)}, u32[]{:S(2)}) collective-permute-start(f32[24,512]{1,0:T(8,128)S(1)} %get-tuple-element.74), channel_id=1, source_target_pairs={{0,192},{64,0},{128,64},{192,128},{1,193},{65,1},{129,65},{193,129... | collective-permute-start | bytes 147464 | tf_op jit(solution)/shard_map/ppermute | solution.py:42
  49.8 34.6 %all-to-all-start = ((f32[16,64,512]{2,1,0:T(8,128)}), f32[16,64,512]{2,1,0:T(8,128)S(1)}, u32[]{:S(2)}, u32[]{:S(2)}) async-start(f32[16,64,512]{2,1,0:T(8,128)} %get-tuple-element.77), calls=%async_computation | async-start | bytes 4194304 | tf_op jit(solution)/shard_map/all_to_all | solution.py:47
  56.6 1.3 collective-permute-start.16
  57.9 3.6 %collective-permute-start.17 = (f32[8,128]{1,0:T(8,128)S(1)}, f32[8,128]{1,0:T(8,128)S(1)}, u32[]{:S(2)}, u32[]{:S(2)}) collective-permute-start(f32[8,128]{1,0:T(8,128)S(1)} %add.19), channel_id=1, source_target_pairs={{0,2},{2,0},{4,6},{6,4},{8,10},{10,8},{12,14},{14,12},{1,3},{3,1},... | collective-permute-start | bytes 12296 | tf_op jit(solution)/shard_map/ppermute | solution.py:61
  61.5 4.5 %collective-permute-start.18 = (f32[8,128]{1,0:T(8,128)S(1)}, f32[8,128]{1,0:T(8,128)S(1)}, u32[]{:S(2)}, u32[]{:S(2)}) collective-permute-start(f32[8,128]{1,0:T(8,128)S(1)} %add.20), channel_id=1, source_target_pairs={{0,4},{2,6},{4,0},{6,2},{8,12},{10,14},{12,8},{14,10},{1,5},{3,7},... | collective-permute-start | bytes 12296 | tf_op jit(solution)/shard_map/ppermute | solution.py:61
  66.0 7.5 %collective-permute-start.19 = (f32[8,128]{1,0:T(8,128)S(1)}, f32[8,128]{1,0:T(8,128)S(1)}, u32[]{:S(2)}, u32[]{:S(2)}) collective-permute-start(f32[8,128]{1,0:T(8,128)S(1)} %add.21), channel_id=1, source_target_pairs={{0,8},{2,10},{4,12},{6,14},{8,0},{10,2},{12,4},{14,6},{1,9},{3,11}... | collective-permute-start | bytes 12296 | tf_op jit(solution)/shard_map/ppermute | solution.py:61
  88.8 46.2 %copy-start.2 = (f32[32,512]{1,0:T(8,128)S(1)}, f32[32,512]{1,0:T(8,128)}, u32[]{:S(2)}) copy-start(f32[32,512]{1,0:T(8,128)} %get-tuple-element.75.refs_9_) | copy-start | bytes 196612
  88.9 13.9 %collective-permute-start.20 = (f32[16,16,512]{2,1,0:T(8,128)S(1)}, f32[16,16,512]{2,1,0:T(8,128)S(1)}, u32[]{:S(2)}, u32[]{:S(2)}) collective-permute-start(f32[16,16,512]{2,1,0:T(8,128)S(1)} %get-tuple-element.79), channel_id=1, source_target_pairs={{1,2},{3,4},{5,6},{7,8},{9,10},{11,12},{13,14},{2,1},{4,3},{6,5},{... | collective-permute-start | bytes 1572872 | tf_op jit(solution)/shard_map/ppermute | solution.py:26
  90.9 11.9 %collective-permute-start.21 = (f32[16,16,512]{2,1,0:T(8,128)S(1)}, f32[16,16,512]{2,1,0:T(8,128)S(1)}, u32[]{:S(2)}, u32[]{:S(2)}) collective-permute-start(f32[16,16,512]{2,1,0:T(8,128)S(1)} %get-tuple-element.80), channel_id=1, source_target_pairs={{0,1},{1,0},{2,3},{3,2},{4,5},{5,4},{6,7},{7,6},{8,9},{9,8},{10,11... | collective-permute-start | bytes 1572872 | tf_op jit(solution)/shard_map/ppermute | solution.py:26
  100.8 12.2 %collective-permute-start.28 = (f32[16,16,512]{2,1,0:T(8,128)S(1)}, f32[16,16,512]{2,1,0:T(8,128)S(1)}, u32[]{:S(2)}, u32[]{:S(2)}) collective-permute-start(f32[16,16,512]{2,1,0:T(8,128)S(1)} %get-tuple-element.90), channel_id=1, source_target_pairs={{1,2},{3,4},{5,6},{7,8},{9,10},{11,12},{13,14},{2,1},{4,3},{6,5},{... | collective-permute-start | bytes 1572872 | tf_op jit(solution)/shard_map/ppermute | solution.py:26
  102.7 10.3 %collective-permute-start.29 = (f32[16,16,512]{2,1,0:T(8,128)S(1)}, f32[16,16,512]{2,1,0:T(8,128)S(1)}, u32[]{:S(2)}, u32[]{:S(2)}) collective-permute-start(f32[16,16,512]{2,1,0:T(8,128)S(1)} %get-tuple-element.91), channel_id=1, source_target_pairs={{0,1},{1,0},{2,3},{3,2},{4,5},{5,4},{6,7},{7,6},{8,9},{9,8},{10,11... | collective-permute-start | bytes 1572872 | tf_op jit(solution)/shard_map/ppermute | solution.py:26
  102.9 13.8 %collective-permute-start.22 = (f32[64,512]{1,0:T(8,128)S(1)}, f32[64,512]{1,0:T(8,128)S(1)}, u32[]{:S(2)}, u32[]{:S(2)}) collective-permute-start(f32[64,512]{1,0:T(8,128)S(1)} %get-tuple-element.82), channel_id=1, source_target_pairs={{0,64},{64,128},{128,192},{192,0},{1,65},{65,129},{129,193},{193,1... | collective-permute-start | bytes 393224 | tf_op jit(solution)/shard_map/ppermute | solution.py:42
  104.6 8.4 %collective-permute-start.30 = (f32[8,128]{1,0:T(8,128)S(1)}, f32[8,128]{1,0:T(8,128)S(1)}, u32[]{:S(2)}, u32[]{:S(2)}) collective-permute-start(f32[8,128]{1,0:T(8,128)S(1)} %get-tuple-element.92), channel_id=1, source_target_pairs={{0,0},{1,1},{2,2},{3,3},{4,4},{5,5},{6,6},{7,7},{8,8},{9,9},{10,10... | collective-permute-start | bytes 12296 | tf_op jit(solution)/shard_map/ppermute | solution.py:36
  105.2 14.0 %collective-permute-start.23 = (f32[64,512]{1,0:T(8,128)S(1)}, f32[64,512]{1,0:T(8,128)S(1)}, u32[]{:S(2)}, u32[]{:S(2)}) collective-permute-start(f32[64,512]{1,0:T(8,128)S(1)} %get-tuple-element.83), channel_id=1, source_target_pairs={{0,128},{64,192},{128,0},{192,64},{1,129},{65,193},{129,1},{193,65... | collective-permute-start | bytes 393224 | tf_op jit(solution)/shard_map/ppermute | solution.py:42
  113.0 6.2 %collective-permute-start.24 = (f32[64,512]{1,0:T(8,128)S(1)}, f32[64,512]{1,0:T(8,128)S(1)}, u32[]{:S(2)}, u32[]{:S(2)}) collective-permute-start(f32[64,512]{1,0:T(8,128)S(1)} %get-tuple-element.84), channel_id=1, source_target_pairs={{0,192},{64,0},{128,64},{192,128},{1,193},{65,1},{129,65},{193,129... | collective-permute-start | bytes 393224 | tf_op jit(solution)/shard_map/ppermute | solution.py:42
  113.1 8.1 %collective-permute-start.31 = (f32[72,512]{1,0:T(8,128)S(1)}, f32[72,512]{1,0:T(8,128)S(1)}, u32[]{:S(2)}, u32[]{:S(2)}) collective-permute-start(f32[72,512]{1,0:T(8,128)S(1)} %get-tuple-element.94), channel_id=1, source_target_pairs={{0,16},{16,32},{32,48},{48,0},{1,17},{17,33},{33,49},{49,1},{2,18}... | collective-permute-start | bytes 442376 | tf_op jit(solution)/shard_map/ppermute | solution.py:42
  115.2 8.6 %collective-permute-start.32 = (f32[72,512]{1,0:T(8,128)S(1)}, f32[72,512]{1,0:T(8,128)S(1)}, u32[]{:S(2)}, u32[]{:S(2)}) collective-permute-start(f32[72,512]{1,0:T(8,128)S(1)} %get-tuple-element.95), channel_id=1, source_target_pairs={{0,32},{16,48},{32,0},{48,16},{1,33},{17,49},{33,1},{49,17},{2,34}... | collective-permute-start | bytes 442376 | tf_op jit(solution)/shard_map/ppermute | solution.py:42
  116.7 7.6 %collective-permute-start.33 = (f32[72,512]{1,0:T(8,128)S(1)}, f32[72,512]{1,0:T(8,128)S(1)}, u32[]{:S(2)}, u32[]{:S(2)}) collective-permute-start(f32[72,512]{1,0:T(8,128)S(1)} %get-tuple-element.96), channel_id=1, source_target_pairs={{0,48},{16,0},{32,16},{48,32},{1,49},{17,1},{33,17},{49,33},{2,50}... | collective-permute-start | bytes 442376 | tf_op jit(solution)/shard_map/ppermute | solution.py:42
  119.3 11.7 %collective-permute-start.25 = (f32[16,512]{1,0:T(8,128)S(1)}, f32[16,512]{1,0:T(8,128)S(1)}, u32[]{:S(2)}, u32[]{:S(2)}) collective-permute-start(f32[16,512]{1,0:T(8,128)S(1)} %get-tuple-element.86), channel_id=1, source_target_pairs={{0,16},{16,32},{32,48},{48,0},{1,17},{17,33},{33,49},{49,1},{2,18}... | collective-permute-start | bytes 98312 | tf_op jit(solution)/shard_map/ppermute | solution.py:42
  120.8 11.0 %collective-permute-start.26 = (f32[16,512]{1,0:T(8,128)S(1)}, f32[16,512]{1,0:T(8,128)S(1)}, u32[]{:S(2)}, u32[]{:S(2)}) collective-permute-start(f32[16,512]{1,0:T(8,128)S(1)} %get-tuple-element.87), channel_id=1, source_target_pairs={{0,32},{16,48},{32,0},{48,16},{1,33},{17,49},{33,1},{49,17},{2,34}... | collective-permute-start | bytes 98312 | tf_op jit(solution)/shard_map/ppermute | solution.py:42
  121.3 10.5 %collective-permute-start.27 = (f32[16,512]{1,0:T(8,128)S(1)}, f32[16,512]{1,0:T(8,128)S(1)}, u32[]{:S(2)}, u32[]{:S(2)}) collective-permute-start(f32[16,512]{1,0:T(8,128)S(1)} %get-tuple-element.88), channel_id=1, source_target_pairs={{0,48},{16,0},{32,16},{48,32},{1,49},{17,1},{33,17},{49,33},{2,50}... | collective-permute-start | bytes 98312 | tf_op jit(solution)/shard_map/ppermute | solution.py:42
  124.3 7.8 %collective-permute-start.34 = (f32[24,512]{1,0:T(8,128)S(1)}, f32[24,512]{1,0:T(8,128)S(1)}, u32[]{:S(2)}, u32[]{:S(2)}) collective-permute-start(f32[24,512]{1,0:T(8,128)S(1)} %get-tuple-element.98), channel_id=1, source_target_pairs={{0,64},{64,128},{128,192},{192,0},{1,65},{65,129},{129,193},{193,1... | collective-permute-start | bytes 147464 | tf_op jit(solution)/shard_map/ppermute | solution.py:42
  127.3 6.2 %collective-permute-start.35 = (f32[24,512]{1,0:T(8,128)S(1)}, f32[24,512]{1,0:T(8,128)S(1)}, u32[]{:S(2)}, u32[]{:S(2)}) collective-permute-start(f32[24,512]{1,0:T(8,128)S(1)} %get-tuple-element.99), channel_id=1, source_target_pairs={{0,128},{64,192},{128,0},{192,64},{1,129},{65,193},{129,1},{193,65... | collective-permute-start | bytes 147464 | tf_op jit(solution)/shard_map/ppermute | solution.py:42
  131.0 4.1 %collective-permute-start.36 = (f32[24,512]{1,0:T(8,128)S(1)}, f32[24,512]{1,0:T(8,128)S(1)}, u32[]{:S(2)}, u32[]{:S(2)}) collective-permute-start(f32[24,512]{1,0:T(8,128)S(1)} %get-tuple-element.100), channel_id=1, source_target_pairs={{0,192},{64,0},{128,64},{192,128},{1,193},{65,1},{129,65},{193,129... | collective-permute-start | bytes 147464 | tf_op jit(solution)/shard_map/ppermute | solution.py:42

commit v7 on v6

--- a/solution.py
+++ b/solution.py
@@ -43,28 +43,10 @@
     return [pieces[0], *sent]
 
 
-def swapped(x):
-    return lax.all_to_all(x, TERM, 0, 0, tiled=True)
-
-
-def sector_steps():
-    for axis in SECTOR[::-1]:
-        count = lax.axis_size(axis)
-        mask = 1
-        while mask < count:
-            yield functools.partial(exchanged, axis=axis, mask=mask)
-            mask *= 2
-
-
-def exchanged(x, axis, mask):
-    pairs = [(i, i ^ mask) for i in range(lax.axis_size(axis))]
-    return x + lax.ppermute(x, axis, pairs)
-
-
-def over_sectors(x):
-    for step in sector_steps():
-        x = step(x)
-    return x
+def copied_along(piece, axis):
+    size = lax.axis_size(axis)
+    routes = [[(i, (i + k) % size) for i in range(size)] for k in range(size)]
+    return [piece, *[lax.ppermute(piece, axis, route) for route in routes[1:]]]
 
 
 def halves(x):
@@ -118,20 +100,35 @@
     accumulate(lax.axis_index(SECTOR), count, target, left, right, f_high, f_low, outs)
 
 
-def second_kernel(count, target, left, right, sums, field, gathered, *rest):
-    *outs, overlap, f_high, f_low = rest
+def second_kernel(count, target, left, right, field, *rest):
+    *rings, tile, f_high, f_low = rest
+    outs = rings[-3 * HALVES :]
+    rings = rings[: -3 * HALVES]
     peers, slab, width = field.shape
+    rows = slab // HALVES
 
     @pl.when(pl.program_id(0) == 0)
     def _():
+        size = len(rings) // HALVES
+        tails = [ring[k, 2 * rows :] for ring in rings[size:] for k in range(size)]
+        sums = functools.reduce(lambda x, y: x + y, tails)
         rayleigh = sums[0:1, 0:1] / sums[1:2, 0:1]
-        weighted = jnp.zeros((slab, width), F32)
-        for peer in range(peers):
-            vector = field[peer]
-            raw = gathered[peer, slab:] * (gathered[peer, :slab] - rayleigh * vector)
-            f_high[peer], f_low[peer] = halves(raw)
-            weighted += vector * raw
-        overlap[...] = jnp.broadcast_to(jnp.sum(weighted, keepdims=True), overlap.shape)
+        weighted = jnp.zeros((rows, width), F32)
+        for half in range(HALVES):
+            lines = slice(half * rows, (half + 1) * rows)
+            first, last = (lax.axis_index(TERM[i]) for i in (1 - half, half))
+            for j, ring in enumerate(rings[half * size : (half + 1) * size]):
+                for k in range(size):
+                    along = lax.rem(last + size - j, size)
+                    peer = place(half, along, lax.rem(first + size - k, size), size)
+                    vector = field[peer, lines]
+                    image, scaling = ring[k, :rows], ring[k, rows : 2 * rows]
+                    raw = scaling * (image - rayleigh * vector)
+                    f_high[peer, lines], f_low[peer, lines] = halves(raw)
+                    weighted += vector * raw
+        line = lax.broadcasted_iota(jnp.int32, tile.shape, 0)
+        overlap = jnp.sum(weighted, keepdims=True)
+        tile[...] = jnp.where(line == 2, overlap, sums[:, : tile.shape[1]])
 
     flat = (peers * slab, width)
     f_high, f_low = f_high.reshape(flat), f_low.reshape(flat)
@@ -239,38 +236,57 @@
             piece[rows:] = summed(pl.ds(size * rows, piece.shape[0] - rows))
 
 
-def landed(refs, rows):
-    size = len(refs) // HALVES
-    groups = [refs[h * size : (h + 1) * size] for h in range(HALVES)]
-    totals = [functools.reduce(lambda x, y: x + y, [r[...] for r in g]) for g in groups]
-    tails = [t[rows:] for t in totals if t.shape[0] > rows]
-    return [t[:rows] for t in totals], functools.reduce(lambda x, y: x + y, tails)
+def added(refs):
+    return functools.reduce(lambda x, y: x + y, [ref[...] for ref in refs])
 
 
 def first_landing(*refs):
-    *arrived, scaling, image, copies, sums = refs
-    peers, slab = copies.shape[0], image.shape[0]
-    rows = slab // HALVES
-    parts, tail = landed(arrived, rows)
-    for half, part in enumerate(parts):
-        image[half * rows : (half + 1) * rows] = part
-    for peer in range(peers):
-        copies[peer, :slab] = image[...]
-        copies[peer, slab:] = scaling[...]
-    sums[...] = tail[:, : sums.shape[1]]
+    *arrived, scaling, first, last, piece, tile = refs
+    rows = first.shape[0]
+    size = len(arrived) // HALVES
+    totals = [added(arrived[h * size : (h + 1) * size]) for h in range(HALVES)]
+    first[...] = totals[0][:rows]
+    last[...] = totals[1][:rows]
+    piece[:rows] = totals[0][:rows]
+    piece[rows:] = scaling[:rows]
+    tile[...] = (totals[0] + totals[1])[rows:, : tile.shape[1]]
+
+
+def tailed(image, scaling, tile, piece):
+    rows, width = image.shape
+    piece[:rows] = image[...]
+    piece[rows : 2 * rows] = scaling[rows:]
+    for start in range(0, width, tile.shape[1]):
+        piece[2 * rows :, start : start + tile.shape[1]] = tile[...]
+
+
+def stacked(*refs):
+    pieces, stacks = refs[:-HALVES], refs[-HALVES:]
+    size = len(pieces) // HALVES
+    for i, piece in enumerate(pieces):
+        stacks[i // size][i % size] = piece[...]
 
 
 def second_landing(*refs):
-    *arrived, sums, first_image, scaling, own, correction, image = refs
-    rows = image.shape[0] // HALVES
-    parts, tail = landed(arrived, rows)
+    *arrived, sums, first, last, scaling, own, correction, image = refs
+    rows = first.shape[0]
+    size = len(arrived) // HALVES
+    totals = [added(arrived[h * size : (h + 1) * size]) for h in range(HALVES)]
     rayleigh = sums[0:1, 0:1] / sums[1:2, 0:1]
-    share = tail[0:1, 0:1] / sums[1:2, 0:1]
-    vector = own[...]
-    correction[...] = scaling[...] * (first_image[...] - rayleigh * vector) - share * vector
-    for half, part in enumerate(parts):
+    share = totals[-1][rows + 2 : rows + 3, 0:1] / sums[1:2, 0:1]
+    for half, part in enumerate((first, last)):
         lines = slice(half * rows, (half + 1) * rows)
-        image[lines] = part - share * first_image[lines]
+        vector = own[lines]
+        raw = scaling[lines] * (part[...] - rayleigh * vector)
+        correction[lines] = raw - share * vector
+        image[lines] = totals[half][:rows] - share * part[...]
+
+
+def gathered(ends):
+    pieces = [copied_along(x, TERM[1 - half]) for half, x in enumerate(ends)]
+    shapes = [(len(p), *x.shape) for p, x in zip(pieces, ends)]
+    stacks = small_call(stacked, shapes, sum(pieces, []))
+    return sum((copied_along(x, TERM[half]) for half, x in enumerate(stacks)), [])
 
 
 def relayed(half, pieces, rows):
@@ -283,19 +299,13 @@
     return exchanged_along(onward, other)
 
 
-def small_call(body, out_shapes, args, scratch=(), spaces=None):
-    spaces = spaces or [pltpu.VMEM] * len(out_shapes)
+def small_call(body, out_shapes, args, scratch=()):
+    in_vmem = pl.BlockSpec(memory_space=pltpu.VMEM)
     return pl.pallas_call(
         body,
-        in_specs=[pl.BlockSpec(memory_space=pltpu.VMEM)] * len(args),
-        out_specs=[
-            pl.BlockSpec() if space == pltpu.HBM else pl.BlockSpec(memory_space=space)
-            for space in spaces
-        ],
-        out_shape=[
-            pltpu.HBM(s, F32) if space == pltpu.HBM else jax.ShapeDtypeStruct(s, F32)
-            for s, space in zip(out_shapes, spaces)
-        ],
+        in_specs=[in_vmem] * len(args),
+        out_specs=[in_vmem] * len(out_shapes),
+        out_shape=[jax.ShapeDtypeStruct(s, F32) for s in out_shapes],
         scratch_shapes=scratch,
         compiler_params=pltpu.CompilerParams(vmem_limit_bytes=32 * MIB),
     )(*args)
@@ -334,20 +344,20 @@
             [pltpu.VMEM((EXTRA, width), F32)],
         )
         arrived += relayed(half, pieces, rows)
-    first_image, copies, sums = small_call(
-        first_landing,
-        [(slab, width), (peers, 2 * slab, width), (EXTRA, LANES)],
-        [*arrived, scaling],
-        spaces=[pltpu.VMEM, pltpu.HBM, pltpu.VMEM],
-    )
-    gathered = swapped(copies)
-    sums = over_sectors(sums)
-
-    *parts, overlap = image_of(
-        second_kernel, fields=(sums, blocked, gathered), extra=[(EXTRA, LANES)], scratch=split
+    part, tile = (rows, width), (EXTRA, LANES)
+    first, last, end, sums = small_call(
+        first_landing, [part, part, (2 * rows, width), tile], [*arrived, scaling]
+    )
+    (tailed_end,) = small_call(
+        tailed, [(2 * rows + EXTRA, width)], [last, scaling, rotated(sums)]
+    )
+    rings = gathered([end, tailed_end])
+
+    *parts, sums = image_of(
+        second_kernel, fields=(blocked, *rings), extra=[tile], scratch=split
     )
     parts = moved_parts(parts)
-    overlap = rotated(overlap)
+    overlap = rotated(sums)
     arrived = []
     for half in range(HALVES):
         tail = [overlap] if half else []
@@ -361,8 +371,9 @@
     correction, second_image = small_call(
         second_landing,
         [(slab, width)] * 2,
-        [*arrived, sums, first_image, scaling, own],
-    )
+        [*arrived, sums, first, last, scaling, own],
+    )
+    first_image = jnp.concatenate([first, last], axis=0)
     return (first_image[None], correction[None], second_image[None])
 
 

time: 136 us -> 141 us (1.037)
  starting transfers between devices: 90.6 us -> 104 us
  waiting for transfers between devices: 31.8 us -> 25.1 us
  Pallas kernels: 11.9 us -> 10.4 us
    ppermute x4 -> x12, starting transfers between devices: 5.71 us -> 25.2 us  [copied_along(): return [piece, *[lax.ppermute(piece, axis, route) for route in routes[1:]]]]
    all_to_all x1 -> x0, waiting for transfers between devices: 10.9 us -> none  [swapped(): return lax.all_to_all(x, TERM, 0, 0, tiled=True)]
    ppermute x4, starting transfers between devices: 12.6 us -> 22.6 us  [moved(): lax.ppermute(local, SECTOR, swap)]
    all_to_all x1 -> x0, starting transfers between devices: 6.79 us -> none  [swapped(): return lax.all_to_all(x, TERM, 0, 0, tiled=True)]
    ppermute x4, starting transfers between devices: 13.1 us -> 7.79 us  [moved(): lax.ppermute(crossing, SECTOR, upward + downward)]
    ppermute x24, starting transfers between devices: 51.7 us -> 46.4 us  [exchanged_along(): sent = [lax.ppermute(pieces[k], axis, routes[k]) for k in range(1, size)]]
    ppermute x4 -> x12, waiting for transfers between devices: 11.2 us -> 16 us  [copied_along(): return [piece, *[lax.ppermute(piece, axis, route) for route in routes[1:]]]]
    ppermute x4, waiting for transfers between devices: 2.26 us -> 0.07 us  [moved(): lax.ppermute(crossing, SECTOR, upward + downward)]
  transfers between devices with their start and end apart: 38 -> 46, of which waited for: 14 -> 12; matrix products, arithmetic and copies ran while one was open for 0% -> 0% of each run, Pallas kernels for 1% -> 1%
where the time goes in v7:
time: 141 us
  starting transfers between devices  104 us (74%)
  waiting for transfers between devices  25.1 us (18%)
  Pallas kernels  10.4 us (7%)
  between operations  1.54 us (1%)
    ppermute x24, starting transfers between devices, exchanged_along(): sent = [lax.ppermute(pieces[k], axis, routes[k]) for k in range(1, size)]  46.4 us
    ppermute x12, starting transfers between devices, copied_along(): return [piece, *[lax.ppermute(piece, axis, route) for route in routes[1:]]]  25.2 us
    ppermute x4, starting transfers between devices, moved(): lax.ppermute(local, SECTOR, swap)  22.6 us
    ppermute x12, waiting for transfers between devices, copied_along(): return [piece, *[lax.ppermute(piece, axis, route) for route in routes[1:]]]  16 us
    ppermute x24, waiting for transfers between devices, exchanged_along(): sent = [lax.ppermute(pieces[k], axis, routes[k]) for k in range(1, size)]  9.03 us
    pallas_call x2, Pallas kernels, partial_image(): pl.pallas_call(body, out_shape=[jax.ShapeDtypeStruct(x, F32) for x in (*[...  8.84 us
    ppermute x4, starting transfers between devices, moved(): lax.ppermute(crossing, SECTOR, upward + downward)  7.79 us
  transfers between devices with their start and end apart: 46, of which 12 were waited for; matrix products, arithmetic and copies ran while one was open for 0% of the time, Pallas kernels for 1%

profile of v7, /device:TPU:64, one launch (start us, length us, event | category | flops | bytes accessed | tf_op | source)
XLA Modules:
  0.0 141.2 jit_solution(10531184316496986100)
XLA Ops:
  1.3 4.4 %shard_map.85 = (f32[16,16,512]{2,1,0:T(8,128)S(1)}, f32[16,16,512]{2,1,0:T(8,128)S(1)}, f32[16,16,512]{2,1,0:T(8,128)S(1)}, f32[16,16,512]{2,1,0:T(8,128)S(1)},...) custom-call(s32[1,1]{1,0:T(1,128)S(6)} %copy.9.count, s32[1,4]{1,0:T(1,128)} %target.3, f32[4,512,512]{2,1,0:T(8,128)} %bitcast.19, ...), custom_call_target="tpu_custom_call" | custom-call | flops 6442450944 | bytes 8388608 | tf_op jit(solution)/shard_map/pallas_call | solution.py:156
  5.7 2.1 %collective-permute-start.8 = (f32[16,16,512]{2,1,0:T(8,128)S(1)}, f32[16,16,512]{2,1,0:T(8,128)S(1)}, u32[]{:S(2)}, u32[]{:S(2)}) collective-permute-start(f32[16,16,512]{2,1,0:T(8,128)S(1)} %get-tuple-element.68), channel_id=1, source_target_pairs={{1,2},{3,4},{5,6},{7,8},{9,10},{11,12},{13,14},{2,1},{4,3},{6,5},{... | collective-permute-start | bytes 1572872 | tf_op jit(solution)/shard_map/ppermute | solution.py:26
  7.8 7.8 %collective-permute-start.9 = (f32[16,16,512]{2,1,0:T(8,128)S(1)}, f32[16,16,512]{2,1,0:T(8,128)S(1)}, u32[]{:S(2)}, u32[]{:S(2)}) collective-permute-start(f32[16,16,512]{2,1,0:T(8,128)S(1)} %get-tuple-element.69), channel_id=1, source_target_pairs={{0,1},{1,0},{2,3},{3,2},{4,5},{5,4},{6,7},{7,6},{8,9},{9,8},{10,11... | collective-permute-start | bytes 1572872 | tf_op jit(solution)/shard_map/ppermute | solution.py:26
  15.6 1.9 %collective-permute-start = (f32[16,16,512]{2,1,0:T(8,128)S(1)}, f32[16,16,512]{2,1,0:T(8,128)S(1)}, u32[]{:S(2)}, u32[]{:S(2)}) collective-permute-start(f32[16,16,512]{2,1,0:T(8,128)S(1)} %get-tuple-element.57), channel_id=1, source_target_pairs={{1,2},{3,4},{5,6},{7,8},{9,10},{11,12},{13,14},{2,1},{4,3},{6,5},{... | collective-permute-start | bytes 1572872 | tf_op jit(solution)/shard_map/ppermute | solution.py:26
  17.5 3.3 %collective-permute-start.1 = (f32[16,16,512]{2,1,0:T(8,128)S(1)}, f32[16,16,512]{2,1,0:T(8,128)S(1)}, u32[]{:S(2)}, u32[]{:S(2)}) collective-permute-start(f32[16,16,512]{2,1,0:T(8,128)S(1)} %get-tuple-element.58), channel_id=1, source_target_pairs={{0,1},{1,0},{2,3},{3,2},{4,5},{5,4},{6,7},{7,6},{8,9},{9,8},{10,11... | collective-permute-start | bytes 1572872 | tf_op jit(solution)/shard_map/ppermute | solution.py:26
  20.8 0.2 shard_map.88
  21.1 1.7 %collective-permute-start.10 = (f32[72,512]{1,0:T(8,128)S(1)}, f32[72,512]{1,0:T(8,128)S(1)}, u32[]{:S(2)}, u32[]{:S(2)}) collective-permute-start(f32[72,512]{1,0:T(8,128)S(1)} %get-tuple-element.71), channel_id=1, source_target_pairs={{0,16},{16,32},{32,48},{48,0},{1,17},{17,33},{33,49},{49,1},{2,18}... | collective-permute-start | bytes 442376 | tf_op jit(solution)/shard_map/ppermute | solution.py:42
  22.7 2.9 %collective-permute-start.11 = (f32[72,512]{1,0:T(8,128)S(1)}, f32[72,512]{1,0:T(8,128)S(1)}, u32[]{:S(2)}, u32[]{:S(2)}) collective-permute-start(f32[72,512]{1,0:T(8,128)S(1)} %get-tuple-element.72), channel_id=1, source_target_pairs={{0,32},{16,48},{32,0},{48,16},{1,33},{17,49},{33,1},{49,17},{2,34}... | collective-permute-start | bytes 442376 | tf_op jit(solution)/shard_map/ppermute | solution.py:42
  25.6 0.4 collective-permute-start.12
  26.0 0.1 collective-permute-done.crossed
  26.1 0.2 shard_map.86
  26.3 2.2 %collective-permute-start.2 = (f32[72,512]{1,0:T(8,128)S(1)}, f32[72,512]{1,0:T(8,128)S(1)}, u32[]{:S(2)}, u32[]{:S(2)}) collective-permute-start(f32[72,512]{1,0:T(8,128)S(1)} %get-tuple-element.60), channel_id=1, source_target_pairs={{0,64},{64,128},{128,192},{192,0},{1,65},{65,129},{129,193},{193,1... | collective-permute-start | bytes 442376 | tf_op jit(solution)/shard_map/ppermute | solution.py:42
  28.5 4.2 %collective-permute-start.3 = (f32[72,512]{1,0:T(8,128)S(1)}, f32[72,512]{1,0:T(8,128)S(1)}, u32[]{:S(2)}, u32[]{:S(2)}) collective-permute-start(f32[72,512]{1,0:T(8,128)S(1)} %get-tuple-element.61), channel_id=1, source_target_pairs={{0,128},{64,192},{128,0},{192,64},{1,129},{65,193},{129,1},{193,65... | collective-permute-start | bytes 442376 | tf_op jit(solution)/shard_map/ppermute | solution.py:42
  32.7 0.1 collective-permute-start.4
  32.9 2.0 %collective-permute-start.13 = (f32[24,512]{1,0:T(8,128)S(1)}, f32[24,512]{1,0:T(8,128)S(1)}, u32[]{:S(2)}, u32[]{:S(2)}) collective-permute-start(f32[24,512]{1,0:T(8,128)S(1)} %get-tuple-element.75), channel_id=1, source_target_pairs={{0,64},{64,128},{128,192},{192,0},{1,65},{65,129},{129,193},{193,1... | collective-permute-start | bytes 147464 | tf_op jit(solution)/shard_map/ppermute | solution.py:42
  34.9 3.4 %collective-permute-start.14 = (f32[24,512]{1,0:T(8,128)S(1)}, f32[24,512]{1,0:T(8,128)S(1)}, u32[]{:S(2)}, u32[]{:S(2)}) collective-permute-start(f32[24,512]{1,0:T(8,128)S(1)} %get-tuple-element.76), channel_id=1, source_target_pairs={{0,128},{64,192},{128,0},{192,64},{1,129},{65,193},{129,1},{193,65... | collective-permute-start | bytes 147464 | tf_op jit(solution)/shard_map/ppermute | solution.py:42
  38.3 1.2 collective-permute-start.15
  39.5 0.8 collective-permute-done.3.refs_2_
  40.4 0.1 collective-permute-start.5
  40.4 3.0 %collective-permute-start.6 = (f32[24,512]{1,0:T(8,128)S(1)}, f32[24,512]{1,0:T(8,128)S(1)}, u32[]{:S(2)}, u32[]{:S(2)}) collective-permute-start(f32[24,512]{1,0:T(8,128)S(1)} %get-tuple-element.65), channel_id=1, source_target_pairs={{0,32},{16,48},{32,0},{48,16},{1,33},{17,49},{33,1},{49,17},{2,34}... | collective-permute-start | bytes 147464 | tf_op jit(solution)/shard_map/ppermute | solution.py:42
  43.4 2.5 %collective-permute-start.7 = (f32[24,512]{1,0:T(8,128)S(1)}, f32[24,512]{1,0:T(8,128)S(1)}, u32[]{:S(2)}, u32[]{:S(2)}) collective-permute-start(f32[24,512]{1,0:T(8,128)S(1)} %get-tuple-element.66), channel_id=1, source_target_pairs={{0,48},{16,0},{32,16},{48,32},{1,49},{17,1},{33,17},{49,33},{2,50}... | collective-permute-start | bytes 147464 | tf_op jit(solution)/shard_map/ppermute | solution.py:42
  45.9 0.4 collective-permute-done.5.refs_1_
  46.3 1.3 collective-permute-done.7.refs_3_
  47.7 1.7 %collective-permute-start.16 = (f32[32,512]{1,0:T(8,128)S(1)}, f32[32,512]{1,0:T(8,128)S(1)}, u32[]{:S(2)}, u32[]{:S(2)}) collective-permute-start(f32[32,512]{1,0:T(8,128)S(1)} %get-tuple-element.80.refs_0_), channel_id=1, source_target_pairs={{0,16},{16,32},{32,48},{48,0},{1,17},{17,33},{33,49},{49,1},{2,18}... | collective-permute-start | bytes 196616 | tf_op jit(solution)/shard_map/ppermute | solution.py:49
  49.4 0.6 collective-permute-start.19
  50.1 8.2 %collective-permute-start.20 = (f32[40,512]{1,0:T(8,128)S(1)}, f32[40,512]{1,0:T(8,128)S(1)}, u32[]{:S(2)}, u32[]{:S(2)}) collective-permute-start(f32[40,512]{1,0:T(8,128)S(1)} %shard_map.91.refs_4_), channel_id=1, source_target_pairs={{0,64},{64,128},{128,192},{192,0},{1,65},{65,129},{129,193},{193,1... | collective-permute-start | bytes 245768 | tf_op jit(solution)/shard_map/ppermute | solution.py:49
  58.3 3.0 %collective-permute-start.21 = (f32[40,512]{1,0:T(8,128)S(1)}, f32[40,512]{1,0:T(8,128)S(1)}, u32[]{:S(2)}, u32[]{:S(2)}) collective-permute-start(f32[40,512]{1,0:T(8,128)S(1)} %shard_map.91.refs_4_), channel_id=1, source_target_pairs={{0,128},{64,192},{128,0},{192,64},{1,129},{65,193},{129,1},{193,65... | collective-permute-start | bytes 245768 | tf_op jit(solution)/shard_map/ppermute | solution.py:49
  61.3 2.5 %collective-permute-start.22 = (f32[40,512]{1,0:T(8,128)S(1)}, f32[40,512]{1,0:T(8,128)S(1)}, u32[]{:S(2)}, u32[]{:S(2)}) collective-permute-start(f32[40,512]{1,0:T(8,128)S(1)} %shard_map.91.refs_4_), channel_id=1, source_target_pairs={{0,192},{64,0},{128,64},{192,128},{1,193},{65,1},{129,65},{193,129... | collective-permute-start | bytes 245768 | tf_op jit(solution)/shard_map/ppermute | solution.py:49
  63.9 1.8 %collective-permute-start.17 = (f32[32,512]{1,0:T(8,128)S(1)}, f32[32,512]{1,0:T(8,128)S(1)}, u32[]{:S(2)}, u32[]{:S(2)}) collective-permute-start(f32[32,512]{1,0:T(8,128)S(1)} %get-tuple-element.80.refs_0_), channel_id=1, source_target_pairs={{0,32},{16,48},{32,0},{48,16},{1,33},{17,49},{33,1},{49,17},{2,34}... | collective-permute-start | bytes 196616 | tf_op jit(solution)/shard_map/ppermute | solution.py:49
  65.6 1.8 %collective-permute-start.18 = (f32[32,512]{1,0:T(8,128)S(1)}, f32[32,512]{1,0:T(8,128)S(1)}, u32[]{:S(2)}, u32[]{:S(2)}) collective-permute-start(f32[32,512]{1,0:T(8,128)S(1)} %get-tuple-element.80.refs_0_), channel_id=1, source_target_pairs={{0,48},{16,0},{32,16},{48,32},{1,49},{17,1},{33,17},{49,33},{2,50}... | collective-permute-start | bytes 196616 | tf_op jit(solution)/shard_map/ppermute | solution.py:49
  67.4 2.2 %collective-permute-done.17.refs_2_ = f32[32,512]{1,0:T(8,128)S(1)} collective-permute-done((f32[32,512]{1,0:T(8,128)S(1)}, f32[32,512]{1,0:T(8,128)S(1)}, u32[]{:S(2)}, u32[]{:S(2)}) %collective-permute-start.17) | collective-permute-done | bytes 65568 | tf_op jit(solution)/shard_map/ppermute | solution.py:49
  69.6 0.3 collective-permute-done.18.refs_3_
  69.9 0.1 collective-permute-start.23
  70.0 1.4 %collective-permute-start.26 = (f32[4,40,512]{2,1,0:T(8,128)S(1)}, f32[4,40,512]{2,1,0:T(8,128)S(1)}, u32[]{:S(2)}, u32[]{:S(2)}) collective-permute-start(f32[4,40,512]{2,1,0:T(8,128)S(1)} %get-tuple-element.83.rest_4_), channel_id=1, source_target_pairs={{0,16},{16,32},{32,48},{48,0},{1,17},{17,33},{33,49},{49,1},{2,18}... | collective-permute-start | bytes 983048 | tf_op jit(solution)/shard_map/ppermute | solution.py:49
  71.5 3.1 %collective-permute-start.27 = (f32[4,40,512]{2,1,0:T(8,128)S(1)}, f32[4,40,512]{2,1,0:T(8,128)S(1)}, u32[]{:S(2)}, u32[]{:S(2)}) collective-permute-start(f32[4,40,512]{2,1,0:T(8,128)S(1)} %get-tuple-element.83.rest_4_), channel_id=1, source_target_pairs={{0,32},{16,48},{32,0},{48,16},{1,33},{17,49},{33,1},{49,17},{2,34}... | collective-permute-start | bytes 983048 | tf_op jit(solution)/shard_map/ppermute | solution.py:49
  74.6 0.1 collective-permute-start.28
  74.7 1.4 collective-permute-start.24
  76.1 7.1 %collective-permute-done.23.rest_1_ = f32[4,32,512]{2,1,0:T(8,128)S(1)} collective-permute-done((f32[4,32,512]{2,1,0:T(8,128)S(1)}, f32[4,32,512]{2,1,0:T(8,128)S(1)}, u32[]{:S(2)}, u32[]{:S(2)}) %collective-permute-start.23) | collective-permute-done | bytes 262176 | tf_op jit(solution)/shard_map/ppermute | solution.py:49
  83.2 6.4 %collective-permute-done.25.rest_3_ = f32[4,32,512]{2,1,0:T(8,128)S(1)} collective-permute-done((f32[4,32,512]{2,1,0:T(8,128)S(1)}, f32[4,32,512]{2,1,0:T(8,128)S(1)}, u32[]{:S(2)}, u32[]{:S(2)}) %collective-permute-start.25) | collective-permute-done | bytes 262176 | tf_op jit(solution)/shard_map/ppermute | solution.py:49
  89.6 4.4 %shard_map.93 = (f32[16,16,512]{2,1,0:T(8,128)S(1)}, f32[16,16,512]{2,1,0:T(8,128)S(1)}, f32[16,16,512]{2,1,0:T(8,128)S(1)}, f32[16,16,512]{2,1,0:T(8,128)S(1)},...) custom-call(s32[1,1]{1,0:T(1,128)S(6)} %copy.9.count, s32[1,4]{1,0:T(1,128)} %target.3, ...), custom_call_target="tpu_custom_call" | custom-call | flops 6442450944 | bytes 8388608 | tf_op jit(solution)/shard_map/pallas_call | solution.py:156
  94.0 1.9 %collective-permute-start.29 = (f32[16,16,512]{2,1,0:T(8,128)S(1)}, f32[16,16,512]{2,1,0:T(8,128)S(1)}, u32[]{:S(2)}, u32[]{:S(2)}) collective-permute-start(f32[16,16,512]{2,1,0:T(8,128)S(1)} %get-tuple-element.85), channel_id=1, source_target_pairs={{1,2},{3,4},{5,6},{7,8},{9,10},{11,12},{13,14},{2,1},{4,3},{6,5},{... | collective-permute-start | bytes 1572872 | tf_op jit(solution)/shard_map/ppermute | solution.py:26
  96.0 7.4 %collective-permute-start.30 = (f32[16,16,512]{2,1,0:T(8,128)S(1)}, f32[16,16,512]{2,1,0:T(8,128)S(1)}, u32[]{:S(2)}, u32[]{:S(2)}) collective-permute-start(f32[16,16,512]{2,1,0:T(8,128)S(1)} %get-tuple-element.86), channel_id=1, source_target_pairs={{0,1},{1,0},{2,3},{3,2},{4,5},{5,4},{6,7},{7,6},{8,9},{9,8},{10,11... | collective-permute-start | bytes 1572872 | tf_op jit(solution)/shard_map/ppermute | solution.py:26
  103.3 1.9 %collective-permute-start.37 = (f32[16,16,512]{2,1,0:T(8,128)S(1)}, f32[16,16,512]{2,1,0:T(8,128)S(1)}, u32[]{:S(2)}, u32[]{:S(2)}) collective-permute-start(f32[16,16,512]{2,1,0:T(8,128)S(1)} %get-tuple-element.96), channel_id=1, source_target_pairs={{1,2},{3,4},{5,6},{7,8},{9,10},{11,12},{13,14},{2,1},{4,3},{6,5},{... | collective-permute-start | bytes 1572872 | tf_op jit(solution)/shard_map/ppermute | solution.py:26
  105.3 4.1 %collective-permute-start.38 = (f32[16,16,512]{2,1,0:T(8,128)S(1)}, f32[16,16,512]{2,1,0:T(8,128)S(1)}, u32[]{:S(2)}, u32[]{:S(2)}) collective-permute-start(f32[16,16,512]{2,1,0:T(8,128)S(1)} %get-tuple-element.97), channel_id=1, source_target_pairs={{0,1},{1,0},{2,3},{3,2},{4,5},{5,4},{6,7},{7,6},{8,9},{9,8},{10,11... | collective-permute-start | bytes 1572872 | tf_op jit(solution)/shard_map/ppermute | solution.py:26
  109.4 0.1 shard_map.94
  109.5 0.1 collective-permute-start.31
  109.6 0.9 collective-permute-start.39
  110.5 5.0 %collective-permute-start.32 = (f32[64,512]{1,0:T(8,128)S(1)}, f32[64,512]{1,0:T(8,128)S(1)}, u32[]{:S(2)}, u32[]{:S(2)}) collective-permute-start(f32[64,512]{1,0:T(8,128)S(1)} %get-tuple-element.89), channel_id=1, source_target_pairs={{0,128},{64,192},{128,0},{192,64},{1,129},{65,193},{129,1},{193,65... | collective-permute-start | bytes 393224 | tf_op jit(solution)/shard_map/ppermute | solution.py:42
  115.5 7.4 %collective-permute-start.33 = (f32[64,512]{1,0:T(8,128)S(1)}, f32[64,512]{1,0:T(8,128)S(1)}, u32[]{:S(2)}, u32[]{:S(2)}) collective-permute-start(f32[64,512]{1,0:T(8,128)S(1)} %get-tuple-element.90), channel_id=1, source_target_pairs={{0,192},{64,0},{128,64},{192,128},{1,193},{65,1},{129,65},{193,129... | collective-permute-start | bytes 393224 | tf_op jit(solution)/shard_map/ppermute | solution.py:42
  122.9 0.1 shard_map.96
  123.0 0.1 collective-permute-start.40
  123.1 0.1 collective-permute-start.41
  123.2 3.1 %collective-permute-start.42 = (f32[72,512]{1,0:T(8,128)S(1)}, f32[72,512]{1,0:T(8,128)S(1)}, u32[]{:S(2)}, u32[]{:S(2)}) collective-permute-start(f32[72,512]{1,0:T(8,128)S(1)} %get-tuple-element.102), channel_id=1, source_target_pairs={{0,48},{16,0},{32,16},{48,32},{1,49},{17,1},{33,17},{49,33},{2,50}... | collective-permute-start | bytes 442376 | tf_op jit(solution)/shard_map/ppermute | solution.py:42
  126.3 0.6 collective-permute-done.33.refs_3_
  126.9 0.4 collective-permute-start.34
  127.3 2.2 %collective-permute-start.35 = (f32[16,512]{1,0:T(8,128)S(1)}, f32[16,512]{1,0:T(8,128)S(1)}, u32[]{:S(2)}, u32[]{:S(2)}) collective-permute-start(f32[16,512]{1,0:T(8,128)S(1)} %get-tuple-element.93), channel_id=1, source_target_pairs={{0,32},{16,48},{32,0},{48,16},{1,33},{17,49},{33,1},{49,17},{2,34}... | collective-permute-start | bytes 98312 | tf_op jit(solution)/shard_map/ppermute | solution.py:42
  129.5 4.2 %collective-permute-done.40.refs_1_ = f32[72,512]{1,0:T(8,128)S(1)} collective-permute-done((f32[72,512]{1,0:T(8,128)S(1)}, f32[72,512]{1,0:T(8,128)S(1)}, u32[]{:S(2)}, u32[]{:S(2)}) %collective-permute-start.40) | collective-permute-done | bytes 147488 | tf_op jit(solution)/shard_map/ppermute | solution.py:42
  133.7 0.1 collective-permute-start.43
  133.8 1.8 %collective-permute-start.44 = (f32[24,512]{1,0:T(8,128)S(1)}, f32[24,512]{1,0:T(8,128)S(1)}, u32[]{:S(2)}, u32[]{:S(2)}) collective-permute-start(f32[24,512]{1,0:T(8,128)S(1)} %get-tuple-element.105), channel_id=1, source_target_pairs={{0,128},{64,192},{128,0},{192,64},{1,129},{65,193},{129,1},{193,65... | collective-permute-start | bytes 147464 | tf_op jit(solution)/shard_map/ppermute | solution.py:42
  135.6 2.5 %collective-permute-start.45 = (f32[24,512]{1,0:T(8,128)S(1)}, f32[24,512]{1,0:T(8,128)S(1)}, u32[]{:S(2)}, u32[]{:S(2)}) collective-permute-start(f32[24,512]{1,0:T(8,128)S(1)} %get-tuple-element.106), channel_id=1, source_target_pairs={{0,192},{64,0},{128,64},{192,128},{1,193},{65,1},{129,65},{193,129... | collective-permute-start | bytes 147464 | tf_op jit(solution)/shard_map/ppermute | solution.py:42
  138.1 0.6 maximum_bitcast_fusion
  138.8 0.8 collective-permute-done.43.refs_5_
  139.6 0.9 collective-permute-done.45.refs_7_
  140.5 0.7 shard_map.98
  (48 shorter events, 0.3 us)
Async XLA Ops:
  1.3 19.5 %copy-start = (f32[1,512,512]{2,1,0:T(8,128)S(1)}, f32[1,512,512]{2,1,0:T(8,128)}, u32[]{:S(2)}) copy-start(f32[1,512,512]{2,1,0:T(8,128)} %param.6) | copy-start | bytes 3145732
  5.7 41.9 %copy-start.1 = (f32[1,32,512]{2,1,0:T(8,128)S(1)}, f32[1,32,512]{2,1,0:T(8,128)}, u32[]{:S(2)}) copy-start(f32[1,32,512]{2,1,0:T(8,128)} %param.7) | copy-start | bytes 196612
  5.7 15.1 %collective-permute-start.8 = (f32[16,16,512]{2,1,0:T(8,128)S(1)}, f32[16,16,512]{2,1,0:T(8,128)S(1)}, u32[]{:S(2)}, u32[]{:S(2)}) collective-permute-start(f32[16,16,512]{2,1,0:T(8,128)S(1)} %get-tuple-element.68), channel_id=1, source_target_pairs={{1,2},{3,4},{5,6},{7,8},{9,10},{11,12},{13,14},{2,1},{4,3},{6,5},{... | collective-permute-start | bytes 1572872 | tf_op jit(solution)/shard_map/ppermute | solution.py:26
  7.8 13.0 %collective-permute-start.9 = (f32[16,16,512]{2,1,0:T(8,128)S(1)}, f32[16,16,512]{2,1,0:T(8,128)S(1)}, u32[]{:S(2)}, u32[]{:S(2)}) collective-permute-start(f32[16,16,512]{2,1,0:T(8,128)S(1)} %get-tuple-element.69), channel_id=1, source_target_pairs={{0,1},{1,0},{2,3},{3,2},{4,5},{5,4},{6,7},{7,6},{8,9},{9,8},{10,11... | collective-permute-start | bytes 1572872 | tf_op jit(solution)/shard_map/ppermute | solution.py:26
  15.6 10.5 %collective-permute-start = (f32[16,16,512]{2,1,0:T(8,128)S(1)}, f32[16,16,512]{2,1,0:T(8,128)S(1)}, u32[]{:S(2)}, u32[]{:S(2)}) collective-permute-start(f32[16,16,512]{2,1,0:T(8,128)S(1)} %get-tuple-element.57), channel_id=1, source_target_pairs={{1,2},{3,4},{5,6},{7,8},{9,10},{11,12},{13,14},{2,1},{4,3},{6,5},{... | collective-permute-start | bytes 1572872 | tf_op jit(solution)/shard_map/ppermute | solution.py:26
  17.5 8.6 %collective-permute-start.1 = (f32[16,16,512]{2,1,0:T(8,128)S(1)}, f32[16,16,512]{2,1,0:T(8,128)S(1)}, u32[]{:S(2)}, u32[]{:S(2)}) collective-permute-start(f32[16,16,512]{2,1,0:T(8,128)S(1)} %get-tuple-element.58), channel_id=1, source_target_pairs={{0,1},{1,0},{2,3},{3,2},{4,5},{5,4},{6,7},{7,6},{8,9},{9,8},{10,11... | collective-permute-start | bytes 1572872 | tf_op jit(solution)/shard_map/ppermute | solution.py:26
  21.1 11.7 %collective-permute-start.10 = (f32[72,512]{1,0:T(8,128)S(1)}, f32[72,512]{1,0:T(8,128)S(1)}, u32[]{:S(2)}, u32[]{:S(2)}) collective-permute-start(f32[72,512]{1,0:T(8,128)S(1)} %get-tuple-element.71), channel_id=1, source_target_pairs={{0,16},{16,32},{32,48},{48,0},{1,17},{17,33},{33,49},{49,1},{2,18}... | collective-permute-start | bytes 442376 | tf_op jit(solution)/shard_map/ppermute | solution.py:42
  22.7 10.1 %collective-permute-start.11 = (f32[72,512]{1,0:T(8,128)S(1)}, f32[72,512]{1,0:T(8,128)S(1)}, u32[]{:S(2)}, u32[]{:S(2)}) collective-permute-start(f32[72,512]{1,0:T(8,128)S(1)} %get-tuple-element.72), channel_id=1, source_target_pairs={{0,32},{16,48},{32,0},{48,16},{1,33},{17,49},{33,1},{49,17},{2,34}... | collective-permute-start | bytes 442376 | tf_op jit(solution)/shard_map/ppermute | solution.py:42
  25.6 7.2 %collective-permute-start.12 = (f32[72,512]{1,0:T(8,128)S(1)}, f32[72,512]{1,0:T(8,128)S(1)}, u32[]{:S(2)}, u32[]{:S(2)}) collective-permute-start(f32[72,512]{1,0:T(8,128)S(1)} %get-tuple-element.73), channel_id=1, source_target_pairs={{0,48},{16,0},{32,16},{48,32},{1,49},{17,1},{33,17},{49,33},{2,50}... | collective-permute-start | bytes 442376 | tf_op jit(solution)/shard_map/ppermute | solution.py:42
  26.3 12.0 %collective-permute-start.2 = (f32[72,512]{1,0:T(8,128)S(1)}, f32[72,512]{1,0:T(8,128)S(1)}, u32[]{:S(2)}, u32[]{:S(2)}) collective-permute-start(f32[72,512]{1,0:T(8,128)S(1)} %get-tuple-element.60), channel_id=1, source_target_pairs={{0,64},{64,128},{128,192},{192,0},{1,65},{65,129},{129,193},{193,1... | collective-permute-start | bytes 442376 | tf_op jit(solution)/shard_map/ppermute | solution.py:42
  28.5 11.8 %collective-permute-start.3 = (f32[72,512]{1,0:T(8,128)S(1)}, f32[72,512]{1,0:T(8,128)S(1)}, u32[]{:S(2)}, u32[]{:S(2)}) collective-permute-start(f32[72,512]{1,0:T(8,128)S(1)} %get-tuple-element.61), channel_id=1, source_target_pairs={{0,128},{64,192},{128,0},{192,64},{1,129},{65,193},{129,1},{193,65... | collective-permute-start | bytes 442376 | tf_op jit(solution)/shard_map/ppermute | solution.py:42
  32.7 7.6 %collective-permute-start.4 = (f32[72,512]{1,0:T(8,128)S(1)}, f32[72,512]{1,0:T(8,128)S(1)}, u32[]{:S(2)}, u32[]{:S(2)}) collective-permute-start(f32[72,512]{1,0:T(8,128)S(1)} %get-tuple-element.62), channel_id=1, source_target_pairs={{0,192},{64,0},{128,64},{192,128},{1,193},{65,1},{129,65},{193,129... | collective-permute-start | bytes 442376 | tf_op jit(solution)/shard_map/ppermute | solution.py:42
  32.9 10.5 %collective-permute-start.13 = (f32[24,512]{1,0:T(8,128)S(1)}, f32[24,512]{1,0:T(8,128)S(1)}, u32[]{:S(2)}, u32[]{:S(2)}) collective-permute-start(f32[24,512]{1,0:T(8,128)S(1)} %get-tuple-element.75), channel_id=1, source_target_pairs={{0,64},{64,128},{128,192},{192,0},{1,65},{65,129},{129,193},{193,1... | collective-permute-start | bytes 147464 | tf_op jit(solution)/shard_map/ppermute | solution.py:42
  34.9 11.0 %collective-permute-start.14 = (f32[24,512]{1,0:T(8,128)S(1)}, f32[24,512]{1,0:T(8,128)S(1)}, u32[]{:S(2)}, u32[]{:S(2)}) collective-permute-start(f32[24,512]{1,0:T(8,128)S(1)} %get-tuple-element.76), channel_id=1, source_target_pairs={{0,128},{64,192},{128,0},{192,64},{1,129},{65,193},{129,1},{193,65... | collective-permute-start | bytes 147464 | tf_op jit(solution)/shard_map/ppermute | solution.py:42
  38.3 7.7 %collective-permute-start.15 = (f32[24,512]{1,0:T(8,128)S(1)}, f32[24,512]{1,0:T(8,128)S(1)}, u32[]{:S(2)}, u32[]{:S(2)}) collective-permute-start(f32[24,512]{1,0:T(8,128)S(1)} %get-tuple-element.77), channel_id=1, source_target_pairs={{0,192},{64,0},{128,64},{192,128},{1,193},{65,1},{129,65},{193,129... | collective-permute-start | bytes 147464 | tf_op jit(solution)/shard_map/ppermute | solution.py:42
  40.4 6.0 %collective-permute-start.5 = (f32[24,512]{1,0:T(8,128)S(1)}, f32[24,512]{1,0:T(8,128)S(1)}, u32[]{:S(2)}, u32[]{:S(2)}) collective-permute-start(f32[24,512]{1,0:T(8,128)S(1)} %get-tuple-element.64), channel_id=1, source_target_pairs={{0,16},{16,32},{32,48},{48,0},{1,17},{17,33},{33,49},{49,1},{2,18}... | collective-permute-start | bytes 147464 | tf_op jit(solution)/shard_map/ppermute | solution.py:42
  40.4 5.9 %collective-permute-start.6 = (f32[24,512]{1,0:T(8,128)S(1)}, f32[24,512]{1,0:T(8,128)S(1)}, u32[]{:S(2)}, u32[]{:S(2)}) collective-permute-start(f32[24,512]{1,0:T(8,128)S(1)} %get-tuple-element.65), channel_id=1, source_target_pairs={{0,32},{16,48},{32,0},{48,16},{1,33},{17,49},{33,1},{49,17},{2,34}... | collective-permute-start | bytes 147464 | tf_op jit(solution)/shard_map/ppermute | solution.py:42
  43.4 4.3 %collective-permute-start.7 = (f32[24,512]{1,0:T(8,128)S(1)}, f32[24,512]{1,0:T(8,128)S(1)}, u32[]{:S(2)}, u32[]{:S(2)}) collective-permute-start(f32[24,512]{1,0:T(8,128)S(1)} %get-tuple-element.66), channel_id=1, source_target_pairs={{0,48},{16,0},{32,16},{48,32},{1,49},{17,1},{33,17},{49,33},{2,50}... | collective-permute-start | bytes 147464 | tf_op jit(solution)/shard_map/ppermute | solution.py:42
  47.7 17.9 %collective-permute-start.16 = (f32[32,512]{1,0:T(8,128)S(1)}, f32[32,512]{1,0:T(8,128)S(1)}, u32[]{:S(2)}, u32[]{:S(2)}) collective-permute-start(f32[32,512]{1,0:T(8,128)S(1)} %get-tuple-element.80.refs_0_), channel_id=1, source_target_pairs={{0,16},{16,32},{32,48},{48,0},{1,17},{17,33},{33,49},{49,1},{2,18}... | collective-permute-start | bytes 196616 | tf_op jit(solution)/shard_map/ppermute | solution.py:49
  49.4 0.7 collective-permute-start.19
  50.1 19.8 %collective-permute-start.20 = (f32[40,512]{1,0:T(8,128)S(1)}, f32[40,512]{1,0:T(8,128)S(1)}, u32[]{:S(2)}, u32[]{:S(2)}) collective-permute-start(f32[40,512]{1,0:T(8,128)S(1)} %shard_map.91.refs_4_), channel_id=1, source_target_pairs={{0,64},{64,128},{128,192},{192,0},{1,65},{65,129},{129,193},{193,1... | collective-permute-start | bytes 245768 | tf_op jit(solution)/shard_map/ppermute | solution.py:49
  58.3 11.6 %collective-permute-start.21 = (f32[40,512]{1,0:T(8,128)S(1)}, f32[40,512]{1,0:T(8,128)S(1)}, u32[]{:S(2)}, u32[]{:S(2)}) collective-permute-start(f32[40,512]{1,0:T(8,128)S(1)} %shard_map.91.refs_4_), channel_id=1, source_target_pairs={{0,128},{64,192},{128,0},{192,64},{1,129},{65,193},{129,1},{193,65... | collective-permute-start | bytes 245768 | tf_op jit(solution)/shard_map/ppermute | solution.py:49
  61.3 8.6 %collective-permute-start.22 = (f32[40,512]{1,0:T(8,128)S(1)}, f32[40,512]{1,0:T(8,128)S(1)}, u32[]{:S(2)}, u32[]{:S(2)}) collective-permute-start(f32[40,512]{1,0:T(8,128)S(1)} %shard_map.91.refs_4_), channel_id=1, source_target_pairs={{0,192},{64,0},{128,64},{192,128},{1,193},{65,1},{129,65},{193,129... | collective-permute-start | bytes 245768 | tf_op jit(solution)/shard_map/ppermute | solution.py:49
  63.9 5.8 %collective-permute-start.17 = (f32[32,512]{1,0:T(8,128)S(1)}, f32[32,512]{1,0:T(8,128)S(1)}, u32[]{:S(2)}, u32[]{:S(2)}) collective-permute-start(f32[32,512]{1,0:T(8,128)S(1)} %get-tuple-element.80.refs_0_), channel_id=1, source_target_pairs={{0,32},{16,48},{32,0},{48,16},{1,33},{17,49},{33,1},{49,17},{2,34}... | collective-permute-start | bytes 196616 | tf_op jit(solution)/shard_map/ppermute | solution.py:49
  65.6 4.3 %collective-permute-start.18 = (f32[32,512]{1,0:T(8,128)S(1)}, f32[32,512]{1,0:T(8,128)S(1)}, u32[]{:S(2)}, u32[]{:S(2)}) collective-permute-start(f32[32,512]{1,0:T(8,128)S(1)} %get-tuple-element.80.refs_0_), channel_id=1, source_target_pairs={{0,48},{16,0},{32,16},{48,32},{1,49},{17,1},{33,17},{49,33},{2,50}... | collective-permute-start | bytes 196616 | tf_op jit(solution)/shard_map/ppermute | solution.py:49
  69.9 13.3 %collective-permute-start.23 = (f32[4,32,512]{2,1,0:T(8,128)S(1)}, f32[4,32,512]{2,1,0:T(8,128)S(1)}, u32[]{:S(2)}, u32[]{:S(2)}) collective-permute-start(f32[4,32,512]{2,1,0:T(8,128)S(1)} %get-tuple-element.82.rest_0_), channel_id=1, source_target_pairs={{0,64},{64,128},{128,192},{192,0},{1,65},{65,129},{129,193},{193,1... | collective-permute-start | bytes 786440 | tf_op jit(solution)/shard_map/ppermute | solution.py:49
  70.0 19.6 %collective-permute-start.26 = (f32[4,40,512]{2,1,0:T(8,128)S(1)}, f32[4,40,512]{2,1,0:T(8,128)S(1)}, u32[]{:S(2)}, u32[]{:S(2)}) collective-permute-start(f32[4,40,512]{2,1,0:T(8,128)S(1)} %get-tuple-element.83.rest_4_), channel_id=1, source_target_pairs={{0,16},{16,32},{32,48},{48,0},{1,17},{17,33},{33,49},{49,1},{2,18}... | collective-permute-start | bytes 983048 | tf_op jit(solution)/shard_map/ppermute | solution.py:49
  71.5 18.1 %collective-permute-start.27 = (f32[4,40,512]{2,1,0:T(8,128)S(1)}, f32[4,40,512]{2,1,0:T(8,128)S(1)}, u32[]{:S(2)}, u32[]{:S(2)}) collective-permute-start(f32[4,40,512]{2,1,0:T(8,128)S(1)} %get-tuple-element.83.rest_4_), channel_id=1, source_target_pairs={{0,32},{16,48},{32,0},{48,16},{1,33},{17,49},{33,1},{49,17},{2,34}... | collective-permute-start | bytes 983048 | tf_op jit(solution)/shard_map/ppermute | solution.py:49
  74.6 15.0 %collective-permute-start.28 = (f32[4,40,512]{2,1,0:T(8,128)S(1)}, f32[4,40,512]{2,1,0:T(8,128)S(1)}, u32[]{:S(2)}, u32[]{:S(2)}) collective-permute-start(f32[4,40,512]{2,1,0:T(8,128)S(1)} %get-tuple-element.83.rest_4_), channel_id=1, source_target_pairs={{0,48},{16,0},{32,16},{48,32},{1,49},{17,1},{33,17},{49,33},{2,50}... | collective-permute-start | bytes 983048 | tf_op jit(solution)/shard_map/ppermute | solution.py:49
  74.7 8.5 %collective-permute-start.24 = (f32[4,32,512]{2,1,0:T(8,128)S(1)}, f32[4,32,512]{2,1,0:T(8,128)S(1)}, u32[]{:S(2)}, u32[]{:S(2)}) collective-permute-start(f32[4,32,512]{2,1,0:T(8,128)S(1)} %get-tuple-element.82.rest_0_), channel_id=1, source_target_pairs={{0,128},{64,192},{128,0},{192,64},{1,129},{65,193},{129,1},{193,65... | collective-permute-start | bytes 786440 | tf_op jit(solution)/shard_map/ppermute | solution.py:49
  83.2 6.4 %collective-permute-start.25 = (f32[4,32,512]{2,1,0:T(8,128)S(1)}, f32[4,32,512]{2,1,0:T(8,128)S(1)}, u32[]{:S(2)}, u32[]{:S(2)}) collective-permute-start(f32[4,32,512]{2,1,0:T(8,128)S(1)} %get-tuple-element.82.rest_0_), channel_id=1, source_target_pairs={{0,192},{64,0},{128,64},{192,128},{1,193},{65,1},{129,65},{193,129... | collective-permute-start | bytes 786440 | tf_op jit(solution)/shard_map/ppermute | solution.py:49
  94.0 15.3 %collective-permute-start.29 = (f32[16,16,512]{2,1,0:T(8,128)S(1)}, f32[16,16,512]{2,1,0:T(8,128)S(1)}, u32[]{:S(2)}, u32[]{:S(2)}) collective-permute-start(f32[16,16,512]{2,1,0:T(8,128)S(1)} %get-tuple-element.85), channel_id=1, source_target_pairs={{1,2},{3,4},{5,6},{7,8},{9,10},{11,12},{13,14},{2,1},{4,3},{6,5},{... | collective-permute-start | bytes 1572872 | tf_op jit(solution)/shard_map/ppermute | solution.py:26
  96.0 13.4 %collective-permute-start.30 = (f32[16,16,512]{2,1,0:T(8,128)S(1)}, f32[16,16,512]{2,1,0:T(8,128)S(1)}, u32[]{:S(2)}, u32[]{:S(2)}) collective-permute-start(f32[16,16,512]{2,1,0:T(8,128)S(1)} %get-tuple-element.86), channel_id=1, source_target_pairs={{0,1},{1,0},{2,3},{3,2},{4,5},{5,4},{6,7},{7,6},{8,9},{9,8},{10,11... | collective-permute-start | bytes 1572872 | tf_op jit(solution)/shard_map/ppermute | solution.py:26
  103.3 19.6 %collective-permute-start.37 = (f32[16,16,512]{2,1,0:T(8,128)S(1)}, f32[16,16,512]{2,1,0:T(8,128)S(1)}, u32[]{:S(2)}, u32[]{:S(2)}) collective-permute-start(f32[16,16,512]{2,1,0:T(8,128)S(1)} %get-tuple-element.96), channel_id=1, source_target_pairs={{1,2},{3,4},{5,6},{7,8},{9,10},{11,12},{13,14},{2,1},{4,3},{6,5},{... | collective-permute-start | bytes 1572872 | tf_op jit(solution)/shard_map/ppermute | solution.py:26
  105.3 17.7 %collective-permute-start.38 = (f32[16,16,512]{2,1,0:T(8,128)S(1)}, f32[16,16,512]{2,1,0:T(8,128)S(1)}, u32[]{:S(2)}, u32[]{:S(2)}) collective-permute-start(f32[16,16,512]{2,1,0:T(8,128)S(1)} %get-tuple-element.97), channel_id=1, source_target_pairs={{0,1},{1,0},{2,3},{3,2},{4,5},{5,4},{6,7},{7,6},{8,9},{9,8},{10,11... | collective-permute-start | bytes 1572872 | tf_op jit(solution)/shard_map/ppermute | solution.py:26
  109.5 13.7 %collective-permute-start.31 = (f32[64,512]{1,0:T(8,128)S(1)}, f32[64,512]{1,0:T(8,128)S(1)}, u32[]{:S(2)}, u32[]{:S(2)}) collective-permute-start(f32[64,512]{1,0:T(8,128)S(1)} %get-tuple-element.88), channel_id=1, source_target_pairs={{0,64},{64,128},{128,192},{192,0},{1,65},{65,129},{129,193},{193,1... | collective-permute-start | bytes 393224 | tf_op jit(solution)/shard_map/ppermute | solution.py:42
  109.6 5.9 %collective-permute-start.39 = (f32[8,128]{1,0:T(8,128)S(1)}, f32[8,128]{1,0:T(8,128)S(1)}, u32[]{:S(2)}, u32[]{:S(2)}) collective-permute-start(f32[8,128]{1,0:T(8,128)S(1)} %get-tuple-element.98.refs_8_), channel_id=1, source_target_pairs={{0,0},{1,1},{2,2},{3,3},{4,4},{5,5},{6,6},{7,7},{8,8},{9,9},{10,10... | collective-permute-start | bytes 12296 | tf_op jit(solution)/shard_map/ppermute | solution.py:36
  110.5 15.9 %collective-permute-start.32 = (f32[64,512]{1,0:T(8,128)S(1)}, f32[64,512]{1,0:T(8,128)S(1)}, u32[]{:S(2)}, u32[]{:S(2)}) collective-permute-start(f32[64,512]{1,0:T(8,128)S(1)} %get-tuple-element.89), channel_id=1, source_target_pairs={{0,128},{64,192},{128,0},{192,64},{1,129},{65,193},{129,1},{193,65... | collective-permute-start | bytes 393224 | tf_op jit(solution)/shard_map/ppermute | solution.py:42
  115.5 11.4 %collective-permute-start.33 = (f32[64,512]{1,0:T(8,128)S(1)}, f32[64,512]{1,0:T(8,128)S(1)}, u32[]{:S(2)}, u32[]{:S(2)}) collective-permute-start(f32[64,512]{1,0:T(8,128)S(1)} %get-tuple-element.90), channel_id=1, source_target_pairs={{0,192},{64,0},{128,64},{192,128},{1,193},{65,1},{129,65},{193,129... | collective-permute-start | bytes 393224 | tf_op jit(solution)/shard_map/ppermute | solution.py:42
  123.0 10.6 %collective-permute-start.40 = (f32[72,512]{1,0:T(8,128)S(1)}, f32[72,512]{1,0:T(8,128)S(1)}, u32[]{:S(2)}, u32[]{:S(2)}) collective-permute-start(f32[72,512]{1,0:T(8,128)S(1)} %get-tuple-element.100), channel_id=1, source_target_pairs={{0,16},{16,32},{32,48},{48,0},{1,17},{17,33},{33,49},{49,1},{2,18}... | collective-permute-start | bytes 442376 | tf_op jit(solution)/shard_map/ppermute | solution.py:42
  123.1 10.6 %collective-permute-start.41 = (f32[72,512]{1,0:T(8,128)S(1)}, f32[72,512]{1,0:T(8,128)S(1)}, u32[]{:S(2)}, u32[]{:S(2)}) collective-permute-start(f32[72,512]{1,0:T(8,128)S(1)} %get-tuple-element.101), channel_id=1, source_target_pairs={{0,32},{16,48},{32,0},{48,16},{1,33},{17,49},{33,1},{49,17},{2,34}... | collective-permute-start | bytes 442376 | tf_op jit(solution)/shard_map/ppermute | solution.py:42
  123.2 10.5 %collective-permute-start.42 = (f32[72,512]{1,0:T(8,128)S(1)}, f32[72,512]{1,0:T(8,128)S(1)}, u32[]{:S(2)}, u32[]{:S(2)}) collective-permute-start(f32[72,512]{1,0:T(8,128)S(1)} %get-tuple-element.102), channel_id=1, source_target_pairs={{0,48},{16,0},{32,16},{48,32},{1,49},{17,1},{33,17},{49,33},{2,50}... | collective-permute-start | bytes 442376 | tf_op jit(solution)/shard_map/ppermute | solution.py:42
  126.9 8.7 %collective-permute-start.34 = (f32[16,512]{1,0:T(8,128)S(1)}, f32[16,512]{1,0:T(8,128)S(1)}, u32[]{:S(2)}, u32[]{:S(2)}) collective-permute-start(f32[16,512]{1,0:T(8,128)S(1)} %get-tuple-element.92), channel_id=1, source_target_pairs={{0,16},{16,32},{32,48},{48,0},{1,17},{17,33},{33,49},{49,1},{2,18}... | collective-permute-start | bytes 98312 | tf_op jit(solution)/shard_map/ppermute | solution.py:42
  127.3 11.4 %collective-permute-start.35 = (f32[16,512]{1,0:T(8,128)S(1)}, f32[16,512]{1,0:T(8,128)S(1)}, u32[]{:S(2)}, u32[]{:S(2)}) collective-permute-start(f32[16,512]{1,0:T(8,128)S(1)} %get-tuple-element.93), channel_id=1, source_target_pairs={{0,32},{16,48},{32,0},{48,16},{1,33},{17,49},{33,1},{49,17},{2,34}... | collective-permute-start | bytes 98312 | tf_op jit(solution)/shard_map/ppermute | solution.py:42
  133.7 5.1 %collective-permute-start.36 = (f32[16,512]{1,0:T(8,128)S(1)}, f32[16,512]{1,0:T(8,128)S(1)}, u32[]{:S(2)}, u32[]{:S(2)}) collective-permute-start(f32[16,512]{1,0:T(8,128)S(1)} %get-tuple-element.94), channel_id=1, source_target_pairs={{0,48},{16,0},{32,16},{48,32},{1,49},{17,1},{33,17},{49,33},{2,50}... | collective-permute-start | bytes 98312 | tf_op jit(solution)/shard_map/ppermute | solution.py:42
  133.7 5.9 %collective-permute-start.43 = (f32[24,512]{1,0:T(8,128)S(1)}, f32[24,512]{1,0:T(8,128)S(1)}, u32[]{:S(2)}, u32[]{:S(2)}) collective-permute-start(f32[24,512]{1,0:T(8,128)S(1)} %get-tuple-element.104), channel_id=1, source_target_pairs={{0,64},{64,128},{128,192},{192,0},{1,65},{65,129},{129,193},{193,1... | collective-permute-start | bytes 147464 | tf_op jit(solution)/shard_map/ppermute | solution.py:42
  133.8 5.8 %collective-permute-start.44 = (f32[24,512]{1,0:T(8,128)S(1)}, f32[24,512]{1,0:T(8,128)S(1)}, u32[]{:S(2)}, u32[]{:S(2)}) collective-permute-start(f32[24,512]{1,0:T(8,128)S(1)} %get-tuple-element.105), channel_id=1, source_target_pairs={{0,128},{64,192},{128,0},{192,64},{1,129},{65,193},{129,1},{193,65... | collective-permute-start | bytes 147464 | tf_op jit(solution)/shard_map/ppermute | solution.py:42
  135.6 4.9 %collective-permute-start.45 = (f32[24,512]{1,0:T(8,128)S(1)}, f32[24,512]{1,0:T(8,128)S(1)}, u32[]{:S(2)}, u32[]{:S(2)}) collective-permute-start(f32[24,512]{1,0:T(8,128)S(1)} %get-tuple-element.106), channel_id=1, source_target_pairs={{0,192},{64,0},{128,64},{192,128},{1,193},{65,1},{129,65},{193,129... | collective-permute-start | bytes 147464 | tf_op jit(solution)/shard_map/ppermute | solution.py:42

commit v8 on v6

--- a/solution.py
+++ b/solution.py
@@ -14,7 +14,8 @@
 EXTRA = 8
 HALVES = 2
 MIB = 1 << 20
-KERNEL_VMEM = 20 * MIB
+KERNEL_VMEM = 18 * MIB
+SMALL_VMEM = 8 * MIB
 F32 = jnp.float32
 
 
@@ -24,16 +25,6 @@
     downward = [(j, i) for i, j in upward]
     swap = [(i, i ^ 1) for i in range(count)]
     return lax.ppermute(crossing, SECTOR, upward + downward), lax.ppermute(local, SECTOR, swap)
-
-
-def rotated(x):
-    terms, sectors = lax.axis_size(TERM), lax.axis_size(SECTOR)
-    pairs = [
-        (t * sectors + (s + t) % sectors, t * sectors + s)
-        for t in range(terms)
-        for s in range(sectors)
-    ]
-    return lax.ppermute(x, (*TERM, *SECTOR), pairs)
 
 
 def exchanged_along(pieces, axis):
@@ -118,27 +109,35 @@
     accumulate(lax.axis_index(SECTOR), count, target, left, right, f_high, f_low, outs)
 
 
-def second_kernel(count, target, left, right, sums, field, gathered, *rest):
-    *outs, overlap, f_high, f_low = rest
+def coefficients(sums):
+    cross, norm_sq = sums[0:1, 0:1], sums[1:2, 0:1]
+    scaled_cross, scaled_norm = sums[2:3, 0:1], sums[3:4, 0:1]
+    rayleigh = cross / norm_sq
+    return rayleigh, (scaled_cross - rayleigh * scaled_norm) / norm_sq
+
+
+def corrected(coefs, vector, scaling, image):
+    rayleigh, share = coefs
+    return scaling * (image - rayleigh * vector) - share * vector
+
+
+def second_kernel(count, target, left, right, sums, field, scaling, image, *rest):
+    *outs, f_high, f_low = rest
     peers, slab, width = field.shape
 
     @pl.when(pl.program_id(0) == 0)
     def _():
-        rayleigh = sums[0:1, 0:1] / sums[1:2, 0:1]
-        weighted = jnp.zeros((slab, width), F32)
+        coefs = coefficients(sums)
         for peer in range(peers):
-            vector = field[peer]
-            raw = gathered[peer, slab:] * (gathered[peer, :slab] - rayleigh * vector)
-            f_high[peer], f_low[peer] = halves(raw)
-            weighted += vector * raw
-        overlap[...] = jnp.broadcast_to(jnp.sum(weighted, keepdims=True), overlap.shape)
+            value = corrected(coefs, field[peer], scaling[peer], image[peer])
+            f_high[peer], f_low[peer] = halves(value)
 
     flat = (peers * slab, width)
     f_high, f_low = f_high.reshape(flat), f_low.reshape(flat)
     accumulate(lax.axis_index(SECTOR), count, target, left, right, f_high, f_low, outs)
 
 
-def partial_image(body, counts, targets, left_stack, right_stack, fields, split, extra=(), scratch=None, streamed=False):
+def partial_image(body, counts, targets, left_stack, right_stack, fields, split, scratch=None, streamed=False):
     slots, width, _ = right_stack.shape
 
     def operand(i, count):
@@ -152,13 +151,16 @@
     block = (width, width)
     part = (split[0], split[1] // HALVES, width)
     parts = 3 * HALVES
-    field_spec = in_vmem
+    field_spec = out_spec = in_vmem
+    kind = jax.ShapeDtypeStruct
     if streamed:
         fields = [pltpu.with_memory_space_constraint(x, pltpu.HBM) for x in fields]
         field_spec = pl.BlockSpec(block, lambda i, *_: (0, 0), pipeline_mode=pl.Buffered(1))
+        kind = pltpu.HBM
+        out_spec = pl.BlockSpec(part, lambda i, *_: (0, 0, 0), pipeline_mode=pl.Buffered(1))
     return pl.pallas_call(
         body,
-        out_shape=[jax.ShapeDtypeStruct(x, F32) for x in (*[part] * parts, *extra)],
+        out_shape=[kind(part, F32)] * parts,
         grid_spec=pltpu.PrefetchScalarGridSpec(
             num_scalar_prefetch=1,
             grid=(slots,),
@@ -168,7 +170,7 @@
                 pl.BlockSpec((1, width, width), operand),
                 *[field_spec] * len(fields),
             ],
-            out_specs=[in_vmem] * (parts + len(extra)),
+            out_specs=[out_spec] * parts,
             scratch_shapes=[pltpu.VMEM(scratch or block, jnp.bfloat16)] * 2,
         ),
         compiler_params=pltpu.CompilerParams(
@@ -184,44 +186,43 @@
     return along * size + across if half == 0 else across * size + along
 
 
-def spread(half, pieces, kept, crossed, local, weight=None):
+def spread(half, pieces, kept, crossed, local, weights=()):
     peers, rows, width = kept.shape
     size = len(pieces)
     me = lax.axis_index(TERM[half])
-    weighted = jnp.zeros((rows, width), F32)
+    lines = slice(half * rows, (half + 1) * rows)
+    cross = scaled_cross = jnp.zeros((rows, width), F32)
     for k, piece in enumerate(pieces):
         for across in range(size):
             peer = place(half, lax.rem(me + k, size), across, size)
             total = kept[peer] + (crossed[peer] + local[peer])
             piece[across * rows : (across + 1) * rows] = total
-            if weight is not None:
-                weighted += weight[peer, half * rows : (half + 1) * rows] * total
-    return weighted
-
-
-def first_spread(half, kept, crossed, local, field, *rest):
+            if weights:
+                field, scaling = weights
+                weighted = field[peer, lines] * total
+                cross += weighted
+                scaled_cross += scaling[peer, lines] * weighted
+    return cross, scaled_cross
+
+
+def first_spread(half, kept, crossed, local, field, scaling, *rest):
     *pieces, tail = rest
     rows = kept.shape[1]
-    cross = spread(half, pieces, kept, crossed, local, field)
-    own = field[lax.axis_index(TERM), half * rows : (half + 1) * rows]
+    cross, scaled_cross = spread(half, pieces, kept, crossed, local, (field, scaling))
+    me, lines = lax.axis_index(TERM), slice(half * rows, (half + 1) * rows)
+    own = field[me, lines]
+    square = own * own
     line = lax.broadcasted_iota(jnp.int32, tail.shape, 0)
-    tail[...] = jnp.where(
-        line == 0, jnp.sum(cross, keepdims=True), jnp.sum(own * own, keepdims=True)
-    )
+    tile = jnp.zeros(tail.shape, F32)
+    for i, part in enumerate((cross, square, scaled_cross, scaling[me, lines] * square)):
+        tile = jnp.where(line == i, jnp.sum(part, keepdims=True), tile)
+    tail[...] = tile
     for piece in pieces:
         piece[len(pieces) * rows :] = tail[...]
 
 
-def second_spread(half, kept, crossed, local, *rest):
-    if half == 0:
-        spread(half, rest, kept, crossed, local)
-        return
-    tail, *pieces = rest
+def second_spread(half, kept, crossed, local, *pieces):
     spread(half, pieces, kept, crossed, local)
-    lanes = tail.shape[1]
-    for piece in pieces:
-        for start in range(0, piece.shape[1], lanes):
-            piece[len(pieces) * kept.shape[1] :, start : start + lanes] = tail[...]
 
 
 def relay(axis, rows, *refs):
@@ -239,38 +240,35 @@
             piece[rows:] = summed(pl.ds(size * rows, piece.shape[0] - rows))
 
 
-def landed(refs, rows):
+def landed(refs):
     size = len(refs) // HALVES
     groups = [refs[h * size : (h + 1) * size] for h in range(HALVES)]
-    totals = [functools.reduce(lambda x, y: x + y, [r[...] for r in g]) for g in groups]
-    tails = [t[rows:] for t in totals if t.shape[0] > rows]
-    return [t[:rows] for t in totals], functools.reduce(lambda x, y: x + y, tails)
+    return [functools.reduce(lambda x, y: x + y, [r[...] for r in g]) for g in groups]
 
 
 def first_landing(*refs):
-    *arrived, scaling, image, copies, sums = refs
-    peers, slab = copies.shape[0], image.shape[0]
-    rows = slab // HALVES
-    parts, tail = landed(arrived, rows)
-    for half, part in enumerate(parts):
-        image[half * rows : (half + 1) * rows] = part
-    for peer in range(peers):
-        copies[peer, :slab] = image[...]
-        copies[peer, slab:] = scaling[...]
-    sums[...] = tail[:, : sums.shape[1]]
+    *arrived, image, copies, sums = refs
+    rows = image.shape[0] // HALVES
+    totals = landed(arrived)
+    for half, total in enumerate(totals):
+        image[half * rows : (half + 1) * rows] = total[:rows]
+    for peer in range(copies.shape[0]):
+        copies[peer] = image[...]
+    sums[...] = functools.reduce(lambda x, y: x + y, totals)[rows:, : sums.shape[1]]
 
 
 def second_landing(*refs):
     *arrived, sums, first_image, scaling, own, correction, image = refs
     rows = image.shape[0] // HALVES
-    parts, tail = landed(arrived, rows)
-    rayleigh = sums[0:1, 0:1] / sums[1:2, 0:1]
-    share = tail[0:1, 0:1] / sums[1:2, 0:1]
-    vector = own[...]
-    correction[...] = scaling[...] * (first_image[...] - rayleigh * vector) - share * vector
-    for half, part in enumerate(parts):
-        lines = slice(half * rows, (half + 1) * rows)
-        image[lines] = part - share * first_image[lines]
+    coefs = coefficients(sums)
+    correction[...] = corrected(coefs, own[...], scaling[...], first_image[...])
+    for half, total in enumerate(landed(arrived)):
+        image[half * rows : (half + 1) * rows] = total
+
+
+def repeated(x, copies):
+    for peer in range(copies.shape[0]):
+        copies[peer] = x[...]
 
 
 def relayed(half, pieces, rows):
@@ -297,7 +295,7 @@
             for s, space in zip(out_shapes, spaces)
         ],
         scratch_shapes=scratch,
-        compiler_params=pltpu.CompilerParams(vmem_limit_bytes=32 * MIB),
+        compiler_params=pltpu.CompilerParams(vmem_limit_bytes=SMALL_VMEM),
     )(*args)
 
 
@@ -324,37 +322,35 @@
         crossing, kept, local = (parts[i * HALVES : (i + 1) * HALVES] for i in range(3))
         return [(k, *moved(c, l)) for c, k, l in zip(crossing, kept, local)]
 
-    parts = moved_parts(image_of(first_kernel, fields=(field,), streamed=True))
+    (copies,) = small_call(repeated, [split], [scaling], spaces=[pltpu.HBM])
+    full_scaling = swapped(copies)
+    parts = image_of(first_kernel, fields=(field,), streamed=True)
+    parts, full_scaling = lax.optimization_barrier((parts, full_scaling))
+    parts = moved_parts(parts)
     arrived = []
     for half in range(HALVES):
         pieces = small_call(
             functools.partial(first_spread, half),
             [(size * rows + EXTRA, width)] * size,
-            [*parts[half], blocked],
+            [*parts[half], blocked, full_scaling],
             [pltpu.VMEM((EXTRA, width), F32)],
         )
         arrived += relayed(half, pieces, rows)
     first_image, copies, sums = small_call(
         first_landing,
-        [(slab, width), (peers, 2 * slab, width), (EXTRA, LANES)],
-        [*arrived, scaling],
+        [(slab, width), split, (EXTRA, LANES)],
+        arrived,
         spaces=[pltpu.VMEM, pltpu.HBM, pltpu.VMEM],
     )
-    gathered = swapped(copies)
+    full_image = swapped(copies)
     sums = over_sectors(sums)
 
-    *parts, overlap = image_of(
-        second_kernel, fields=(sums, blocked, gathered), extra=[(EXTRA, LANES)], scratch=split
-    )
-    parts = moved_parts(parts)
-    overlap = rotated(overlap)
+    fields = (sums, blocked, full_scaling, full_image)
+    parts = moved_parts(image_of(second_kernel, fields=fields, scratch=split))
     arrived = []
     for half in range(HALVES):
-        tail = [overlap] if half else []
         pieces = small_call(
-            functools.partial(second_spread, half),
-            [(size * rows + EXTRA * half, width)] * size,
-            [*parts[half], *tail],
+            functools.partial(second_spread, half), [(size * rows, width)] * size, parts[half]
         )
         arrived += relayed(half, pieces, rows)
     own = lax.dynamic_index_in_dim(blocked, lax.axis_index(TERM), 0, keepdims=False)

time: 136 us -> 136 us (level); the launches traced: 136 us -> 134 us
  starting transfers between devices: 90.6 us -> 77 us
  waiting for transfers between devices: 31.8 us -> 38.8 us
  local copies, waits for them, and re-layouts: 0.02 us -> 2.94 us
  Pallas kernels: 11.9 us -> 14.1 us
    ppermute x24, starting transfers between devices: 51.7 us -> 37.9 us  [exchanged_along(): sent = [lax.ppermute(pieces[k], axis, routes[k]) for k in range(1, size)]]
    all_to_all x1 -> x2, starting transfers between devices: 6.79 us -> 13.3 us  [swapped(): return lax.all_to_all(x, TERM, 0, 0, tiled=True)]
    ppermute x4, starting transfers between devices: 12.6 us -> 7.31 us  [moved(): lax.ppermute(local, SECTOR, swap)]
    ppermute x24, waiting for transfers between devices: 7.46 us -> 11.9 us  [exchanged_along(): sent = [lax.ppermute(pieces[k], axis, routes[k]) for k in range(1, size)]]
    ppermute x4, waiting for transfers between devices: 2.26 us -> 5.42 us  [moved(): lax.ppermute(crossing, SECTOR, upward + downward)]
    unnamed x6 -> x12, local copies, waits for them, and re-layouts: 0.02 us -> 2.94 us
    ppermute x4, starting transfers between devices: 13.1 us -> 11.5 us  [moved(): lax.ppermute(crossing, SECTOR, upward + downward)]
    pallas_call x2, Pallas kernels: 8.82 us -> 10.3 us  [partial_image(): pl.pallas_call(body, out_shape=[kind(part, F32)] * parts, grid_spec=pltpu...]
  transfers between devices with their start and end apart: 38 -> 38, of which waited for: 14 -> 16; matrix products, arithmetic and copies ran while one was open for 0% -> 0% of each run, Pallas kernels for 1% -> 5%
where the time goes in v8:
time: 136 us; the launch traced here: 134 us
  starting transfers between devices  77 us (57%)
  waiting for transfers between devices  38.8 us (29%)
  Pallas kernels  14.1 us (10%)
  local copies, waits for them, and re-layouts  2.94 us (2%)
  between operations  1.52 us (1%)
    ppermute x24, starting transfers between devices, exchanged_along(): sent = [lax.ppermute(pieces[k], axis, routes[k]) for k in range(1, size)]  37.9 us
    all_to_all x2, starting transfers between devices, swapped(): return lax.all_to_all(x, TERM, 0, 0, tiled=True)  13.3 us
    ppermute x24, waiting for transfers between devices, exchanged_along(): sent = [lax.ppermute(pieces[k], axis, routes[k]) for k in range(1, size)]  11.9 us
    ppermute x4, starting transfers between devices, moved(): lax.ppermute(crossing, SECTOR, upward + downward)  11.5 us
    all_to_all x2, waiting for transfers between devices, swapped(): return lax.all_to_all(x, TERM, 0, 0, tiled=True)  10.9 us
    ppermute x4, waiting for transfers between devices, exchanged(): return x + lax.ppermute(x, axis, pairs)  10.5 us
    pallas_call x2, Pallas kernels, partial_image(): pl.pallas_call(body, out_shape=[kind(part, F32)] * parts, grid_spec=pltpu...  10.3 us
    ppermute x4, starting transfers between devices, moved(): lax.ppermute(local, SECTOR, swap)  7.31 us
  transfers between devices with their start and end apart: 38, of which 16 were waited for; matrix products, arithmetic and copies ran while one was open for 0% of the time, Pallas kernels for 5%

profile of v8, /device:TPU:64, one launch (start us, length us, event | category | flops | bytes accessed | tf_op | source)
XLA Modules:
  0.0 134.3 jit_solution(3372905480350488885)
XLA Ops:
  0.6 0.8 copy-done.3
  1.5 1.1 shard_map.86
  2.6 7.0 %all-to-all-start = ((f32[16,32,512]{2,1,0:T(8,128)}), f32[16,32,512]{2,1,0:T(8,128)S(1)}, u32[]{:S(2)}, u32[]{:S(2)}) async-start(f32[16,32,512]{2,1,0:T(8,128)} %shard_map.86), calls=%async_computation | async-start | bytes 2097152 | tf_op jit(solution)/shard_map/all_to_all | solution.py:38
  10.3 6.1 %shard_map.85 = (f32[16,16,512]{2,1,0:T(8,128)}, f32[16,16,512]{2,1,0:T(8,128)}, f32[16,16,512]{2,1,0:T(8,128)}, f32[16,16,512]{2,1,0:T(8,128)}, f32[16,16,512]{2,1,0:T(8,128)}, /*index=5*/f32[16,16,512]{2,1,0:T(8,128)}) custom-call(s32[1,1]{1,0:T(1,128)S(6)} %copy.9.count, s32[1,4]{1,0:T(1,128)} %target.3, f32[4,512,512]{2,1,0:T(8,128)} %bitcast.18, ...), custom_call_target="tpu_custom_call" | custom-call | flops 6442450944 | bytes 8388608 | tf_op jit(solution)/shard_map/pallas_call | solution.py:161
  16.4 10.9 %all-to-all-done.scaling = f32[16,32,512]{2,1,0:T(8,128)S(1)} async-done(((f32[16,32,512]{2,1,0:T(8,128)}), f32[16,32,512]{2,1,0:T(8,128)S(1)}, u32[]{:S(2)}, u32[]{:S(2)}) %all-to-all-start) | async-done | bytes 1048608 | tf_op jit(solution)/shard_map/all_to_all | solution.py:38
  27.3 1.9 %collective-permute-start = (f32[16,16,512]{2,1,0:T(8,128)}, f32[16,16,512]{2,1,0:T(8,128)S(1)}, u32[]{:S(2)}, u32[]{:S(2)}) collective-permute-start(f32[16,16,512]{2,1,0:T(8,128)} %get-tuple-element.66), channel_id=1, source_target_pairs={{1,2},{3,4},{5,6},{7,8},{9,10},{11,12},{13,14},{2,1},{4,3},{6,5},{... | collective-permute-start | bytes 1572872 | tf_op jit(solution)/shard_map/ppermute | solution.py:27
  29.2 2.1 %collective-permute-start.1 = (f32[16,16,512]{2,1,0:T(8,128)}, f32[16,16,512]{2,1,0:T(8,128)S(1)}, u32[]{:S(2)}, u32[]{:S(2)}) collective-permute-start(f32[16,16,512]{2,1,0:T(8,128)} %get-tuple-element.67), channel_id=1, source_target_pairs={{0,1},{1,0},{2,3},{3,2},{4,5},{5,4},{6,7},{7,6},{8,9},{9,8},{10,11... | collective-permute-start | bytes 1572872 | tf_op jit(solution)/shard_map/ppermute | solution.py:27
  31.3 1.9 %collective-permute-start.8 = (f32[16,16,512]{2,1,0:T(8,128)}, f32[16,16,512]{2,1,0:T(8,128)S(1)}, u32[]{:S(2)}, u32[]{:S(2)}) collective-permute-start(f32[16,16,512]{2,1,0:T(8,128)} %get-tuple-element.78), channel_id=1, source_target_pairs={{1,2},{3,4},{5,6},{7,8},{9,10},{11,12},{13,14},{2,1},{4,3},{6,5},{... | collective-permute-start | bytes 1572872 | tf_op jit(solution)/shard_map/ppermute | solution.py:27
  33.2 3.3 %collective-permute-start.9 = (f32[16,16,512]{2,1,0:T(8,128)}, f32[16,16,512]{2,1,0:T(8,128)S(1)}, u32[]{:S(2)}, u32[]{:S(2)}) collective-permute-start(f32[16,16,512]{2,1,0:T(8,128)} %get-tuple-element.79), channel_id=1, source_target_pairs={{0,1},{1,0},{2,3},{3,2},{4,5},{5,4},{6,7},{7,6},{8,9},{9,8},{10,11... | collective-permute-start | bytes 1572872 | tf_op jit(solution)/shard_map/ppermute | solution.py:27
  36.6 1.4 %collective-permute-done.crossed = f32[16,16,512]{2,1,0:T(8,128)S(1)} collective-permute-done((f32[16,16,512]{2,1,0:T(8,128)}, f32[16,16,512]{2,1,0:T(8,128)S(1)}, u32[]{:S(2)}, u32[]{:S(2)}) %collective-permute-start) | collective-permute-done | bytes 524320 | tf_op jit(solution)/shard_map/ppermute | solution.py:27
  38.0 1.0 copy-done.2
  39.0 0.3 shard_map.87
  39.3 0.1 collective-permute-start.2
  39.4 2.1 %collective-permute-start.3 = (f32[72,512]{1,0:T(8,128)S(1)}, f32[72,512]{1,0:T(8,128)S(1)}, u32[]{:S(2)}, u32[]{:S(2)}) collective-permute-start(f32[72,512]{1,0:T(8,128)S(1)} %get-tuple-element.71), channel_id=1, source_target_pairs={{0,128},{64,192},{128,0},{192,64},{1,129},{65,193},{129,1},{193,65... | collective-permute-start | bytes 442376 | tf_op jit(solution)/shard_map/ppermute | solution.py:33
  41.5 1.1 collective-permute-start.4
  42.7 0.9 collective-permute-done.8.crossed
  43.6 1.0 copy-done.1
  44.7 0.3 shard_map.89
  44.9 0.6 collective-permute-start.10
  45.6 1.2 collective-permute-start.11
  46.8 3.4 %collective-permute-done.2.refs_1_ = f32[72,512]{1,0:T(8,128)S(1)} collective-permute-done((f32[72,512]{1,0:T(8,128)S(1)}, f32[72,512]{1,0:T(8,128)S(1)}, u32[]{:S(2)}, u32[]{:S(2)}) %collective-permute-start.2) | collective-permute-done | bytes 147488 | tf_op jit(solution)/shard_map/ppermute | solution.py:33
  50.1 0.2 collective-permute-start.12
  50.3 0.5 collective-permute-done.4.refs_3_
  50.8 1.5 %collective-permute-start.5 = (f32[24,512]{1,0:T(8,128)S(1)}, f32[24,512]{1,0:T(8,128)S(1)}, u32[]{:S(2)}, u32[]{:S(2)}) collective-permute-start(f32[24,512]{1,0:T(8,128)S(1)} %get-tuple-element.74), channel_id=1, source_target_pairs={{0,16},{16,32},{32,48},{48,0},{1,17},{17,33},{33,49},{49,1},{2,18}... | collective-permute-start | bytes 147464 | tf_op jit(solution)/shard_map/ppermute | solution.py:33
  52.3 0.8 collective-permute-start.6
  53.0 3.5 %collective-permute-done.10.refs_1_ = f32[72,512]{1,0:T(8,128)S(1)} collective-permute-done((f32[72,512]{1,0:T(8,128)S(1)}, f32[72,512]{1,0:T(8,128)S(1)}, u32[]{:S(2)}, u32[]{:S(2)}) %collective-permute-start.10) | collective-permute-done | bytes 147488 | tf_op jit(solution)/shard_map/ppermute | solution.py:33
  56.5 0.0 collective-permute-done.12.refs_3_
  56.6 0.1 collective-permute-start.13
  56.7 2.0 %collective-permute-start.14 = (f32[24,512]{1,0:T(8,128)S(1)}, f32[24,512]{1,0:T(8,128)S(1)}, u32[]{:S(2)}, u32[]{:S(2)}) collective-permute-start(f32[24,512]{1,0:T(8,128)S(1)} %get-tuple-element.86), channel_id=1, source_target_pairs={{0,128},{64,192},{128,0},{192,64},{1,129},{65,193},{129,1},{193,65... | collective-permute-start | bytes 147464 | tf_op jit(solution)/shard_map/ppermute | solution.py:33
  58.7 2.5 %collective-permute-start.15 = (f32[24,512]{1,0:T(8,128)S(1)}, f32[24,512]{1,0:T(8,128)S(1)}, u32[]{:S(2)}, u32[]{:S(2)}) collective-permute-start(f32[24,512]{1,0:T(8,128)S(1)} %get-tuple-element.87), channel_id=1, source_target_pairs={{0,192},{64,0},{128,64},{192,128},{1,193},{65,1},{129,65},{193,129... | collective-permute-start | bytes 147464 | tf_op jit(solution)/shard_map/ppermute | solution.py:33
  61.2 1.2 collective-permute-done.13.refs_5_
  62.5 0.9 collective-permute-done.15.refs_7_
  63.4 1.1 shard_map.91
  64.5 6.3 %all-to-all-start.1 = ((f32[16,32,512]{2,1,0:T(8,128)}), f32[16,32,512]{2,1,0:T(8,128)S(1)}, u32[]{:S(2)}, u32[]{:S(2)}) async-start(f32[16,32,512]{2,1,0:T(8,128)} %get-tuple-element.90), calls=%async_computation.1 | async-start | bytes 2097152 | tf_op jit(solution)/shard_map/all_to_all | solution.py:38
  70.7 0.1 collective-permute-start.16
  70.8 1.2 collective-permute-done.16
  72.0 2.7 %collective-permute-start.17 = (f32[8,128]{1,0:T(8,128)S(1)}, f32[8,128]{1,0:T(8,128)S(1)}, u32[]{:S(2)}, u32[]{:S(2)}) collective-permute-start(f32[8,128]{1,0:T(8,128)S(1)} %add.19), channel_id=1, source_target_pairs={{0,2},{2,0},{4,6},{6,4},{8,10},{10,8},{12,14},{14,12},{1,3},{3,1},... | collective-permute-start | bytes 12296 | tf_op jit(solution)/shard_map/ppermute | solution.py:52
  74.7 1.6 %collective-permute-done.17 = f32[8,128]{1,0:T(8,128)S(1)} collective-permute-done((f32[8,128]{1,0:T(8,128)S(1)}, f32[8,128]{1,0:T(8,128)S(1)}, u32[]{:S(2)}, u32[]{:S(2)}) %collective-permute-start.17) | collective-permute-done | bytes 4128 | tf_op jit(solution)/shard_map/ppermute | solution.py:52
  76.3 4.5 %collective-permute-done.18 = f32[8,128]{1,0:T(8,128)S(1)} collective-permute-done((f32[8,128]{1,0:T(8,128)S(1)}, f32[8,128]{1,0:T(8,128)S(1)}, u32[]{:S(2)}, u32[]{:S(2)}) %collective-permute-start.18) | collective-permute-done | bytes 4128 | tf_op jit(solution)/shard_map/ppermute | solution.py:52
  80.8 4.2 %collective-permute-start.19 = (f32[8,128]{1,0:T(8,128)S(1)}, f32[8,128]{1,0:T(8,128)S(1)}, u32[]{:S(2)}, u32[]{:S(2)}) collective-permute-start(f32[8,128]{1,0:T(8,128)S(1)} %add.21), channel_id=1, source_target_pairs={{0,8},{2,10},{4,12},{6,14},{8,0},{10,2},{12,4},{14,6},{1,9},{3,11}... | collective-permute-start | bytes 12296 | tf_op jit(solution)/shard_map/ppermute | solution.py:52
  85.0 3.3 %collective-permute-done.19 = f32[8,128]{1,0:T(8,128)S(1)} collective-permute-done((f32[8,128]{1,0:T(8,128)S(1)}, f32[8,128]{1,0:T(8,128)S(1)}, u32[]{:S(2)}, u32[]{:S(2)}) %collective-permute-start.19) | collective-permute-done | bytes 4128 | tf_op jit(solution)/shard_map/ppermute | solution.py:52
  88.3 4.2 %shard_map.92 = (f32[16,16,512]{2,1,0:T(8,128)S(1)}, f32[16,16,512]{2,1,0:T(8,128)S(1)}, f32[16,16,512]{2,1,0:T(8,128)S(1)}, f32[16,16,512]{2,1,0:T(8,128)S(1)},...) custom-call(s32[1,1]{1,0:T(1,128)S(6)} %copy.9.count, s32[1,4]{1,0:T(1,128)} %target.3, f32[4,512,512]{2,1,0:T(8,128)} %bitcast.19, ...), custom_call_target="tpu_custom_call" | custom-call | flops 6442450944 | bytes 8388608 | tf_op jit(solution)/shard_map/pallas_call | solution.py:161
  92.6 5.7 %collective-permute-start.20 = (f32[16,16,512]{2,1,0:T(8,128)S(1)}, f32[16,16,512]{2,1,0:T(8,128)S(1)}, u32[]{:S(2)}, u32[]{:S(2)}) collective-permute-start(f32[16,16,512]{2,1,0:T(8,128)S(1)} %get-tuple-element.92), channel_id=1, source_target_pairs={{1,2},{3,4},{5,6},{7,8},{9,10},{11,12},{13,14},{2,1},{4,3},{6,5},{... | collective-permute-start | bytes 1572872 | tf_op jit(solution)/shard_map/ppermute | solution.py:27
  98.3 0.1 collective-permute-start.21
  98.4 1.9 %collective-permute-start.28 = (f32[16,16,512]{2,1,0:T(8,128)S(1)}, f32[16,16,512]{2,1,0:T(8,128)S(1)}, u32[]{:S(2)}, u32[]{:S(2)}) collective-permute-start(f32[16,16,512]{2,1,0:T(8,128)S(1)} %get-tuple-element.103), channel_id=1, source_target_pairs={{1,2},{3,4},{5,6},{7,8},{9,10},{11,12},{13,14},{2,1},{4,3},{6,5},{... | collective-permute-start | bytes 1572872 | tf_op jit(solution)/shard_map/ppermute | solution.py:27
  100.3 1.8 %collective-permute-start.29 = (f32[16,16,512]{2,1,0:T(8,128)S(1)}, f32[16,16,512]{2,1,0:T(8,128)S(1)}, u32[]{:S(2)}, u32[]{:S(2)}) collective-permute-start(f32[16,16,512]{2,1,0:T(8,128)S(1)} %get-tuple-element.104), channel_id=1, source_target_pairs={{0,1},{1,0},{2,3},{3,2},{4,5},{5,4},{6,7},{7,6},{8,9},{9,8},{10,11... | collective-permute-start | bytes 1572872 | tf_op jit(solution)/shard_map/ppermute | solution.py:27
  102.1 3.0 %collective-permute-done.20.crossed = f32[16,16,512]{2,1,0:T(8,128)S(1)} collective-permute-done((f32[16,16,512]{2,1,0:T(8,128)S(1)}, f32[16,16,512]{2,1,0:T(8,128)S(1)}, u32[]{:S(2)}, u32[]{:S(2)}) %collective-permute-start.20) | collective-permute-done | bytes 524320 | tf_op jit(solution)/shard_map/ppermute | solution.py:27
  105.2 0.1 shard_map.93
  105.2 0.1 collective-permute-start.22
  105.3 6.0 %collective-permute-start.23 = (f32[64,512]{1,0:T(8,128)S(1)}, f32[64,512]{1,0:T(8,128)S(1)}, u32[]{:S(2)}, u32[]{:S(2)}) collective-permute-start(f32[64,512]{1,0:T(8,128)S(1)} %get-tuple-element.96), channel_id=1, source_target_pairs={{0,128},{64,192},{128,0},{192,64},{1,129},{65,193},{129,1},{193,65... | collective-permute-start | bytes 393224 | tf_op jit(solution)/shard_map/ppermute | solution.py:33
  111.3 0.1 shard_map.95
  111.4 3.9 %collective-permute-start.30 = (f32[64,512]{1,0:T(8,128)S(1)}, f32[64,512]{1,0:T(8,128)S(1)}, u32[]{:S(2)}, u32[]{:S(2)}) collective-permute-start(f32[64,512]{1,0:T(8,128)S(1)} %get-tuple-element.106), channel_id=1, source_target_pairs={{0,16},{16,32},{32,48},{48,0},{1,17},{17,33},{33,49},{49,1},{2,18}... | collective-permute-start | bytes 393224 | tf_op jit(solution)/shard_map/ppermute | solution.py:33
  115.3 4.0 %collective-permute-start.31 = (f32[64,512]{1,0:T(8,128)S(1)}, f32[64,512]{1,0:T(8,128)S(1)}, u32[]{:S(2)}, u32[]{:S(2)}) collective-permute-start(f32[64,512]{1,0:T(8,128)S(1)} %get-tuple-element.107), channel_id=1, source_target_pairs={{0,32},{16,48},{32,0},{48,16},{1,33},{17,49},{33,1},{49,17},{2,34}... | collective-permute-start | bytes 393224 | tf_op jit(solution)/shard_map/ppermute | solution.py:33
  119.3 0.1 collective-permute-start.32
  119.5 2.0 %collective-permute-start.25 = (f32[16,512]{1,0:T(8,128)S(1)}, f32[16,512]{1,0:T(8,128)S(1)}, u32[]{:S(2)}, u32[]{:S(2)}) collective-permute-start(f32[16,512]{1,0:T(8,128)S(1)} %get-tuple-element.99), channel_id=1, source_target_pairs={{0,16},{16,32},{32,48},{48,0},{1,17},{17,33},{33,49},{49,1},{2,18}... | collective-permute-start | bytes 98312 | tf_op jit(solution)/shard_map/ppermute | solution.py:33
  121.5 2.3 %collective-permute-start.26 = (f32[16,512]{1,0:T(8,128)S(1)}, f32[16,512]{1,0:T(8,128)S(1)}, u32[]{:S(2)}, u32[]{:S(2)}) collective-permute-start(f32[16,512]{1,0:T(8,128)S(1)} %get-tuple-element.100), channel_id=1, source_target_pairs={{0,32},{16,48},{32,0},{48,16},{1,33},{17,49},{33,1},{49,17},{2,34}... | collective-permute-start | bytes 98312 | tf_op jit(solution)/shard_map/ppermute | solution.py:33
  123.8 1.5 %collective-permute-start.27 = (f32[16,512]{1,0:T(8,128)S(1)}, f32[16,512]{1,0:T(8,128)S(1)}, u32[]{:S(2)}, u32[]{:S(2)}) collective-permute-start(f32[16,512]{1,0:T(8,128)S(1)} %get-tuple-element.101), channel_id=1, source_target_pairs={{0,48},{16,0},{32,16},{48,32},{1,49},{17,1},{33,17},{49,33},{2,50}... | collective-permute-start | bytes 98312 | tf_op jit(solution)/shard_map/ppermute | solution.py:33
  125.3 0.9 collective-permute-done.31.refs_2_
  126.2 0.6 collective-permute-start.33
  126.8 2.7 %collective-permute-start.34 = (f32[16,512]{1,0:T(8,128)S(1)}, f32[16,512]{1,0:T(8,128)S(1)}, u32[]{:S(2)}, u32[]{:S(2)}) collective-permute-start(f32[16,512]{1,0:T(8,128)S(1)} %get-tuple-element.111), channel_id=1, source_target_pairs={{0,128},{64,192},{128,0},{192,64},{1,129},{65,193},{129,1},{193,65... | collective-permute-start | bytes 98312 | tf_op jit(solution)/shard_map/ppermute | solution.py:33
  129.5 2.5 %collective-permute-start.35 = (f32[16,512]{1,0:T(8,128)S(1)}, f32[16,512]{1,0:T(8,128)S(1)}, u32[]{:S(2)}, u32[]{:S(2)}) collective-permute-start(f32[16,512]{1,0:T(8,128)S(1)} %get-tuple-element.112), channel_id=1, source_target_pairs={{0,192},{64,0},{128,64},{192,128},{1,193},{65,1},{129,65},{193,129... | collective-permute-start | bytes 98312 | tf_op jit(solution)/shard_map/ppermute | solution.py:33
  132.1 0.2 collective-permute-done.34.refs_6_
  132.2 1.4 %collective-permute-done.35.refs_7_ = f32[16,512]{1,0:T(8,128)S(1)} collective-permute-done((f32[16,512]{1,0:T(8,128)S(1)}, f32[16,512]{1,0:T(8,128)S(1)}, u32[]{:S(2)}, u32[]{:S(2)}) %collective-permute-start.35) | collective-permute-done | bytes 32800 | tf_op jit(solution)/shard_map/ppermute | solution.py:33
  133.6 0.7 shard_map.97
  (42 shorter events, 0.2 us)
Async XLA Ops:
  0.6 0.8 copy-start.3
  2.6 24.7 %all-to-all-start = ((f32[16,32,512]{2,1,0:T(8,128)}), f32[16,32,512]{2,1,0:T(8,128)S(1)}, u32[]{:S(2)}, u32[]{:S(2)}) async-start(f32[16,32,512]{2,1,0:T(8,128)} %shard_map.86), calls=%async_computation | async-start | bytes 2097152 | tf_op jit(solution)/shard_map/all_to_all | solution.py:38
  10.2 27.8 %copy-start = (f32[1,512,512]{2,1,0:T(8,128)S(1)}, f32[1,512,512]{2,1,0:T(8,128)}, u32[]{:S(2)}) copy-start(f32[1,512,512]{2,1,0:T(8,128)} %param.6) | copy-start | bytes 3145732
  27.3 10.7 %collective-permute-start = (f32[16,16,512]{2,1,0:T(8,128)}, f32[16,16,512]{2,1,0:T(8,128)S(1)}, u32[]{:S(2)}, u32[]{:S(2)}) collective-permute-start(f32[16,16,512]{2,1,0:T(8,128)} %get-tuple-element.66), channel_id=1, source_target_pairs={{1,2},{3,4},{5,6},{7,8},{9,10},{11,12},{13,14},{2,1},{4,3},{6,5},{... | collective-permute-start | bytes 1572872 | tf_op jit(solution)/shard_map/ppermute | solution.py:27
  29.2 8.8 %collective-permute-start.1 = (f32[16,16,512]{2,1,0:T(8,128)}, f32[16,16,512]{2,1,0:T(8,128)S(1)}, u32[]{:S(2)}, u32[]{:S(2)}) collective-permute-start(f32[16,16,512]{2,1,0:T(8,128)} %get-tuple-element.67), channel_id=1, source_target_pairs={{0,1},{1,0},{2,3},{3,2},{4,5},{5,4},{6,7},{7,6},{8,9},{9,8},{10,11... | collective-permute-start | bytes 1572872 | tf_op jit(solution)/shard_map/ppermute | solution.py:27
  31.3 12.3 %collective-permute-start.8 = (f32[16,16,512]{2,1,0:T(8,128)}, f32[16,16,512]{2,1,0:T(8,128)S(1)}, u32[]{:S(2)}, u32[]{:S(2)}) collective-permute-start(f32[16,16,512]{2,1,0:T(8,128)} %get-tuple-element.78), channel_id=1, source_target_pairs={{1,2},{3,4},{5,6},{7,8},{9,10},{11,12},{13,14},{2,1},{4,3},{6,5},{... | collective-permute-start | bytes 1572872 | tf_op jit(solution)/shard_map/ppermute | solution.py:27
  33.2 10.4 %collective-permute-start.9 = (f32[16,16,512]{2,1,0:T(8,128)}, f32[16,16,512]{2,1,0:T(8,128)S(1)}, u32[]{:S(2)}, u32[]{:S(2)}) collective-permute-start(f32[16,16,512]{2,1,0:T(8,128)} %get-tuple-element.79), channel_id=1, source_target_pairs={{0,1},{1,0},{2,3},{3,2},{4,5},{5,4},{6,7},{7,6},{8,9},{9,8},{10,11... | collective-permute-start | bytes 1572872 | tf_op jit(solution)/shard_map/ppermute | solution.py:27
  38.0 1.0 copy-start.2
  39.3 10.8 %collective-permute-start.2 = (f32[72,512]{1,0:T(8,128)S(1)}, f32[72,512]{1,0:T(8,128)S(1)}, u32[]{:S(2)}, u32[]{:S(2)}) collective-permute-start(f32[72,512]{1,0:T(8,128)S(1)} %get-tuple-element.70), channel_id=1, source_target_pairs={{0,64},{64,128},{128,192},{192,0},{1,65},{65,129},{129,193},{193,1... | collective-permute-start | bytes 442376 | tf_op jit(solution)/shard_map/ppermute | solution.py:33
  39.4 10.9 %collective-permute-start.3 = (f32[72,512]{1,0:T(8,128)S(1)}, f32[72,512]{1,0:T(8,128)S(1)}, u32[]{:S(2)}, u32[]{:S(2)}) collective-permute-start(f32[72,512]{1,0:T(8,128)S(1)} %get-tuple-element.71), channel_id=1, source_target_pairs={{0,128},{64,192},{128,0},{192,64},{1,129},{65,193},{129,1},{193,65... | collective-permute-start | bytes 442376 | tf_op jit(solution)/shard_map/ppermute | solution.py:33
  41.5 9.2 %collective-permute-start.4 = (f32[72,512]{1,0:T(8,128)S(1)}, f32[72,512]{1,0:T(8,128)S(1)}, u32[]{:S(2)}, u32[]{:S(2)}) collective-permute-start(f32[72,512]{1,0:T(8,128)S(1)} %get-tuple-element.72), channel_id=1, source_target_pairs={{0,192},{64,0},{128,64},{192,128},{1,193},{65,1},{129,65},{193,129... | collective-permute-start | bytes 442376 | tf_op jit(solution)/shard_map/ppermute | solution.py:33
  43.6 1.0 copy-start.1
  44.9 11.6 %collective-permute-start.10 = (f32[72,512]{1,0:T(8,128)S(1)}, f32[72,512]{1,0:T(8,128)S(1)}, u32[]{:S(2)}, u32[]{:S(2)}) collective-permute-start(f32[72,512]{1,0:T(8,128)S(1)} %get-tuple-element.81), channel_id=1, source_target_pairs={{0,16},{16,32},{32,48},{48,0},{1,17},{17,33},{33,49},{49,1},{2,18}... | collective-permute-start | bytes 442376 | tf_op jit(solution)/shard_map/ppermute | solution.py:33
  45.6 10.9 %collective-permute-start.11 = (f32[72,512]{1,0:T(8,128)S(1)}, f32[72,512]{1,0:T(8,128)S(1)}, u32[]{:S(2)}, u32[]{:S(2)}) collective-permute-start(f32[72,512]{1,0:T(8,128)S(1)} %get-tuple-element.82), channel_id=1, source_target_pairs={{0,32},{16,48},{32,0},{48,16},{1,33},{17,49},{33,1},{49,17},{2,34}... | collective-permute-start | bytes 442376 | tf_op jit(solution)/shard_map/ppermute | solution.py:33
  50.1 6.4 %collective-permute-start.12 = (f32[72,512]{1,0:T(8,128)S(1)}, f32[72,512]{1,0:T(8,128)S(1)}, u32[]{:S(2)}, u32[]{:S(2)}) collective-permute-start(f32[72,512]{1,0:T(8,128)S(1)} %get-tuple-element.83), channel_id=1, source_target_pairs={{0,48},{16,0},{32,16},{48,32},{1,49},{17,1},{33,17},{49,33},{2,50}... | collective-permute-start | bytes 442376 | tf_op jit(solution)/shard_map/ppermute | solution.py:33
  50.8 7.9 %collective-permute-start.5 = (f32[24,512]{1,0:T(8,128)S(1)}, f32[24,512]{1,0:T(8,128)S(1)}, u32[]{:S(2)}, u32[]{:S(2)}) collective-permute-start(f32[24,512]{1,0:T(8,128)S(1)} %get-tuple-element.74), channel_id=1, source_target_pairs={{0,16},{16,32},{32,48},{48,0},{1,17},{17,33},{33,49},{49,1},{2,18}... | collective-permute-start | bytes 147464 | tf_op jit(solution)/shard_map/ppermute | solution.py:33
  52.3 9.0 %collective-permute-start.6 = (f32[24,512]{1,0:T(8,128)S(1)}, f32[24,512]{1,0:T(8,128)S(1)}, u32[]{:S(2)}, u32[]{:S(2)}) collective-permute-start(f32[24,512]{1,0:T(8,128)S(1)} %get-tuple-element.75), channel_id=1, source_target_pairs={{0,32},{16,48},{32,0},{48,16},{1,33},{17,49},{33,1},{49,17},{2,34}... | collective-permute-start | bytes 147464 | tf_op jit(solution)/shard_map/ppermute | solution.py:33
  56.5 4.8 %collective-permute-start.7 = (f32[24,512]{1,0:T(8,128)S(1)}, f32[24,512]{1,0:T(8,128)S(1)}, u32[]{:S(2)}, u32[]{:S(2)}) collective-permute-start(f32[24,512]{1,0:T(8,128)S(1)} %get-tuple-element.76), channel_id=1, source_target_pairs={{0,48},{16,0},{32,16},{48,32},{1,49},{17,1},{33,17},{49,33},{2,50}... | collective-permute-start | bytes 147464 | tf_op jit(solution)/shard_map/ppermute | solution.py:33
  56.6 5.9 %collective-permute-start.13 = (f32[24,512]{1,0:T(8,128)S(1)}, f32[24,512]{1,0:T(8,128)S(1)}, u32[]{:S(2)}, u32[]{:S(2)}) collective-permute-start(f32[24,512]{1,0:T(8,128)S(1)} %get-tuple-element.85), channel_id=1, source_target_pairs={{0,64},{64,128},{128,192},{192,0},{1,65},{65,129},{129,193},{193,1... | collective-permute-start | bytes 147464 | tf_op jit(solution)/shard_map/ppermute | solution.py:33
  56.7 5.8 %collective-permute-start.14 = (f32[24,512]{1,0:T(8,128)S(1)}, f32[24,512]{1,0:T(8,128)S(1)}, u32[]{:S(2)}, u32[]{:S(2)}) collective-permute-start(f32[24,512]{1,0:T(8,128)S(1)} %get-tuple-element.86), channel_id=1, source_target_pairs={{0,128},{64,192},{128,0},{192,64},{1,129},{65,193},{129,1},{193,65... | collective-permute-start | bytes 147464 | tf_op jit(solution)/shard_map/ppermute | solution.py:33
  58.7 4.6 %collective-permute-start.15 = (f32[24,512]{1,0:T(8,128)S(1)}, f32[24,512]{1,0:T(8,128)S(1)}, u32[]{:S(2)}, u32[]{:S(2)}) collective-permute-start(f32[24,512]{1,0:T(8,128)S(1)} %get-tuple-element.87), channel_id=1, source_target_pairs={{0,192},{64,0},{128,64},{192,128},{1,193},{65,1},{129,65},{193,129... | collective-permute-start | bytes 147464 | tf_op jit(solution)/shard_map/ppermute | solution.py:33
  64.5 23.8 %all-to-all-start.1 = ((f32[16,32,512]{2,1,0:T(8,128)}), f32[16,32,512]{2,1,0:T(8,128)S(1)}, u32[]{:S(2)}, u32[]{:S(2)}) async-start(f32[16,32,512]{2,1,0:T(8,128)} %get-tuple-element.90), calls=%async_computation.1 | async-start | bytes 2097152 | tf_op jit(solution)/shard_map/all_to_all | solution.py:38
  70.7 1.3 collective-permute-start.16
  72.0 4.3 %collective-permute-start.17 = (f32[8,128]{1,0:T(8,128)S(1)}, f32[8,128]{1,0:T(8,128)S(1)}, u32[]{:S(2)}, u32[]{:S(2)}) collective-permute-start(f32[8,128]{1,0:T(8,128)S(1)} %add.19), channel_id=1, source_target_pairs={{0,2},{2,0},{4,6},{6,4},{8,10},{10,8},{12,14},{14,12},{1,3},{3,1},... | collective-permute-start | bytes 12296 | tf_op jit(solution)/shard_map/ppermute | solution.py:52
  76.3 4.5 %collective-permute-start.18 = (f32[8,128]{1,0:T(8,128)S(1)}, f32[8,128]{1,0:T(8,128)S(1)}, u32[]{:S(2)}, u32[]{:S(2)}) collective-permute-start(f32[8,128]{1,0:T(8,128)S(1)} %add.20), channel_id=1, source_target_pairs={{0,4},{2,6},{4,0},{6,2},{8,12},{10,14},{12,8},{14,10},{1,5},{3,7},... | collective-permute-start | bytes 12296 | tf_op jit(solution)/shard_map/ppermute | solution.py:52
  80.8 7.5 %collective-permute-start.19 = (f32[8,128]{1,0:T(8,128)S(1)}, f32[8,128]{1,0:T(8,128)S(1)}, u32[]{:S(2)}, u32[]{:S(2)}) collective-permute-start(f32[8,128]{1,0:T(8,128)S(1)} %add.21), channel_id=1, source_target_pairs={{0,8},{2,10},{4,12},{6,14},{8,0},{10,2},{12,4},{14,6},{1,9},{3,11}... | collective-permute-start | bytes 12296 | tf_op jit(solution)/shard_map/ppermute | solution.py:52
  92.5 41.1 %copy-start.4 = (f32[1,32,512]{2,1,0:T(8,128)S(1)}, f32[1,32,512]{2,1,0:T(8,128)}, u32[]{:S(2)}) copy-start(f32[1,32,512]{2,1,0:T(8,128)} %param.7) | copy-start | bytes 196612
  92.6 41.1 %copy-start.5 = (f32[32,512]{1,0:T(8,128)S(1)}, f32[32,512]{1,0:T(8,128)}, u32[]{:S(2)}) copy-start(f32[32,512]{1,0:T(8,128)} %get-tuple-element.88.refs_9_) | copy-start | bytes 196612
  92.6 12.6 %collective-permute-start.20 = (f32[16,16,512]{2,1,0:T(8,128)S(1)}, f32[16,16,512]{2,1,0:T(8,128)S(1)}, u32[]{:S(2)}, u32[]{:S(2)}) collective-permute-start(f32[16,16,512]{2,1,0:T(8,128)S(1)} %get-tuple-element.92), channel_id=1, source_target_pairs={{1,2},{3,4},{5,6},{7,8},{9,10},{11,12},{13,14},{2,1},{4,3},{6,5},{... | collective-permute-start | bytes 1572872 | tf_op jit(solution)/shard_map/ppermute | solution.py:27
  98.3 6.9 %collective-permute-start.21 = (f32[16,16,512]{2,1,0:T(8,128)S(1)}, f32[16,16,512]{2,1,0:T(8,128)S(1)}, u32[]{:S(2)}, u32[]{:S(2)}) collective-permute-start(f32[16,16,512]{2,1,0:T(8,128)S(1)} %get-tuple-element.93), channel_id=1, source_target_pairs={{0,1},{1,0},{2,3},{3,2},{4,5},{5,4},{6,7},{7,6},{8,9},{9,8},{10,11... | collective-permute-start | bytes 1572872 | tf_op jit(solution)/shard_map/ppermute | solution.py:27
  98.4 12.9 %collective-permute-start.28 = (f32[16,16,512]{2,1,0:T(8,128)S(1)}, f32[16,16,512]{2,1,0:T(8,128)S(1)}, u32[]{:S(2)}, u32[]{:S(2)}) collective-permute-start(f32[16,16,512]{2,1,0:T(8,128)S(1)} %get-tuple-element.103), channel_id=1, source_target_pairs={{1,2},{3,4},{5,6},{7,8},{9,10},{11,12},{13,14},{2,1},{4,3},{6,5},{... | collective-permute-start | bytes 1572872 | tf_op jit(solution)/shard_map/ppermute | solution.py:27
  100.3 11.0 %collective-permute-start.29 = (f32[16,16,512]{2,1,0:T(8,128)S(1)}, f32[16,16,512]{2,1,0:T(8,128)S(1)}, u32[]{:S(2)}, u32[]{:S(2)}) collective-permute-start(f32[16,16,512]{2,1,0:T(8,128)S(1)} %get-tuple-element.104), channel_id=1, source_target_pairs={{0,1},{1,0},{2,3},{3,2},{4,5},{5,4},{6,7},{7,6},{8,9},{9,8},{10,11... | collective-permute-start | bytes 1572872 | tf_op jit(solution)/shard_map/ppermute | solution.py:27
  105.2 14.1 %collective-permute-start.22 = (f32[64,512]{1,0:T(8,128)S(1)}, f32[64,512]{1,0:T(8,128)S(1)}, u32[]{:S(2)}, u32[]{:S(2)}) collective-permute-start(f32[64,512]{1,0:T(8,128)S(1)} %get-tuple-element.95), channel_id=1, source_target_pairs={{0,64},{64,128},{128,192},{192,0},{1,65},{65,129},{129,193},{193,1... | collective-permute-start | bytes 393224 | tf_op jit(solution)/shard_map/ppermute | solution.py:33
  105.3 14.1 %collective-permute-start.23 = (f32[64,512]{1,0:T(8,128)S(1)}, f32[64,512]{1,0:T(8,128)S(1)}, u32[]{:S(2)}, u32[]{:S(2)}) collective-permute-start(f32[64,512]{1,0:T(8,128)S(1)} %get-tuple-element.96), channel_id=1, source_target_pairs={{0,128},{64,192},{128,0},{192,64},{1,129},{65,193},{129,1},{193,65... | collective-permute-start | bytes 393224 | tf_op jit(solution)/shard_map/ppermute | solution.py:33
  111.3 8.1 %collective-permute-start.24 = (f32[64,512]{1,0:T(8,128)S(1)}, f32[64,512]{1,0:T(8,128)S(1)}, u32[]{:S(2)}, u32[]{:S(2)}) collective-permute-start(f32[64,512]{1,0:T(8,128)S(1)} %get-tuple-element.97), channel_id=1, source_target_pairs={{0,192},{64,0},{128,64},{192,128},{1,193},{65,1},{129,65},{193,129... | collective-permute-start | bytes 393224 | tf_op jit(solution)/shard_map/ppermute | solution.py:33
  111.4 12.4 %collective-permute-start.30 = (f32[64,512]{1,0:T(8,128)S(1)}, f32[64,512]{1,0:T(8,128)S(1)}, u32[]{:S(2)}, u32[]{:S(2)}) collective-permute-start(f32[64,512]{1,0:T(8,128)S(1)} %get-tuple-element.106), channel_id=1, source_target_pairs={{0,16},{16,32},{32,48},{48,0},{1,17},{17,33},{33,49},{49,1},{2,18}... | collective-permute-start | bytes 393224 | tf_op jit(solution)/shard_map/ppermute | solution.py:33
  115.3 10.9 %collective-permute-start.31 = (f32[64,512]{1,0:T(8,128)S(1)}, f32[64,512]{1,0:T(8,128)S(1)}, u32[]{:S(2)}, u32[]{:S(2)}) collective-permute-start(f32[64,512]{1,0:T(8,128)S(1)} %get-tuple-element.107), channel_id=1, source_target_pairs={{0,32},{16,48},{32,0},{48,16},{1,33},{17,49},{33,1},{49,17},{2,34}... | collective-permute-start | bytes 393224 | tf_op jit(solution)/shard_map/ppermute | solution.py:33
  119.3 6.8 %collective-permute-start.32 = (f32[64,512]{1,0:T(8,128)S(1)}, f32[64,512]{1,0:T(8,128)S(1)}, u32[]{:S(2)}, u32[]{:S(2)}) collective-permute-start(f32[64,512]{1,0:T(8,128)S(1)} %get-tuple-element.108), channel_id=1, source_target_pairs={{0,48},{16,0},{32,16},{48,32},{1,49},{17,1},{33,17},{49,33},{2,50}... | collective-permute-start | bytes 393224 | tf_op jit(solution)/shard_map/ppermute | solution.py:33
  119.5 10.1 %collective-permute-start.25 = (f32[16,512]{1,0:T(8,128)S(1)}, f32[16,512]{1,0:T(8,128)S(1)}, u32[]{:S(2)}, u32[]{:S(2)}) collective-permute-start(f32[16,512]{1,0:T(8,128)S(1)} %get-tuple-element.99), channel_id=1, source_target_pairs={{0,16},{16,32},{32,48},{48,0},{1,17},{17,33},{33,49},{49,1},{2,18}... | collective-permute-start | bytes 98312 | tf_op jit(solution)/shard_map/ppermute | solution.py:33
  121.5 10.6 %collective-permute-start.26 = (f32[16,512]{1,0:T(8,128)S(1)}, f32[16,512]{1,0:T(8,128)S(1)}, u32[]{:S(2)}, u32[]{:S(2)}) collective-permute-start(f32[16,512]{1,0:T(8,128)S(1)} %get-tuple-element.100), channel_id=1, source_target_pairs={{0,32},{16,48},{32,0},{48,16},{1,33},{17,49},{33,1},{49,17},{2,34}... | collective-permute-start | bytes 98312 | tf_op jit(solution)/shard_map/ppermute | solution.py:33
  123.8 8.3 %collective-permute-start.27 = (f32[16,512]{1,0:T(8,128)S(1)}, f32[16,512]{1,0:T(8,128)S(1)}, u32[]{:S(2)}, u32[]{:S(2)}) collective-permute-start(f32[16,512]{1,0:T(8,128)S(1)} %get-tuple-element.101), channel_id=1, source_target_pairs={{0,48},{16,0},{32,16},{48,32},{1,49},{17,1},{33,17},{49,33},{2,50}... | collective-permute-start | bytes 98312 | tf_op jit(solution)/shard_map/ppermute | solution.py:33
  126.2 5.9 %collective-permute-start.33 = (f32[16,512]{1,0:T(8,128)S(1)}, f32[16,512]{1,0:T(8,128)S(1)}, u32[]{:S(2)}, u32[]{:S(2)}) collective-permute-start(f32[16,512]{1,0:T(8,128)S(1)} %get-tuple-element.110), channel_id=1, source_target_pairs={{0,64},{64,128},{128,192},{192,0},{1,65},{65,129},{129,193},{193,1... | collective-permute-start | bytes 98312 | tf_op jit(solution)/shard_map/ppermute | solution.py:33
  126.8 5.4 %collective-permute-start.34 = (f32[16,512]{1,0:T(8,128)S(1)}, f32[16,512]{1,0:T(8,128)S(1)}, u32[]{:S(2)}, u32[]{:S(2)}) collective-permute-start(f32[16,512]{1,0:T(8,128)S(1)} %get-tuple-element.111), channel_id=1, source_target_pairs={{0,128},{64,192},{128,0},{192,64},{1,129},{65,193},{129,1},{193,65... | collective-permute-start | bytes 98312 | tf_op jit(solution)/shard_map/ppermute | solution.py:33
  129.5 4.1 %collective-permute-start.35 = (f32[16,512]{1,0:T(8,128)S(1)}, f32[16,512]{1,0:T(8,128)S(1)}, u32[]{:S(2)}, u32[]{:S(2)}) collective-permute-start(f32[16,512]{1,0:T(8,128)S(1)} %get-tuple-element.112), channel_id=1, source_target_pairs={{0,192},{64,0},{128,64},{192,128},{1,193},{65,1},{129,65},{193,129... | collective-permute-start | bytes 98312 | tf_op jit(solution)/shard_map/ppermute | solution.py:33

commit v9 on v8

--- a/solution.py
+++ b/solution.py
@@ -90,13 +90,14 @@
         kept = goal == sector
         swapped_here = goal == (sector ^ 1)
         roles = (jnp.logical_not(kept | swapped_here), kept, swapped_here)
-        result = result.reshape(peers, HALVES * rows, width)
+        cuts = len(outs) // len(roles)
+        result = result.reshape(peers, cuts * rows, width)
         for i, role in enumerate(roles):
 
             @pl.when(role)
             def _(i=i):
-                for half in range(HALVES):
-                    outs[i * HALVES + half][...] += result[:, half * rows : (half + 1) * rows]
+                for cut in range(cuts):
+                    outs[i * cuts + cut][...] += result[:, cut * rows : (cut + 1) * rows]
 
 
 def first_kernel(count, target, left, right, field, *rest):
@@ -137,7 +138,7 @@
     accumulate(lax.axis_index(SECTOR), count, target, left, right, f_high, f_low, outs)
 
 
-def partial_image(body, counts, targets, left_stack, right_stack, fields, split, scratch=None, streamed=False):
+def partial_image(body, counts, targets, left_stack, right_stack, fields, split, cuts, scratch=None, streamed=False):
     slots, width, _ = right_stack.shape
 
     def operand(i, count):
@@ -149,18 +150,14 @@
         for x in (targets, left_stack, right_stack)
     )
     block = (width, width)
-    part = (split[0], split[1] // HALVES, width)
-    parts = 3 * HALVES
-    field_spec = out_spec = in_vmem
-    kind = jax.ShapeDtypeStruct
+    part = (split[0], split[1] // cuts, width)
+    field_spec = in_vmem
     if streamed:
         fields = [pltpu.with_memory_space_constraint(x, pltpu.HBM) for x in fields]
         field_spec = pl.BlockSpec(block, lambda i, *_: (0, 0), pipeline_mode=pl.Buffered(1))
-        kind = pltpu.HBM
-        out_spec = pl.BlockSpec(part, lambda i, *_: (0, 0, 0), pipeline_mode=pl.Buffered(1))
     return pl.pallas_call(
         body,
-        out_shape=[kind(part, F32)] * parts,
+        out_shape=[jax.ShapeDtypeStruct(part, F32)] * (3 * cuts),
         grid_spec=pltpu.PrefetchScalarGridSpec(
             num_scalar_prefetch=1,
             grid=(slots,),
@@ -170,7 +167,7 @@
                 pl.BlockSpec((1, width, width), operand),
                 *[field_spec] * len(fields),
             ],
-            out_specs=[out_spec] * parts,
+            out_specs=[in_vmem] * (3 * cuts),
             scratch_shapes=[pltpu.VMEM(scratch or block, jnp.bfloat16)] * 2,
         ),
         compiler_params=pltpu.CompilerParams(
@@ -186,58 +183,24 @@
     return along * size + across if half == 0 else across * size + along
 
 
-def spread(half, pieces, kept, crossed, local, weights=()):
-    peers, rows, width = kept.shape
+def spread(half, kept, crossed, local, *pieces):
+    rows = kept.shape[1]
     size = len(pieces)
     me = lax.axis_index(TERM[half])
-    lines = slice(half * rows, (half + 1) * rows)
-    cross = scaled_cross = jnp.zeros((rows, width), F32)
     for k, piece in enumerate(pieces):
         for across in range(size):
             peer = place(half, lax.rem(me + k, size), across, size)
             total = kept[peer] + (crossed[peer] + local[peer])
             piece[across * rows : (across + 1) * rows] = total
-            if weights:
-                field, scaling = weights
-                weighted = field[peer, lines] * total
-                cross += weighted
-                scaled_cross += scaling[peer, lines] * weighted
-    return cross, scaled_cross
-
-
-def first_spread(half, kept, crossed, local, field, scaling, *rest):
-    *pieces, tail = rest
-    rows = kept.shape[1]
-    cross, scaled_cross = spread(half, pieces, kept, crossed, local, (field, scaling))
-    me, lines = lax.axis_index(TERM), slice(half * rows, (half + 1) * rows)
-    own = field[me, lines]
-    square = own * own
-    line = lax.broadcasted_iota(jnp.int32, tail.shape, 0)
-    tile = jnp.zeros(tail.shape, F32)
-    for i, part in enumerate((cross, square, scaled_cross, scaling[me, lines] * square)):
-        tile = jnp.where(line == i, jnp.sum(part, keepdims=True), tile)
-    tail[...] = tile
-    for piece in pieces:
-        piece[len(pieces) * rows :] = tail[...]
-
-
-def second_spread(half, kept, crossed, local, *pieces):
-    spread(half, pieces, kept, crossed, local)
 
 
 def relay(axis, rows, *refs):
     size = len(refs) // 2
     arrived, pieces = refs[:size], refs[size:]
     me = lax.axis_index(axis)
-
-    def summed(where):
-        return functools.reduce(lambda x, y: x + y, [ref[where] for ref in arrived])
-
     for k, piece in enumerate(pieces):
-        start = pl.multiple_of(lax.rem(me + k, size) * rows, rows)
-        piece[:rows] = summed(pl.ds(start, rows))
-        if piece.shape[0] > rows:
-            piece[rows:] = summed(pl.ds(size * rows, piece.shape[0] - rows))
+        lines = pl.ds(pl.multiple_of(lax.rem(me + k, size) * rows, rows), rows)
+        piece[...] = functools.reduce(lambda x, y: x + y, [ref[lines] for ref in arrived])
 
 
 def landed(refs):
@@ -246,15 +209,42 @@
     return [functools.reduce(lambda x, y: x + y, [r[...] for r in g]) for g in groups]
 
 
-def first_landing(*refs):
-    *arrived, image, copies, sums = refs
-    rows = image.shape[0] // HALVES
-    totals = landed(arrived)
-    for half, total in enumerate(totals):
-        image[half * rows : (half + 1) * rows] = total[:rows]
+def tiles(x, slab, width):
+    return [(c * slab, slice(c * LANES, (c + 1) * LANES)) for c in range(width // LANES)]
+
+
+def combine(kept, crossed, local, field, scaling, packed, tail):
+    peers, slab, width = kept.shape
+    where = tiles(kept, slab, width)
+    cross = scaled_cross = jnp.zeros((slab, width), F32)
+    for peer in range(peers):
+        total = kept[peer] + (crossed[peer] + local[peer])
+        for row, lanes in where:
+            packed[peer, row : row + slab] = total[:, lanes]
+        weighted = field[peer] * total
+        cross += weighted
+        scaled_cross += scaling[peer] * weighted
+    me = lax.axis_index(TERM)
+    own = field[me]
+    square = own * own
+    line = lax.broadcasted_iota(jnp.int32, tail.shape, 0)
+    tile = jnp.zeros(tail.shape, F32)
+    for i, part in enumerate((cross, square, scaled_cross, scaling[me] * square)):
+        tile = jnp.where(line == i, jnp.sum(part, keepdims=True), tile)
+    tail[...] = tile
+    for peer in range(peers):
+        packed[peer, len(where) * slab :] = tail[...]
+
+
+def first_landing(arrived, image, copies, sums):
+    slab, width = image.shape
+    total = functools.reduce(lambda x, y: x + y, [arrived[i] for i in range(arrived.shape[0])])
+    where = tiles(image, slab, width)
+    for row, lanes in where:
+        image[:, lanes] = total[row : row + slab]
     for peer in range(copies.shape[0]):
         copies[peer] = image[...]
-    sums[...] = functools.reduce(lambda x, y: x + y, totals)[rows:, : sums.shape[1]]
+    sums[...] = total[len(where) * slab :]
 
 
 def second_landing(*refs):
@@ -266,15 +256,10 @@
         image[half * rows : (half + 1) * rows] = total
 
 
-def repeated(x, copies):
-    for peer in range(copies.shape[0]):
-        copies[peer] = x[...]
-
-
 def relayed(half, pieces, rows):
     arrived = exchanged_along(pieces, TERM[half])
     other = TERM[1 - half]
-    shape = (rows + pieces[0].shape[0] - len(pieces) * rows, pieces[0].shape[1])
+    shape = (rows, pieces[0].shape[1])
     onward = small_call(
         functools.partial(relay, other, rows), [shape] * len(pieces), arrived
     )
@@ -318,39 +303,35 @@
         split=split,
     )
 
-    def moved_parts(parts):
-        crossing, kept, local = (parts[i * HALVES : (i + 1) * HALVES] for i in range(3))
-        return [(k, *moved(c, l)) for c, k, l in zip(crossing, kept, local)]
-
-    (copies,) = small_call(repeated, [split], [scaling], spaces=[pltpu.HBM])
-    full_scaling = swapped(copies)
-    parts = image_of(first_kernel, fields=(field,), streamed=True)
-    parts, full_scaling = lax.optimization_barrier((parts, full_scaling))
-    parts = moved_parts(parts)
+    crossing, kept, local = image_of(first_kernel, fields=(field,), cuts=1, streamed=True)
+    crossed, local = moved(crossing, local)
+    scaling_late, _ = lax.optimization_barrier((scaling, kept))
+    full_scaling = swapped(jnp.broadcast_to(scaling_late[None], split))
+    (packed,) = small_call(
+        combine,
+        [(peers, slab * (width // LANES) + EXTRA, LANES)],
+        [kept, crossed, local, blocked, full_scaling],
+        [pltpu.VMEM((EXTRA, LANES), F32)],
+    )
+    first_image, copies, sums = small_call(
+        first_landing,
+        [(slab, width), split, (EXTRA, LANES)],
+        [swapped(packed)],
+        spaces=[pltpu.VMEM, pltpu.HBM, pltpu.VMEM],
+    )
+    full_image = swapped(copies)
+    sums = over_sectors(sums)
+
+    fields = (sums, blocked, full_scaling, full_image)
+    parts = image_of(second_kernel, fields=fields, cuts=HALVES, scratch=split)
+    crossing, kept, local = (parts[i * HALVES : (i + 1) * HALVES] for i in range(3))
+    moves = [moved(c, l) for c, l in zip(crossing, local)]
     arrived = []
     for half in range(HALVES):
         pieces = small_call(
-            functools.partial(first_spread, half),
-            [(size * rows + EXTRA, width)] * size,
-            [*parts[half], blocked, full_scaling],
-            [pltpu.VMEM((EXTRA, width), F32)],
-        )
-        arrived += relayed(half, pieces, rows)
-    first_image, copies, sums = small_call(
-        first_landing,
-        [(slab, width), split, (EXTRA, LANES)],
-        arrived,
-        spaces=[pltpu.VMEM, pltpu.HBM, pltpu.VMEM],
-    )
-    full_image = swapped(copies)
-    sums = over_sectors(sums)
-
-    fields = (sums, blocked, full_scaling, full_image)
-    parts = moved_parts(image_of(second_kernel, fields=fields, scratch=split))
-    arrived = []
-    for half in range(HALVES):
-        pieces = small_call(
-            functools.partial(second_spread, half), [(size * rows, width)] * size, parts[half]
+            functools.partial(spread, half),
+            [(size * rows, width)] * size,
+            [kept[half], *moves[half]],
         )
         arrived += relayed(half, pieces, rows)
     own = lax.dynamic_index_in_dim(blocked, lax.axis_index(TERM), 0, keepdims=False)

time: 136 us -> 130 us (0.956)
  blocking collectives: 0 us -> 44.4 us
  starting transfers between devices: 77 us -> 40.9 us
  waiting for transfers between devices: 38.8 us -> 18.9 us
  Pallas kernels: 14.1 us -> 22.8 us
  local copies, waits for them, and re-layouts: 2.94 us -> 0.13 us
    all_to_all x0 -> x2, blocking collectives: none -> 44.4 us  [swapped(): return lax.all_to_all(x, TERM, 0, 0, tiled=True)]
    ppermute x24 -> x12, starting transfers between devices: 37.9 us -> 21.2 us  [exchanged_along(): sent = [lax.ppermute(pieces[k], axis, routes[k]) for k in range(1, size)]]
    all_to_all x2 -> x1, waiting for transfers between devices: 10.9 us -> 0.01 us  [swapped(): return lax.all_to_all(x, TERM, 0, 0, tiled=True)]
    pallas_call x2, Pallas kernels: 10.3 us -> 20.3 us  [partial_image(): pl.pallas_call(body, out_shape=[jax.ShapeDtypeStruct(part, F32)] * (3 * c...]
    all_to_all x2 -> x1, starting transfers between devices: 13.3 us -> 3.65 us  [swapped(): return lax.all_to_all(x, TERM, 0, 0, tiled=True)]
    ppermute x24 -> x12, waiting for transfers between devices: 11.9 us -> 2.46 us  [exchanged_along(): sent = [lax.ppermute(pieces[k], axis, routes[k]) for k in range(1, size)]]
    ppermute x4 -> x3, starting transfers between devices: 11.5 us -> 6.01 us  [moved(): lax.ppermute(crossing, SECTOR, upward + downward)]
    ppermute x4 -> x3, starting transfers between devices: 7.31 us -> 3.9 us  [moved(): lax.ppermute(local, SECTOR, swap)]
  transfers between devices with their start and end apart: 38 -> 23, of which waited for: 16 -> 9; matrix products, arithmetic and copies ran while one was open for 0% -> 0% of each run, Pallas kernels for 5% -> 0%
where the time goes in v9:
time: 130 us; the launch traced here: 129 us
  blocking collectives  44.4 us (34%)
  starting transfers between devices  40.9 us (31%)
  Pallas kernels  22.8 us (18%)
  waiting for transfers between devices  18.9 us (15%)
  between operations  1.45 us (1%)
    all_to_all x2, blocking collectives, swapped(): return lax.all_to_all(x, TERM, 0, 0, tiled=True)  44.4 us
    ppermute x12, starting transfers between devices, exchanged_along(): sent = [lax.ppermute(pieces[k], axis, routes[k]) for k in range(1, size)]  21.2 us
    pallas_call x2, Pallas kernels, partial_image(): pl.pallas_call(body, out_shape=[jax.ShapeDtypeStruct(part, F32)] * (3 * c...  20.3 us
    ppermute x4, waiting for transfers between devices, exchanged(): return x + lax.ppermute(x, axis, pairs)  10.8 us
    ppermute x4, starting transfers between devices, exchanged(): return x + lax.ppermute(x, axis, pairs)  6.11 us
    ppermute x3, starting transfers between devices, moved(): lax.ppermute(crossing, SECTOR, upward + downward)  6.01 us
    ppermute x3, waiting for transfers between devices, moved(): lax.ppermute(crossing, SECTOR, upward + downward)  5.65 us
    ppermute x3, starting transfers between devices, moved(): lax.ppermute(local, SECTOR, swap)  3.9 us
  transfers between devices with their start and end apart: 23, of which 9 were waited for; matrix products, arithmetic and copies ran while one was open for 0% of the time, Pallas kernels for 0%

profile of v9, /device:TPU:64, one launch (start us, length us, event | category | flops | bytes accessed | tf_op | source)
XLA Modules:
  0.0 128.6 jit_solution(2549201400014974399)
XLA Ops:
  1.3 0.0 copy-start.1
  1.3 0.0 copy-start
  1.3 10.4 %shard_map.85 = (f32[16,32,512]{2,1,0:T(8,128)S(1)}, f32[16,32,512]{2,1,0:T(8,128)S(1)}, f32[16,32,512]{2,1,0:T(8,128)S(1)}) custom-call(s32[1,1]{1,0:T(1,128)S(6)} %copy.9.count, s32[1,4]{1,0:T(1,128)} %target.3, f32[4,512,512]{2,1,0:T(8,128)} %bitcast.17, f32[4,512,512]{2,1,0:T(8,128)} %bitcast.19, f32[512,512]{1,0:T(8,128)} %bitcast.10), custom_call_target="tpu_custom_call" | custom-call | flops 6442450944 | bytes 8388608 | tf_op jit(solution)/shard_map/pallas_call | solution.py:158
  11.7 1.9 %collective-permute-start = (f32[16,32,512]{2,1,0:T(8,128)S(1)}, f32[16,32,512]{2,1,0:T(8,128)S(1)}, u32[]{:S(2)}, u32[]{:S(2)}) collective-permute-start(f32[16,32,512]{2,1,0:T(8,128)S(1)} %get-tuple-element.35), channel_id=1, source_target_pairs={{1,2},{3,4},{5,6},{7,8},{9,10},{11,12},{13,14},{2,1},{4,3},{6,5},{... | collective-permute-start | bytes 3145736 | tf_op jit(solution)/shard_map/ppermute | solution.py:27
  13.6 2.1 %collective-permute-start.1 = (f32[16,32,512]{2,1,0:T(8,128)S(1)}, f32[16,32,512]{2,1,0:T(8,128)S(1)}, u32[]{:S(2)}, u32[]{:S(2)}) collective-permute-start(f32[16,32,512]{2,1,0:T(8,128)S(1)} %get-tuple-element.36), channel_id=1, source_target_pairs={{0,1},{1,0},{2,3},{3,2},{4,5},{5,4},{6,7},{7,6},{8,9},{9,8},{10,11... | collective-permute-start | bytes 3145736 | tf_op jit(solution)/shard_map/ppermute | solution.py:27
  15.7 0.0 copy-done.1
  15.7 0.1 broadcast_in_dim.15
  15.8 23.9 %all_to_all.15.scaling = f32[16,32,512]{2,1,0:T(8,128)S(1)} all-to-all(f32[16,32,512]{2,1,0:T(8,128)S(1)} %broadcast_in_dim.15), channel_id=1, replica_groups=mesh['term_0'=4,'term_1'=4,'sector_0'=8,'sector_1'=2] {'term_0','term_1'}, dimensions={0} | all-to-all | bytes 2097152 | tf_op jit(solution)/shard_map/all_to_all | solution.py:38
  39.7 0.0 collective-permute-done.crossed
  39.7 0.0 collective-permute-done.1.local
  39.7 0.0 copy-done
  39.7 0.5 shard_map.86
  40.2 20.5 %all_to_all.16.arrived = f32[16,136,128]{2,1,0:T(8,128)S(1)} all-to-all(f32[16,136,128]{2,1,0:T(8,128)S(1)} %shard_map.86), channel_id=1, replica_groups=mesh['term_0'=4,'term_1'=4,'sector_0'=8,'sector_1'=2] {'term_0','term_1'}, dimensions={0} | all-to-all | bytes 2228224 | tf_op jit(solution)/shard_map/all_to_all | solution.py:38
  60.7 1.2 shard_map.87
  61.9 3.7 %all-to-all-start.2 = ((f32[16,32,512]{2,1,0:T(8,128)}), f32[16,32,512]{2,1,0:T(8,128)S(1)}, u32[]{:S(2)}, u32[]{:S(2)}) async-start(f32[16,32,512]{2,1,0:T(8,128)} %get-tuple-element.40), calls=%async_computation.2 | async-start | bytes 2097152 | tf_op jit(solution)/shard_map/all_to_all | solution.py:38
  65.6 0.1 collective-permute-start.2
  65.7 1.2 collective-permute-done.2
  66.8 1.5 %collective-permute-start.3 = (f32[8,128]{1,0:T(8,128)S(1)}, f32[8,128]{1,0:T(8,128)S(1)}, u32[]{:S(2)}, u32[]{:S(2)}) collective-permute-start(f32[8,128]{1,0:T(8,128)S(1)} %add.19), channel_id=1, source_target_pairs={{0,2},{2,0},{4,6},{6,4},{8,10},{10,8},{12,14},{14,12},{1,3},{3,1},... | collective-permute-start | bytes 12296 | tf_op jit(solution)/shard_map/ppermute | solution.py:52
  68.3 2.1 %collective-permute-done.3 = f32[8,128]{1,0:T(8,128)S(1)} collective-permute-done((f32[8,128]{1,0:T(8,128)S(1)}, f32[8,128]{1,0:T(8,128)S(1)}, u32[]{:S(2)}, u32[]{:S(2)}) %collective-permute-start.3) | collective-permute-done | bytes 4128 | tf_op jit(solution)/shard_map/ppermute | solution.py:52
  70.4 0.0 collective-permute-start.4
  70.4 4.5 %collective-permute-done.4 = f32[8,128]{1,0:T(8,128)S(1)} collective-permute-done((f32[8,128]{1,0:T(8,128)S(1)}, f32[8,128]{1,0:T(8,128)S(1)}, u32[]{:S(2)}, u32[]{:S(2)}) %collective-permute-start.4) | collective-permute-done | bytes 4128 | tf_op jit(solution)/shard_map/ppermute | solution.py:52
  74.9 4.5 %collective-permute-start.5 = (f32[8,128]{1,0:T(8,128)S(1)}, f32[8,128]{1,0:T(8,128)S(1)}, u32[]{:S(2)}, u32[]{:S(2)}) collective-permute-start(f32[8,128]{1,0:T(8,128)S(1)} %add.21), channel_id=1, source_target_pairs={{0,8},{2,10},{4,12},{6,14},{8,0},{10,2},{12,4},{14,6},{1,9},{3,11}... | collective-permute-start | bytes 12296 | tf_op jit(solution)/shard_map/ppermute | solution.py:52
  79.4 3.0 %collective-permute-done.5 = f32[8,128]{1,0:T(8,128)S(1)} collective-permute-done((f32[8,128]{1,0:T(8,128)S(1)}, f32[8,128]{1,0:T(8,128)S(1)}, u32[]{:S(2)}, u32[]{:S(2)}) %collective-permute-start.5) | collective-permute-done | bytes 4128 | tf_op jit(solution)/shard_map/ppermute | solution.py:52
  82.5 0.0 all-to-all-done.2.image
  82.5 9.9 %shard_map.88 = (f32[16,16,512]{2,1,0:T(8,128)S(1)}, f32[16,16,512]{2,1,0:T(8,128)S(1)}, f32[16,16,512]{2,1,0:T(8,128)S(1)}, f32[16,16,512]{2,1,0:T(8,128)S(1)},...) custom-call(s32[1,1]{1,0:T(1,128)S(6)} %copy.9.count, s32[1,4]{1,0:T(1,128)} %target.3, f32[4,512,512]{2,1,0:T(8,128)} %bitcast.18, ...), custom_call_target="tpu_custom_call" | custom-call | flops 6442450944 | bytes 8388608 | tf_op jit(solution)/shard_map/pallas_call | solution.py:158
  92.4 0.0 copy-start.2
  92.4 2.1 %collective-permute-start.6 = (f32[16,16,512]{2,1,0:T(8,128)S(1)}, f32[16,16,512]{2,1,0:T(8,128)S(1)}, u32[]{:S(2)}, u32[]{:S(2)}) collective-permute-start(f32[16,16,512]{2,1,0:T(8,128)S(1)} %get-tuple-element.42), channel_id=1, source_target_pairs={{1,2},{3,4},{5,6},{7,8},{9,10},{11,12},{13,14},{2,1},{4,3},{6,5},{... | collective-permute-start | bytes 1572872 | tf_op jit(solution)/shard_map/ppermute | solution.py:27
  94.5 1.7 %collective-permute-start.7 = (f32[16,16,512]{2,1,0:T(8,128)S(1)}, f32[16,16,512]{2,1,0:T(8,128)S(1)}, u32[]{:S(2)}, u32[]{:S(2)}) collective-permute-start(f32[16,16,512]{2,1,0:T(8,128)S(1)} %get-tuple-element.43), channel_id=1, source_target_pairs={{0,1},{1,0},{2,3},{3,2},{4,5},{5,4},{6,7},{7,6},{8,9},{9,8},{10,11... | collective-permute-start | bytes 1572872 | tf_op jit(solution)/shard_map/ppermute | solution.py:27
  96.2 2.0 %collective-permute-start.14 = (f32[16,16,512]{2,1,0:T(8,128)S(1)}, f32[16,16,512]{2,1,0:T(8,128)S(1)}, u32[]{:S(2)}, u32[]{:S(2)}) collective-permute-start(f32[16,16,512]{2,1,0:T(8,128)S(1)} %get-tuple-element.53), channel_id=1, source_target_pairs={{1,2},{3,4},{5,6},{7,8},{9,10},{11,12},{13,14},{2,1},{4,3},{6,5},{... | collective-permute-start | bytes 1572872 | tf_op jit(solution)/shard_map/ppermute | solution.py:27
  98.2 0.1 collective-permute-start.15
  98.3 4.7 %collective-permute-done.6.crossed = f32[16,16,512]{2,1,0:T(8,128)S(1)} collective-permute-done((f32[16,16,512]{2,1,0:T(8,128)S(1)}, f32[16,16,512]{2,1,0:T(8,128)S(1)}, u32[]{:S(2)}, u32[]{:S(2)}) %collective-permute-start.6) | collective-permute-done | bytes 524320 | tf_op jit(solution)/shard_map/ppermute | solution.py:27
  103.0 0.0 collective-permute-done.7.local
  103.0 0.1 shard_map.89
  103.1 1.8 %collective-permute-start.8 = (f32[64,512]{1,0:T(8,128)S(1)}, f32[64,512]{1,0:T(8,128)S(1)}, u32[]{:S(2)}, u32[]{:S(2)}) collective-permute-start(f32[64,512]{1,0:T(8,128)S(1)} %get-tuple-element.45), channel_id=1, source_target_pairs={{0,64},{64,128},{128,192},{192,0},{1,65},{65,129},{129,193},{193,1... | collective-permute-start | bytes 393224 | tf_op jit(solution)/shard_map/ppermute | solution.py:33
  104.9 0.0 collective-permute-start.9
  104.9 2.8 %collective-permute-start.10 = (f32[64,512]{1,0:T(8,128)S(1)}, f32[64,512]{1,0:T(8,128)S(1)}, u32[]{:S(2)}, u32[]{:S(2)}) collective-permute-start(f32[64,512]{1,0:T(8,128)S(1)} %get-tuple-element.47), channel_id=1, source_target_pairs={{0,192},{64,0},{128,64},{192,128},{1,193},{65,1},{129,65},{193,129... | collective-permute-start | bytes 393224 | tf_op jit(solution)/shard_map/ppermute | solution.py:33
  107.7 0.9 collective-permute-done.14.crossed
  108.6 0.0 collective-permute-done.15.local
  108.6 0.1 shard_map.91
  108.7 0.3 collective-permute-start.16
  109.0 4.6 %collective-permute-start.17 = (f32[64,512]{1,0:T(8,128)S(1)}, f32[64,512]{1,0:T(8,128)S(1)}, u32[]{:S(2)}, u32[]{:S(2)}) collective-permute-start(f32[64,512]{1,0:T(8,128)S(1)} %get-tuple-element.57), channel_id=1, source_target_pairs={{0,32},{16,48},{32,0},{48,16},{1,33},{17,49},{33,1},{49,17},{2,34}... | collective-permute-start | bytes 393224 | tf_op jit(solution)/shard_map/ppermute | solution.py:33
  113.6 0.0 collective-permute-done.8.refs_1_
  113.6 1.5 %collective-permute-start.18 = (f32[64,512]{1,0:T(8,128)S(1)}, f32[64,512]{1,0:T(8,128)S(1)}, u32[]{:S(2)}, u32[]{:S(2)}) collective-permute-start(f32[64,512]{1,0:T(8,128)S(1)} %get-tuple-element.58), channel_id=1, source_target_pairs={{0,48},{16,0},{32,16},{48,32},{1,49},{17,1},{33,17},{49,33},{2,50}... | collective-permute-start | bytes 393224 | tf_op jit(solution)/shard_map/ppermute | solution.py:33
  115.1 0.0 collective-permute-done.9.refs_2_
  115.1 0.0 collective-permute-done.10.refs_3_
  115.1 0.6 collective-permute-start.11
  115.7 1.7 %collective-permute-start.12 = (f32[16,512]{1,0:T(8,128)S(1)}, f32[16,512]{1,0:T(8,128)S(1)}, u32[]{:S(2)}, u32[]{:S(2)}) collective-permute-start(f32[16,512]{1,0:T(8,128)S(1)} %get-tuple-element.50), channel_id=1, source_target_pairs={{0,32},{16,48},{32,0},{48,16},{1,33},{17,49},{33,1},{49,17},{2,34}... | collective-permute-start | bytes 98312 | tf_op jit(solution)/shard_map/ppermute | solution.py:33
  117.4 0.0 collective-permute-done.16.refs_1_
  117.4 1.6 %collective-permute-start.13 = (f32[16,512]{1,0:T(8,128)S(1)}, f32[16,512]{1,0:T(8,128)S(1)}, u32[]{:S(2)}, u32[]{:S(2)}) collective-permute-start(f32[16,512]{1,0:T(8,128)S(1)} %get-tuple-element.51), channel_id=1, source_target_pairs={{0,48},{16,0},{32,16},{48,32},{1,49},{17,1},{33,17},{49,33},{2,50}... | collective-permute-start | bytes 98312 | tf_op jit(solution)/shard_map/ppermute | solution.py:33
  119.0 0.8 collective-permute-done.17.refs_2_
  119.8 0.0 collective-permute-done.18.refs_3_
  119.9 2.3 %collective-permute-start.19 = (f32[16,512]{1,0:T(8,128)S(1)}, f32[16,512]{1,0:T(8,128)S(1)}, u32[]{:S(2)}, u32[]{:S(2)}) collective-permute-start(f32[16,512]{1,0:T(8,128)S(1)} %get-tuple-element.60), channel_id=1, source_target_pairs={{0,64},{64,128},{128,192},{192,0},{1,65},{65,129},{129,193},{193,1... | collective-permute-start | bytes 98312 | tf_op jit(solution)/shard_map/ppermute | solution.py:33
  122.2 1.6 %collective-permute-start.20 = (f32[16,512]{1,0:T(8,128)S(1)}, f32[16,512]{1,0:T(8,128)S(1)}, u32[]{:S(2)}, u32[]{:S(2)}) collective-permute-start(f32[16,512]{1,0:T(8,128)S(1)} %get-tuple-element.61), channel_id=1, source_target_pairs={{0,128},{64,192},{128,0},{192,64},{1,129},{65,193},{129,1},{193,65... | collective-permute-start | bytes 98312 | tf_op jit(solution)/shard_map/ppermute | solution.py:33
  123.8 0.0 collective-permute-done.11.refs_1_
  123.8 2.5 %collective-permute-start.21 = (f32[16,512]{1,0:T(8,128)S(1)}, f32[16,512]{1,0:T(8,128)S(1)}, u32[]{:S(2)}, u32[]{:S(2)}) collective-permute-start(f32[16,512]{1,0:T(8,128)S(1)} %get-tuple-element.62), channel_id=1, source_target_pairs={{0,192},{64,0},{128,64},{192,128},{1,193},{65,1},{129,65},{193,129... | collective-permute-start | bytes 98312 | tf_op jit(solution)/shard_map/ppermute | solution.py:33
  126.3 0.0 collective-permute-done.12.refs_2_
  126.3 0.0 collective-permute-done.13.refs_3_
  126.3 0.0 collective-permute-done.19.refs_5_
  126.3 1.3 collective-permute-done.20.refs_6_
  127.6 0.3 collective-permute-done.21.refs_7_
  127.9 0.0 copy-done.2
  127.9 0.7 shard_map.93
  (7 shorter events, 0.1 us)
Async XLA Ops:
  1.3 14.4 %copy-start.1 = (f32[1,32,512]{2,1,0:T(8,128)S(1)}, f32[1,32,512]{2,1,0:T(8,128)}, u32[]{:S(2)}) copy-start(f32[1,32,512]{2,1,0:T(8,128)} %param.7) | copy-start | bytes 196612
  1.3 38.4 %copy-start = (f32[1,512,512]{2,1,0:T(8,128)S(1)}, f32[1,512,512]{2,1,0:T(8,128)}, u32[]{:S(2)}) copy-start(f32[1,512,512]{2,1,0:T(8,128)} %param.6) | copy-start | bytes 3145732
  11.7 28.0 %collective-permute-start = (f32[16,32,512]{2,1,0:T(8,128)S(1)}, f32[16,32,512]{2,1,0:T(8,128)S(1)}, u32[]{:S(2)}, u32[]{:S(2)}) collective-permute-start(f32[16,32,512]{2,1,0:T(8,128)S(1)} %get-tuple-element.35), channel_id=1, source_target_pairs={{1,2},{3,4},{5,6},{7,8},{9,10},{11,12},{13,14},{2,1},{4,3},{6,5},{... | collective-permute-start | bytes 3145736 | tf_op jit(solution)/shard_map/ppermute | solution.py:27
  13.6 26.1 %collective-permute-start.1 = (f32[16,32,512]{2,1,0:T(8,128)S(1)}, f32[16,32,512]{2,1,0:T(8,128)S(1)}, u32[]{:S(2)}, u32[]{:S(2)}) collective-permute-start(f32[16,32,512]{2,1,0:T(8,128)S(1)} %get-tuple-element.36), channel_id=1, source_target_pairs={{0,1},{1,0},{2,3},{3,2},{4,5},{5,4},{6,7},{7,6},{8,9},{9,8},{10,11... | collective-permute-start | bytes 3145736 | tf_op jit(solution)/shard_map/ppermute | solution.py:27
  61.9 20.6 %all-to-all-start.2 = ((f32[16,32,512]{2,1,0:T(8,128)}), f32[16,32,512]{2,1,0:T(8,128)S(1)}, u32[]{:S(2)}, u32[]{:S(2)}) async-start(f32[16,32,512]{2,1,0:T(8,128)} %get-tuple-element.40), calls=%async_computation.2 | async-start | bytes 2097152 | tf_op jit(solution)/shard_map/all_to_all | solution.py:38
  65.6 1.3 collective-permute-start.2
  66.8 3.6 %collective-permute-start.3 = (f32[8,128]{1,0:T(8,128)S(1)}, f32[8,128]{1,0:T(8,128)S(1)}, u32[]{:S(2)}, u32[]{:S(2)}) collective-permute-start(f32[8,128]{1,0:T(8,128)S(1)} %add.19), channel_id=1, source_target_pairs={{0,2},{2,0},{4,6},{6,4},{8,10},{10,8},{12,14},{14,12},{1,3},{3,1},... | collective-permute-start | bytes 12296 | tf_op jit(solution)/shard_map/ppermute | solution.py:52
  70.4 4.5 %collective-permute-start.4 = (f32[8,128]{1,0:T(8,128)S(1)}, f32[8,128]{1,0:T(8,128)S(1)}, u32[]{:S(2)}, u32[]{:S(2)}) collective-permute-start(f32[8,128]{1,0:T(8,128)S(1)} %add.20), channel_id=1, source_target_pairs={{0,4},{2,6},{4,0},{6,2},{8,12},{10,14},{12,8},{14,10},{1,5},{3,7},... | collective-permute-start | bytes 12296 | tf_op jit(solution)/shard_map/ppermute | solution.py:52
  74.9 7.5 %collective-permute-start.5 = (f32[8,128]{1,0:T(8,128)S(1)}, f32[8,128]{1,0:T(8,128)S(1)}, u32[]{:S(2)}, u32[]{:S(2)}) collective-permute-start(f32[8,128]{1,0:T(8,128)S(1)} %add.21), channel_id=1, source_target_pairs={{0,8},{2,10},{4,12},{6,14},{8,0},{10,2},{12,4},{14,6},{1,9},{3,11}... | collective-permute-start | bytes 12296 | tf_op jit(solution)/shard_map/ppermute | solution.py:52
  92.4 35.5 %copy-start.2 = (f32[32,512]{1,0:T(8,128)S(1)}, f32[32,512]{1,0:T(8,128)}, u32[]{:S(2)}) copy-start(f32[32,512]{1,0:T(8,128)} %get-tuple-element.38.refs_9_) | copy-start | bytes 196612
  92.4 10.6 %collective-permute-start.6 = (f32[16,16,512]{2,1,0:T(8,128)S(1)}, f32[16,16,512]{2,1,0:T(8,128)S(1)}, u32[]{:S(2)}, u32[]{:S(2)}) collective-permute-start(f32[16,16,512]{2,1,0:T(8,128)S(1)} %get-tuple-element.42), channel_id=1, source_target_pairs={{1,2},{3,4},{5,6},{7,8},{9,10},{11,12},{13,14},{2,1},{4,3},{6,5},{... | collective-permute-start | bytes 1572872 | tf_op jit(solution)/shard_map/ppermute | solution.py:27
  94.5 8.6 %collective-permute-start.7 = (f32[16,16,512]{2,1,0:T(8,128)S(1)}, f32[16,16,512]{2,1,0:T(8,128)S(1)}, u32[]{:S(2)}, u32[]{:S(2)}) collective-permute-start(f32[16,16,512]{2,1,0:T(8,128)S(1)} %get-tuple-element.43), channel_id=1, source_target_pairs={{0,1},{1,0},{2,3},{3,2},{4,5},{5,4},{6,7},{7,6},{8,9},{9,8},{10,11... | collective-permute-start | bytes 1572872 | tf_op jit(solution)/shard_map/ppermute | solution.py:27
  96.2 12.5 %collective-permute-start.14 = (f32[16,16,512]{2,1,0:T(8,128)S(1)}, f32[16,16,512]{2,1,0:T(8,128)S(1)}, u32[]{:S(2)}, u32[]{:S(2)}) collective-permute-start(f32[16,16,512]{2,1,0:T(8,128)S(1)} %get-tuple-element.53), channel_id=1, source_target_pairs={{1,2},{3,4},{5,6},{7,8},{9,10},{11,12},{13,14},{2,1},{4,3},{6,5},{... | collective-permute-start | bytes 1572872 | tf_op jit(solution)/shard_map/ppermute | solution.py:27
  98.2 10.4 %collective-permute-start.15 = (f32[16,16,512]{2,1,0:T(8,128)S(1)}, f32[16,16,512]{2,1,0:T(8,128)S(1)}, u32[]{:S(2)}, u32[]{:S(2)}) collective-permute-start(f32[16,16,512]{2,1,0:T(8,128)S(1)} %get-tuple-element.54), channel_id=1, source_target_pairs={{0,1},{1,0},{2,3},{3,2},{4,5},{5,4},{6,7},{7,6},{8,9},{9,8},{10,11... | collective-permute-start | bytes 1572872 | tf_op jit(solution)/shard_map/ppermute | solution.py:27
  103.1 10.5 %collective-permute-start.8 = (f32[64,512]{1,0:T(8,128)S(1)}, f32[64,512]{1,0:T(8,128)S(1)}, u32[]{:S(2)}, u32[]{:S(2)}) collective-permute-start(f32[64,512]{1,0:T(8,128)S(1)} %get-tuple-element.45), channel_id=1, source_target_pairs={{0,64},{64,128},{128,192},{192,0},{1,65},{65,129},{129,193},{193,1... | collective-permute-start | bytes 393224 | tf_op jit(solution)/shard_map/ppermute | solution.py:33
  104.9 10.1 %collective-permute-start.9 = (f32[64,512]{1,0:T(8,128)S(1)}, f32[64,512]{1,0:T(8,128)S(1)}, u32[]{:S(2)}, u32[]{:S(2)}) collective-permute-start(f32[64,512]{1,0:T(8,128)S(1)} %get-tuple-element.46), channel_id=1, source_target_pairs={{0,128},{64,192},{128,0},{192,64},{1,129},{65,193},{129,1},{193,65... | collective-permute-start | bytes 393224 | tf_op jit(solution)/shard_map/ppermute | solution.py:33
  104.9 10.1 %collective-permute-start.10 = (f32[64,512]{1,0:T(8,128)S(1)}, f32[64,512]{1,0:T(8,128)S(1)}, u32[]{:S(2)}, u32[]{:S(2)}) collective-permute-start(f32[64,512]{1,0:T(8,128)S(1)} %get-tuple-element.47), channel_id=1, source_target_pairs={{0,192},{64,0},{128,64},{192,128},{1,193},{65,1},{129,65},{193,129... | collective-permute-start | bytes 393224 | tf_op jit(solution)/shard_map/ppermute | solution.py:33
  108.7 8.7 %collective-permute-start.16 = (f32[64,512]{1,0:T(8,128)S(1)}, f32[64,512]{1,0:T(8,128)S(1)}, u32[]{:S(2)}, u32[]{:S(2)}) collective-permute-start(f32[64,512]{1,0:T(8,128)S(1)} %get-tuple-element.56), channel_id=1, source_target_pairs={{0,16},{16,32},{32,48},{48,0},{1,17},{17,33},{33,49},{49,1},{2,18}... | collective-permute-start | bytes 393224 | tf_op jit(solution)/shard_map/ppermute | solution.py:33
  109.0 10.8 %collective-permute-start.17 = (f32[64,512]{1,0:T(8,128)S(1)}, f32[64,512]{1,0:T(8,128)S(1)}, u32[]{:S(2)}, u32[]{:S(2)}) collective-permute-start(f32[64,512]{1,0:T(8,128)S(1)} %get-tuple-element.57), channel_id=1, source_target_pairs={{0,32},{16,48},{32,0},{48,16},{1,33},{17,49},{33,1},{49,17},{2,34}... | collective-permute-start | bytes 393224 | tf_op jit(solution)/shard_map/ppermute | solution.py:33
  113.6 6.3 %collective-permute-start.18 = (f32[64,512]{1,0:T(8,128)S(1)}, f32[64,512]{1,0:T(8,128)S(1)}, u32[]{:S(2)}, u32[]{:S(2)}) collective-permute-start(f32[64,512]{1,0:T(8,128)S(1)} %get-tuple-element.58), channel_id=1, source_target_pairs={{0,48},{16,0},{32,16},{48,32},{1,49},{17,1},{33,17},{49,33},{2,50}... | collective-permute-start | bytes 393224 | tf_op jit(solution)/shard_map/ppermute | solution.py:33
  115.1 8.7 %collective-permute-start.11 = (f32[16,512]{1,0:T(8,128)S(1)}, f32[16,512]{1,0:T(8,128)S(1)}, u32[]{:S(2)}, u32[]{:S(2)}) collective-permute-start(f32[16,512]{1,0:T(8,128)S(1)} %get-tuple-element.49), channel_id=1, source_target_pairs={{0,16},{16,32},{32,48},{48,0},{1,17},{17,33},{33,49},{49,1},{2,18}... | collective-permute-start | bytes 98312 | tf_op jit(solution)/shard_map/ppermute | solution.py:33
  115.7 10.6 %collective-permute-start.12 = (f32[16,512]{1,0:T(8,128)S(1)}, f32[16,512]{1,0:T(8,128)S(1)}, u32[]{:S(2)}, u32[]{:S(2)}) collective-permute-start(f32[16,512]{1,0:T(8,128)S(1)} %get-tuple-element.50), channel_id=1, source_target_pairs={{0,32},{16,48},{32,0},{48,16},{1,33},{17,49},{33,1},{49,17},{2,34}... | collective-permute-start | bytes 98312 | tf_op jit(solution)/shard_map/ppermute | solution.py:33
  117.4 8.9 %collective-permute-start.13 = (f32[16,512]{1,0:T(8,128)S(1)}, f32[16,512]{1,0:T(8,128)S(1)}, u32[]{:S(2)}, u32[]{:S(2)}) collective-permute-start(f32[16,512]{1,0:T(8,128)S(1)} %get-tuple-element.51), channel_id=1, source_target_pairs={{0,48},{16,0},{32,16},{48,32},{1,49},{17,1},{33,17},{49,33},{2,50}... | collective-permute-start | bytes 98312 | tf_op jit(solution)/shard_map/ppermute | solution.py:33
  119.9 6.4 %collective-permute-start.19 = (f32[16,512]{1,0:T(8,128)S(1)}, f32[16,512]{1,0:T(8,128)S(1)}, u32[]{:S(2)}, u32[]{:S(2)}) collective-permute-start(f32[16,512]{1,0:T(8,128)S(1)} %get-tuple-element.60), channel_id=1, source_target_pairs={{0,64},{64,128},{128,192},{192,0},{1,65},{65,129},{129,193},{193,1... | collective-permute-start | bytes 98312 | tf_op jit(solution)/shard_map/ppermute | solution.py:33
  122.2 5.4 %collective-permute-start.20 = (f32[16,512]{1,0:T(8,128)S(1)}, f32[16,512]{1,0:T(8,128)S(1)}, u32[]{:S(2)}, u32[]{:S(2)}) collective-permute-start(f32[16,512]{1,0:T(8,128)S(1)} %get-tuple-element.61), channel_id=1, source_target_pairs={{0,128},{64,192},{128,0},{192,64},{1,129},{65,193},{129,1},{193,65... | collective-permute-start | bytes 98312 | tf_op jit(solution)/shard_map/ppermute | solution.py:33
  123.8 4.1 %collective-permute-start.21 = (f32[16,512]{1,0:T(8,128)S(1)}, f32[16,512]{1,0:T(8,128)S(1)}, u32[]{:S(2)}, u32[]{:S(2)}) collective-permute-start(f32[16,512]{1,0:T(8,128)S(1)} %get-tuple-element.62), channel_id=1, source_target_pairs={{0,192},{64,0},{128,64},{192,128},{1,193},{65,1},{129,65},{193,129... | collective-permute-start | bytes 98312 | tf_op jit(solution)/shard_map/ppermute | solution.py:33

commit v10 on v9

--- a/solution.py
+++ b/solution.py
@@ -14,7 +14,7 @@
 EXTRA = 8
 HALVES = 2
 MIB = 1 << 20
-KERNEL_VMEM = 18 * MIB
+KERNEL_VMEM = 22 * MIB
 SMALL_VMEM = 8 * MIB
 F32 = jnp.float32
 
@@ -69,22 +69,40 @@
     return dot(a_high, b_high) + (dot(a_high, b_low) + dot(a_low, b_high))
 
 
-def accumulate(sector, count, target, left, right, field_high, field_low, outs):
+def fetches(slot, stacks, held, landed):
+    return [
+        pltpu.make_async_copy(stack.at[slot], place.at[slot], landed.at[i, slot])
+        for i, (stack, place) in enumerate(zip(stacks, held))
+    ]
+
+
+def begin(stacks, held, landed, outs):
+    for fetch in fetches(0, stacks, held, landed):
+        fetch.start()
+    for out in outs:
+        out[...] = jnp.zeros_like(out)
+
+
+def accumulate(sector, count, target, stacks, held, landed, field_high, field_low, outs):
     slot = pl.program_id(0)
-
-    @pl.when(slot == 0)
-    def _():
-        for out in outs:
-            out[...] = jnp.zeros_like(out)
-
     peers, rows, width = outs[0].shape
 
     @pl.when(slot < count[0, 0])
     def _():
-        left_high, left_low = halves(left[0])
+        for fetch in fetches(slot, stacks, held, landed):
+            fetch.wait()
+        for later in range(1, stacks[0].shape[0]):
+
+            @pl.when((slot == 0) & (later < count[0, 0]))
+            def _(later=later):
+                for fetch in fetches(later, stacks, held, landed):
+                    fetch.start()
+
+        left, right = held
+        left_high, left_low = halves(left[slot])
         inner = product(left_high, left_low, field_high[...], field_low[...])
         inner_high, inner_low = halves(inner)
-        right_high, right_low = halves(right[0])
+        right_high, right_low = halves(right[slot])
         result = product(inner_high, inner_low, right_high, right_low)
         goal = target[0, slot]
         kept = goal == sector
@@ -101,13 +119,19 @@
 
 
 def first_kernel(count, target, left, right, field, *rest):
-    *outs, f_high, f_low = rest
+    *outs, f_high, f_low, held_left, held_right, landed, whole, arrived = rest
+    stacks, held = (left, right), (held_left, held_right)
 
     @pl.when(pl.program_id(0) == 0)
     def _():
-        f_high[...], f_low[...] = halves(field[...])
-
-    accumulate(lax.axis_index(SECTOR), count, target, left, right, f_high, f_low, outs)
+        fetch = pltpu.make_async_copy(field, whole, arrived)
+        fetch.start()
+        begin(stacks, held, landed, outs)
+        fetch.wait()
+        f_high[...], f_low[...] = halves(whole[...])
+
+    sector = lax.axis_index(SECTOR)
+    accumulate(sector, count, target, stacks, held, landed, f_high, f_low, outs)
 
 
 def coefficients(sums):
@@ -123,11 +147,13 @@
 
 
 def second_kernel(count, target, left, right, sums, field, scaling, image, *rest):
-    *outs, f_high, f_low = rest
+    *outs, f_high, f_low, held_left, held_right, landed = rest
+    stacks, held = (left, right), (held_left, held_right)
     peers, slab, width = field.shape
 
     @pl.when(pl.program_id(0) == 0)
     def _():
+        begin(stacks, held, landed, outs)
         coefs = coefficients(sums)
         for peer in range(peers):
             value = corrected(coefs, field[peer], scaling[peer], image[peer])
@@ -135,26 +161,29 @@
 
     flat = (peers * slab, width)
     f_high, f_low = f_high.reshape(flat), f_low.reshape(flat)
-    accumulate(lax.axis_index(SECTOR), count, target, left, right, f_high, f_low, outs)
-
-
-def partial_image(body, counts, targets, left_stack, right_stack, fields, split, cuts, scratch=None, streamed=False):
+    sector = lax.axis_index(SECTOR)
+    accumulate(sector, count, target, stacks, held, landed, f_high, f_low, outs)
+
+
+def partial_image(body, counts, targets, left_stack, right_stack, fields, cuts, split):
     slots, width, _ = right_stack.shape
-
-    def operand(i, count):
-        return (jnp.minimum(i, count[0, 0] - 1), 0, 0)
-
     in_vmem = pl.BlockSpec(memory_space=pltpu.VMEM)
+    in_hbm = pl.BlockSpec(memory_space=pltpu.HBM)
+    streamed = body is first_kernel
     targets, left_stack, right_stack = (
         pltpu.with_memory_space_constraint(x, pltpu.HBM)
         for x in (targets, left_stack, right_stack)
     )
     block = (width, width)
     part = (split[0], split[1] // cuts, width)
-    field_spec = in_vmem
+    scratch = [
+        *[pltpu.VMEM(block if streamed else split, jnp.bfloat16)] * 2,
+        *[pltpu.VMEM((slots, *block), F32)] * 2,
+        pltpu.SemaphoreType.DMA((2, slots)),
+    ]
     if streamed:
         fields = [pltpu.with_memory_space_constraint(x, pltpu.HBM) for x in fields]
-        field_spec = pl.BlockSpec(block, lambda i, *_: (0, 0), pipeline_mode=pl.Buffered(1))
+        scratch += [pltpu.VMEM(block, F32), pltpu.SemaphoreType.DMA]
     return pl.pallas_call(
         body,
         out_shape=[jax.ShapeDtypeStruct(part, F32)] * (3 * cuts),
@@ -163,12 +192,12 @@
             grid=(slots,),
             in_specs=[
                 pl.BlockSpec(targets.shape, lambda i, *_: (0, 0), memory_space=pltpu.SMEM),
-                pl.BlockSpec((1, width, width), operand),
-                pl.BlockSpec((1, width, width), operand),
-                *[field_spec] * len(fields),
+                in_hbm,
+                in_hbm,
+                *[in_hbm if streamed else in_vmem] * len(fields),
             ],
             out_specs=[in_vmem] * (3 * cuts),
-            scratch_shapes=[pltpu.VMEM(scratch or block, jnp.bfloat16)] * 2,
+            scratch_shapes=scratch,
         ),
         compiler_params=pltpu.CompilerParams(
             dimension_semantics=("arbitrary",), vmem_limit_bytes=KERNEL_VMEM
@@ -303,7 +332,7 @@
         split=split,
     )
 
-    crossing, kept, local = image_of(first_kernel, fields=(field,), cuts=1, streamed=True)
+    crossing, kept, local = image_of(first_kernel, fields=(field,), cuts=1)
     crossed, local = moved(crossing, local)
     scaling_late, _ = lax.optimization_barrier((scaling, kept))
     full_scaling = swapped(jnp.broadcast_to(scaling_late[None], split))
@@ -323,7 +352,7 @@
     sums = over_sectors(sums)
 
     fields = (sums, blocked, full_scaling, full_image)
-    parts = image_of(second_kernel, fields=fields, cuts=HALVES, scratch=split)
+    parts = image_of(second_kernel, fields=fields, cuts=HALVES)
     crossing, kept, local = (parts[i * HALVES : (i + 1) * HALVES] for i in range(3))
     moves = [moved(c, l) for c, l in zip(crossing, local)]
     arrived = []

time: 130 us -> 130 us (level); the launches traced: 129 us -> 131 us
  starting transfers between devices: 40.9 us -> 56.9 us
  Pallas kernels: 22.8 us -> 11.6 us
  waiting for transfers between devices: 18.9 us -> 16.1 us
    pallas_call x2, Pallas kernels: 20.3 us -> 9.05 us  [partial_image(): pl.pallas_call(body, out_shape=[jax.ShapeDtypeStruct(part, F32)] * (3 * c...]
    ppermute x3, starting transfers between devices: 6.01 us -> 14.6 us  [moved(): lax.ppermute(crossing, SECTOR, upward + downward)]
    ppermute x3, waiting for transfers between devices: 5.65 us -> 0.01 us  [moved(): lax.ppermute(crossing, SECTOR, upward + downward)]
    ppermute x3, starting transfers between devices: 3.9 us -> 8.02 us  [moved(): lax.ppermute(local, SECTOR, swap)]
    ppermute x12, starting transfers between devices: 21.2 us -> 24.3 us  [exchanged_along(): sent = [lax.ppermute(pieces[k], axis, routes[k]) for k in range(1, size)]]
    ppermute x12, waiting for transfers between devices: 2.46 us -> 4.57 us  [exchanged_along(): sent = [lax.ppermute(pieces[k], axis, routes[k]) for k in range(1, size)]]
  transfers between devices with their start and end apart: 23 -> 23, of which waited for: 9 -> 8; matrix products, arithmetic and copies ran while one was open for 0% -> 0% of each run, Pallas kernels for 0% -> 0%
where the time goes in v10:
time: 130 us; the launch traced here: 131 us
  starting transfers between devices  56.9 us (44%)
  blocking collectives  44.4 us (34%)
  waiting for transfers between devices  16.1 us (12%)
  Pallas kernels  11.6 us (9%)
  between operations  1.43 us (1%)
    all_to_all x2, blocking collectives, swapped(): return lax.all_to_all(x, TERM, 0, 0, tiled=True)  44.4 us
    ppermute x12, starting transfers between devices, exchanged_along(): sent = [lax.ppermute(pieces[k], axis, routes[k]) for k in range(1, size)]  24.3 us
    ppermute x3, starting transfers between devices, moved(): lax.ppermute(crossing, SECTOR, upward + downward)  14.6 us
    ppermute x4, waiting for transfers between devices, exchanged(): return x + lax.ppermute(x, axis, pairs)  11.6 us
    pallas_call x2, Pallas kernels, partial_image(): pl.pallas_call(body, out_shape=[jax.ShapeDtypeStruct(part, F32)] * (3 * c...  9.05 us
    ppermute x3, starting transfers between devices, moved(): lax.ppermute(local, SECTOR, swap)  8.02 us
    ppermute x4, starting transfers between devices, exchanged(): return x + lax.ppermute(x, axis, pairs)  6.42 us
    ppermute x12, waiting for transfers between devices, exchanged_along(): sent = [lax.ppermute(pieces[k], axis, routes[k]) for k in range(1, size)]  4.57 us
  transfers between devices with their start and end apart: 23, of which 8 were waited for; matrix products, arithmetic and copies ran while one was open for 0% of the time, Pallas kernels for 0%

profile of v10, /device:TPU:64, one launch (start us, length us, event | category | flops | bytes accessed | tf_op | source)
XLA Modules:
  0.0 130.6 jit_solution(1978339373516418731)
XLA Ops:
  1.3 0.0 copy-start.1
  1.3 0.0 copy-start
  1.3 4.8 %shard_map.85 = (f32[16,32,512]{2,1,0:T(8,128)S(1)}, f32[16,32,512]{2,1,0:T(8,128)S(1)}, f32[16,32,512]{2,1,0:T(8,128)S(1)}) custom-call(s32[1,1]{1,0:T(1,128)S(6)} %copy.9.count, s32[1,4]{1,0:T(1,128)} %target.3, f32[4,512,512]{2,1,0:T(8,128)} %bitcast.17, f32[4,512,512]{2,1,0:T(8,128)} %bitcast.19, f32[512,512]{1,0:T(8,128)} %bitcast.10), custom_call_target="tpu_custom_call" | custom-call | flops 6442450944 | bytes 8388608 | tf_op jit(solution)/shard_map/pallas_call | solution.py:187
  6.1 7.2 %collective-permute-start = (f32[16,32,512]{2,1,0:T(8,128)S(1)}, f32[16,32,512]{2,1,0:T(8,128)S(1)}, u32[]{:S(2)}, u32[]{:S(2)}) collective-permute-start(f32[16,32,512]{2,1,0:T(8,128)S(1)} %get-tuple-element.35), channel_id=1, source_target_pairs={{1,2},{3,4},{5,6},{7,8},{9,10},{11,12},{13,14},{2,1},{4,3},{6,5},{... | collective-permute-start | bytes 3145736 | tf_op jit(solution)/shard_map/ppermute | solution.py:27
  13.2 2.6 %collective-permute-start.1 = (f32[16,32,512]{2,1,0:T(8,128)S(1)}, f32[16,32,512]{2,1,0:T(8,128)S(1)}, u32[]{:S(2)}, u32[]{:S(2)}) collective-permute-start(f32[16,32,512]{2,1,0:T(8,128)S(1)} %get-tuple-element.36), channel_id=1, source_target_pairs={{0,1},{1,0},{2,3},{3,2},{4,5},{5,4},{6,7},{7,6},{8,9},{9,8},{10,11... | collective-permute-start | bytes 3145736 | tf_op jit(solution)/shard_map/ppermute | solution.py:27
  15.8 0.0 copy-done.1
  15.8 0.1 broadcast_in_dim.15
  15.9 23.9 %all_to_all.15.scaling = f32[16,32,512]{2,1,0:T(8,128)S(1)} all-to-all(f32[16,32,512]{2,1,0:T(8,128)S(1)} %broadcast_in_dim.15), channel_id=1, replica_groups=mesh['term_0'=4,'term_1'=4,'sector_0'=8,'sector_1'=2] {'term_0','term_1'}, dimensions={0} | all-to-all | bytes 2097152 | tf_op jit(solution)/shard_map/all_to_all | solution.py:38
  39.8 0.0 collective-permute-done.crossed
  39.8 0.0 collective-permute-done.1.local
  39.8 0.0 copy-done
  39.8 0.5 shard_map.86
  40.3 20.5 %all_to_all.16.arrived = f32[16,136,128]{2,1,0:T(8,128)S(1)} all-to-all(f32[16,136,128]{2,1,0:T(8,128)S(1)} %shard_map.86), channel_id=1, replica_groups=mesh['term_0'=4,'term_1'=4,'sector_0'=8,'sector_1'=2] {'term_0','term_1'}, dimensions={0} | all-to-all | bytes 2228224 | tf_op jit(solution)/shard_map/all_to_all | solution.py:38
  60.8 1.2 shard_map.87
  62.0 3.7 %all-to-all-start.2 = ((f32[16,32,512]{2,1,0:T(8,128)}), f32[16,32,512]{2,1,0:T(8,128)S(1)}, u32[]{:S(2)}, u32[]{:S(2)}) async-start(f32[16,32,512]{2,1,0:T(8,128)} %get-tuple-element.40), calls=%async_computation.2 | async-start | bytes 2097152 | tf_op jit(solution)/shard_map/all_to_all | solution.py:38
  65.7 0.1 collective-permute-start.2
  65.8 1.2 collective-permute-done.2
  66.9 3.1 %collective-permute-start.3 = (f32[8,128]{1,0:T(8,128)S(1)}, f32[8,128]{1,0:T(8,128)S(1)}, u32[]{:S(2)}, u32[]{:S(2)}) collective-permute-start(f32[8,128]{1,0:T(8,128)S(1)} %add.19), channel_id=1, source_target_pairs={{0,2},{2,0},{4,6},{6,4},{8,10},{10,8},{12,14},{14,12},{1,3},{3,1},... | collective-permute-start | bytes 12296 | tf_op jit(solution)/shard_map/ppermute | solution.py:52
  70.1 1.6 %collective-permute-done.3 = f32[8,128]{1,0:T(8,128)S(1)} collective-permute-done((f32[8,128]{1,0:T(8,128)S(1)}, f32[8,128]{1,0:T(8,128)S(1)}, u32[]{:S(2)}, u32[]{:S(2)}) %collective-permute-start.3) | collective-permute-done | bytes 4128 | tf_op jit(solution)/shard_map/ppermute | solution.py:52
  71.6 0.0 collective-permute-start.4
  71.6 4.5 %collective-permute-done.4 = f32[8,128]{1,0:T(8,128)S(1)} collective-permute-done((f32[8,128]{1,0:T(8,128)S(1)}, f32[8,128]{1,0:T(8,128)S(1)}, u32[]{:S(2)}, u32[]{:S(2)}) %collective-permute-start.4) | collective-permute-done | bytes 4128 | tf_op jit(solution)/shard_map/ppermute | solution.py:52
  76.2 3.2 %collective-permute-start.5 = (f32[8,128]{1,0:T(8,128)S(1)}, f32[8,128]{1,0:T(8,128)S(1)}, u32[]{:S(2)}, u32[]{:S(2)}) collective-permute-start(f32[8,128]{1,0:T(8,128)S(1)} %add.21), channel_id=1, source_target_pairs={{0,8},{2,10},{4,12},{6,14},{8,0},{10,2},{12,4},{14,6},{1,9},{3,11}... | collective-permute-start | bytes 12296 | tf_op jit(solution)/shard_map/ppermute | solution.py:52
  79.4 4.3 %collective-permute-done.5 = f32[8,128]{1,0:T(8,128)S(1)} collective-permute-done((f32[8,128]{1,0:T(8,128)S(1)}, f32[8,128]{1,0:T(8,128)S(1)}, u32[]{:S(2)}, u32[]{:S(2)}) %collective-permute-start.5) | collective-permute-done | bytes 4128 | tf_op jit(solution)/shard_map/ppermute | solution.py:52
  83.7 0.0 all-to-all-done.2.image
  83.7 4.3 %shard_map.88 = (f32[16,16,512]{2,1,0:T(8,128)S(1)}, f32[16,16,512]{2,1,0:T(8,128)S(1)}, f32[16,16,512]{2,1,0:T(8,128)S(1)}, f32[16,16,512]{2,1,0:T(8,128)S(1)},...) custom-call(s32[1,1]{1,0:T(1,128)S(6)} %copy.9.count, s32[1,4]{1,0:T(1,128)} %target.3, f32[4,512,512]{2,1,0:T(8,128)} %bitcast.18, ...), custom_call_target="tpu_custom_call" | custom-call | flops 6442450944 | bytes 8388608 | tf_op jit(solution)/shard_map/pallas_call | solution.py:187
  88.0 0.0 copy-start.2
  88.0 5.5 %collective-permute-start.6 = (f32[16,16,512]{2,1,0:T(8,128)S(1)}, f32[16,16,512]{2,1,0:T(8,128)S(1)}, u32[]{:S(2)}, u32[]{:S(2)}) collective-permute-start(f32[16,16,512]{2,1,0:T(8,128)S(1)} %get-tuple-element.42), channel_id=1, source_target_pairs={{1,2},{3,4},{5,6},{7,8},{9,10},{11,12},{13,14},{2,1},{4,3},{6,5},{... | collective-permute-start | bytes 1572872 | tf_op jit(solution)/shard_map/ppermute | solution.py:27
  93.5 4.5 %collective-permute-start.7 = (f32[16,16,512]{2,1,0:T(8,128)S(1)}, f32[16,16,512]{2,1,0:T(8,128)S(1)}, u32[]{:S(2)}, u32[]{:S(2)}) collective-permute-start(f32[16,16,512]{2,1,0:T(8,128)S(1)} %get-tuple-element.43), channel_id=1, source_target_pairs={{0,1},{1,0},{2,3},{3,2},{4,5},{5,4},{6,7},{7,6},{8,9},{9,8},{10,11... | collective-permute-start | bytes 1572872 | tf_op jit(solution)/shard_map/ppermute | solution.py:27
  98.0 1.9 %collective-permute-start.14 = (f32[16,16,512]{2,1,0:T(8,128)S(1)}, f32[16,16,512]{2,1,0:T(8,128)S(1)}, u32[]{:S(2)}, u32[]{:S(2)}) collective-permute-start(f32[16,16,512]{2,1,0:T(8,128)S(1)} %get-tuple-element.53), channel_id=1, source_target_pairs={{1,2},{3,4},{5,6},{7,8},{9,10},{11,12},{13,14},{2,1},{4,3},{6,5},{... | collective-permute-start | bytes 1572872 | tf_op jit(solution)/shard_map/ppermute | solution.py:27
  99.9 1.0 collective-permute-start.15
  100.9 0.0 collective-permute-done.6.crossed
  100.9 0.0 collective-permute-done.7.local
  100.9 0.1 shard_map.89
  100.9 1.8 %collective-permute-start.8 = (f32[64,512]{1,0:T(8,128)S(1)}, f32[64,512]{1,0:T(8,128)S(1)}, u32[]{:S(2)}, u32[]{:S(2)}) collective-permute-start(f32[64,512]{1,0:T(8,128)S(1)} %get-tuple-element.45), channel_id=1, source_target_pairs={{0,64},{64,128},{128,192},{192,0},{1,65},{65,129},{129,193},{193,1... | collective-permute-start | bytes 393224 | tf_op jit(solution)/shard_map/ppermute | solution.py:33
  102.8 5.1 %collective-permute-start.9 = (f32[64,512]{1,0:T(8,128)S(1)}, f32[64,512]{1,0:T(8,128)S(1)}, u32[]{:S(2)}, u32[]{:S(2)}) collective-permute-start(f32[64,512]{1,0:T(8,128)S(1)} %get-tuple-element.46), channel_id=1, source_target_pairs={{0,128},{64,192},{128,0},{192,64},{1,129},{65,193},{129,1},{193,65... | collective-permute-start | bytes 393224 | tf_op jit(solution)/shard_map/ppermute | solution.py:33
  107.8 2.5 %collective-permute-start.10 = (f32[64,512]{1,0:T(8,128)S(1)}, f32[64,512]{1,0:T(8,128)S(1)}, u32[]{:S(2)}, u32[]{:S(2)}) collective-permute-start(f32[64,512]{1,0:T(8,128)S(1)} %get-tuple-element.47), channel_id=1, source_target_pairs={{0,192},{64,0},{128,64},{192,128},{1,193},{65,1},{129,65},{193,129... | collective-permute-start | bytes 393224 | tf_op jit(solution)/shard_map/ppermute | solution.py:33
  110.4 0.0 collective-permute-done.14.crossed
  110.4 0.0 collective-permute-done.15.local
  110.4 0.1 shard_map.91
  110.5 1.6 %collective-permute-start.16 = (f32[64,512]{1,0:T(8,128)S(1)}, f32[64,512]{1,0:T(8,128)S(1)}, u32[]{:S(2)}, u32[]{:S(2)}) collective-permute-start(f32[64,512]{1,0:T(8,128)S(1)} %get-tuple-element.56), channel_id=1, source_target_pairs={{0,16},{16,32},{32,48},{48,0},{1,17},{17,33},{33,49},{49,1},{2,18}... | collective-permute-start | bytes 393224 | tf_op jit(solution)/shard_map/ppermute | solution.py:33
  112.0 2.7 %collective-permute-start.17 = (f32[64,512]{1,0:T(8,128)S(1)}, f32[64,512]{1,0:T(8,128)S(1)}, u32[]{:S(2)}, u32[]{:S(2)}) collective-permute-start(f32[64,512]{1,0:T(8,128)S(1)} %get-tuple-element.57), channel_id=1, source_target_pairs={{0,32},{16,48},{32,0},{48,16},{1,33},{17,49},{33,1},{49,17},{2,34}... | collective-permute-start | bytes 393224 | tf_op jit(solution)/shard_map/ppermute | solution.py:33
  114.7 0.0 collective-permute-done.8.refs_1_
  114.7 0.1 collective-permute-start.18
  114.8 0.0 collective-permute-done.9.refs_2_
  114.8 0.0 collective-permute-done.10.refs_3_
  114.8 2.2 %collective-permute-start.11 = (f32[16,512]{1,0:T(8,128)S(1)}, f32[16,512]{1,0:T(8,128)S(1)}, u32[]{:S(2)}, u32[]{:S(2)}) collective-permute-start(f32[16,512]{1,0:T(8,128)S(1)} %get-tuple-element.49), channel_id=1, source_target_pairs={{0,16},{16,32},{32,48},{48,0},{1,17},{17,33},{33,49},{49,1},{2,18}... | collective-permute-start | bytes 98312 | tf_op jit(solution)/shard_map/ppermute | solution.py:33
  117.0 3.1 %collective-permute-start.12 = (f32[16,512]{1,0:T(8,128)S(1)}, f32[16,512]{1,0:T(8,128)S(1)}, u32[]{:S(2)}, u32[]{:S(2)}) collective-permute-start(f32[16,512]{1,0:T(8,128)S(1)} %get-tuple-element.50), channel_id=1, source_target_pairs={{0,32},{16,48},{32,0},{48,16},{1,33},{17,49},{33,1},{49,17},{2,34}... | collective-permute-start | bytes 98312 | tf_op jit(solution)/shard_map/ppermute | solution.py:33
  120.1 0.0 collective-permute-done.16.refs_1_
  120.1 0.0 collective-permute-start.13
  120.1 1.7 %collective-permute-done.17.refs_2_ = f32[64,512]{1,0:T(8,128)S(1)} collective-permute-done((f32[64,512]{1,0:T(8,128)S(1)}, f32[64,512]{1,0:T(8,128)S(1)}, u32[]{:S(2)}, u32[]{:S(2)}) %collective-permute-start.17) | collective-permute-done | bytes 131104 | tf_op jit(solution)/shard_map/ppermute | solution.py:33
  121.8 0.0 collective-permute-done.18.refs_3_
  121.8 0.3 collective-permute-start.19
  122.2 3.8 %collective-permute-start.20 = (f32[16,512]{1,0:T(8,128)S(1)}, f32[16,512]{1,0:T(8,128)S(1)}, u32[]{:S(2)}, u32[]{:S(2)}) collective-permute-start(f32[16,512]{1,0:T(8,128)S(1)} %get-tuple-element.61), channel_id=1, source_target_pairs={{0,128},{64,192},{128,0},{192,64},{1,129},{65,193},{129,1},{193,65... | collective-permute-start | bytes 98312 | tf_op jit(solution)/shard_map/ppermute | solution.py:33
  126.0 0.0 collective-permute-done.11.refs_1_
  126.0 1.0 collective-permute-start.21
  127.1 0.0 collective-permute-done.12.refs_2_
  127.1 0.0 collective-permute-done.13.refs_3_
  127.1 0.1 collective-permute-done.19.refs_5_
  127.2 1.0 collective-permute-done.20.refs_6_
  128.3 1.7 %collective-permute-done.21.refs_7_ = f32[16,512]{1,0:T(8,128)S(1)} collective-permute-done((f32[16,512]{1,0:T(8,128)S(1)}, f32[16,512]{1,0:T(8,128)S(1)}, u32[]{:S(2)}, u32[]{:S(2)}) %collective-permute-start.21) | collective-permute-done | bytes 32800 | tf_op jit(solution)/shard_map/ppermute | solution.py:33
  130.0 0.0 copy-done.2
  130.0 0.7 shard_map.93
  (7 shorter events, 0.1 us)
Async XLA Ops:
  1.3 14.5 %copy-start.1 = (f32[1,32,512]{2,1,0:T(8,128)S(1)}, f32[1,32,512]{2,1,0:T(8,128)}, u32[]{:S(2)}) copy-start(f32[1,32,512]{2,1,0:T(8,128)} %param.7) | copy-start | bytes 196612
  1.3 38.5 %copy-start = (f32[1,512,512]{2,1,0:T(8,128)S(1)}, f32[1,512,512]{2,1,0:T(8,128)}, u32[]{:S(2)}) copy-start(f32[1,512,512]{2,1,0:T(8,128)} %param.6) | copy-start | bytes 3145732
  6.1 33.7 %collective-permute-start = (f32[16,32,512]{2,1,0:T(8,128)S(1)}, f32[16,32,512]{2,1,0:T(8,128)S(1)}, u32[]{:S(2)}, u32[]{:S(2)}) collective-permute-start(f32[16,32,512]{2,1,0:T(8,128)S(1)} %get-tuple-element.35), channel_id=1, source_target_pairs={{1,2},{3,4},{5,6},{7,8},{9,10},{11,12},{13,14},{2,1},{4,3},{6,5},{... | collective-permute-start | bytes 3145736 | tf_op jit(solution)/shard_map/ppermute | solution.py:27
  13.2 26.6 %collective-permute-start.1 = (f32[16,32,512]{2,1,0:T(8,128)S(1)}, f32[16,32,512]{2,1,0:T(8,128)S(1)}, u32[]{:S(2)}, u32[]{:S(2)}) collective-permute-start(f32[16,32,512]{2,1,0:T(8,128)S(1)} %get-tuple-element.36), channel_id=1, source_target_pairs={{0,1},{1,0},{2,3},{3,2},{4,5},{5,4},{6,7},{7,6},{8,9},{9,8},{10,11... | collective-permute-start | bytes 3145736 | tf_op jit(solution)/shard_map/ppermute | solution.py:27
  62.0 21.7 %all-to-all-start.2 = ((f32[16,32,512]{2,1,0:T(8,128)}), f32[16,32,512]{2,1,0:T(8,128)S(1)}, u32[]{:S(2)}, u32[]{:S(2)}) async-start(f32[16,32,512]{2,1,0:T(8,128)} %get-tuple-element.40), calls=%async_computation.2 | async-start | bytes 2097152 | tf_op jit(solution)/shard_map/all_to_all | solution.py:38
  65.7 1.3 collective-permute-start.2
  66.9 4.7 %collective-permute-start.3 = (f32[8,128]{1,0:T(8,128)S(1)}, f32[8,128]{1,0:T(8,128)S(1)}, u32[]{:S(2)}, u32[]{:S(2)}) collective-permute-start(f32[8,128]{1,0:T(8,128)S(1)} %add.19), channel_id=1, source_target_pairs={{0,2},{2,0},{4,6},{6,4},{8,10},{10,8},{12,14},{14,12},{1,3},{3,1},... | collective-permute-start | bytes 12296 | tf_op jit(solution)/shard_map/ppermute | solution.py:52
  71.6 4.5 %collective-permute-start.4 = (f32[8,128]{1,0:T(8,128)S(1)}, f32[8,128]{1,0:T(8,128)S(1)}, u32[]{:S(2)}, u32[]{:S(2)}) collective-permute-start(f32[8,128]{1,0:T(8,128)S(1)} %add.20), channel_id=1, source_target_pairs={{0,4},{2,6},{4,0},{6,2},{8,12},{10,14},{12,8},{14,10},{1,5},{3,7},... | collective-permute-start | bytes 12296 | tf_op jit(solution)/shard_map/ppermute | solution.py:52
  76.2 7.5 %collective-permute-start.5 = (f32[8,128]{1,0:T(8,128)S(1)}, f32[8,128]{1,0:T(8,128)S(1)}, u32[]{:S(2)}, u32[]{:S(2)}) collective-permute-start(f32[8,128]{1,0:T(8,128)S(1)} %add.21), channel_id=1, source_target_pairs={{0,8},{2,10},{4,12},{6,14},{8,0},{10,2},{12,4},{14,6},{1,9},{3,11}... | collective-permute-start | bytes 12296 | tf_op jit(solution)/shard_map/ppermute | solution.py:52
  88.0 42.0 %copy-start.2 = (f32[32,512]{1,0:T(8,128)S(1)}, f32[32,512]{1,0:T(8,128)}, u32[]{:S(2)}) copy-start(f32[32,512]{1,0:T(8,128)} %get-tuple-element.38.refs_9_) | copy-start | bytes 196612
  88.0 12.9 %collective-permute-start.6 = (f32[16,16,512]{2,1,0:T(8,128)S(1)}, f32[16,16,512]{2,1,0:T(8,128)S(1)}, u32[]{:S(2)}, u32[]{:S(2)}) collective-permute-start(f32[16,16,512]{2,1,0:T(8,128)S(1)} %get-tuple-element.42), channel_id=1, source_target_pairs={{1,2},{3,4},{5,6},{7,8},{9,10},{11,12},{13,14},{2,1},{4,3},{6,5},{... | collective-permute-start | bytes 1572872 | tf_op jit(solution)/shard_map/ppermute | solution.py:27
  93.5 7.4 %collective-permute-start.7 = (f32[16,16,512]{2,1,0:T(8,128)S(1)}, f32[16,16,512]{2,1,0:T(8,128)S(1)}, u32[]{:S(2)}, u32[]{:S(2)}) collective-permute-start(f32[16,16,512]{2,1,0:T(8,128)S(1)} %get-tuple-element.43), channel_id=1, source_target_pairs={{0,1},{1,0},{2,3},{3,2},{4,5},{5,4},{6,7},{7,6},{8,9},{9,8},{10,11... | collective-permute-start | bytes 1572872 | tf_op jit(solution)/shard_map/ppermute | solution.py:27
  98.0 12.4 %collective-permute-start.14 = (f32[16,16,512]{2,1,0:T(8,128)S(1)}, f32[16,16,512]{2,1,0:T(8,128)S(1)}, u32[]{:S(2)}, u32[]{:S(2)}) collective-permute-start(f32[16,16,512]{2,1,0:T(8,128)S(1)} %get-tuple-element.53), channel_id=1, source_target_pairs={{1,2},{3,4},{5,6},{7,8},{9,10},{11,12},{13,14},{2,1},{4,3},{6,5},{... | collective-permute-start | bytes 1572872 | tf_op jit(solution)/shard_map/ppermute | solution.py:27
  99.9 10.5 %collective-permute-start.15 = (f32[16,16,512]{2,1,0:T(8,128)S(1)}, f32[16,16,512]{2,1,0:T(8,128)S(1)}, u32[]{:S(2)}, u32[]{:S(2)}) collective-permute-start(f32[16,16,512]{2,1,0:T(8,128)S(1)} %get-tuple-element.54), channel_id=1, source_target_pairs={{0,1},{1,0},{2,3},{3,2},{4,5},{5,4},{6,7},{7,6},{8,9},{9,8},{10,11... | collective-permute-start | bytes 1572872 | tf_op jit(solution)/shard_map/ppermute | solution.py:27
  100.9 13.8 %collective-permute-start.8 = (f32[64,512]{1,0:T(8,128)S(1)}, f32[64,512]{1,0:T(8,128)S(1)}, u32[]{:S(2)}, u32[]{:S(2)}) collective-permute-start(f32[64,512]{1,0:T(8,128)S(1)} %get-tuple-element.45), channel_id=1, source_target_pairs={{0,64},{64,128},{128,192},{192,0},{1,65},{65,129},{129,193},{193,1... | collective-permute-start | bytes 393224 | tf_op jit(solution)/shard_map/ppermute | solution.py:33
  102.8 12.0 %collective-permute-start.9 = (f32[64,512]{1,0:T(8,128)S(1)}, f32[64,512]{1,0:T(8,128)S(1)}, u32[]{:S(2)}, u32[]{:S(2)}) collective-permute-start(f32[64,512]{1,0:T(8,128)S(1)} %get-tuple-element.46), channel_id=1, source_target_pairs={{0,128},{64,192},{128,0},{192,64},{1,129},{65,193},{129,1},{193,65... | collective-permute-start | bytes 393224 | tf_op jit(solution)/shard_map/ppermute | solution.py:33
  107.8 7.0 %collective-permute-start.10 = (f32[64,512]{1,0:T(8,128)S(1)}, f32[64,512]{1,0:T(8,128)S(1)}, u32[]{:S(2)}, u32[]{:S(2)}) collective-permute-start(f32[64,512]{1,0:T(8,128)S(1)} %get-tuple-element.47), channel_id=1, source_target_pairs={{0,192},{64,0},{128,64},{192,128},{1,193},{65,1},{129,65},{193,129... | collective-permute-start | bytes 393224 | tf_op jit(solution)/shard_map/ppermute | solution.py:33
  110.5 9.6 %collective-permute-start.16 = (f32[64,512]{1,0:T(8,128)S(1)}, f32[64,512]{1,0:T(8,128)S(1)}, u32[]{:S(2)}, u32[]{:S(2)}) collective-permute-start(f32[64,512]{1,0:T(8,128)S(1)} %get-tuple-element.56), channel_id=1, source_target_pairs={{0,16},{16,32},{32,48},{48,0},{1,17},{17,33},{33,49},{49,1},{2,18}... | collective-permute-start | bytes 393224 | tf_op jit(solution)/shard_map/ppermute | solution.py:33
  112.0 9.8 %collective-permute-start.17 = (f32[64,512]{1,0:T(8,128)S(1)}, f32[64,512]{1,0:T(8,128)S(1)}, u32[]{:S(2)}, u32[]{:S(2)}) collective-permute-start(f32[64,512]{1,0:T(8,128)S(1)} %get-tuple-element.57), channel_id=1, source_target_pairs={{0,32},{16,48},{32,0},{48,16},{1,33},{17,49},{33,1},{49,17},{2,34}... | collective-permute-start | bytes 393224 | tf_op jit(solution)/shard_map/ppermute | solution.py:33
  114.7 7.1 %collective-permute-start.18 = (f32[64,512]{1,0:T(8,128)S(1)}, f32[64,512]{1,0:T(8,128)S(1)}, u32[]{:S(2)}, u32[]{:S(2)}) collective-permute-start(f32[64,512]{1,0:T(8,128)S(1)} %get-tuple-element.58), channel_id=1, source_target_pairs={{0,48},{16,0},{32,16},{48,32},{1,49},{17,1},{33,17},{49,33},{2,50}... | collective-permute-start | bytes 393224 | tf_op jit(solution)/shard_map/ppermute | solution.py:33
  114.8 11.2 %collective-permute-start.11 = (f32[16,512]{1,0:T(8,128)S(1)}, f32[16,512]{1,0:T(8,128)S(1)}, u32[]{:S(2)}, u32[]{:S(2)}) collective-permute-start(f32[16,512]{1,0:T(8,128)S(1)} %get-tuple-element.49), channel_id=1, source_target_pairs={{0,16},{16,32},{32,48},{48,0},{1,17},{17,33},{33,49},{49,1},{2,18}... | collective-permute-start | bytes 98312 | tf_op jit(solution)/shard_map/ppermute | solution.py:33
  117.0 10.0 %collective-permute-start.12 = (f32[16,512]{1,0:T(8,128)S(1)}, f32[16,512]{1,0:T(8,128)S(1)}, u32[]{:S(2)}, u32[]{:S(2)}) collective-permute-start(f32[16,512]{1,0:T(8,128)S(1)} %get-tuple-element.50), channel_id=1, source_target_pairs={{0,32},{16,48},{32,0},{48,16},{1,33},{17,49},{33,1},{49,17},{2,34}... | collective-permute-start | bytes 98312 | tf_op jit(solution)/shard_map/ppermute | solution.py:33
  120.1 7.0 %collective-permute-start.13 = (f32[16,512]{1,0:T(8,128)S(1)}, f32[16,512]{1,0:T(8,128)S(1)}, u32[]{:S(2)}, u32[]{:S(2)}) collective-permute-start(f32[16,512]{1,0:T(8,128)S(1)} %get-tuple-element.51), channel_id=1, source_target_pairs={{0,48},{16,0},{32,16},{48,32},{1,49},{17,1},{33,17},{49,33},{2,50}... | collective-permute-start | bytes 98312 | tf_op jit(solution)/shard_map/ppermute | solution.py:33
  121.8 5.4 %collective-permute-start.19 = (f32[16,512]{1,0:T(8,128)S(1)}, f32[16,512]{1,0:T(8,128)S(1)}, u32[]{:S(2)}, u32[]{:S(2)}) collective-permute-start(f32[16,512]{1,0:T(8,128)S(1)} %get-tuple-element.60), channel_id=1, source_target_pairs={{0,64},{64,128},{128,192},{192,0},{1,65},{65,129},{129,193},{193,1... | collective-permute-start | bytes 98312 | tf_op jit(solution)/shard_map/ppermute | solution.py:33
  122.2 6.1 %collective-permute-start.20 = (f32[16,512]{1,0:T(8,128)S(1)}, f32[16,512]{1,0:T(8,128)S(1)}, u32[]{:S(2)}, u32[]{:S(2)}) collective-permute-start(f32[16,512]{1,0:T(8,128)S(1)} %get-tuple-element.61), channel_id=1, source_target_pairs={{0,128},{64,192},{128,0},{192,64},{1,129},{65,193},{129,1},{193,65... | collective-permute-start | bytes 98312 | tf_op jit(solution)/shard_map/ppermute | solution.py:33
  126.0 3.9 %collective-permute-start.21 = (f32[16,512]{1,0:T(8,128)S(1)}, f32[16,512]{1,0:T(8,128)S(1)}, u32[]{:S(2)}, u32[]{:S(2)}) collective-permute-start(f32[16,512]{1,0:T(8,128)S(1)} %get-tuple-element.62), channel_id=1, source_target_pairs={{0,192},{64,0},{128,64},{192,128},{1,193},{65,1},{129,65},{193,129... | collective-permute-start | bytes 98312 | tf_op jit(solution)/shard_map/ppermute | solution.py:33

commit v11 on v10

--- a/solution.py
+++ b/solution.py
@@ -208,34 +208,32 @@
     )(counts, targets, left_stack, right_stack, *fields)
 
 
-def place(half, along, across, size):
-    return along * size + across if half == 0 else across * size + along
-
-
-def spread(half, kept, crossed, local, *pieces):
+def spread(kept, crossed, local, *pieces):
     rows = kept.shape[1]
     size = len(pieces)
-    me = lax.axis_index(TERM[half])
+    me = lax.axis_index(TERM[0])
     for k, piece in enumerate(pieces):
+        first = lax.rem(me + k, size) * size
         for across in range(size):
-            peer = place(half, lax.rem(me + k, size), across, size)
+            peer = first + across
             total = kept[peer] + (crossed[peer] + local[peer])
             piece[across * rows : (across + 1) * rows] = total
 
 
-def relay(axis, rows, *refs):
-    size = len(refs) // 2
-    arrived, pieces = refs[:size], refs[size:]
-    me = lax.axis_index(axis)
+def summed(refs, lines):
+    return functools.reduce(lambda x, y: x + y, [ref[lines] for ref in refs])
+
+
+def relay(*refs):
+    size = len(refs) // (HALVES + 1)
+    arrived, pieces = refs[: HALVES * size], refs[HALVES * size :]
+    rows = pieces[0].shape[0] // HALVES
+    me = lax.axis_index(TERM[1])
     for k, piece in enumerate(pieces):
         lines = pl.ds(pl.multiple_of(lax.rem(me + k, size) * rows, rows), rows)
-        piece[...] = functools.reduce(lambda x, y: x + y, [ref[lines] for ref in arrived])
-
-
-def landed(refs):
-    size = len(refs) // HALVES
-    groups = [refs[h * size : (h + 1) * size] for h in range(HALVES)]
-    return [functools.reduce(lambda x, y: x + y, [r[...] for r in g]) for g in groups]
+        for half in range(HALVES):
+            group = arrived[half * size : (half + 1) * size]
+            piece[half * rows : (half + 1) * rows] = summed(group, lines)
 
 
 def tiles(x, slab, width):
@@ -278,21 +276,9 @@
 
 def second_landing(*refs):
     *arrived, sums, first_image, scaling, own, correction, image = refs
-    rows = image.shape[0] // HALVES
     coefs = coefficients(sums)
     correction[...] = corrected(coefs, own[...], scaling[...], first_image[...])
-    for half, total in enumerate(landed(arrived)):
-        image[half * rows : (half + 1) * rows] = total
-
-
-def relayed(half, pieces, rows):
-    arrived = exchanged_along(pieces, TERM[half])
-    other = TERM[1 - half]
-    shape = (rows, pieces[0].shape[1])
-    onward = small_call(
-        functools.partial(relay, other, rows), [shape] * len(pieces), arrived
-    )
-    return exchanged_along(onward, other)
+    image[...] = summed(arrived, ...)
 
 
 def small_call(body, out_shapes, args, scratch=(), spaces=None):
@@ -358,11 +344,11 @@
     arrived = []
     for half in range(HALVES):
         pieces = small_call(
-            functools.partial(spread, half),
-            [(size * rows, width)] * size,
-            [kept[half], *moves[half]],
+            spread, [(size * rows, width)] * size, [kept[half], *moves[half]]
         )
-        arrived += relayed(half, pieces, rows)
+        arrived += exchanged_along(pieces, TERM[0])
+    pieces = small_call(relay, [(slab, width)] * size, arrived)
+    arrived = exchanged_along(pieces, TERM[1])
     own = lax.dynamic_index_in_dim(blocked, lax.axis_index(TERM), 0, keepdims=False)
     correction, second_image = small_call(
         second_landing,

time: 130 us -> 131 us (level)
  starting transfers between devices: 56.9 us -> 46.4 us
  waiting for transfers between devices: 16.1 us -> 22.3 us
  blocking collectives: 44.4 us -> 48.8 us
    ppermute x12 -> x9, starting transfers between devices: 24.3 us -> 17.4 us  [exchanged_along(): sent = [lax.ppermute(pieces[k], axis, routes[k]) for k in range(1, size)]]
    ppermute x3, starting transfers between devices: 14.6 us -> 7.76 us  [moved(): lax.ppermute(crossing, SECTOR, upward + downward)]
    ppermute x12 -> x9, waiting for transfers between devices: 4.57 us -> 10.9 us  [exchanged_along(): sent = [lax.ppermute(pieces[k], axis, routes[k]) for k in range(1, size)]]
    all_to_all x2, blocking collectives: 44.4 us -> 48.8 us  [swapped(): return lax.all_to_all(x, TERM, 0, 0, tiled=True)]
    ppermute x4, starting transfers between devices: 6.42 us -> 8.03 us  [exchanged(): return x + lax.ppermute(x, axis, pairs)]
    ppermute x3, starting transfers between devices: 8.02 us -> 9.53 us  [moved(): lax.ppermute(local, SECTOR, swap)]
  transfers between devices with their start and end apart: 23 -> 20, of which waited for: 8 -> 11; matrix products, arithmetic and copies ran while one was open for 0% -> 0% of each run, Pallas kernels for 0% -> 0%
where the time goes in v11:
time: 131 us
  blocking collectives  48.8 us (37%)
  starting transfers between devices  46.4 us (35%)
  waiting for transfers between devices  22.3 us (17%)
  Pallas kernels  11.7 us (9%)
  between operations  1.43 us (1%)
    all_to_all x2, blocking collectives, swapped(): return lax.all_to_all(x, TERM, 0, 0, tiled=True)  48.8 us
    ppermute x9, starting transfers between devices, exchanged_along(): sent = [lax.ppermute(pieces[k], axis, routes[k]) for k in range(1, size)]  17.4 us
    ppermute x4, waiting for transfers between devices, exchanged(): return x + lax.ppermute(x, axis, pairs)  11.3 us
    ppermute x9, waiting for transfers between devices, exchanged_along(): sent = [lax.ppermute(pieces[k], axis, routes[k]) for k in range(1, size)]  10.9 us
    ppermute x3, starting transfers between devices, moved(): lax.ppermute(local, SECTOR, swap)  9.53 us
    pallas_call x2, Pallas kernels, partial_image(): pl.pallas_call(body, out_shape=[jax.ShapeDtypeStruct(part, F32)] * (3 * c...  9.16 us
    ppermute x4, starting transfers between devices, exchanged(): return x + lax.ppermute(x, axis, pairs)  8.03 us
    ppermute x3, starting transfers between devices, moved(): lax.ppermute(crossing, SECTOR, upward + downward)  7.76 us
  transfers between devices with their start and end apart: 20, of which 11 were waited for; matrix products, arithmetic and copies ran while one was open for 0% of the time, Pallas kernels for 0%

profile of v11, /device:TPU:64, one launch (start us, length us, event | category | flops | bytes accessed | tf_op | source)
XLA Modules:
  0.0 130.8 jit_solution(1329087834293264656)
XLA Ops:
  1.3 0.0 copy-start.1
  1.3 0.0 copy-start
  1.3 4.8 %shard_map.85 = (f32[16,32,512]{2,1,0:T(8,128)S(1)}, f32[16,32,512]{2,1,0:T(8,128)S(1)}, f32[16,32,512]{2,1,0:T(8,128)S(1)}) custom-call(s32[1,1]{1,0:T(1,128)S(6)} %copy.9.count, s32[1,4]{1,0:T(1,128)} %target.3, f32[4,512,512]{2,1,0:T(8,128)} %bitcast.17, f32[4,512,512]{2,1,0:T(8,128)} %bitcast.19, f32[512,512]{1,0:T(8,128)} %bitcast.10), custom_call_target="tpu_custom_call" | custom-call | flops 6442450944 | bytes 8388608 | tf_op jit(solution)/shard_map/pallas_call | solution.py:187
  6.1 1.9 %collective-permute-start = (f32[16,32,512]{2,1,0:T(8,128)S(1)}, f32[16,32,512]{2,1,0:T(8,128)S(1)}, u32[]{:S(2)}, u32[]{:S(2)}) collective-permute-start(f32[16,32,512]{2,1,0:T(8,128)S(1)} %get-tuple-element.31), channel_id=1, source_target_pairs={{1,2},{3,4},{5,6},{7,8},{9,10},{11,12},{13,14},{2,1},{4,3},{6,5},{... | collective-permute-start | bytes 3145736 | tf_op jit(solution)/shard_map/ppermute | solution.py:27
  8.0 2.1 %collective-permute-start.1 = (f32[16,32,512]{2,1,0:T(8,128)S(1)}, f32[16,32,512]{2,1,0:T(8,128)S(1)}, u32[]{:S(2)}, u32[]{:S(2)}) collective-permute-start(f32[16,32,512]{2,1,0:T(8,128)S(1)} %get-tuple-element.32), channel_id=1, source_target_pairs={{0,1},{1,0},{2,3},{3,2},{4,5},{5,4},{6,7},{7,6},{8,9},{9,8},{10,11... | collective-permute-start | bytes 3145736 | tf_op jit(solution)/shard_map/ppermute | solution.py:27
  10.2 0.0 copy-done.1
  10.2 0.1 broadcast_in_dim.15
  10.3 28.2 %all_to_all.15.scaling = f32[16,32,512]{2,1,0:T(8,128)S(1)} all-to-all(f32[16,32,512]{2,1,0:T(8,128)S(1)} %broadcast_in_dim.15), channel_id=1, replica_groups=mesh['term_0'=4,'term_1'=4,'sector_0'=8,'sector_1'=2] {'term_0','term_1'}, dimensions={0} | all-to-all | bytes 2097152 | tf_op jit(solution)/shard_map/all_to_all | solution.py:38
  38.5 0.0 collective-permute-done.crossed
  38.5 0.0 collective-permute-done.1.local
  38.5 0.0 copy-done
  38.5 0.5 shard_map.86
  39.0 20.6 %all_to_all.16.arrived = f32[16,136,128]{2,1,0:T(8,128)S(1)} all-to-all(f32[16,136,128]{2,1,0:T(8,128)S(1)} %shard_map.86), channel_id=1, replica_groups=mesh['term_0'=4,'term_1'=4,'sector_0'=8,'sector_1'=2] {'term_0','term_1'}, dimensions={0} | all-to-all | bytes 2228224 | tf_op jit(solution)/shard_map/all_to_all | solution.py:38
  59.6 1.2 shard_map.87
  60.8 3.7 %all-to-all-start.2 = ((f32[16,32,512]{2,1,0:T(8,128)}), f32[16,32,512]{2,1,0:T(8,128)S(1)}, u32[]{:S(2)}, u32[]{:S(2)}) async-start(f32[16,32,512]{2,1,0:T(8,128)} %get-tuple-element.36), calls=%async_computation.2 | async-start | bytes 2097152 | tf_op jit(solution)/shard_map/all_to_all | solution.py:38
  64.5 0.1 collective-permute-start.2
  64.6 1.2 collective-permute-done.2
  65.7 4.5 %collective-permute-start.3 = (f32[8,128]{1,0:T(8,128)S(1)}, f32[8,128]{1,0:T(8,128)S(1)}, u32[]{:S(2)}, u32[]{:S(2)}) collective-permute-start(f32[8,128]{1,0:T(8,128)S(1)} %add.19), channel_id=1, source_target_pairs={{0,2},{2,0},{4,6},{6,4},{8,10},{10,8},{12,14},{14,12},{1,3},{3,1},... | collective-permute-start | bytes 12296 | tf_op jit(solution)/shard_map/ppermute | solution.py:52
  70.2 1.6 %collective-permute-done.3 = f32[8,128]{1,0:T(8,128)S(1)} collective-permute-done((f32[8,128]{1,0:T(8,128)S(1)}, f32[8,128]{1,0:T(8,128)S(1)}, u32[]{:S(2)}, u32[]{:S(2)}) %collective-permute-start.3) | collective-permute-done | bytes 4128 | tf_op jit(solution)/shard_map/ppermute | solution.py:52
  71.8 0.0 collective-permute-start.4
  71.8 4.5 %collective-permute-done.4 = f32[8,128]{1,0:T(8,128)S(1)} collective-permute-done((f32[8,128]{1,0:T(8,128)S(1)}, f32[8,128]{1,0:T(8,128)S(1)}, u32[]{:S(2)}, u32[]{:S(2)}) %collective-permute-start.4) | collective-permute-done | bytes 4128 | tf_op jit(solution)/shard_map/ppermute | solution.py:52
  76.3 3.4 %collective-permute-start.5 = (f32[8,128]{1,0:T(8,128)S(1)}, f32[8,128]{1,0:T(8,128)S(1)}, u32[]{:S(2)}, u32[]{:S(2)}) collective-permute-start(f32[8,128]{1,0:T(8,128)S(1)} %add.21), channel_id=1, source_target_pairs={{0,8},{2,10},{4,12},{6,14},{8,0},{10,2},{12,4},{14,6},{1,9},{3,11}... | collective-permute-start | bytes 12296 | tf_op jit(solution)/shard_map/ppermute | solution.py:52
  79.8 4.1 %collective-permute-done.5 = f32[8,128]{1,0:T(8,128)S(1)} collective-permute-done((f32[8,128]{1,0:T(8,128)S(1)}, f32[8,128]{1,0:T(8,128)S(1)}, u32[]{:S(2)}, u32[]{:S(2)}) %collective-permute-start.5) | collective-permute-done | bytes 4128 | tf_op jit(solution)/shard_map/ppermute | solution.py:52
  83.9 0.0 all-to-all-done.2.image
  83.9 4.3 %shard_map.88 = (f32[16,16,512]{2,1,0:T(8,128)S(1)}, f32[16,16,512]{2,1,0:T(8,128)S(1)}, f32[16,16,512]{2,1,0:T(8,128)S(1)}, f32[16,16,512]{2,1,0:T(8,128)S(1)},...) custom-call(s32[1,1]{1,0:T(1,128)S(6)} %copy.9.count, s32[1,4]{1,0:T(1,128)} %target.3, f32[4,512,512]{2,1,0:T(8,128)} %bitcast.18, ...), custom_call_target="tpu_custom_call" | custom-call | flops 6442450944 | bytes 8388608 | tf_op jit(solution)/shard_map/pallas_call | solution.py:187
  88.2 0.0 copy-start.2
  88.2 2.1 %collective-permute-start.6 = (f32[16,16,512]{2,1,0:T(8,128)S(1)}, f32[16,16,512]{2,1,0:T(8,128)S(1)}, u32[]{:S(2)}, u32[]{:S(2)}) collective-permute-start(f32[16,16,512]{2,1,0:T(8,128)S(1)} %get-tuple-element.38), channel_id=1, source_target_pairs={{1,2},{3,4},{5,6},{7,8},{9,10},{11,12},{13,14},{2,1},{4,3},{6,5},{... | collective-permute-start | bytes 1572872 | tf_op jit(solution)/shard_map/ppermute | solution.py:27
  90.3 2.2 %collective-permute-start.7 = (f32[16,16,512]{2,1,0:T(8,128)S(1)}, f32[16,16,512]{2,1,0:T(8,128)S(1)}, u32[]{:S(2)}, u32[]{:S(2)}) collective-permute-start(f32[16,16,512]{2,1,0:T(8,128)S(1)} %get-tuple-element.39), channel_id=1, source_target_pairs={{0,1},{1,0},{2,3},{3,2},{4,5},{5,4},{6,7},{7,6},{8,9},{9,8},{10,11... | collective-permute-start | bytes 1572872 | tf_op jit(solution)/shard_map/ppermute | solution.py:27
  92.5 3.8 %collective-permute-start.11 = (f32[16,16,512]{2,1,0:T(8,128)S(1)}, f32[16,16,512]{2,1,0:T(8,128)S(1)}, u32[]{:S(2)}, u32[]{:S(2)}) collective-permute-start(f32[16,16,512]{2,1,0:T(8,128)S(1)} %get-tuple-element.45), channel_id=1, source_target_pairs={{1,2},{3,4},{5,6},{7,8},{9,10},{11,12},{13,14},{2,1},{4,3},{6,5},{... | collective-permute-start | bytes 1572872 | tf_op jit(solution)/shard_map/ppermute | solution.py:27
  96.3 5.2 %collective-permute-start.12 = (f32[16,16,512]{2,1,0:T(8,128)S(1)}, f32[16,16,512]{2,1,0:T(8,128)S(1)}, u32[]{:S(2)}, u32[]{:S(2)}) collective-permute-start(f32[16,16,512]{2,1,0:T(8,128)S(1)} %get-tuple-element.46), channel_id=1, source_target_pairs={{0,1},{1,0},{2,3},{3,2},{4,5},{5,4},{6,7},{7,6},{8,9},{9,8},{10,11... | collective-permute-start | bytes 1572872 | tf_op jit(solution)/shard_map/ppermute | solution.py:27
  101.5 0.0 collective-permute-done.6.crossed
  101.5 0.0 collective-permute-done.7.local
  101.5 0.1 shard_map.89
  101.6 0.1 collective-permute-start.8
  101.7 3.7 %collective-permute-start.9 = (f32[64,512]{1,0:T(8,128)S(1)}, f32[64,512]{1,0:T(8,128)S(1)}, u32[]{:S(2)}, u32[]{:S(2)}) collective-permute-start(f32[64,512]{1,0:T(8,128)S(1)} %get-tuple-element.42), channel_id=1, source_target_pairs={{0,128},{64,192},{128,0},{192,64},{1,129},{65,193},{129,1},{193,65... | collective-permute-start | bytes 393224 | tf_op jit(solution)/shard_map/ppermute | solution.py:33
  105.4 0.0 collective-permute-start.10
  105.4 0.0 collective-permute-done.11.crossed
  105.4 0.0 collective-permute-done.12.local
  105.4 0.1 shard_map.90
  105.5 2.1 %collective-permute-start.13 = (f32[64,512]{1,0:T(8,128)S(1)}, f32[64,512]{1,0:T(8,128)S(1)}, u32[]{:S(2)}, u32[]{:S(2)}) collective-permute-start(f32[64,512]{1,0:T(8,128)S(1)} %get-tuple-element.48), channel_id=1, source_target_pairs={{0,64},{64,128},{128,192},{192,0},{1,65},{65,129},{129,193},{193,1... | collective-permute-start | bytes 393224 | tf_op jit(solution)/shard_map/ppermute | solution.py:33
  107.6 3.4 %collective-permute-start.14 = (f32[64,512]{1,0:T(8,128)S(1)}, f32[64,512]{1,0:T(8,128)S(1)}, u32[]{:S(2)}, u32[]{:S(2)}) collective-permute-start(f32[64,512]{1,0:T(8,128)S(1)} %get-tuple-element.49), channel_id=1, source_target_pairs={{0,128},{64,192},{128,0},{192,64},{1,129},{65,193},{129,1},{193,65... | collective-permute-start | bytes 393224 | tf_op jit(solution)/shard_map/ppermute | solution.py:33
  111.0 0.0 collective-permute-done.8.refs_1_
  111.0 0.7 collective-permute-start.15
  111.8 0.0 collective-permute-done.9.refs_2_
  111.8 1.2 collective-permute-done.10.refs_3_
  113.0 3.0 %collective-permute-done.13.refs_5_ = f32[64,512]{1,0:T(8,128)S(1)} collective-permute-done((f32[64,512]{1,0:T(8,128)S(1)}, f32[64,512]{1,0:T(8,128)S(1)}, u32[]{:S(2)}, u32[]{:S(2)}) %collective-permute-start.13) | collective-permute-done | bytes 131104 | tf_op jit(solution)/shard_map/ppermute | solution.py:33
  116.0 1.3 collective-permute-done.14.refs_6_
  117.3 1.1 collective-permute-done.15.refs_7_
  118.5 2.9 %collective-permute-start.16 = (f32[32,512]{1,0:T(8,128)S(1)}, f32[32,512]{1,0:T(8,128)S(1)}, u32[]{:S(2)}, u32[]{:S(2)}) collective-permute-start(f32[32,512]{1,0:T(8,128)S(1)} %get-tuple-element.52), channel_id=1, source_target_pairs={{0,16},{16,32},{32,48},{48,0},{1,17},{17,33},{33,49},{49,1},{2,18}... | collective-permute-start | bytes 196616 | tf_op jit(solution)/shard_map/ppermute | solution.py:33
  121.4 4.5 %collective-permute-start.17 = (f32[32,512]{1,0:T(8,128)S(1)}, f32[32,512]{1,0:T(8,128)S(1)}, u32[]{:S(2)}, u32[]{:S(2)}) collective-permute-start(f32[32,512]{1,0:T(8,128)S(1)} %get-tuple-element.53), channel_id=1, source_target_pairs={{0,32},{16,48},{32,0},{48,16},{1,33},{17,49},{33,1},{49,17},{2,34}... | collective-permute-start | bytes 196616 | tf_op jit(solution)/shard_map/ppermute | solution.py:33
  125.8 0.0 collective-permute-start.18
  125.8 0.8 collective-permute-done.16.refs_1_
  126.6 2.3 %collective-permute-done.17.refs_2_ = f32[32,512]{1,0:T(8,128)S(1)} collective-permute-done((f32[32,512]{1,0:T(8,128)S(1)}, f32[32,512]{1,0:T(8,128)S(1)}, u32[]{:S(2)}, u32[]{:S(2)}) %collective-permute-start.17) | collective-permute-done | bytes 65568 | tf_op jit(solution)/shard_map/ppermute | solution.py:33
  128.9 1.2 collective-permute-done.18.refs_3_
  130.1 0.0 copy-done.2
  130.1 0.7 shard_map.92
  (6 shorter events, 0.1 us)
Async XLA Ops:
  1.3 8.9 %copy-start.1 = (f32[1,32,512]{2,1,0:T(8,128)S(1)}, f32[1,32,512]{2,1,0:T(8,128)}, u32[]{:S(2)}) copy-start(f32[1,32,512]{2,1,0:T(8,128)} %param.7) | copy-start | bytes 196612
  1.3 37.2 %copy-start = (f32[1,512,512]{2,1,0:T(8,128)S(1)}, f32[1,512,512]{2,1,0:T(8,128)}, u32[]{:S(2)}) copy-start(f32[1,512,512]{2,1,0:T(8,128)} %param.6) | copy-start | bytes 3145732
  6.1 32.3 %collective-permute-start = (f32[16,32,512]{2,1,0:T(8,128)S(1)}, f32[16,32,512]{2,1,0:T(8,128)S(1)}, u32[]{:S(2)}, u32[]{:S(2)}) collective-permute-start(f32[16,32,512]{2,1,0:T(8,128)S(1)} %get-tuple-element.31), channel_id=1, source_target_pairs={{1,2},{3,4},{5,6},{7,8},{9,10},{11,12},{13,14},{2,1},{4,3},{6,5},{... | collective-permute-start | bytes 3145736 | tf_op jit(solution)/shard_map/ppermute | solution.py:27
  8.0 30.4 %collective-permute-start.1 = (f32[16,32,512]{2,1,0:T(8,128)S(1)}, f32[16,32,512]{2,1,0:T(8,128)S(1)}, u32[]{:S(2)}, u32[]{:S(2)}) collective-permute-start(f32[16,32,512]{2,1,0:T(8,128)S(1)} %get-tuple-element.32), channel_id=1, source_target_pairs={{0,1},{1,0},{2,3},{3,2},{4,5},{5,4},{6,7},{7,6},{8,9},{9,8},{10,11... | collective-permute-start | bytes 3145736 | tf_op jit(solution)/shard_map/ppermute | solution.py:27
  60.8 23.1 %all-to-all-start.2 = ((f32[16,32,512]{2,1,0:T(8,128)}), f32[16,32,512]{2,1,0:T(8,128)S(1)}, u32[]{:S(2)}, u32[]{:S(2)}) async-start(f32[16,32,512]{2,1,0:T(8,128)} %get-tuple-element.36), calls=%async_computation.2 | async-start | bytes 2097152 | tf_op jit(solution)/shard_map/all_to_all | solution.py:38
  64.5 1.3 collective-permute-start.2
  65.7 6.1 %collective-permute-start.3 = (f32[8,128]{1,0:T(8,128)S(1)}, f32[8,128]{1,0:T(8,128)S(1)}, u32[]{:S(2)}, u32[]{:S(2)}) collective-permute-start(f32[8,128]{1,0:T(8,128)S(1)} %add.19), channel_id=1, source_target_pairs={{0,2},{2,0},{4,6},{6,4},{8,10},{10,8},{12,14},{14,12},{1,3},{3,1},... | collective-permute-start | bytes 12296 | tf_op jit(solution)/shard_map/ppermute | solution.py:52
  71.8 4.5 %collective-permute-start.4 = (f32[8,128]{1,0:T(8,128)S(1)}, f32[8,128]{1,0:T(8,128)S(1)}, u32[]{:S(2)}, u32[]{:S(2)}) collective-permute-start(f32[8,128]{1,0:T(8,128)S(1)} %add.20), channel_id=1, source_target_pairs={{0,4},{2,6},{4,0},{6,2},{8,12},{10,14},{12,8},{14,10},{1,5},{3,7},... | collective-permute-start | bytes 12296 | tf_op jit(solution)/shard_map/ppermute | solution.py:52
  76.3 7.5 %collective-permute-start.5 = (f32[8,128]{1,0:T(8,128)S(1)}, f32[8,128]{1,0:T(8,128)S(1)}, u32[]{:S(2)}, u32[]{:S(2)}) collective-permute-start(f32[8,128]{1,0:T(8,128)S(1)} %add.21), channel_id=1, source_target_pairs={{0,8},{2,10},{4,12},{6,14},{8,0},{10,2},{12,4},{14,6},{1,9},{3,11}... | collective-permute-start | bytes 12296 | tf_op jit(solution)/shard_map/ppermute | solution.py:52
  88.2 41.9 %copy-start.2 = (f32[32,512]{1,0:T(8,128)S(1)}, f32[32,512]{1,0:T(8,128)}, u32[]{:S(2)}) copy-start(f32[32,512]{1,0:T(8,128)} %get-tuple-element.34.refs_5_) | copy-start | bytes 196612
  88.2 13.3 %collective-permute-start.6 = (f32[16,16,512]{2,1,0:T(8,128)S(1)}, f32[16,16,512]{2,1,0:T(8,128)S(1)}, u32[]{:S(2)}, u32[]{:S(2)}) collective-permute-start(f32[16,16,512]{2,1,0:T(8,128)S(1)} %get-tuple-element.38), channel_id=1, source_target_pairs={{1,2},{3,4},{5,6},{7,8},{9,10},{11,12},{13,14},{2,1},{4,3},{6,5},{... | collective-permute-start | bytes 1572872 | tf_op jit(solution)/shard_map/ppermute | solution.py:27
  90.3 11.2 %collective-permute-start.7 = (f32[16,16,512]{2,1,0:T(8,128)S(1)}, f32[16,16,512]{2,1,0:T(8,128)S(1)}, u32[]{:S(2)}, u32[]{:S(2)}) collective-permute-start(f32[16,16,512]{2,1,0:T(8,128)S(1)} %get-tuple-element.39), channel_id=1, source_target_pairs={{0,1},{1,0},{2,3},{3,2},{4,5},{5,4},{6,7},{7,6},{8,9},{9,8},{10,11... | collective-permute-start | bytes 1572872 | tf_op jit(solution)/shard_map/ppermute | solution.py:27
  92.5 12.9 %collective-permute-start.11 = (f32[16,16,512]{2,1,0:T(8,128)S(1)}, f32[16,16,512]{2,1,0:T(8,128)S(1)}, u32[]{:S(2)}, u32[]{:S(2)}) collective-permute-start(f32[16,16,512]{2,1,0:T(8,128)S(1)} %get-tuple-element.45), channel_id=1, source_target_pairs={{1,2},{3,4},{5,6},{7,8},{9,10},{11,12},{13,14},{2,1},{4,3},{6,5},{... | collective-permute-start | bytes 1572872 | tf_op jit(solution)/shard_map/ppermute | solution.py:27
  96.3 9.1 %collective-permute-start.12 = (f32[16,16,512]{2,1,0:T(8,128)S(1)}, f32[16,16,512]{2,1,0:T(8,128)S(1)}, u32[]{:S(2)}, u32[]{:S(2)}) collective-permute-start(f32[16,16,512]{2,1,0:T(8,128)S(1)} %get-tuple-element.46), channel_id=1, source_target_pairs={{0,1},{1,0},{2,3},{3,2},{4,5},{5,4},{6,7},{7,6},{8,9},{9,8},{10,11... | collective-permute-start | bytes 1572872 | tf_op jit(solution)/shard_map/ppermute | solution.py:27
  101.6 9.4 %collective-permute-start.8 = (f32[64,512]{1,0:T(8,128)S(1)}, f32[64,512]{1,0:T(8,128)S(1)}, u32[]{:S(2)}, u32[]{:S(2)}) collective-permute-start(f32[64,512]{1,0:T(8,128)S(1)} %get-tuple-element.41), channel_id=1, source_target_pairs={{0,64},{64,128},{128,192},{192,0},{1,65},{65,129},{129,193},{193,1... | collective-permute-start | bytes 393224 | tf_op jit(solution)/shard_map/ppermute | solution.py:33
  101.7 10.1 %collective-permute-start.9 = (f32[64,512]{1,0:T(8,128)S(1)}, f32[64,512]{1,0:T(8,128)S(1)}, u32[]{:S(2)}, u32[]{:S(2)}) collective-permute-start(f32[64,512]{1,0:T(8,128)S(1)} %get-tuple-element.42), channel_id=1, source_target_pairs={{0,128},{64,192},{128,0},{192,64},{1,129},{65,193},{129,1},{193,65... | collective-permute-start | bytes 393224 | tf_op jit(solution)/shard_map/ppermute | solution.py:33
  105.4 7.6 %collective-permute-start.10 = (f32[64,512]{1,0:T(8,128)S(1)}, f32[64,512]{1,0:T(8,128)S(1)}, u32[]{:S(2)}, u32[]{:S(2)}) collective-permute-start(f32[64,512]{1,0:T(8,128)S(1)} %get-tuple-element.43), channel_id=1, source_target_pairs={{0,192},{64,0},{128,64},{192,128},{1,193},{65,1},{129,65},{193,129... | collective-permute-start | bytes 393224 | tf_op jit(solution)/shard_map/ppermute | solution.py:33
  105.5 10.5 %collective-permute-start.13 = (f32[64,512]{1,0:T(8,128)S(1)}, f32[64,512]{1,0:T(8,128)S(1)}, u32[]{:S(2)}, u32[]{:S(2)}) collective-permute-start(f32[64,512]{1,0:T(8,128)S(1)} %get-tuple-element.48), channel_id=1, source_target_pairs={{0,64},{64,128},{128,192},{192,0},{1,65},{65,129},{129,193},{193,1... | collective-permute-start | bytes 393224 | tf_op jit(solution)/shard_map/ppermute | solution.py:33
  107.6 9.7 %collective-permute-start.14 = (f32[64,512]{1,0:T(8,128)S(1)}, f32[64,512]{1,0:T(8,128)S(1)}, u32[]{:S(2)}, u32[]{:S(2)}) collective-permute-start(f32[64,512]{1,0:T(8,128)S(1)} %get-tuple-element.49), channel_id=1, source_target_pairs={{0,128},{64,192},{128,0},{192,64},{1,129},{65,193},{129,1},{193,65... | collective-permute-start | bytes 393224 | tf_op jit(solution)/shard_map/ppermute | solution.py:33
  111.0 7.4 %collective-permute-start.15 = (f32[64,512]{1,0:T(8,128)S(1)}, f32[64,512]{1,0:T(8,128)S(1)}, u32[]{:S(2)}, u32[]{:S(2)}) collective-permute-start(f32[64,512]{1,0:T(8,128)S(1)} %get-tuple-element.50), channel_id=1, source_target_pairs={{0,192},{64,0},{128,64},{192,128},{1,193},{65,1},{129,65},{193,129... | collective-permute-start | bytes 393224 | tf_op jit(solution)/shard_map/ppermute | solution.py:33
  118.5 8.1 %collective-permute-start.16 = (f32[32,512]{1,0:T(8,128)S(1)}, f32[32,512]{1,0:T(8,128)S(1)}, u32[]{:S(2)}, u32[]{:S(2)}) collective-permute-start(f32[32,512]{1,0:T(8,128)S(1)} %get-tuple-element.52), channel_id=1, source_target_pairs={{0,16},{16,32},{32,48},{48,0},{1,17},{17,33},{33,49},{49,1},{2,18}... | collective-permute-start | bytes 196616 | tf_op jit(solution)/shard_map/ppermute | solution.py:33
  121.4 7.5 %collective-permute-start.17 = (f32[32,512]{1,0:T(8,128)S(1)}, f32[32,512]{1,0:T(8,128)S(1)}, u32[]{:S(2)}, u32[]{:S(2)}) collective-permute-start(f32[32,512]{1,0:T(8,128)S(1)} %get-tuple-element.53), channel_id=1, source_target_pairs={{0,32},{16,48},{32,0},{48,16},{1,33},{17,49},{33,1},{49,17},{2,34}... | collective-permute-start | bytes 196616 | tf_op jit(solution)/shard_map/ppermute | solution.py:33
  125.8 4.3 %collective-permute-start.18 = (f32[32,512]{1,0:T(8,128)S(1)}, f32[32,512]{1,0:T(8,128)S(1)}, u32[]{:S(2)}, u32[]{:S(2)}) collective-permute-start(f32[32,512]{1,0:T(8,128)S(1)} %get-tuple-element.54), channel_id=1, source_target_pairs={{0,48},{16,0},{32,16},{48,32},{1,49},{17,1},{33,17},{49,33},{2,50}... | collective-permute-start | bytes 196616 | tf_op jit(solution)/shard_map/ppermute | solution.py:33

commit v12 on v11

--- a/solution.py
+++ b/solution.py
@@ -12,7 +12,7 @@
 SECTOR = ("sector_0", "sector_1")
 LANES = 128
 EXTRA = 8
-HALVES = 2
+SHARES = (3, 1)
 MIB = 1 << 20
 KERNEL_VMEM = 22 * MIB
 SMALL_VMEM = 8 * MIB
@@ -85,7 +85,7 @@
 
 def accumulate(sector, count, target, stacks, held, landed, field_high, field_low, outs):
     slot = pl.program_id(0)
-    peers, rows, width = outs[0].shape
+    peers, _, width = outs[0].shape
 
     @pl.when(slot < count[0, 0])
     def _():
@@ -109,13 +109,15 @@
         swapped_here = goal == (sector ^ 1)
         roles = (jnp.logical_not(kept | swapped_here), kept, swapped_here)
         cuts = len(outs) // len(roles)
-        result = result.reshape(peers, cuts * rows, width)
+        rows = [out.shape[1] for out in outs[:cuts]]
+        ends = [sum(rows[: i + 1]) for i in range(cuts)]
+        result = result.reshape(peers, ends[-1], width)
         for i, role in enumerate(roles):
 
             @pl.when(role)
             def _(i=i):
                 for cut in range(cuts):
-                    outs[i * cuts + cut][...] += result[:, cut * rows : (cut + 1) * rows]
+                    outs[i * cuts + cut][...] += result[:, ends[cut] - rows[cut] : ends[cut]]
 
 
 def first_kernel(count, target, left, right, field, *rest):
@@ -175,7 +177,7 @@
         for x in (targets, left_stack, right_stack)
     )
     block = (width, width)
-    part = (split[0], split[1] // cuts, width)
+    parts = [(split[0], rows, width) for rows in cuts] * 3
     scratch = [
         *[pltpu.VMEM(block if streamed else split, jnp.bfloat16)] * 2,
         *[pltpu.VMEM((slots, *block), F32)] * 2,
@@ -186,7 +188,7 @@
         scratch += [pltpu.VMEM(block, F32), pltpu.SemaphoreType.DMA]
     return pl.pallas_call(
         body,
-        out_shape=[jax.ShapeDtypeStruct(part, F32)] * (3 * cuts),
+        out_shape=[jax.ShapeDtypeStruct(part, F32) for part in parts],
         grid_spec=pltpu.PrefetchScalarGridSpec(
             num_scalar_prefetch=1,
             grid=(slots,),
@@ -196,7 +198,7 @@
                 in_hbm,
                 *[in_hbm if streamed else in_vmem] * len(fields),
             ],
-            out_specs=[in_vmem] * (3 * cuts),
+            out_specs=[in_vmem] * len(parts),
             scratch_shapes=scratch,
         ),
         compiler_params=pltpu.CompilerParams(
@@ -225,15 +227,17 @@
 
 
 def relay(*refs):
-    size = len(refs) // (HALVES + 1)
-    arrived, pieces = refs[: HALVES * size], refs[HALVES * size :]
-    rows = pieces[0].shape[0] // HALVES
+    size = len(refs) // (len(SHARES) + 1)
+    arrived, pieces = refs[: len(SHARES) * size], refs[len(SHARES) * size :]
     me = lax.axis_index(TERM[1])
     for k, piece in enumerate(pieces):
-        lines = pl.ds(pl.multiple_of(lax.rem(me + k, size) * rows, rows), rows)
-        for half in range(HALVES):
-            group = arrived[half * size : (half + 1) * size]
-            piece[half * rows : (half + 1) * rows] = summed(group, lines)
+        end = 0
+        for part in range(len(SHARES)):
+            group = arrived[part * size : (part + 1) * size]
+            rows = group[0].shape[0] // size
+            lines = pl.ds(pl.multiple_of(lax.rem(me + k, size) * rows, rows), rows)
+            piece[end : end + rows] = summed(group, lines)
+            end += rows
 
 
 def tiles(x, slab, width):
@@ -304,7 +308,7 @@
     width = wavefunction.shape[1]
     slab = width // peers
     split = (peers, slab, width)
-    rows = slab // HALVES
+    cuts = tuple(slab * share // sum(SHARES) for share in SHARES)
     size = lax.axis_size(TERM[0])
     field = wavefunction[0]
     blocked = field.reshape(split)
@@ -318,7 +322,7 @@
         split=split,
     )
 
-    crossing, kept, local = image_of(first_kernel, fields=(field,), cuts=1)
+    crossing, kept, local = image_of(first_kernel, fields=(field,), cuts=(slab,))
     crossed, local = moved(crossing, local)
     scaling_late, _ = lax.optimization_barrier((scaling, kept))
     full_scaling = swapped(jnp.broadcast_to(scaling_late[None], split))
@@ -338,13 +342,13 @@
     sums = over_sectors(sums)
 
     fields = (sums, blocked, full_scaling, full_image)
-    parts = image_of(second_kernel, fields=fields, cuts=HALVES)
-    crossing, kept, local = (parts[i * HALVES : (i + 1) * HALVES] for i in range(3))
+    parts = image_of(second_kernel, fields=fields, cuts=cuts)
+    crossing, kept, local = (parts[i * len(cuts) : (i + 1) * len(cuts)] for i in range(3))
     moves = [moved(c, l) for c, l in zip(crossing, local)]
     arrived = []
-    for half in range(HALVES):
+    for part, rows in enumerate(cuts):
         pieces = small_call(
-            spread, [(size * rows, width)] * size, [kept[half], *moves[half]]
+            spread, [(size * rows, width)] * size, [kept[part], *moves[part]]
         )
         arrived += exchanged_along(pieces, TERM[0])
     pieces = small_call(relay, [(slab, width)] * size, arrived)

time: 131 us -> 136 us (1.038); the launches traced: 131 us -> 137 us
  waiting for transfers between devices: 22.3 us -> 34.2 us
  Pallas kernels: 11.7 us -> 23.5 us
  starting transfers between devices: 46.4 us -> 35.3 us
  blocking collectives: 48.8 us -> 42.8 us
    pallas_call x2, Pallas kernels: 9.16 us -> 20.9 us  [partial_image(): pl.pallas_call(body, out_shape=[jax.ShapeDtypeStruct(part, F32) for part...]
    ppermute x3, waiting for transfers between devices: 0.01 us -> 7.17 us  [moved(): lax.ppermute(crossing, SECTOR, upward + downward)]
    all_to_all x2, blocking collectives: 48.8 us -> 42.8 us  [swapped(): return lax.all_to_all(x, TERM, 0, 0, tiled=True)]
    ppermute x3, starting transfers between devices: 9.53 us -> 4.4 us  [moved(): lax.ppermute(local, SECTOR, swap)]
    ppermute x9, waiting for transfers between devices: 10.9 us -> 15.6 us  [exchanged_along(): sent = [lax.ppermute(pieces[k], axis, routes[k]) for k in range(1, size)]]
    ppermute x9, starting transfers between devices: 17.4 us -> 13.1 us  [exchanged_along(): sent = [lax.ppermute(pieces[k], axis, routes[k]) for k in range(1, size)]]
    ppermute x3, starting transfers between devices: 7.76 us -> 5.88 us  [moved(): lax.ppermute(crossing, SECTOR, upward + downward)]
  transfers between devices with their start and end apart: 20 -> 20, of which waited for: 11 -> 9; matrix products, arithmetic and copies ran while one was open for 0% -> 0% of each run, Pallas kernels for 0% -> 0%
where the time goes in v12:
time: 136 us; the launch traced here: 137 us
  blocking collectives  42.8 us (31%)
  starting transfers between devices  35.3 us (26%)
  waiting for transfers between devices  34.2 us (25%)
  Pallas kernels  23.5 us (17%)
  between operations  1.44 us (1%)
    all_to_all x2, blocking collectives, swapped(): return lax.all_to_all(x, TERM, 0, 0, tiled=True)  42.8 us
    pallas_call x2, Pallas kernels, partial_image(): pl.pallas_call(body, out_shape=[jax.ShapeDtypeStruct(part, F32) for part...  20.9 us
    ppermute x9, waiting for transfers between devices, exchanged_along(): sent = [lax.ppermute(pieces[k], axis, routes[k]) for k in range(1, size)]  15.6 us
    ppermute x9, starting transfers between devices, exchanged_along(): sent = [lax.ppermute(pieces[k], axis, routes[k]) for k in range(1, size)]  13.1 us
    ppermute x4, waiting for transfers between devices, exchanged(): return x + lax.ppermute(x, axis, pairs)  11.4 us
    ppermute x4, starting transfers between devices, exchanged(): return x + lax.ppermute(x, axis, pairs)  8.21 us
    ppermute x3, waiting for transfers between devices, moved(): lax.ppermute(crossing, SECTOR, upward + downward)  7.17 us
    ppermute x3, starting transfers between devices, moved(): lax.ppermute(crossing, SECTOR, upward + downward)  5.88 us
  transfers between devices with their start and end apart: 20, of which 9 were waited for; matrix products, arithmetic and copies ran while one was open for 0% of the time, Pallas kernels for 0%

profile of v12, /device:TPU:64, one launch (start us, length us, event | category | flops | bytes accessed | tf_op | source)
XLA Modules:
  0.0 137.3 jit_solution(11210942334647788652)
XLA Ops:
  1.3 0.0 copy-start.1
  1.3 0.0 copy-start
  1.3 10.7 %shard_map.85 = (f32[16,32,512]{2,1,0:T(8,128)S(1)}, f32[16,32,512]{2,1,0:T(8,128)S(1)}, f32[16,32,512]{2,1,0:T(8,128)S(1)}) custom-call(s32[1,1]{1,0:T(1,128)S(6)} %copy.9.count, s32[1,4]{1,0:T(1,128)} %target.3, f32[4,512,512]{2,1,0:T(8,128)} %bitcast.17, f32[4,512,512]{2,1,0:T(8,128)} %bitcast.19, f32[512,512]{1,0:T(8,128)} %bitcast.10), custom_call_target="tpu_custom_call" | custom-call | flops 6442450944 | bytes 8388608 | tf_op jit(solution)/shard_map/pallas_call | solution.py:189
  12.0 1.9 %collective-permute-start = (f32[16,32,512]{2,1,0:T(8,128)S(1)}, f32[16,32,512]{2,1,0:T(8,128)S(1)}, u32[]{:S(2)}, u32[]{:S(2)}) collective-permute-start(f32[16,32,512]{2,1,0:T(8,128)S(1)} %get-tuple-element.31), channel_id=1, source_target_pairs={{1,2},{3,4},{5,6},{7,8},{9,10},{11,12},{13,14},{2,1},{4,3},{6,5},{... | collective-permute-start | bytes 3145736 | tf_op jit(solution)/shard_map/ppermute | solution.py:27
  13.9 2.1 %collective-permute-start.1 = (f32[16,32,512]{2,1,0:T(8,128)S(1)}, f32[16,32,512]{2,1,0:T(8,128)S(1)}, u32[]{:S(2)}, u32[]{:S(2)}) collective-permute-start(f32[16,32,512]{2,1,0:T(8,128)S(1)} %get-tuple-element.32), channel_id=1, source_target_pairs={{0,1},{1,0},{2,3},{3,2},{4,5},{5,4},{6,7},{7,6},{8,9},{9,8},{10,11... | collective-permute-start | bytes 3145736 | tf_op jit(solution)/shard_map/ppermute | solution.py:27
  16.0 0.0 copy-done.1
  16.0 0.1 broadcast_in_dim.15
  16.1 22.3 %all_to_all.15.scaling = f32[16,32,512]{2,1,0:T(8,128)S(1)} all-to-all(f32[16,32,512]{2,1,0:T(8,128)S(1)} %broadcast_in_dim.15), channel_id=1, replica_groups=mesh['term_0'=4,'term_1'=4,'sector_0'=8,'sector_1'=2] {'term_0','term_1'}, dimensions={0} | all-to-all | bytes 2097152 | tf_op jit(solution)/shard_map/all_to_all | solution.py:38
  38.4 0.0 collective-permute-done.crossed
  38.4 0.0 collective-permute-done.1.local
  38.4 0.0 copy-done
  38.4 0.5 shard_map.86
  38.9 20.5 %all_to_all.16.arrived = f32[16,136,128]{2,1,0:T(8,128)S(1)} all-to-all(f32[16,136,128]{2,1,0:T(8,128)S(1)} %shard_map.86), channel_id=1, replica_groups=mesh['term_0'=4,'term_1'=4,'sector_0'=8,'sector_1'=2] {'term_0','term_1'}, dimensions={0} | all-to-all | bytes 2228224 | tf_op jit(solution)/shard_map/all_to_all | solution.py:38
  59.4 1.2 shard_map.87
  60.6 3.7 %all-to-all-start.2 = ((f32[16,32,512]{2,1,0:T(8,128)}), f32[16,32,512]{2,1,0:T(8,128)S(1)}, u32[]{:S(2)}, u32[]{:S(2)}) async-start(f32[16,32,512]{2,1,0:T(8,128)} %get-tuple-element.36), calls=%async_computation.2 | async-start | bytes 2097152 | tf_op jit(solution)/shard_map/all_to_all | solution.py:38
  64.3 0.1 collective-permute-start.2
  64.4 1.2 collective-permute-done.2
  65.5 4.7 %collective-permute-start.3 = (f32[8,128]{1,0:T(8,128)S(1)}, f32[8,128]{1,0:T(8,128)S(1)}, u32[]{:S(2)}, u32[]{:S(2)}) collective-permute-start(f32[8,128]{1,0:T(8,128)S(1)} %add.19), channel_id=1, source_target_pairs={{0,2},{2,0},{4,6},{6,4},{8,10},{10,8},{12,14},{14,12},{1,3},{3,1},... | collective-permute-start | bytes 12296 | tf_op jit(solution)/shard_map/ppermute | solution.py:52
  70.2 1.6 %collective-permute-done.3 = f32[8,128]{1,0:T(8,128)S(1)} collective-permute-done((f32[8,128]{1,0:T(8,128)S(1)}, f32[8,128]{1,0:T(8,128)S(1)}, u32[]{:S(2)}, u32[]{:S(2)}) %collective-permute-start.3) | collective-permute-done | bytes 4128 | tf_op jit(solution)/shard_map/ppermute | solution.py:52
  71.8 0.0 collective-permute-start.4
  71.8 4.5 %collective-permute-done.4 = f32[8,128]{1,0:T(8,128)S(1)} collective-permute-done((f32[8,128]{1,0:T(8,128)S(1)}, f32[8,128]{1,0:T(8,128)S(1)}, u32[]{:S(2)}, u32[]{:S(2)}) %collective-permute-start.4) | collective-permute-done | bytes 4128 | tf_op jit(solution)/shard_map/ppermute | solution.py:52
  76.3 3.4 %collective-permute-start.5 = (f32[8,128]{1,0:T(8,128)S(1)}, f32[8,128]{1,0:T(8,128)S(1)}, u32[]{:S(2)}, u32[]{:S(2)}) collective-permute-start(f32[8,128]{1,0:T(8,128)S(1)} %add.21), channel_id=1, source_target_pairs={{0,8},{2,10},{4,12},{6,14},{8,0},{10,2},{12,4},{14,6},{1,9},{3,11}... | collective-permute-start | bytes 12296 | tf_op jit(solution)/shard_map/ppermute | solution.py:52
  79.7 4.1 %collective-permute-done.5 = f32[8,128]{1,0:T(8,128)S(1)} collective-permute-done((f32[8,128]{1,0:T(8,128)S(1)}, f32[8,128]{1,0:T(8,128)S(1)}, u32[]{:S(2)}, u32[]{:S(2)}) %collective-permute-start.5) | collective-permute-done | bytes 4128 | tf_op jit(solution)/shard_map/ppermute | solution.py:52
  83.9 0.0 all-to-all-done.2.image
  83.9 10.2 %shard_map.88 = (f32[16,24,512]{2,1,0:T(8,128)S(1)}, f32[16,8,512]{2,1,0:T(8,128)S(1)}, f32[16,24,512]{2,1,0:T(8,128)S(1)}, f32[16,8,512]{2,1,0:T(8,128)S(1)}, f...) custom-call(s32[1,1]{1,0:T(1,128)S(6)} %copy.9.count, s32[1,4]{1,0:T(1,128)} %target.3, f32[4,512,512]{2,1,0:T(8,128)} %bitcast.18, ...), custom_call_target="tpu_custom_call" | custom-call | flops 6442450944 | bytes 8388608 | tf_op jit(solution)/shard_map/pallas_call | solution.py:189
  94.1 0.0 copy-start.2
  94.1 2.1 %collective-permute-start.6 = (f32[16,24,512]{2,1,0:T(8,128)S(1)}, f32[16,24,512]{2,1,0:T(8,128)S(1)}, u32[]{:S(2)}, u32[]{:S(2)}) collective-permute-start(f32[16,24,512]{2,1,0:T(8,128)S(1)} %get-tuple-element.38), channel_id=1, source_target_pairs={{1,2},{3,4},{5,6},{7,8},{9,10},{11,12},{13,14},{2,1},{4,3},{6,5},{... | collective-permute-start | bytes 2359304 | tf_op jit(solution)/shard_map/ppermute | solution.py:27
  96.1 2.2 %collective-permute-start.7 = (f32[16,24,512]{2,1,0:T(8,128)S(1)}, f32[16,24,512]{2,1,0:T(8,128)S(1)}, u32[]{:S(2)}, u32[]{:S(2)}) collective-permute-start(f32[16,24,512]{2,1,0:T(8,128)S(1)} %get-tuple-element.39), channel_id=1, source_target_pairs={{0,1},{1,0},{2,3},{3,2},{4,5},{5,4},{6,7},{7,6},{8,9},{9,8},{10,11... | collective-permute-start | bytes 2359304 | tf_op jit(solution)/shard_map/ppermute | solution.py:27
  98.3 1.9 %collective-permute-start.11 = (f32[16,8,512]{2,1,0:T(8,128)S(1)}, f32[16,8,512]{2,1,0:T(8,128)S(1)}, u32[]{:S(2)}, u32[]{:S(2)}) collective-permute-start(f32[16,8,512]{2,1,0:T(8,128)S(1)} %get-tuple-element.45), channel_id=1, source_target_pairs={{1,2},{3,4},{5,6},{7,8},{9,10},{11,12},{13,14},{2,1},{4,3},{6,5},{... | collective-permute-start | bytes 786440 | tf_op jit(solution)/shard_map/ppermute | solution.py:27
  100.2 0.1 collective-permute-start.12
  100.4 7.2 %collective-permute-done.6.crossed = f32[16,24,512]{2,1,0:T(8,128)S(1)} collective-permute-done((f32[16,24,512]{2,1,0:T(8,128)S(1)}, f32[16,24,512]{2,1,0:T(8,128)S(1)}, u32[]{:S(2)}, u32[]{:S(2)}) %collective-permute-start.6) | collective-permute-done | bytes 786464 | tf_op jit(solution)/shard_map/ppermute | solution.py:27
  107.5 0.0 collective-permute-done.7.local
  107.5 0.1 shard_map.89
  107.6 0.1 collective-permute-start.8
  107.7 4.4 %collective-permute-start.9 = (f32[96,512]{1,0:T(8,128)S(1)}, f32[96,512]{1,0:T(8,128)S(1)}, u32[]{:S(2)}, u32[]{:S(2)}) collective-permute-start(f32[96,512]{1,0:T(8,128)S(1)} %get-tuple-element.42), channel_id=1, source_target_pairs={{0,128},{64,192},{128,0},{192,64},{1,129},{65,193},{129,1},{193,65... | collective-permute-start | bytes 589832 | tf_op jit(solution)/shard_map/ppermute | solution.py:33
  112.2 0.0 collective-permute-start.10
  112.2 0.0 collective-permute-done.11.crossed
  112.2 0.0 collective-permute-done.12.local
  112.2 0.1 shard_map.90
  112.2 2.1 %collective-permute-start.13 = (f32[32,512]{1,0:T(8,128)S(1)}, f32[32,512]{1,0:T(8,128)S(1)}, u32[]{:S(2)}, u32[]{:S(2)}) collective-permute-start(f32[32,512]{1,0:T(8,128)S(1)} %get-tuple-element.48), channel_id=1, source_target_pairs={{0,64},{64,128},{128,192},{192,0},{1,65},{65,129},{129,193},{193,1... | collective-permute-start | bytes 196616 | tf_op jit(solution)/shard_map/ppermute | solution.py:33
  114.3 0.6 collective-permute-start.14
  114.9 8.5 %collective-permute-done.13.refs_5_ = f32[32,512]{1,0:T(8,128)S(1)} collective-permute-done((f32[32,512]{1,0:T(8,128)S(1)}, f32[32,512]{1,0:T(8,128)S(1)}, u32[]{:S(2)}, u32[]{:S(2)}) %collective-permute-start.13) | collective-permute-done | bytes 65568 | tf_op jit(solution)/shard_map/ppermute | solution.py:33
  123.4 0.0 collective-permute-start.15
  123.4 0.0 collective-permute-done.14.refs_6_
  123.4 4.3 %collective-permute-done.15.refs_7_ = f32[32,512]{1,0:T(8,128)S(1)} collective-permute-done((f32[32,512]{1,0:T(8,128)S(1)}, f32[32,512]{1,0:T(8,128)S(1)}, u32[]{:S(2)}, u32[]{:S(2)}) %collective-permute-start.15) | collective-permute-done | bytes 65568 | tf_op jit(solution)/shard_map/ppermute | solution.py:33
  127.7 0.0 collective-permute-done.8.refs_1_
  127.7 0.0 collective-permute-done.9.refs_2_
  127.7 0.0 collective-permute-done.10.refs_3_
  127.7 0.1 shard_map.91
  127.8 0.1 collective-permute-start.16
  127.9 4.4 %collective-permute-start.17 = (f32[32,512]{1,0:T(8,128)S(1)}, f32[32,512]{1,0:T(8,128)S(1)}, u32[]{:S(2)}, u32[]{:S(2)}) collective-permute-start(f32[32,512]{1,0:T(8,128)S(1)} %get-tuple-element.53), channel_id=1, source_target_pairs={{0,32},{16,48},{32,0},{48,16},{1,33},{17,49},{33,1},{49,17},{2,34}... | collective-permute-start | bytes 196616 | tf_op jit(solution)/shard_map/ppermute | solution.py:33
  132.3 1.5 %collective-permute-start.18 = (f32[32,512]{1,0:T(8,128)S(1)}, f32[32,512]{1,0:T(8,128)S(1)}, u32[]{:S(2)}, u32[]{:S(2)}) collective-permute-start(f32[32,512]{1,0:T(8,128)S(1)} %get-tuple-element.54), channel_id=1, source_target_pairs={{0,48},{16,0},{32,16},{48,32},{1,49},{17,1},{33,17},{49,33},{2,50}... | collective-permute-start | bytes 196616 | tf_op jit(solution)/shard_map/ppermute | solution.py:33
  133.8 0.0 collective-permute-done.16.refs_1_
  133.8 1.5 %collective-permute-done.17.refs_2_ = f32[32,512]{1,0:T(8,128)S(1)} collective-permute-done((f32[32,512]{1,0:T(8,128)S(1)}, f32[32,512]{1,0:T(8,128)S(1)}, u32[]{:S(2)}, u32[]{:S(2)}) %collective-permute-start.17) | collective-permute-done | bytes 65568 | tf_op jit(solution)/shard_map/ppermute | solution.py:33
  135.2 1.3 collective-permute-done.18.refs_3_
  136.6 0.0 copy-done.2
  136.6 0.7 shard_map.92
  (5 shorter events, 0.0 us)
Async XLA Ops:
  1.3 14.7 %copy-start.1 = (f32[1,32,512]{2,1,0:T(8,128)S(1)}, f32[1,32,512]{2,1,0:T(8,128)}, u32[]{:S(2)}) copy-start(f32[1,32,512]{2,1,0:T(8,128)} %param.7) | copy-start | bytes 196612
  1.3 37.1 %copy-start = (f32[1,512,512]{2,1,0:T(8,128)S(1)}, f32[1,512,512]{2,1,0:T(8,128)}, u32[]{:S(2)}) copy-start(f32[1,512,512]{2,1,0:T(8,128)} %param.6) | copy-start | bytes 3145732
  12.0 26.4 %collective-permute-start = (f32[16,32,512]{2,1,0:T(8,128)S(1)}, f32[16,32,512]{2,1,0:T(8,128)S(1)}, u32[]{:S(2)}, u32[]{:S(2)}) collective-permute-start(f32[16,32,512]{2,1,0:T(8,128)S(1)} %get-tuple-element.31), channel_id=1, source_target_pairs={{1,2},{3,4},{5,6},{7,8},{9,10},{11,12},{13,14},{2,1},{4,3},{6,5},{... | collective-permute-start | bytes 3145736 | tf_op jit(solution)/shard_map/ppermute | solution.py:27
  13.9 24.5 %collective-permute-start.1 = (f32[16,32,512]{2,1,0:T(8,128)S(1)}, f32[16,32,512]{2,1,0:T(8,128)S(1)}, u32[]{:S(2)}, u32[]{:S(2)}) collective-permute-start(f32[16,32,512]{2,1,0:T(8,128)S(1)} %get-tuple-element.32), channel_id=1, source_target_pairs={{0,1},{1,0},{2,3},{3,2},{4,5},{5,4},{6,7},{7,6},{8,9},{9,8},{10,11... | collective-permute-start | bytes 3145736 | tf_op jit(solution)/shard_map/ppermute | solution.py:27
  60.6 23.3 %all-to-all-start.2 = ((f32[16,32,512]{2,1,0:T(8,128)}), f32[16,32,512]{2,1,0:T(8,128)S(1)}, u32[]{:S(2)}, u32[]{:S(2)}) async-start(f32[16,32,512]{2,1,0:T(8,128)} %get-tuple-element.36), calls=%async_computation.2 | async-start | bytes 2097152 | tf_op jit(solution)/shard_map/all_to_all | solution.py:38
  64.3 1.3 collective-permute-start.2
  65.5 6.3 %collective-permute-start.3 = (f32[8,128]{1,0:T(8,128)S(1)}, f32[8,128]{1,0:T(8,128)S(1)}, u32[]{:S(2)}, u32[]{:S(2)}) collective-permute-start(f32[8,128]{1,0:T(8,128)S(1)} %add.19), channel_id=1, source_target_pairs={{0,2},{2,0},{4,6},{6,4},{8,10},{10,8},{12,14},{14,12},{1,3},{3,1},... | collective-permute-start | bytes 12296 | tf_op jit(solution)/shard_map/ppermute | solution.py:52
  71.8 4.5 %collective-permute-start.4 = (f32[8,128]{1,0:T(8,128)S(1)}, f32[8,128]{1,0:T(8,128)S(1)}, u32[]{:S(2)}, u32[]{:S(2)}) collective-permute-start(f32[8,128]{1,0:T(8,128)S(1)} %add.20), channel_id=1, source_target_pairs={{0,4},{2,6},{4,0},{6,2},{8,12},{10,14},{12,8},{14,10},{1,5},{3,7},... | collective-permute-start | bytes 12296 | tf_op jit(solution)/shard_map/ppermute | solution.py:52
  76.3 7.5 %collective-permute-start.5 = (f32[8,128]{1,0:T(8,128)S(1)}, f32[8,128]{1,0:T(8,128)S(1)}, u32[]{:S(2)}, u32[]{:S(2)}) collective-permute-start(f32[8,128]{1,0:T(8,128)S(1)} %add.21), channel_id=1, source_target_pairs={{0,8},{2,10},{4,12},{6,14},{8,0},{10,2},{12,4},{14,6},{1,9},{3,11}... | collective-permute-start | bytes 12296 | tf_op jit(solution)/shard_map/ppermute | solution.py:52
  94.1 42.5 %copy-start.2 = (f32[32,512]{1,0:T(8,128)S(1)}, f32[32,512]{1,0:T(8,128)}, u32[]{:S(2)}) copy-start(f32[32,512]{1,0:T(8,128)} %get-tuple-element.34.refs_5_) | copy-start | bytes 196612
  94.1 13.4 %collective-permute-start.6 = (f32[16,24,512]{2,1,0:T(8,128)S(1)}, f32[16,24,512]{2,1,0:T(8,128)S(1)}, u32[]{:S(2)}, u32[]{:S(2)}) collective-permute-start(f32[16,24,512]{2,1,0:T(8,128)S(1)} %get-tuple-element.38), channel_id=1, source_target_pairs={{1,2},{3,4},{5,6},{7,8},{9,10},{11,12},{13,14},{2,1},{4,3},{6,5},{... | collective-permute-start | bytes 2359304 | tf_op jit(solution)/shard_map/ppermute | solution.py:27
  96.1 11.4 %collective-permute-start.7 = (f32[16,24,512]{2,1,0:T(8,128)S(1)}, f32[16,24,512]{2,1,0:T(8,128)S(1)}, u32[]{:S(2)}, u32[]{:S(2)}) collective-permute-start(f32[16,24,512]{2,1,0:T(8,128)S(1)} %get-tuple-element.39), channel_id=1, source_target_pairs={{0,1},{1,0},{2,3},{3,2},{4,5},{5,4},{6,7},{7,6},{8,9},{9,8},{10,11... | collective-permute-start | bytes 2359304 | tf_op jit(solution)/shard_map/ppermute | solution.py:27
  98.3 13.8 %collective-permute-start.11 = (f32[16,8,512]{2,1,0:T(8,128)S(1)}, f32[16,8,512]{2,1,0:T(8,128)S(1)}, u32[]{:S(2)}, u32[]{:S(2)}) collective-permute-start(f32[16,8,512]{2,1,0:T(8,128)S(1)} %get-tuple-element.45), channel_id=1, source_target_pairs={{1,2},{3,4},{5,6},{7,8},{9,10},{11,12},{13,14},{2,1},{4,3},{6,5},{... | collective-permute-start | bytes 786440 | tf_op jit(solution)/shard_map/ppermute | solution.py:27
  100.2 11.9 %collective-permute-start.12 = (f32[16,8,512]{2,1,0:T(8,128)S(1)}, f32[16,8,512]{2,1,0:T(8,128)S(1)}, u32[]{:S(2)}, u32[]{:S(2)}) collective-permute-start(f32[16,8,512]{2,1,0:T(8,128)S(1)} %get-tuple-element.46), channel_id=1, source_target_pairs={{0,1},{1,0},{2,3},{3,2},{4,5},{5,4},{6,7},{7,6},{8,9},{9,8},{10,11... | collective-permute-start | bytes 786440 | tf_op jit(solution)/shard_map/ppermute | solution.py:27
  107.6 20.1 %collective-permute-start.8 = (f32[96,512]{1,0:T(8,128)S(1)}, f32[96,512]{1,0:T(8,128)S(1)}, u32[]{:S(2)}, u32[]{:S(2)}) collective-permute-start(f32[96,512]{1,0:T(8,128)S(1)} %get-tuple-element.41), channel_id=1, source_target_pairs={{0,64},{64,128},{128,192},{192,0},{1,65},{65,129},{129,193},{193,1... | collective-permute-start | bytes 589832 | tf_op jit(solution)/shard_map/ppermute | solution.py:33
  107.7 20.0 %collective-permute-start.9 = (f32[96,512]{1,0:T(8,128)S(1)}, f32[96,512]{1,0:T(8,128)S(1)}, u32[]{:S(2)}, u32[]{:S(2)}) collective-permute-start(f32[96,512]{1,0:T(8,128)S(1)} %get-tuple-element.42), channel_id=1, source_target_pairs={{0,128},{64,192},{128,0},{192,64},{1,129},{65,193},{129,1},{193,65... | collective-permute-start | bytes 589832 | tf_op jit(solution)/shard_map/ppermute | solution.py:33
  112.2 15.5 %collective-permute-start.10 = (f32[96,512]{1,0:T(8,128)S(1)}, f32[96,512]{1,0:T(8,128)S(1)}, u32[]{:S(2)}, u32[]{:S(2)}) collective-permute-start(f32[96,512]{1,0:T(8,128)S(1)} %get-tuple-element.43), channel_id=1, source_target_pairs={{0,192},{64,0},{128,64},{192,128},{1,193},{65,1},{129,65},{193,129... | collective-permute-start | bytes 589832 | tf_op jit(solution)/shard_map/ppermute | solution.py:33
  112.2 11.2 %collective-permute-start.13 = (f32[32,512]{1,0:T(8,128)S(1)}, f32[32,512]{1,0:T(8,128)S(1)}, u32[]{:S(2)}, u32[]{:S(2)}) collective-permute-start(f32[32,512]{1,0:T(8,128)S(1)} %get-tuple-element.48), channel_id=1, source_target_pairs={{0,64},{64,128},{128,192},{192,0},{1,65},{65,129},{129,193},{193,1... | collective-permute-start | bytes 196616 | tf_op jit(solution)/shard_map/ppermute | solution.py:33
  114.3 9.1 %collective-permute-start.14 = (f32[32,512]{1,0:T(8,128)S(1)}, f32[32,512]{1,0:T(8,128)S(1)}, u32[]{:S(2)}, u32[]{:S(2)}) collective-permute-start(f32[32,512]{1,0:T(8,128)S(1)} %get-tuple-element.49), channel_id=1, source_target_pairs={{0,128},{64,192},{128,0},{192,64},{1,129},{65,193},{129,1},{193,65... | collective-permute-start | bytes 196616 | tf_op jit(solution)/shard_map/ppermute | solution.py:33
  123.4 4.3 %collective-permute-start.15 = (f32[32,512]{1,0:T(8,128)S(1)}, f32[32,512]{1,0:T(8,128)S(1)}, u32[]{:S(2)}, u32[]{:S(2)}) collective-permute-start(f32[32,512]{1,0:T(8,128)S(1)} %get-tuple-element.50), channel_id=1, source_target_pairs={{0,192},{64,0},{128,64},{192,128},{1,193},{65,1},{129,65},{193,129... | collective-permute-start | bytes 196616 | tf_op jit(solution)/shard_map/ppermute | solution.py:33
  127.8 6.0 %collective-permute-start.16 = (f32[32,512]{1,0:T(8,128)S(1)}, f32[32,512]{1,0:T(8,128)S(1)}, u32[]{:S(2)}, u32[]{:S(2)}) collective-permute-start(f32[32,512]{1,0:T(8,128)S(1)} %get-tuple-element.52), channel_id=1, source_target_pairs={{0,16},{16,32},{32,48},{48,0},{1,17},{17,33},{33,49},{49,1},{2,18}... | collective-permute-start | bytes 196616 | tf_op jit(solution)/shard_map/ppermute | solution.py:33
  127.9 7.4 %collective-permute-start.17 = (f32[32,512]{1,0:T(8,128)S(1)}, f32[32,512]{1,0:T(8,128)S(1)}, u32[]{:S(2)}, u32[]{:S(2)}) collective-permute-start(f32[32,512]{1,0:T(8,128)S(1)} %get-tuple-element.53), channel_id=1, source_target_pairs={{0,32},{16,48},{32,0},{48,16},{1,33},{17,49},{33,1},{49,17},{2,34}... | collective-permute-start | bytes 196616 | tf_op jit(solution)/shard_map/ppermute | solution.py:33
  132.3 4.3 %collective-permute-start.18 = (f32[32,512]{1,0:T(8,128)S(1)}, f32[32,512]{1,0:T(8,128)S(1)}, u32[]{:S(2)}, u32[]{:S(2)}) collective-permute-start(f32[32,512]{1,0:T(8,128)S(1)} %get-tuple-element.54), channel_id=1, source_target_pairs={{0,48},{16,0},{32,16},{48,32},{1,49},{17,1},{33,17},{49,33},{2,50}... | collective-permute-start | bytes 196616 | tf_op jit(solution)/shard_map/ppermute | solution.py:33

commit v13 on v10

--- a/solution.py
+++ b/solution.py
@@ -30,8 +30,9 @@
 def exchanged_along(pieces, axis):
     size = len(pieces)
     routes = [[(i, (i + k) % size) for i in range(size)] for k in range(size)]
-    sent = [lax.ppermute(pieces[k], axis, routes[k]) for k in range(1, size)]
-    return [pieces[0], *sent]
+    farthest_first = sorted(range(1, size), key=lambda k: -min(k, size - k))
+    sent = [lax.ppermute(pieces[k], axis, routes[k]) for k in farthest_first]
+    return [*sent, pieces[0]]
 
 
 def swapped(x):

time: 130 us -> 130 us (level); the launches traced: 131 us -> 128 us
  waiting for transfers between devices: 16.1 us -> 13.2 us
  starting transfers between devices: 56.9 us -> 59 us
    ppermute x3, starting transfers between devices: 14.6 us -> 5.88 us  [moved(): lax.ppermute(crossing, SECTOR, upward + downward)]
    ppermute x3, starting transfers between devices: 8.02 us -> 15.8 us  [moved(): lax.ppermute(local, SECTOR, swap)]
    ppermute x12, waiting for transfers between devices: 4.57 us -> 1.88 us  [exchanged_along(): sent = [lax.ppermute(pieces[k], axis, routes[k]) for k in farthest_first]]
    ppermute x12, starting transfers between devices: 24.3 us -> 25.9 us  [exchanged_along(): sent = [lax.ppermute(pieces[k], axis, routes[k]) for k in farthest_first]]
    ppermute x4, starting transfers between devices: 6.42 us -> 7.74 us  [exchanged(): return x + lax.ppermute(x, axis, pairs)]
    all_to_all x2, blocking collectives: 44.4 us -> 43.1 us  [swapped(): return lax.all_to_all(x, TERM, 0, 0, tiled=True)]
  transfers between devices with their start and end apart: 23 -> 23, of which waited for: 8 -> 5; matrix products, arithmetic and copies ran while one was open for 0% -> 0% of each run, Pallas kernels for 0% -> 0%
where the time goes in v13:
time: 130 us; the launch traced here: 128 us
  starting transfers between devices  59 us (45%)
  blocking collectives  43.1 us (33%)
  waiting for transfers between devices  13.2 us (10%)
  Pallas kernels  11.6 us (9%)
  between operations  1.44 us (1%)
    all_to_all x2, blocking collectives, swapped(): return lax.all_to_all(x, TERM, 0, 0, tiled=True)  43.1 us
    ppermute x12, starting transfers between devices, exchanged_along(): sent = [lax.ppermute(pieces[k], axis, routes[k]) for k in farthest_first]  25.9 us
    ppermute x3, starting transfers between devices, moved(): lax.ppermute(local, SECTOR, swap)  15.8 us
    ppermute x4, waiting for transfers between devices, exchanged(): return x + lax.ppermute(x, axis, pairs)  11.3 us
    pallas_call x2, Pallas kernels, partial_image(): pl.pallas_call(body, out_shape=[jax.ShapeDtypeStruct(part, F32)] * (3 * c...  9.05 us
    ppermute x4, starting transfers between devices, exchanged(): return x + lax.ppermute(x, axis, pairs)  7.74 us
    ppermute x3, starting transfers between devices, moved(): lax.ppermute(crossing, SECTOR, upward + downward)  5.88 us
    all_to_all x1, starting transfers between devices, swapped(): return lax.all_to_all(x, TERM, 0, 0, tiled=True)  3.65 us
  transfers between devices with their start and end apart: 23, of which 5 were waited for; matrix products, arithmetic and copies ran while one was open for 0% of the time, Pallas kernels for 0%

profile of v13, /device:TPU:64, one launch (start us, length us, event | category | flops | bytes accessed | tf_op | source)
XLA Modules:
  0.0 128.5 jit_solution(14750850930851628803)
XLA Ops:
  1.3 0.0 copy-start.1
  1.3 0.0 copy-start
  1.3 4.8 %shard_map.85 = (f32[16,32,512]{2,1,0:T(8,128)S(1)}, f32[16,32,512]{2,1,0:T(8,128)S(1)}, f32[16,32,512]{2,1,0:T(8,128)S(1)}) custom-call(s32[1,1]{1,0:T(1,128)S(6)} %copy.9.count, s32[1,4]{1,0:T(1,128)} %target.3, f32[4,512,512]{2,1,0:T(8,128)} %bitcast.17, f32[4,512,512]{2,1,0:T(8,128)} %bitcast.19, f32[512,512]{1,0:T(8,128)} %bitcast.10), custom_call_target="tpu_custom_call" | custom-call | flops 6442450944 | bytes 8388608 | tf_op jit(solution)/shard_map/pallas_call | solution.py:188
  6.1 1.9 %collective-permute-start = (f32[16,32,512]{2,1,0:T(8,128)S(1)}, f32[16,32,512]{2,1,0:T(8,128)S(1)}, u32[]{:S(2)}, u32[]{:S(2)}) collective-permute-start(f32[16,32,512]{2,1,0:T(8,128)S(1)} %get-tuple-element.35), channel_id=1, source_target_pairs={{1,2},{3,4},{5,6},{7,8},{9,10},{11,12},{13,14},{2,1},{4,3},{6,5},{... | collective-permute-start | bytes 3145736 | tf_op jit(solution)/shard_map/ppermute | solution.py:27
  8.0 7.8 %collective-permute-start.1 = (f32[16,32,512]{2,1,0:T(8,128)S(1)}, f32[16,32,512]{2,1,0:T(8,128)S(1)}, u32[]{:S(2)}, u32[]{:S(2)}) collective-permute-start(f32[16,32,512]{2,1,0:T(8,128)S(1)} %get-tuple-element.36), channel_id=1, source_target_pairs={{0,1},{1,0},{2,3},{3,2},{4,5},{5,4},{6,7},{7,6},{8,9},{9,8},{10,11... | collective-permute-start | bytes 3145736 | tf_op jit(solution)/shard_map/ppermute | solution.py:27
  15.8 0.0 copy-done.1
  15.8 0.1 broadcast_in_dim.15
  15.9 22.4 %all_to_all.15.scaling = f32[16,32,512]{2,1,0:T(8,128)S(1)} all-to-all(f32[16,32,512]{2,1,0:T(8,128)S(1)} %broadcast_in_dim.15), channel_id=1, replica_groups=mesh['term_0'=4,'term_1'=4,'sector_0'=8,'sector_1'=2] {'term_0','term_1'}, dimensions={0} | all-to-all | bytes 2097152 | tf_op jit(solution)/shard_map/all_to_all | solution.py:39
  38.4 0.0 collective-permute-done.crossed
  38.4 0.0 collective-permute-done.1.local
  38.4 0.0 copy-done
  38.4 0.5 shard_map.86
  38.9 20.6 %all_to_all.16.arrived = f32[16,136,128]{2,1,0:T(8,128)S(1)} all-to-all(f32[16,136,128]{2,1,0:T(8,128)S(1)} %shard_map.86), channel_id=1, replica_groups=mesh['term_0'=4,'term_1'=4,'sector_0'=8,'sector_1'=2] {'term_0','term_1'}, dimensions={0} | all-to-all | bytes 2228224 | tf_op jit(solution)/shard_map/all_to_all | solution.py:39
  59.5 1.2 shard_map.87
  60.7 3.7 %all-to-all-start.2 = ((f32[16,32,512]{2,1,0:T(8,128)}), f32[16,32,512]{2,1,0:T(8,128)S(1)}, u32[]{:S(2)}, u32[]{:S(2)}) async-start(f32[16,32,512]{2,1,0:T(8,128)} %get-tuple-element.40), calls=%async_computation.2 | async-start | bytes 2097152 | tf_op jit(solution)/shard_map/all_to_all | solution.py:39
  64.4 0.1 collective-permute-start.2
  64.5 1.2 collective-permute-done.2
  65.6 4.2 %collective-permute-start.3 = (f32[8,128]{1,0:T(8,128)S(1)}, f32[8,128]{1,0:T(8,128)S(1)}, u32[]{:S(2)}, u32[]{:S(2)}) collective-permute-start(f32[8,128]{1,0:T(8,128)S(1)} %add.19), channel_id=1, source_target_pairs={{0,2},{2,0},{4,6},{6,4},{8,10},{10,8},{12,14},{14,12},{1,3},{3,1},... | collective-permute-start | bytes 12296 | tf_op jit(solution)/shard_map/ppermute | solution.py:53
  69.8 1.6 %collective-permute-done.3 = f32[8,128]{1,0:T(8,128)S(1)} collective-permute-done((f32[8,128]{1,0:T(8,128)S(1)}, f32[8,128]{1,0:T(8,128)S(1)}, u32[]{:S(2)}, u32[]{:S(2)}) %collective-permute-start.3) | collective-permute-done | bytes 4128 | tf_op jit(solution)/shard_map/ppermute | solution.py:53
  71.4 0.0 collective-permute-start.4
  71.4 4.5 %collective-permute-done.4 = f32[8,128]{1,0:T(8,128)S(1)} collective-permute-done((f32[8,128]{1,0:T(8,128)S(1)}, f32[8,128]{1,0:T(8,128)S(1)}, u32[]{:S(2)}, u32[]{:S(2)}) %collective-permute-start.4) | collective-permute-done | bytes 4128 | tf_op jit(solution)/shard_map/ppermute | solution.py:53
  75.9 3.5 %collective-permute-start.5 = (f32[8,128]{1,0:T(8,128)S(1)}, f32[8,128]{1,0:T(8,128)S(1)}, u32[]{:S(2)}, u32[]{:S(2)}) collective-permute-start(f32[8,128]{1,0:T(8,128)S(1)} %add.21), channel_id=1, source_target_pairs={{0,8},{2,10},{4,12},{6,14},{8,0},{10,2},{12,4},{14,6},{1,9},{3,11}... | collective-permute-start | bytes 12296 | tf_op jit(solution)/shard_map/ppermute | solution.py:53
  79.3 4.0 %collective-permute-done.5 = f32[8,128]{1,0:T(8,128)S(1)} collective-permute-done((f32[8,128]{1,0:T(8,128)S(1)}, f32[8,128]{1,0:T(8,128)S(1)}, u32[]{:S(2)}, u32[]{:S(2)}) %collective-permute-start.5) | collective-permute-done | bytes 4128 | tf_op jit(solution)/shard_map/ppermute | solution.py:53
  83.4 0.0 all-to-all-done.2.image
  83.4 4.3 %shard_map.88 = (f32[16,16,512]{2,1,0:T(8,128)S(1)}, f32[16,16,512]{2,1,0:T(8,128)S(1)}, f32[16,16,512]{2,1,0:T(8,128)S(1)}, f32[16,16,512]{2,1,0:T(8,128)S(1)},...) custom-call(s32[1,1]{1,0:T(1,128)S(6)} %copy.9.count, s32[1,4]{1,0:T(1,128)} %target.3, f32[4,512,512]{2,1,0:T(8,128)} %bitcast.18, ...), custom_call_target="tpu_custom_call" | custom-call | flops 6442450944 | bytes 8388608 | tf_op jit(solution)/shard_map/pallas_call | solution.py:188
  87.7 0.0 copy-start.2
  87.7 2.1 %collective-permute-start.6 = (f32[16,16,512]{2,1,0:T(8,128)S(1)}, f32[16,16,512]{2,1,0:T(8,128)S(1)}, u32[]{:S(2)}, u32[]{:S(2)}) collective-permute-start(f32[16,16,512]{2,1,0:T(8,128)S(1)} %get-tuple-element.42), channel_id=1, source_target_pairs={{1,2},{3,4},{5,6},{7,8},{9,10},{11,12},{13,14},{2,1},{4,3},{6,5},{... | collective-permute-start | bytes 1572872 | tf_op jit(solution)/shard_map/ppermute | solution.py:27
  89.8 7.9 %collective-permute-start.7 = (f32[16,16,512]{2,1,0:T(8,128)S(1)}, f32[16,16,512]{2,1,0:T(8,128)S(1)}, u32[]{:S(2)}, u32[]{:S(2)}) collective-permute-start(f32[16,16,512]{2,1,0:T(8,128)S(1)} %get-tuple-element.43), channel_id=1, source_target_pairs={{0,1},{1,0},{2,3},{3,2},{4,5},{5,4},{6,7},{7,6},{8,9},{9,8},{10,11... | collective-permute-start | bytes 1572872 | tf_op jit(solution)/shard_map/ppermute | solution.py:27
  97.7 1.9 %collective-permute-start.14 = (f32[16,16,512]{2,1,0:T(8,128)S(1)}, f32[16,16,512]{2,1,0:T(8,128)S(1)}, u32[]{:S(2)}, u32[]{:S(2)}) collective-permute-start(f32[16,16,512]{2,1,0:T(8,128)S(1)} %get-tuple-element.53), channel_id=1, source_target_pairs={{1,2},{3,4},{5,6},{7,8},{9,10},{11,12},{13,14},{2,1},{4,3},{6,5},{... | collective-permute-start | bytes 1572872 | tf_op jit(solution)/shard_map/ppermute | solution.py:27
  99.6 0.1 collective-permute-start.15
  99.7 0.0 collective-permute-done.6.crossed
  99.7 0.0 collective-permute-done.7.local
  99.7 0.1 shard_map.89
  99.8 4.5 %collective-permute-start.8 = (f32[64,512]{1,0:T(8,128)S(1)}, f32[64,512]{1,0:T(8,128)S(1)}, u32[]{:S(2)}, u32[]{:S(2)}) collective-permute-start(f32[64,512]{1,0:T(8,128)S(1)} %get-tuple-element.44), channel_id=1, source_target_pairs={{0,128},{64,192},{128,0},{192,64},{1,129},{65,193},{129,1},{193,65... | collective-permute-start | bytes 393224 | tf_op jit(solution)/shard_map/ppermute | solution.py:34
  104.3 3.7 %collective-permute-start.9 = (f32[64,512]{1,0:T(8,128)S(1)}, f32[64,512]{1,0:T(8,128)S(1)}, u32[]{:S(2)}, u32[]{:S(2)}) collective-permute-start(f32[64,512]{1,0:T(8,128)S(1)} %get-tuple-element.45), channel_id=1, source_target_pairs={{0,64},{64,128},{128,192},{192,0},{1,65},{65,129},{129,193},{193,1... | collective-permute-start | bytes 393224 | tf_op jit(solution)/shard_map/ppermute | solution.py:34
  108.1 0.6 collective-permute-start.10
  108.6 0.0 collective-permute-done.14.crossed
  108.6 0.0 collective-permute-done.15.local
  108.6 0.1 shard_map.91
  108.7 2.5 %collective-permute-start.16 = (f32[64,512]{1,0:T(8,128)S(1)}, f32[64,512]{1,0:T(8,128)S(1)}, u32[]{:S(2)}, u32[]{:S(2)}) collective-permute-start(f32[64,512]{1,0:T(8,128)S(1)} %get-tuple-element.55), channel_id=1, source_target_pairs={{0,32},{16,48},{32,0},{48,16},{1,33},{17,49},{33,1},{49,17},{2,34}... | collective-permute-start | bytes 393224 | tf_op jit(solution)/shard_map/ppermute | solution.py:34
  111.3 3.2 %collective-permute-start.17 = (f32[64,512]{1,0:T(8,128)S(1)}, f32[64,512]{1,0:T(8,128)S(1)}, u32[]{:S(2)}, u32[]{:S(2)}) collective-permute-start(f32[64,512]{1,0:T(8,128)S(1)} %get-tuple-element.56), channel_id=1, source_target_pairs={{0,16},{16,32},{32,48},{48,0},{1,17},{17,33},{33,49},{49,1},{2,18}... | collective-permute-start | bytes 393224 | tf_op jit(solution)/shard_map/ppermute | solution.py:34
  114.5 0.0 collective-permute-done.8.refs_0_
  114.5 0.0 collective-permute-start.18
  114.5 0.0 collective-permute-done.9.refs_1_
  114.5 0.0 collective-permute-done.10.refs_2_
  114.5 2.1 %collective-permute-start.11 = (f32[16,512]{1,0:T(8,128)S(1)}, f32[16,512]{1,0:T(8,128)S(1)}, u32[]{:S(2)}, u32[]{:S(2)}) collective-permute-start(f32[16,512]{1,0:T(8,128)S(1)} %get-tuple-element.48), channel_id=1, source_target_pairs={{0,32},{16,48},{32,0},{48,16},{1,33},{17,49},{33,1},{49,17},{2,34}... | collective-permute-start | bytes 98312 | tf_op jit(solution)/shard_map/ppermute | solution.py:34
  116.7 0.7 collective-permute-start.12
  117.3 0.0 collective-permute-done.16.refs_0_
  117.3 3.0 %collective-permute-start.13 = (f32[16,512]{1,0:T(8,128)S(1)}, f32[16,512]{1,0:T(8,128)S(1)}, u32[]{:S(2)}, u32[]{:S(2)}) collective-permute-start(f32[16,512]{1,0:T(8,128)S(1)} %get-tuple-element.50), channel_id=1, source_target_pairs={{0,48},{16,0},{32,16},{48,32},{1,49},{17,1},{33,17},{49,33},{2,50}... | collective-permute-start | bytes 98312 | tf_op jit(solution)/shard_map/ppermute | solution.py:34
  120.3 0.0 collective-permute-done.17.refs_1_
  120.3 0.0 collective-permute-done.18.refs_2_
  120.3 2.3 %collective-permute-start.19 = (f32[16,512]{1,0:T(8,128)S(1)}, f32[16,512]{1,0:T(8,128)S(1)}, u32[]{:S(2)}, u32[]{:S(2)}) collective-permute-start(f32[16,512]{1,0:T(8,128)S(1)} %get-tuple-element.59), channel_id=1, source_target_pairs={{0,128},{64,192},{128,0},{192,64},{1,129},{65,193},{129,1},{193,65... | collective-permute-start | bytes 98312 | tf_op jit(solution)/shard_map/ppermute | solution.py:34
  122.6 1.0 collective-permute-start.20
  123.6 0.0 collective-permute-done.11.refs_0_
  123.6 2.2 %collective-permute-start.21 = (f32[16,512]{1,0:T(8,128)S(1)}, f32[16,512]{1,0:T(8,128)S(1)}, u32[]{:S(2)}, u32[]{:S(2)}) collective-permute-start(f32[16,512]{1,0:T(8,128)S(1)} %get-tuple-element.61), channel_id=1, source_target_pairs={{0,192},{64,0},{128,64},{192,128},{1,193},{65,1},{129,65},{193,129... | collective-permute-start | bytes 98312 | tf_op jit(solution)/shard_map/ppermute | solution.py:34
  125.9 0.0 collective-permute-done.12.refs_1_
  125.9 0.0 collective-permute-done.13.refs_2_
  125.9 0.0 collective-permute-done.19.refs_4_
  125.9 1.9 %collective-permute-done.20.refs_5_ = f32[16,512]{1,0:T(8,128)S(1)} collective-permute-done((f32[16,512]{1,0:T(8,128)S(1)}, f32[16,512]{1,0:T(8,128)S(1)}, u32[]{:S(2)}, u32[]{:S(2)}) %collective-permute-start.20) | collective-permute-done | bytes 32800 | tf_op jit(solution)/shard_map/ppermute | solution.py:34
  127.8 0.0 collective-permute-done.21.refs_6_
  127.8 0.0 copy-done.2
  127.8 0.7 shard_map.93
  (7 shorter events, 0.1 us)
Async XLA Ops:
  1.3 14.5 %copy-start.1 = (f32[1,32,512]{2,1,0:T(8,128)S(1)}, f32[1,32,512]{2,1,0:T(8,128)}, u32[]{:S(2)}) copy-start(f32[1,32,512]{2,1,0:T(8,128)} %param.7) | copy-start | bytes 196612
  1.3 37.1 %copy-start = (f32[1,512,512]{2,1,0:T(8,128)S(1)}, f32[1,512,512]{2,1,0:T(8,128)}, u32[]{:S(2)}) copy-start(f32[1,512,512]{2,1,0:T(8,128)} %param.6) | copy-start | bytes 3145732
  6.1 32.3 %collective-permute-start = (f32[16,32,512]{2,1,0:T(8,128)S(1)}, f32[16,32,512]{2,1,0:T(8,128)S(1)}, u32[]{:S(2)}, u32[]{:S(2)}) collective-permute-start(f32[16,32,512]{2,1,0:T(8,128)S(1)} %get-tuple-element.35), channel_id=1, source_target_pairs={{1,2},{3,4},{5,6},{7,8},{9,10},{11,12},{13,14},{2,1},{4,3},{6,5},{... | collective-permute-start | bytes 3145736 | tf_op jit(solution)/shard_map/ppermute | solution.py:27
  8.0 30.4 %collective-permute-start.1 = (f32[16,32,512]{2,1,0:T(8,128)S(1)}, f32[16,32,512]{2,1,0:T(8,128)S(1)}, u32[]{:S(2)}, u32[]{:S(2)}) collective-permute-start(f32[16,32,512]{2,1,0:T(8,128)S(1)} %get-tuple-element.36), channel_id=1, source_target_pairs={{0,1},{1,0},{2,3},{3,2},{4,5},{5,4},{6,7},{7,6},{8,9},{9,8},{10,11... | collective-permute-start | bytes 3145736 | tf_op jit(solution)/shard_map/ppermute | solution.py:27
  60.7 22.7 %all-to-all-start.2 = ((f32[16,32,512]{2,1,0:T(8,128)}), f32[16,32,512]{2,1,0:T(8,128)S(1)}, u32[]{:S(2)}, u32[]{:S(2)}) async-start(f32[16,32,512]{2,1,0:T(8,128)} %get-tuple-element.40), calls=%async_computation.2 | async-start | bytes 2097152 | tf_op jit(solution)/shard_map/all_to_all | solution.py:39
  64.4 1.3 collective-permute-start.2
  65.6 5.8 %collective-permute-start.3 = (f32[8,128]{1,0:T(8,128)S(1)}, f32[8,128]{1,0:T(8,128)S(1)}, u32[]{:S(2)}, u32[]{:S(2)}) collective-permute-start(f32[8,128]{1,0:T(8,128)S(1)} %add.19), channel_id=1, source_target_pairs={{0,2},{2,0},{4,6},{6,4},{8,10},{10,8},{12,14},{14,12},{1,3},{3,1},... | collective-permute-start | bytes 12296 | tf_op jit(solution)/shard_map/ppermute | solution.py:53
  71.4 4.5 %collective-permute-start.4 = (f32[8,128]{1,0:T(8,128)S(1)}, f32[8,128]{1,0:T(8,128)S(1)}, u32[]{:S(2)}, u32[]{:S(2)}) collective-permute-start(f32[8,128]{1,0:T(8,128)S(1)} %add.20), channel_id=1, source_target_pairs={{0,4},{2,6},{4,0},{6,2},{8,12},{10,14},{12,8},{14,10},{1,5},{3,7},... | collective-permute-start | bytes 12296 | tf_op jit(solution)/shard_map/ppermute | solution.py:53
  75.9 7.5 %collective-permute-start.5 = (f32[8,128]{1,0:T(8,128)S(1)}, f32[8,128]{1,0:T(8,128)S(1)}, u32[]{:S(2)}, u32[]{:S(2)}) collective-permute-start(f32[8,128]{1,0:T(8,128)S(1)} %add.21), channel_id=1, source_target_pairs={{0,8},{2,10},{4,12},{6,14},{8,0},{10,2},{12,4},{14,6},{1,9},{3,11}... | collective-permute-start | bytes 12296 | tf_op jit(solution)/shard_map/ppermute | solution.py:53
  87.7 40.1 %copy-start.2 = (f32[32,512]{1,0:T(8,128)S(1)}, f32[32,512]{1,0:T(8,128)}, u32[]{:S(2)}) copy-start(f32[32,512]{1,0:T(8,128)} %get-tuple-element.38.refs_9_) | copy-start | bytes 196612
  87.7 12.0 %collective-permute-start.6 = (f32[16,16,512]{2,1,0:T(8,128)S(1)}, f32[16,16,512]{2,1,0:T(8,128)S(1)}, u32[]{:S(2)}, u32[]{:S(2)}) collective-permute-start(f32[16,16,512]{2,1,0:T(8,128)S(1)} %get-tuple-element.42), channel_id=1, source_target_pairs={{1,2},{3,4},{5,6},{7,8},{9,10},{11,12},{13,14},{2,1},{4,3},{6,5},{... | collective-permute-start | bytes 1572872 | tf_op jit(solution)/shard_map/ppermute | solution.py:27
  89.8 9.9 %collective-permute-start.7 = (f32[16,16,512]{2,1,0:T(8,128)S(1)}, f32[16,16,512]{2,1,0:T(8,128)S(1)}, u32[]{:S(2)}, u32[]{:S(2)}) collective-permute-start(f32[16,16,512]{2,1,0:T(8,128)S(1)} %get-tuple-element.43), channel_id=1, source_target_pairs={{0,1},{1,0},{2,3},{3,2},{4,5},{5,4},{6,7},{7,6},{8,9},{9,8},{10,11... | collective-permute-start | bytes 1572872 | tf_op jit(solution)/shard_map/ppermute | solution.py:27
  97.7 11.0 %collective-permute-start.14 = (f32[16,16,512]{2,1,0:T(8,128)S(1)}, f32[16,16,512]{2,1,0:T(8,128)S(1)}, u32[]{:S(2)}, u32[]{:S(2)}) collective-permute-start(f32[16,16,512]{2,1,0:T(8,128)S(1)} %get-tuple-element.53), channel_id=1, source_target_pairs={{1,2},{3,4},{5,6},{7,8},{9,10},{11,12},{13,14},{2,1},{4,3},{6,5},{... | collective-permute-start | bytes 1572872 | tf_op jit(solution)/shard_map/ppermute | solution.py:27
  99.6 9.0 %collective-permute-start.15 = (f32[16,16,512]{2,1,0:T(8,128)S(1)}, f32[16,16,512]{2,1,0:T(8,128)S(1)}, u32[]{:S(2)}, u32[]{:S(2)}) collective-permute-start(f32[16,16,512]{2,1,0:T(8,128)S(1)} %get-tuple-element.54), channel_id=1, source_target_pairs={{0,1},{1,0},{2,3},{3,2},{4,5},{5,4},{6,7},{7,6},{8,9},{9,8},{10,11... | collective-permute-start | bytes 1572872 | tf_op jit(solution)/shard_map/ppermute | solution.py:27
  99.8 14.6 %collective-permute-start.8 = (f32[64,512]{1,0:T(8,128)S(1)}, f32[64,512]{1,0:T(8,128)S(1)}, u32[]{:S(2)}, u32[]{:S(2)}) collective-permute-start(f32[64,512]{1,0:T(8,128)S(1)} %get-tuple-element.44), channel_id=1, source_target_pairs={{0,128},{64,192},{128,0},{192,64},{1,129},{65,193},{129,1},{193,65... | collective-permute-start | bytes 393224 | tf_op jit(solution)/shard_map/ppermute | solution.py:34
  104.3 10.2 %collective-permute-start.9 = (f32[64,512]{1,0:T(8,128)S(1)}, f32[64,512]{1,0:T(8,128)S(1)}, u32[]{:S(2)}, u32[]{:S(2)}) collective-permute-start(f32[64,512]{1,0:T(8,128)S(1)} %get-tuple-element.45), channel_id=1, source_target_pairs={{0,64},{64,128},{128,192},{192,0},{1,65},{65,129},{129,193},{193,1... | collective-permute-start | bytes 393224 | tf_op jit(solution)/shard_map/ppermute | solution.py:34
  108.1 6.4 %collective-permute-start.10 = (f32[64,512]{1,0:T(8,128)S(1)}, f32[64,512]{1,0:T(8,128)S(1)}, u32[]{:S(2)}, u32[]{:S(2)}) collective-permute-start(f32[64,512]{1,0:T(8,128)S(1)} %get-tuple-element.46), channel_id=1, source_target_pairs={{0,192},{64,0},{128,64},{192,128},{1,193},{65,1},{129,65},{193,129... | collective-permute-start | bytes 393224 | tf_op jit(solution)/shard_map/ppermute | solution.py:34
  108.7 8.6 %collective-permute-start.16 = (f32[64,512]{1,0:T(8,128)S(1)}, f32[64,512]{1,0:T(8,128)S(1)}, u32[]{:S(2)}, u32[]{:S(2)}) collective-permute-start(f32[64,512]{1,0:T(8,128)S(1)} %get-tuple-element.55), channel_id=1, source_target_pairs={{0,32},{16,48},{32,0},{48,16},{1,33},{17,49},{33,1},{49,17},{2,34}... | collective-permute-start | bytes 393224 | tf_op jit(solution)/shard_map/ppermute | solution.py:34
  111.3 9.1 %collective-permute-start.17 = (f32[64,512]{1,0:T(8,128)S(1)}, f32[64,512]{1,0:T(8,128)S(1)}, u32[]{:S(2)}, u32[]{:S(2)}) collective-permute-start(f32[64,512]{1,0:T(8,128)S(1)} %get-tuple-element.56), channel_id=1, source_target_pairs={{0,16},{16,32},{32,48},{48,0},{1,17},{17,33},{33,49},{49,1},{2,18}... | collective-permute-start | bytes 393224 | tf_op jit(solution)/shard_map/ppermute | solution.py:34
  114.5 5.9 %collective-permute-start.18 = (f32[64,512]{1,0:T(8,128)S(1)}, f32[64,512]{1,0:T(8,128)S(1)}, u32[]{:S(2)}, u32[]{:S(2)}) collective-permute-start(f32[64,512]{1,0:T(8,128)S(1)} %get-tuple-element.57), channel_id=1, source_target_pairs={{0,48},{16,0},{32,16},{48,32},{1,49},{17,1},{33,17},{49,33},{2,50}... | collective-permute-start | bytes 393224 | tf_op jit(solution)/shard_map/ppermute | solution.py:34
  114.5 9.1 %collective-permute-start.11 = (f32[16,512]{1,0:T(8,128)S(1)}, f32[16,512]{1,0:T(8,128)S(1)}, u32[]{:S(2)}, u32[]{:S(2)}) collective-permute-start(f32[16,512]{1,0:T(8,128)S(1)} %get-tuple-element.48), channel_id=1, source_target_pairs={{0,32},{16,48},{32,0},{48,16},{1,33},{17,49},{33,1},{49,17},{2,34}... | collective-permute-start | bytes 98312 | tf_op jit(solution)/shard_map/ppermute | solution.py:34
  116.7 9.2 %collective-permute-start.12 = (f32[16,512]{1,0:T(8,128)S(1)}, f32[16,512]{1,0:T(8,128)S(1)}, u32[]{:S(2)}, u32[]{:S(2)}) collective-permute-start(f32[16,512]{1,0:T(8,128)S(1)} %get-tuple-element.49), channel_id=1, source_target_pairs={{0,16},{16,32},{32,48},{48,0},{1,17},{17,33},{33,49},{49,1},{2,18}... | collective-permute-start | bytes 98312 | tf_op jit(solution)/shard_map/ppermute | solution.py:34
  117.3 8.5 %collective-permute-start.13 = (f32[16,512]{1,0:T(8,128)S(1)}, f32[16,512]{1,0:T(8,128)S(1)}, u32[]{:S(2)}, u32[]{:S(2)}) collective-permute-start(f32[16,512]{1,0:T(8,128)S(1)} %get-tuple-element.50), channel_id=1, source_target_pairs={{0,48},{16,0},{32,16},{48,32},{1,49},{17,1},{33,17},{49,33},{2,50}... | collective-permute-start | bytes 98312 | tf_op jit(solution)/shard_map/ppermute | solution.py:34
  120.3 5.6 %collective-permute-start.19 = (f32[16,512]{1,0:T(8,128)S(1)}, f32[16,512]{1,0:T(8,128)S(1)}, u32[]{:S(2)}, u32[]{:S(2)}) collective-permute-start(f32[16,512]{1,0:T(8,128)S(1)} %get-tuple-element.59), channel_id=1, source_target_pairs={{0,128},{64,192},{128,0},{192,64},{1,129},{65,193},{129,1},{193,65... | collective-permute-start | bytes 98312 | tf_op jit(solution)/shard_map/ppermute | solution.py:34
  122.6 5.1 %collective-permute-start.20 = (f32[16,512]{1,0:T(8,128)S(1)}, f32[16,512]{1,0:T(8,128)S(1)}, u32[]{:S(2)}, u32[]{:S(2)}) collective-permute-start(f32[16,512]{1,0:T(8,128)S(1)} %get-tuple-element.60), channel_id=1, source_target_pairs={{0,64},{64,128},{128,192},{192,0},{1,65},{65,129},{129,193},{193,1... | collective-permute-start | bytes 98312 | tf_op jit(solution)/shard_map/ppermute | solution.py:34
  123.6 4.1 %collective-permute-start.21 = (f32[16,512]{1,0:T(8,128)S(1)}, f32[16,512]{1,0:T(8,128)S(1)}, u32[]{:S(2)}, u32[]{:S(2)}) collective-permute-start(f32[16,512]{1,0:T(8,128)S(1)} %get-tuple-element.61), channel_id=1, source_target_pairs={{0,192},{64,0},{128,64},{192,128},{1,193},{65,1},{129,65},{193,129... | collective-permute-start | bytes 98312 | tf_op jit(solution)/shard_map/ppermute | solution.py:34
